TPU v7x, 32 devices: a whole 2x2x4 slice. The times are simulated.
32 devices in a mesh: batch: 4 (over y, x), ctx: 4 (over z), wt: 2 (over core).
Axes of the slice: x: 2, y: 2, z: 4, core: 2. Of those that a mesh axis runs over, the one named last changes fastest.
Arguments:
- inputs: bfloat16 [8, 512, 768], P(('batch', 'wt'), 'ctx'), may hold values from -6 to 6
- prefix_keys: bfloat16 [8, 20, 768], P(('batch', 'wt')), may hold values from -8 to 8
- prefix_values: bfloat16 [8, 20, 768], P(('batch', 'wt')), may hold values from -6 to 6
- gain_attn: bfloat16 [768], P('wt'), may hold values from 0.099609375 to 1.8984375
- w_query: bfloat16 [768, 768], P('wt'), may hold values from -0.02734375 to 0.02734375
- w_key: bfloat16 [768, 768], P('wt'), may hold values from -0.21875 to 0.21875
- w_value: bfloat16 [768, 768], P('wt'), may hold values from -0.21875 to 0.21875
- w_out: bfloat16 [768, 768], P('wt'), may hold values from -2.5 to 2.5
- bias_table: bfloat16 [32, 12], P('wt'), may hold values from -5 to 5
- gain_ffn: bfloat16 [768], P('wt'), may hold values from 0.099609375 to 1.8984375
- w_in: bfloat16 [768, 3072], P('wt'), may hold values from -0.21875 to 0.21875
- w_back: bfloat16 [3072, 768], P('wt'), may hold values from -0.15625 to 0.15625
- buckets: int32 [1023], replicated, may hold values from 0 to 31
- out_grad: bfloat16 [8, 512, 768], P(('batch', 'wt'), 'ctx'), may hold values from -6 to 6
Outputs:
- outputs: bfloat16 [8, 512, 768], P(('batch', 'wt'), 'ctx')
- grad_inputs: bfloat16 [8, 512, 768], P(('batch', 'wt'), 'ctx')
- grad_prefix_keys: float32 [8, 20, 768], P(('batch', 'wt'))
- grad_prefix_values: float32 [8, 20, 768], P(('batch', 'wt'))
- grad_gain_attn: float32 [768], P('wt')
- grad_gain_ffn: float32 [768], P('wt')
- grad_bias_table: float32 [32, 12], P('wt')
- grad_query: float32 [768, 768], P('wt')
- grad_key: float32 [768, 768], P('wt')
- grad_value: float32 [768, 768], P('wt')
- grad_out: float32 [768, 768], P('wt')
- grad_in: float32 [768, 3072], P('wt')
- grad_back: float32 [3072, 768], P('wt')
All inputs are finite; a program needn't handle non-finite values.
Results may differ from a plain program's by a relative error of at most 0.028.
Values may be sent and summed in bfloat16 or wider, within the bound.
No kernel may reach another device: no remote copies, remote signals or barrier semaphores. Data moves between devices by JAX's collectives and lax.ppermute only.
A program may use at most 128 MiB of HBM per device.

v0:
```python
import jax
import jax.numpy as jnp
from jax import lax
from jax.sharding import PartitionSpec as P

KB = 256


EPS = 1e-06


def times_t(left, right):
    return lax.dot_general(
        left, right, (((1,), (1,)), ((), ())), preferred_element_type=jnp.float32
    )


def t_times(left, right):
    return lax.dot_general(
        left, right, (((0,), (0,)), ((), ())), preferred_element_type=jnp.float32
    )


def norm_parts(values):
    inverse = lax.rsqrt(jnp.mean(values * values, axis=-1, keepdims=True) + EPS)
    return (values * inverse, inverse)


def norm_back(grad_norm, gain, scaled, inverse):
    grad_scaled = grad_norm * gain
    return inverse * (grad_scaled - scaled * jnp.mean(grad_scaled * scaled, axis=-1, keepdims=True))


def smooth_act(values):
    return jax.nn.gelu(values, approximate=True)


def shards(
    inputs,
    prefix_keys,
    prefix_values,
    gain_attn,
    w_query,
    w_key,
    w_value,
    w_out,
    bias_table,
    gain_ffn,
    w_in,
    w_back,
    buckets,
    out_grad,
):
    wq, wk, wv, wo, gain_one, table = (
        lax.all_gather(w_query, "wt", axis=0, tiled=True),
        lax.all_gather(w_key, "wt", axis=0, tiled=True),
        lax.all_gather(w_value, "wt", axis=0, tiled=True),
        lax.all_gather(w_out, "wt", axis=0, tiled=True),
        lax.all_gather(gain_attn, "wt", axis=0, tiled=True),
        lax.all_gather(bias_table, "wt", axis=0, tiled=True),
    )
    w_first, w_second, gain_two = (
        lax.all_gather(w_in, "wt", axis=0, tiled=True),
        lax.all_gather(w_back, "wt", axis=0, tiled=True),
        lax.all_gather(gain_ffn, "wt", axis=0, tiled=True),
    )
    tokens = inputs[0].astype(jnp.float32)
    rows, width = tokens.shape
    heads = table.shape[1]
    nbuck = table.shape[0]
    hsize = width // heads
    memory = prefix_keys.shape[1]
    keys_mem = prefix_keys[0].reshape(memory, heads, hsize)
    vals_mem = prefix_values[0].reshape(memory, heads, hsize)
    scaled1, inverse1 = norm_parts(tokens)
    normed1 = (scaled1 * gain_one.astype(jnp.float32)).astype(jnp.bfloat16)
    query = jnp.dot(normed1, wq, preferred_element_type=jnp.float32).astype(jnp.bfloat16)
    keys = jnp.dot(normed1, wk, preferred_element_type=jnp.float32).astype(jnp.bfloat16)
    vals = jnp.dot(normed1, wv, preferred_element_type=jnp.float32).astype(jnp.bfloat16)
    key_full, value_full = (
        lax.all_gather(keys, "ctx", axis=0, tiled=True),
        lax.all_gather(vals, "ctx", axis=0, tiled=True),
    )
    length = key_full.shape[0]
    starts = jnp.arange(length // KB, dtype=jnp.int32) * KB
    bucket_range = jnp.arange(nbuck, dtype=jnp.int32)
    positions = lax.axis_index("ctx") * rows + jnp.arange(rows, dtype=jnp.int32)
    qheads = query.reshape(rows, heads, hsize)

    def scores_at(start, key_all):
        key_block = lax.dynamic_slice_in_dim(key_all, start, KB, 0).reshape(KB, heads, hsize)
        cols = start + jnp.arange(KB, dtype=jnp.int32)
        where = cols[None, :] - positions[:, None] + (length - 1)
        bucket_ids = buckets[where]
        bucket_map = (bucket_ids[:, :, None] == bucket_range[None, None, :]).astype(jnp.bfloat16)
        bias = jnp.einsum("qkb,bh->hqk", bucket_map, table, preferred_element_type=jnp.float32)
        raw = jnp.einsum("qhd,khd->hqk", qheads, key_block, preferred_element_type=jnp.float32)
        return (raw + bias, bucket_map, key_block)

    mem_scores = jnp.einsum("qhd,khd->hqk", qheads, keys_mem, preferred_element_type=jnp.float32)
    top_start = jnp.max(mem_scores, axis=2)
    total_start = jnp.sum(jnp.exp(mem_scores - top_start[:, :, None]), axis=2)

    def stat_step(carry, start):
        top, total = carry
        block, _, _ = scores_at(start, key_full)
        new_top = jnp.maximum(top, jnp.max(block, axis=2))
        total = total * jnp.exp(top - new_top) + jnp.sum(
            jnp.exp(block - new_top[:, :, None]), axis=2
        )
        return ((new_top, total), None)

    (top, total), _ = lax.scan(stat_step, (top_start, total_start), starts)
    mem_prob = jnp.exp(mem_scores - top[:, :, None]) / total[:, :, None]
    mem_low = mem_prob.astype(jnp.bfloat16)
    mixed_start = jnp.einsum("hqk,khd->qhd", mem_low, vals_mem, preferred_element_type=jnp.float32)

    def out_step(acc, start):
        block, _, _ = scores_at(start, key_full)
        prob = (jnp.exp(block - top[:, :, None]) / total[:, :, None]).astype(jnp.bfloat16)
        value_block = lax.dynamic_slice_in_dim(value_full, start, KB, 0).reshape(KB, heads, hsize)
        return (
            acc + jnp.einsum("hqk,khd->qhd", prob, value_block, preferred_element_type=jnp.float32),
            None,
        )

    mixed, _ = lax.scan(out_step, mixed_start, starts)
    attended = mixed.reshape(rows, width).astype(jnp.bfloat16)
    hidden = tokens + jnp.dot(attended, wo, preferred_element_type=jnp.float32)
    scaled2, inverse2 = norm_parts(hidden)
    normed2 = (scaled2 * gain_two.astype(jnp.float32)).astype(jnp.bfloat16)
    inner = jnp.dot(normed2, w_first, preferred_element_type=jnp.float32)
    act_value, act_pull = jax.vjp(smooth_act, inner)
    act_out = act_value.astype(jnp.bfloat16)
    result = hidden + jnp.dot(act_out, w_second, preferred_element_type=jnp.float32)
    wq, wk, wv, wo, gain_one = (
        lax.all_gather(w_query, "wt", axis=0, tiled=True),
        lax.all_gather(w_key, "wt", axis=0, tiled=True),
        lax.all_gather(w_value, "wt", axis=0, tiled=True),
        lax.all_gather(w_out, "wt", axis=0, tiled=True),
        lax.all_gather(gain_attn, "wt", axis=0, tiled=True),
    )
    w_first, w_second, gain_two = (
        lax.all_gather(w_in, "wt", axis=0, tiled=True),
        lax.all_gather(w_back, "wt", axis=0, tiled=True),
        lax.all_gather(gain_ffn, "wt", axis=0, tiled=True),
    )
    key_back, value_back = (
        lax.all_gather(keys, "ctx", axis=0, tiled=True),
        lax.all_gather(vals, "ctx", axis=0, tiled=True),
    )
    cotangent = out_grad[0]
    grad_second = t_times(act_out, cotangent)
    grad_act = times_t(cotangent, w_second).astype(jnp.bfloat16)
    grad_inner = act_pull(grad_act.astype(jnp.float32))[0].astype(jnp.bfloat16)
    grad_first = t_times(normed2, grad_inner)
    grad_normed2 = times_t(grad_inner, w_first)
    grad_gain_two = jnp.sum(grad_normed2 * scaled2, axis=0)
    grad_hidden = cotangent.astype(jnp.float32) + norm_back(
        grad_normed2, gain_two.astype(jnp.float32), scaled2, inverse2
    )
    part_first, part_second, part_gain_two = (
        lax.psum_scatter(
            grad_first.astype(jnp.bfloat16), "wt", scatter_dimension=0, tiled=True
        ).astype(jnp.float32),
        lax.psum_scatter(
            grad_second.astype(jnp.bfloat16), "wt", scatter_dimension=0, tiled=True
        ).astype(jnp.float32),
        lax.psum_scatter(
            grad_gain_two.astype(jnp.bfloat16), "wt", scatter_dimension=0, tiled=True
        ).astype(jnp.float32),
    )
    grad_branch = grad_hidden.astype(jnp.bfloat16)
    grad_wo = t_times(attended, grad_branch)
    grad_mixed = times_t(grad_branch, wo).astype(jnp.bfloat16).reshape(rows, heads, hsize)
    spread = jnp.einsum("qhd,qhd->hq", grad_mixed.astype(jnp.float32), mixed)
    mem_dprob = jnp.einsum("qhd,khd->hqk", grad_mixed, vals_mem, preferred_element_type=jnp.float32)
    mem_dscore = (mem_prob * (mem_dprob - spread[:, :, None])).astype(jnp.bfloat16)
    grad_q_start = jnp.einsum(
        "hqk,khd->qhd", mem_dscore, keys_mem, preferred_element_type=jnp.float32
    )
    grad_mem_keys = jnp.einsum(
        "hqk,qhd->khd", mem_dscore, qheads, preferred_element_type=jnp.float32
    ).reshape(memory, width)
    grad_mem_values = jnp.einsum(
        "hqk,qhd->khd", mem_low, grad_mixed, preferred_element_type=jnp.float32
    ).reshape(memory, width)

    def grad_step(carry, start):
        grad_q, table_acc = carry
        block, bucket_map, key_block = scores_at(start, key_back)
        prob = jnp.exp(block - top[:, :, None]) / total[:, :, None]
        value_block = lax.dynamic_slice_in_dim(value_back, start, KB, 0).reshape(KB, heads, hsize)
        grad_prob = jnp.einsum(
            "qhd,khd->hqk", grad_mixed, value_block, preferred_element_type=jnp.float32
        )
        grad_score = (prob * (grad_prob - spread[:, :, None])).astype(jnp.bfloat16)
        grad_q = grad_q + jnp.einsum(
            "hqk,khd->qhd", grad_score, key_block, preferred_element_type=jnp.float32
        )
        grad_kblock = jnp.einsum(
            "hqk,qhd->khd", grad_score, qheads, preferred_element_type=jnp.float32
        ).reshape(KB, width)
        grad_vblock = jnp.einsum(
            "hqk,qhd->khd",
            prob.astype(jnp.bfloat16),
            grad_mixed,
            preferred_element_type=jnp.float32,
        ).reshape(KB, width)
        table_acc = table_acc + jnp.einsum(
            "hqk,qkb->bh", grad_score, bucket_map, preferred_element_type=jnp.float32
        )
        return ((grad_q, table_acc), (grad_kblock, grad_vblock))

    zero_table = jnp.zeros((nbuck, heads), jnp.float32)
    (grad_q, grad_table), (grad_kblocks, grad_vblocks) = lax.scan(
        grad_step, (grad_q_start, zero_table), starts
    )
    grad_key_all = grad_kblocks.reshape(length, width)
    grad_value_all = grad_vblocks.reshape(length, width)
    grad_key_own, grad_value_own = (
        lax.psum_scatter(
            grad_key_all.astype(jnp.bfloat16), "ctx", scatter_dimension=0, tiled=True
        ).astype(jnp.float32),
        lax.psum_scatter(
            grad_value_all.astype(jnp.bfloat16), "ctx", scatter_dimension=0, tiled=True
        ).astype(jnp.float32),
    )
    mem_key_total, mem_value_total = (
        lax.psum(grad_mem_keys.astype(jnp.bfloat16), "ctx").astype(jnp.float32),
        lax.psum(grad_mem_values.astype(jnp.bfloat16), "ctx").astype(jnp.float32),
    )
    grad_q_low = grad_q.reshape(rows, width).astype(jnp.bfloat16)
    grad_k_low = grad_key_own.astype(jnp.bfloat16)
    grad_v_low = grad_value_own.astype(jnp.bfloat16)
    grad_wq = t_times(normed1, grad_q_low)
    grad_wk = t_times(normed1, grad_k_low)
    grad_wv = t_times(normed1, grad_v_low)
    grad_normed1 = times_t(grad_q_low, wq) + times_t(grad_k_low, wk) + times_t(grad_v_low, wv)
    grad_gain_one = jnp.sum(grad_normed1 * scaled1, axis=0)
    grad_tokens = grad_hidden + norm_back(
        grad_normed1, gain_one.astype(jnp.float32), scaled1, inverse1
    )
    part_wq, part_wk, part_wv, part_wo, part_gain_one, part_table = (
        lax.psum_scatter(
            grad_wq.astype(jnp.bfloat16), "wt", scatter_dimension=0, tiled=True
        ).astype(jnp.float32),
        lax.psum_scatter(
            grad_wk.astype(jnp.bfloat16), "wt", scatter_dimension=0, tiled=True
        ).astype(jnp.float32),
        lax.psum_scatter(
            grad_wv.astype(jnp.bfloat16), "wt", scatter_dimension=0, tiled=True
        ).astype(jnp.float32),
        lax.psum_scatter(
            grad_wo.astype(jnp.bfloat16), "wt", scatter_dimension=0, tiled=True
        ).astype(jnp.float32),
        lax.psum_scatter(
            grad_gain_one.astype(jnp.bfloat16), "wt", scatter_dimension=0, tiled=True
        ).astype(jnp.float32),
        lax.psum_scatter(
            grad_table.astype(jnp.bfloat16), "wt", scatter_dimension=0, tiled=True
        ).astype(jnp.float32),
    )
    sums = (
        lax.psum(part_wq.astype(jnp.bfloat16), ("batch", "ctx")).astype(jnp.float32),
        lax.psum(part_wk.astype(jnp.bfloat16), ("batch", "ctx")).astype(jnp.float32),
        lax.psum(part_wv.astype(jnp.bfloat16), ("batch", "ctx")).astype(jnp.float32),
        lax.psum(part_wo.astype(jnp.bfloat16), ("batch", "ctx")).astype(jnp.float32),
        lax.psum(part_gain_one.astype(jnp.bfloat16), ("batch", "ctx")).astype(jnp.float32),
        lax.psum(part_table.astype(jnp.bfloat16), ("batch", "ctx")).astype(jnp.float32),
        lax.psum(part_first.astype(jnp.bfloat16), ("batch", "ctx")).astype(jnp.float32),
        lax.psum(part_second.astype(jnp.bfloat16), ("batch", "ctx")).astype(jnp.float32),
        lax.psum(part_gain_two.astype(jnp.bfloat16), ("batch", "ctx")).astype(jnp.float32),
    )
    return (
        result.astype(jnp.bfloat16)[None],
        grad_tokens.astype(jnp.bfloat16)[None],
        mem_key_total[None],
        mem_value_total[None],
        sums[4],
        sums[8],
        sums[5],
        sums[0],
        sums[1],
        sums[2],
        sums[3],
        sums[6],
        sums[7],
    )


def solution(mesh):
    in_specs = (
        P(("batch", "wt"), "ctx", None),
        P(("batch", "wt"), None, None),
        P(("batch", "wt"), None, None),
        P("wt"),
        P("wt", None),
        P("wt", None),
        P("wt", None),
        P("wt", None),
        P("wt", None),
        P("wt"),
        P("wt", None),
        P("wt", None),
        P(),
        P(("batch", "wt"), "ctx", None),
    )
    out_specs = (
        P(("batch", "wt"), "ctx", None),
        P(("batch", "wt"), "ctx", None),
        P(("batch", "wt"), None, None),
        P(("batch", "wt"), None, None),
        P("wt"),
        P("wt"),
        P("wt", None),
        P("wt", None),
        P("wt", None),
        P("wt", None),
        P("wt", None),
        P("wt", None),
        P("wt", None),
    )
    return jax.shard_map(shards, mesh=mesh, in_specs=in_specs, out_specs=out_specs, check_vma=False)
```

profile of v0, /device:TPU:0, one launch (start us, length us, event | category | flops | bytes accessed | tf_op | source)
XLA Modules:
  0.0 1362.5 jit_solution(13265489076617069256)
XLA Ops:
  24.0 9.5 all-gather.11.cloned.1.call-done
  35.2 19.8 %all_gather.46 = bf16[512,768]{1,0:T(8,128)(2,1)S(1)} all-gather(bf16[128,768]{1,0:T(8,128)(2,1)S(1)} %convolution_convert_fusion.9), channel_id=1, replica_groups=mesh['batch'=4,'ctx'=4,'wt'=2] {'ctx'}, dimensions={0}, use_global_device_ids=true | all-gather | bytes 983040 | tf_op jit(solution)/shard_map/all_gather | solution.py:81
  58.3 283.1 %while.47 = (s32[]{:T(128)}, f32[12,128]{1,0:T(8,128)}, f32[12,128]{1,0:T(8,128)}, s32[2]{0:T(128)S(1)}, bf16[512,768]{0,1:T(8,128)(2,1)S(1)}, /*index=5*/bf16[1...) while((s32[]{:T(128)}, f32[12,128]{1,0:T(8,128)}, ...), condition=%wide.region_6.7_spmd.clone, body=%wide.region_3.6_spmd.clone.sunk | while | flops 78318976 | bytes 12339127 | solution.py:113
  59.8 130.0 %gather_fusion = s32[32768]{0:T(1024)S(1)} fusion(s32[1023]{0:T(1024)S(1)} %get-tuple-element.1205, s32[32768]{0:T(1024)S(1)} %broadcast_clamp_fusion.6), kind=kCustom, calls=%fused_computation.clone.clone.1 | custom fusion | bytes 393216 | tf_op jit(solution)/shard_map/while/body/eval_jaxpr/gather | solution.py:94
  201.3 130.0 %gather_fusion = s32[32768]{0:T(1024)S(1)} fusion(s32[1023]{0:T(1024)S(1)} %get-tuple-element.1205, s32[32768]{0:T(1024)S(1)} %broadcast_clamp_fusion.6), kind=kCustom, calls=%fused_computation.clone.clone.1 | custom fusion | bytes 393216 | tf_op jit(solution)/shard_map/while/body/eval_jaxpr/gather | solution.py:94
  343.1 18.4 %all_gather.49 = bf16[512,768]{1,0:T(8,128)(2,1)S(1)} all-gather(bf16[128,768]{1,0:T(8,128)(2,1)S(1)} %convolution_convert_fusion.8), channel_id=1, replica_groups=mesh['batch'=4,'ctx'=4,'wt'=2] {'ctx'}, dimensions={0}, use_global_device_ids=true | all-gather | bytes 983040 | tf_op jit(solution)/shard_map/all_gather | solution.py:82
  364.4 284.0 %while.48 = (s32[]{:T(128)}, f32[128,12,64]{0,2,1:T(8,128)}, s32[2]{0:T(128)S(1)}, bf16[512,768]{0,1:T(8,128)(2,1)}, bf16[512,768]{0,1:T(8,128)(2,1)S(1)}, /*ind...) while((s32[]{:T(128)}, f32[128,12,64]{0,2,1:T(8,128)}, ...), condition=%wide.region_8.9_spmd.clone, body=%wide.region_7.8_spmd.clone.sunk | while | flops 128745856 | bytes 12664803 | solution.py:127
  370.1 130.0 %gather_fusion.1 = s32[32768]{0:T(1024)S(1)} fusion(s32[1023]{0:T(1024)S(1)} %get-tuple-element.1245, s32[32768]{0:T(1024)S(1)} %broadcast_clamp_fusion.7), kind=kCustom, calls=%fused_computation.1.clone.clone.1 | custom fusion | bytes 393216 | tf_op jit(solution)/shard_map/while/body/eval_jaxpr/gather | solution.py:94
  512.1 130.0 %gather_fusion.1 = s32[32768]{0:T(1024)S(1)} fusion(s32[1023]{0:T(1024)S(1)} %get-tuple-element.1245, s32[32768]{0:T(1024)S(1)} %broadcast_clamp_fusion.7), kind=kCustom, calls=%fused_computation.1.clone.clone.1 | custom fusion | bytes 393216 | tf_op jit(solution)/shard_map/while/body/eval_jaxpr/gather | solution.py:94
  654.7 4.8 fusion.52
  668.4 294.8 %while.49 = (s32[]{:T(128)}, f32[128,12,64]{0,2,1:T(8,128)}, f32[32,12]{0,1:T(8,128)S(1)}, bf16[2,256,768]{2,1,0:T(8,128)(2,1)}, bf16[2,256,768]{2,1,0:T(8,128)(...) while((s32[]{:T(128)}, f32[128,12,64]{0,2,1:T(8,128)}, ...), condition=%wide.region_12.13_spmd.clone, body=%wide.region_11.12_spmd.clone.sunk | while | flops 307135616 | bytes 21652508 | solution.py:216
  672.0 130.0 %gather_fusion.2 = s32[32768]{0:T(1024)S(1)} fusion(s32[1023]{0:T(1024)S(1)} %get-tuple-element.1299, s32[32768]{0:T(1024)S(1)} %broadcast_clamp_fusion.8), kind=kCustom, calls=%fused_computation.2.clone.clone.1 | custom fusion | bytes 393216 | tf_op jit(solution)/shard_map/while/body/eval_jaxpr/gather | solution.py:94
  819.4 130.0 %gather_fusion.2 = s32[32768]{0:T(1024)S(1)} fusion(s32[1023]{0:T(1024)S(1)} %get-tuple-element.1299, s32[32768]{0:T(1024)S(1)} %broadcast_clamp_fusion.8), kind=kCustom, calls=%fused_computation.2.clone.clone.1 | custom fusion | bytes 393216 | tf_op jit(solution)/shard_map/while/body/eval_jaxpr/gather | solution.py:94
  968.4 17.5 %reduce-scatter.12.cloned.1.call-done = bf16[128,768]{1,0:T(8,128)(2,1)} async-done(((bf16[512,768]{1,0:T(8,128)(2,1)}), bf16[128,768]{1,0:T(8,128)(2,1)}) %reduce-scatter.12.cloned.1.call-update) | async-done | bytes 196624 | tf_op jit(solution)/shard_map/reduce_scatter | solution.py:222
  988.6 22.8 %reduce-scatter.14.cloned.1.call-done = bf16[128,768]{1,0:T(8,128)(2,1)} async-done(((bf16[512,768]{1,0:T(8,128)(2,1)}), bf16[128,768]{1,0:T(8,128)(2,1)}) %reduce-scatter.14.cloned.1.call-update) | async-done | bytes 196624 | tf_op jit(solution)/shard_map/reduce_scatter | solution.py:225
  1023.8 11.0 reduce-scatter.22.cloned.1.call-done
  1034.8 12.7 reduce-scatter.18.cloned.1.call-done
  1047.6 12.6 reduce-scatter.20.cloned.1.call-done
  1060.2 16.7 %reduce-scatter.24.cloned.1.call-done = bf16[384,3072]{1,0:T(8,128)(2,1)} async-done(((bf16[768,3072]{1,0:T(8,128)(2,1)}), bf16[384,3072]{1,0:T(8,128)(2,1)}) %reduce-scatter.24.cloned.1.call-update) | async-done | bytes 2359312 | tf_op jit(solution)/shard_map/reduce_scatter | solution.py:163
  1076.9 16.6 %reduce-scatter.26.cloned.1.call-done = bf16[1536,768]{1,0:T(8,128)(2,1)} async-done(((bf16[3072,768]{1,0:T(8,128)(2,1)}), bf16[1536,768]{1,0:T(8,128)(2,1)}) %reduce-scatter.26.cloned.1.call-update) | async-done | bytes 2359312 | tf_op jit(solution)/shard_map/reduce_scatter | solution.py:166
  1098.1 20.5 %all-reduce.4 = (bf16[1,20,768]{2,1,0:T(8,128)(2,1)S(1)}, bf16[1,20,768]{2,1,0:T(8,128)(2,1)S(1)}) all-reduce(bf16[1,20,768]{2,1,0:T(8,128)(2,1)S(1)} %broadcast_in_dim.44, bf16[1,20,768]{2,1,0:T(8,128)(2,1)S(1)} %broadcast_in_dim.55), channel_id=1, replica_groups=mesh['batch'=4,'ctx'=4,'wt'=2] {'ctx'}, use_global_device_ids=true, to_apply=%region_16.17 | all-reduce | flops 30720 | bytes 122880 | tf_op jit(solution)/shard_map/psum | solution.py:230
  1121.8 4.1 fusion.54
  1131.9 42.3 %all-reduce.2 = (bf16[16,12]{0,1:T(8,128)(2,1)S(1)}, bf16[384]{0:T(512)(128)(2,1)S(1)}, bf16[384]{0:T(512)(128)(2,1)S(1)}) all-reduce(bf16[16,12]{0,1:T(8,128)(2,1)S(1)} %copy.182, bf16[384]{0:T(512)(128)(2,1)S(1)} %dynamic-slice.1, bf16[384]{0:T(512)(128)(2,1)S(1)} %dynamic-slice.3), channel_id=1, replica_groups=mesh['batch'=4,'ctx'=4,'wt'=2] {'batch','ctx'}, use_global_device_ids=true, to_apply=%region_25.26 | all-reduce | flops 960 | bytes 3840 | tf_op jit(solution)/shard_map/psum | solution.py:270
  1176.9 168.2 %all-reduce.8.cloned.1.call-done = (bf16[384,768]{1,0:T(8,128)(2,1)}, bf16[384,768]{1,0:T(8,128)(2,1)}, bf16[384,768]{1,0:T(8,128)(2,1)}, bf16[384,768]{1,0:T(8,...) async-done(((bf16[384,768]{1,0:T(8,128)(2,1)}, bf16[384,768]{1,0:T(8,128)(2,1)}, bf16[384,768]{1,0:T(8,128)(2,1)}, bf16[384,768]{1,0:T(8,128)(2,1)}, ...) | async-done | bytes 7077904 | tf_op jit(solution)/shard_map/psum | solution.py:265
  (326 shorter events, 157.0 us)
Async XLA Ops:
  7.2 14.3 %all-gather.9.cloned.1.call-start = ((), (), s32[]{:S(2)}) async-start(), calls=%async_computation.9 | async-start | bytes 1769472 | tf_op jit(solution)/shard_map/all_gather | solution.py:55
  7.9 25.6 %all-gather.11.cloned.1.call-start = ((), (), s32[]{:S(2)}) async-start(), calls=%async_computation.10 | async-start | bytes 1769472 | tf_op jit(solution)/shard_map/all_gather | solution.py:56
  8.7 332.8 %all-gather.13.cloned.1.call-start = ((), (), s32[]{:S(2)}) async-start(), calls=%async_computation.11 | async-start | bytes 1769472 | tf_op jit(solution)/shard_map/all_gather | solution.py:57
  9.4 640.1 %all-gather.15.cloned.1.call-start = ((), (), s32[]{:S(2)}) async-start(), calls=%async_computation.12 | async-start | bytes 1769472 | tf_op jit(solution)/shard_map/all_gather | solution.py:58
  10.0 641.4 %all-gather.17.cloned.1.call-start = ((), (), s32[]{:S(2)}) async-start(), calls=%async_computation.13 | async-start | bytes 7077888 | tf_op jit(solution)/shard_map/all_gather | solution.py:63
  10.6 644.0 %all-gather.19.cloned.1.call-start = ((), (), s32[]{:S(2)}) async-start(), calls=%async_computation.14 | async-start | bytes 7077888 | tf_op jit(solution)/shard_map/all_gather | solution.py:64
  11.2 974.7 %reduce-scatter.12.cloned.1.call-start = ((), (), s32[]{:S(2)}) async-start(), calls=%async_computation.15 | async-start | bytes 983040 | tf_op jit(solution)/shard_map/reduce_scatter | solution.py:222
  14.3 40.9 %copy-start.27 = (bf16[20,12,64]{2,1,0:T(8,128)(2,1)}, bf16[20,12,64]{2,1,0:T(8,128)(2,1)S(1)}, u32[]{:S(2)}) copy-start(bf16[20,12,64]{2,1,0:T(8,128)(2,1)S(1)} %reshape_squeeze.6) | copy-start | bytes 92164
  58.3 283.1 %copy-start.2 = (bf16[1,128,768]{2,1,0:T(8,128)(2,1)S(1)}, bf16[1,128,768]{2,1,0:T(8,128)(2,1)}, u32[]{:S(2)}) copy-start(bf16[1,128,768]{2,1,0:T(8,128)(2,1)} %param.20) | copy-start | bytes 589828
  58.3 283.1 %copy-start.37 = (f32[768]{0:T(1024)S(1)}, f32[768]{0:T(1024)}, u32[]{:S(2)}) copy-start(f32[768]{0:T(1024)} %copy-done.36) | copy-start | bytes 9220
  58.3 283.1 %copy-start.48 = (f32[128]{0:T(128)S(1)}, f32[128]{0:T(128)}, u32[]{:S(2)}) copy-start(f32[128]{0:T(128)} %copy-done.47) | copy-start | bytes 1540
  364.4 285.1 %copy-start.3 = (bf16[1,128,768]{2,1,0:T(8,128)(2,1)S(1)}, bf16[1,128,768]{2,1,0:T(8,128)(2,1)}, u32[]{:S(2)}) copy-start(bf16[1,128,768]{2,1,0:T(8,128)(2,1)} %param.20) | copy-start | bytes 589828
  963.3 48.2 %reduce-scatter.14.cloned.1.call-start = ((), (), s32[]{:S(2)}) async-start(), calls=%async_computation.16 | async-start | bytes 983040 | tf_op jit(solution)/shard_map/reduce_scatter | solution.py:225
  964.0 59.8 %reduce-scatter.16.cloned.1.call-start = ((), (), s32[]{:S(2)}) async-start(), calls=%async_computation.17 | async-start | bytes 1769472 | tf_op jit(solution)/shard_map/reduce_scatter | solution.py:245
  966.8 68.0 %reduce-scatter.22.cloned.1.call-start = ((), (), s32[]{:S(2)}) async-start(), calls=%async_computation.20 | async-start | bytes 1769472 | tf_op jit(solution)/shard_map/reduce_scatter | solution.py:254
  968.4 79.2 %reduce-scatter.18.cloned.1.call-start = ((), (), s32[]{:S(2)}) async-start(), calls=%async_computation.18 | async-start | bytes 1769472 | tf_op jit(solution)/shard_map/reduce_scatter | solution.py:248
  988.5 25.5 %copy-start.8 = (f32[128,768]{1,0:T(8,128)S(1)}, f32[128,768]{1,0:T(8,128)}, u32[]{:S(2)}) copy-start(f32[128,768]{1,0:T(8,128)} %copy-done.7) | copy-start | bytes 1179652
  988.5 25.5 %copy-start.17 = (bf16[128,3072]{1,0:T(8,128)(2,1)S(1)}, bf16[128,3072]{1,0:T(8,128)(2,1)}, u32[]{:S(2)}) copy-start(bf16[128,3072]{1,0:T(8,128)(2,1)} %copy-done.16) | copy-start | bytes 2359300
  988.5 25.5 %copy-start.42 = (f32[768]{0:T(1024)S(1)}, f32[768]{0:T(1024)}, u32[]{:S(2)}) copy-start(f32[768]{0:T(1024)} %reshape.356) | copy-start | bytes 9220
  988.5 71.7 %reduce-scatter.20.cloned.1.call-start = ((), (), s32[]{:S(2)}) async-start(), calls=%async_computation.19 | async-start | bytes 1769472 | tf_op jit(solution)/shard_map/reduce_scatter | solution.py:251
  1014.0 63.0 %reduce-scatter.24.cloned.1.call-start = ((), (), s32[]{:S(2)}) async-start(), calls=%async_computation.21 | async-start | bytes 7077888 | tf_op jit(solution)/shard_map/reduce_scatter | solution.py:163
  1017.7 75.8 %reduce-scatter.26.cloned.1.call-start = ((), (), s32[]{:S(2)}) async-start(), calls=%async_computation.22 | async-start | bytes 7077888 | tf_op jit(solution)/shard_map/reduce_scatter | solution.py:166
  1023.0 102.9 %reduce-scatter.28.cloned.1.call-start = ((), (), s32[]{:S(2)}) async-start(), calls=%async_computation.23 | async-start | bytes 12288
  1023.7 321.3 %all-reduce.8.cloned.1.call-start = ((), (), s32[]{:S(2)}) async-start(), calls=%async_computation.24 | async-start | bytes 14155776 | tf_op jit(solution)/shard_map/psum | solution.py:265
  (52 other events, 262.4 us)
Sparse Core Ops, SparseCore 0:
  9.6 11.9 all-gather.8
  23.1 10.3 all-gather.10
  35.0 10.3 all-gather.12
  46.9 10.3 all-gather.14
  58.7 15.5 all-gather.16
  75.7 15.6 all-gather.18
  963.4 22.5 reduce-scatter.11
  988.8 22.5 reduce-scatter.13
  1014.2 7.9 reduce-scatter.15
  1025.0 9.8 reduce-scatter.21
  1037.7 9.8 reduce-scatter.17
  1050.3 9.8 reduce-scatter.19
  1063.1 13.7 reduce-scatter.23
  1079.7 13.7 reduce-scatter.25
  1095.6 8.5 reduce-scatter.27
  1110.5 234.5 all-reduce.7
where the time goes:
time: 1360 us
  local copies, waits for them, and re-layouts  816 us (60%)
  waiting for transfers between devices  295 us (22%)
  blocking collectives  109 us (8%)
  matrix products  87.6 us (6%)
  other arithmetic  27.3 us (2%)
  between operations  15.4 us (1%)
    gather x14, local copies, waits for them, and re-layouts, scores_at(): bucket_ids = buckets[where]  781 us
    psum x1, waiting for transfers between devices, shards(): lax.psum(part_wq.astype(jnp.bfloat16), ('batch', 'ctx')).astype(jnp.float32)  168 us
    psum x1, blocking collectives, shards(): lax.psum(part_table.astype(jnp.bfloat16), ('batch', 'ctx'))  42.3 us
  transfers between devices with their start and end apart: 16, of which 10 were waited for; matrix products, arithmetic and copies ran while one was open for 45% of the time, Pallas kernels for 0%

commit v1 on v0

v1 whole, which is shorter than its diff:
```python
import functools

import jax
import jax.numpy as jnp
from jax import lax
from jax.experimental import pallas as pl
from jax.experimental.pallas import tpu as pltpu
from jax.sharding import PartitionSpec as P

EPS = 1e-06
F32 = jnp.float32
BF = jnp.bfloat16
LANES = 128


def nn(left, right):
    return lax.dot_general(left, right, (((1,), (0,)), ((), ())), preferred_element_type=F32)


def nt(left, right):
    return lax.dot_general(left, right, (((1,), (1,)), ((), ())), preferred_element_type=F32)


def tn(left, right):
    return lax.dot_general(left, right, (((0,), (0,)), ((), ())), preferred_element_type=F32)


def vmem(count):
    return [pl.BlockSpec(memory_space=pltpu.VMEM)] * count


def smem():
    return pl.BlockSpec(memory_space=pltpu.SMEM)


def shape(dims, kind):
    return jax.ShapeDtypeStruct(dims, kind)


def params(mib):
    return pltpu.CompilerParams(vmem_limit_bytes=mib << 20)


def flip(value, axis, size, step):
    return lax.ppermute(value, axis, [(i, i ^ step) for i in range(size)])


def gather_flip(value, axis, size):
    return [value] + [flip(value, axis, size, step) for step in range(1, size)]


def canonical(parts, index):
    whole = jnp.zeros((len(parts),) + parts[0].shape, parts[0].dtype)
    for step, part in enumerate(parts):
        whole = lax.dynamic_update_index_in_dim(whole, part, index ^ step, 0)
    return whole


def gather_wt(value, size):
    if size == 2:
        own = lax.axis_index("wt") == 0
        other = flip(value, "wt", 2, 1)
        return jnp.stack([jnp.where(own, value, other), jnp.where(own, other, value)])
    return lax.all_gather(value, "wt", axis=0)


def sum_wt(value, size):
    rows = value.shape[0] // size
    if size == 2:
        index = lax.axis_index("wt")
        mine = lax.dynamic_slice_in_dim(value, index * rows, rows, 0)
        theirs = lax.dynamic_slice_in_dim(value, (1 - index) * rows, rows, 0)
        return mine.astype(F32) + flip(theirs, "wt", 2, 1).astype(F32)
    return lax.psum_scatter(value, "wt", scatter_dimension=0, tiled=True).astype(F32)


def sum_flip(blocks, index, axis, size):
    total = lax.dynamic_index_in_dim(blocks, index, 0, keepdims=False).astype(F32)
    for step in range(1, size):
        block = lax.dynamic_index_in_dim(blocks, index ^ step, 0, keepdims=False)
        total = total + flip(block, axis, size, step).astype(F32)
    return total


def norm(values):
    inverse = lax.rsqrt(jnp.mean(values * values, axis=-1, keepdims=True) + EPS)
    return values * inverse, inverse


def one_hot_rows(bucket_row, buckets):
    ids = lax.broadcasted_iota(jnp.int32, (buckets, bucket_row.shape[1]), 0)
    return (ids == bucket_row).astype(F32)


def attend_kernel(nc, heads, hsize, mem, idx, *refs):
    xs = refs[:nc]
    wq, wk, wv, gain, pk, pv, tab, bucket_row = refs[nc : nc + 8]
    n1_ref, q_ref, k_ref, v_ref, pt_ref, pm_ref, mix_ref = refs[nc + 8 : nc + 15]
    outs = refs[nc + 15 : nc + 15 + nc]
    att_scr = refs[nc + 15 + nc]
    here = idx[0]
    rows = xs[0].shape[0]
    length = nc * rows
    for step in range(nc):
        scaled, _ = norm(xs[step][...].astype(F32))
        at = pl.multiple_of((here ^ step) * rows, rows)
        n1_ref[pl.ds(at, rows), :] = (scaled * gain[...]).astype(BF)
    normed = n1_ref[...]
    q_ref[...] = nn(normed, wq[...]).astype(BF)
    k_ref[...] = nn(normed, wk[...]).astype(BF)
    v_ref[...] = nn(normed, wv[...]).astype(BF)
    vals_t = v_ref[...].T
    pv_t = pv[...].astype(F32).T.astype(BF)
    hot = one_hot_rows(bucket_row[...], tab.shape[1])
    lines = nn(tab[...], hot)
    for h in range(heads):
        part = slice(h * hsize, (h + 1) * hsize)
        query = q_ref[:, part]
        line = jnp.broadcast_to(lines[h : h + 1, :], (LANES, 2 * length))
        spread = pltpu.roll(line, 0, 1, stride=1, stride_axis=0)
        bias = jnp.concatenate(
            [spread[:, length - at : 2 * length - at] for at in range(0, length, LANES)], axis=0
        )
        score = nt(k_ref[:, part], query) + bias
        front = nt(pk[:, part], query)
        top = jnp.maximum(
            jnp.max(score, axis=0, keepdims=True), jnp.max(front, axis=0, keepdims=True)
        )
        score = jnp.exp(score - top)
        front = jnp.exp(front - top)
        total = jnp.sum(score, axis=0, keepdims=True) + jnp.sum(front, axis=0, keepdims=True)
        scale = 1.0 / total
        prob = (score * scale).astype(BF)
        prob_mem = (front * scale).astype(BF)
        pt_ref[h] = prob
        pm_ref[h] = prob_mem
        mix_ref[part, :] = nn(vals_t[part, :], prob) + nn(pv_t[part, :], prob_mem)
    att_scr[...] = mix_ref[...].T.astype(BF)
    for step in range(nc):
        at = pl.multiple_of((here ^ step) * rows, rows)
        outs[step][...] = att_scr[pl.ds(at, rows), :]


def attend(nc, heads, hsize, index, xs, wq, wk, wv, gain, pk, pv, tab, bucket_row):
    rows, width = xs[0].shape
    length = rows * nc
    cols = heads * hsize
    mem = pk.shape[0]
    out = [
        shape((length, width), BF),
        shape((length, cols), BF),
        shape((length, cols), BF),
        shape((length, cols), BF),
        shape((heads, length, length), BF),
        shape((heads, mem, length), BF),
        shape((cols, length), F32),
    ] + [shape((rows, cols), BF)] * nc
    return pl.pallas_call(
        functools.partial(attend_kernel, nc, heads, hsize, mem),
        out_shape=out,
        in_specs=[smem()] + vmem(nc + 8),
        out_specs=vmem(len(out)),
        scratch_shapes=[pltpu.VMEM((length, cols), BF)],
        compiler_params=params(48),
        name="attend",
    )(index, *xs, wq, wk, wv, gain, pk, pv, tab, bucket_row)


def branch_kernel(nc, idx, *refs):
    parts = refs[:nc]
    x, wo, gain = refs[nc : nc + 3]
    hidden_ref, n2_ref, att_ref = refs[nc + 3 : nc + 6]
    here = idx[0]
    cols = parts[0].shape[1]
    for step in range(nc):
        att_ref[here ^ step] = parts[step][...]
    hidden = x[...].astype(F32)
    for c in range(nc):
        hidden = hidden + nn(att_ref[c], wo[c * cols : (c + 1) * cols, :])
    hidden_ref[...] = hidden
    scaled, _ = norm(hidden)
    n2_ref[...] = (scaled * gain[...]).astype(BF)


def branch(nc, index, parts, x, wo, gain):
    rows, cols = parts[0].shape
    out = [shape(x.shape, F32), shape(x.shape, BF), shape((nc, rows, cols), BF)]
    return pl.pallas_call(
        functools.partial(branch_kernel, nc),
        out_shape=out,
        in_specs=[smem()] + vmem(nc + 3),
        out_specs=vmem(3),
        compiler_params=params(32),
        name="branch",
    )(index, *parts, x, wo, gain)


def branch_back_kernel(nb, nc, idx, *refs):
    parts = refs[:nb]
    hidden_ref, gain, g, wo = refs[nb : nb + 4]
    grad_ref, low_ref = refs[nb + 4 : nb + 6]
    outs = refs[nb + 6 : nb + 6 + nc]
    here = idx[0]
    cols = outs[0].shape[1]
    grad_norm = parts[0][...].astype(F32)
    for part in parts[1:]:
        grad_norm = grad_norm + part[...].astype(F32)
    scaled, inverse = norm(hidden_ref[...])
    e = grad_norm * gain[...]
    grad = g[...].astype(F32) + inverse * (
        e - scaled * jnp.mean(e * scaled, axis=-1, keepdims=True)
    )
    grad_ref[...] = grad
    low = grad.astype(BF)
    low_ref[...] = low
    for step in range(nc):
        at = pl.multiple_of((here ^ step) * cols, 8)
        outs[step][...] = nt(low, wo[pl.ds(at, cols), :]).astype(BF)


def branch_back(nb, nc, index, parts, hidden, gain, g, wo):
    rows, width = hidden.shape
    cols = width // nc
    out = [shape((rows, width), F32), shape((rows, width), BF)] + [shape((rows, cols), BF)] * nc
    return pl.pallas_call(
        functools.partial(branch_back_kernel, nb, nc),
        out_shape=out,
        in_specs=[smem()] + vmem(nb + 4),
        out_specs=vmem(len(out)),
        compiler_params=params(32),
        name="branch_back",
    )(index, *parts, hidden, gain, g, wo)


MEM_K, MEM_V, MEM_END = 0, 32, 64


def attend_back_kernel(nc, heads, hsize, idx, *refs):
    gms = refs[:nc]
    pt, pm, q, k, v, mix, pk, pv, bucket_row = refs[nc : nc + 9]
    grad_ref, table_ref = refs[nc + 9 : nc + 11]
    outs = refs[nc + 11 : nc + 11 + nc]
    gm_scr, gqt_scr, acc = refs[nc + 11 + nc :]
    here = idx[0]
    rows, cols = gms[0].shape
    length = rows * nc
    mem = pk.shape[0]
    for step in range(nc):
        at = pl.multiple_of((here ^ step) * rows, rows)
        gm_scr[pl.ds(at, rows), :] = gms[step][...]
    gm_t = gm_scr[...].T
    keys_t = k[...].T
    pk_t = pk[...].astype(F32).T.astype(BF)
    lines = []
    for h in range(heads):
        part = slice(h * hsize, (h + 1) * hsize)
        gm = gm_scr[:, part]
        query = q[:, part]
        spread = jnp.sum(gm_t[part, :].astype(F32) * mix[part, :], axis=0, keepdims=True)
        prob = pt[h]
        prob_mem = pm[h]
        score = prob.astype(F32) * (nt(v[:, part], gm) - spread)
        front = (prob_mem.astype(F32) * (nt(pv[:, part], gm) - spread)).astype(BF)
        low = score.astype(BF)
        gqt_scr[part, :] = nn(keys_t[part, :], low) + nn(pk_t[part, :], front)
        grad_ref[:, cols + h * hsize : cols + (h + 1) * hsize] = nn(low, query).astype(BF)
        grad_ref[:, 2 * cols + h * hsize : 2 * cols + (h + 1) * hsize] = nn(prob, gm).astype(BF)
        mem_k = nn(front, query).astype(BF)
        mem_v = nn(prob_mem, gm).astype(BF)
        for step in range(nc):
            outs[step][3 * rows + MEM_K : 3 * rows + MEM_K + mem, part] = mem_k
            outs[step][3 * rows + MEM_V : 3 * rows + MEM_V + mem, part] = mem_v
        acc[...] = jnp.zeros_like(acc)
        for at in range(0, length, LANES):
            acc[:, length - at : 2 * length - at] += score[at : at + LANES, :]
        fold = acc[...]
        half = LANES // 2
        while half >= 8:
            fold = fold[:half] + pltpu.roll(fold[half:], 2 * length - half, 1)
            half //= 2
        line = fold[0:1]
        for i in range(1, 8):
            line = line + pltpu.roll(fold[i : i + 1], 2 * length - i, 1)
        lines.append(line)
    lines.append(jnp.zeros((8 - heads, 2 * length), F32))
    hot = one_hot_rows(bucket_row[...], table_ref.shape[0])
    table_ref[...] = lax.dot_general(
        hot,
        jnp.concatenate(lines, axis=0),
        (((1,), (1,)), ((), ())),
        precision=lax.Precision.HIGHEST,
        preferred_element_type=F32,
    )
    grad_ref[:, :cols] = gqt_scr[...].T.astype(BF)
    for step in range(nc):
        at = pl.multiple_of((here ^ step) * rows, rows)
        for p in range(3):
            outs[step][p * rows : (p + 1) * rows, :] = grad_ref[
                pl.ds(at, rows), p * cols : (p + 1) * cols
            ]


def attend_back(nc, heads, hsize, index, gms, pt, pm, q, k, v, mix, pk, pv, bucket_row, nbuck):
    rows, cols = gms[0].shape
    length = rows * nc
    out = [shape((length, 3 * cols), BF), shape((nbuck, 8), F32)] + [
        shape((3 * rows + MEM_END, cols), BF)
    ] * nc
    return pl.pallas_call(
        functools.partial(attend_back_kernel, nc, heads, hsize),
        out_shape=out,
        in_specs=[smem()] + vmem(nc + 9),
        out_specs=vmem(len(out)),
        scratch_shapes=[
            pltpu.VMEM((length, cols), BF),
            pltpu.VMEM((cols, length), F32),
            pltpu.VMEM((LANES, 2 * length), F32),
        ],
        compiler_params=params(48),
        name="attend_back",
    )(index, *gms, pt, pm, q, k, v, mix, pk, pv, bucket_row)


def input_back_kernel(nc, mem, idx, *refs):
    parts = refs[:nc]
    x, wq, wk, wv, gain, grad_hidden = refs[nc : nc + 6]
    out_ref, memk_ref, memv_ref = refs[nc + 6 : nc + 9]
    scr = refs[nc + 9]
    here = idx[0]
    rows = x.shape[0]
    for step in range(nc):
        scr[here ^ step] = parts[step][...]

    def wide(at, count):
        return jnp.concatenate([scr[c, at : at + count, :] for c in range(nc)], axis=1)

    grad_norm = (
        nt(wide(0, rows), wq[...])
        + nt(wide(rows, rows), wk[...])
        + nt(wide(2 * rows, rows), wv[...])
    )
    scaled, inverse = norm(x[...].astype(F32))
    e = grad_norm * gain[...]
    grad = grad_hidden[...] + inverse * (
        e - scaled * jnp.mean(e * scaled, axis=-1, keepdims=True)
    )
    out_ref[...] = grad.astype(BF)
    memk_ref[...] = wide(3 * rows + MEM_K, mem).astype(F32)
    memv_ref[...] = wide(3 * rows + MEM_V, mem).astype(F32)


def input_back(nc, mem, index, parts, x, wq, wk, wv, gain, grad_hidden):
    rows, width = x.shape
    out = [shape((rows, width), BF), shape((mem, width), F32), shape((mem, width), F32)]
    return pl.pallas_call(
        functools.partial(input_back_kernel, nc, mem),
        out_shape=out,
        in_specs=[smem()] + vmem(nc + 6),
        out_specs=vmem(3),
        scratch_shapes=[pltpu.VMEM((nc,) + parts[0].shape, BF)],
        compiler_params=params(32),
        name="input_back",
    )(index, *parts, x, wq, wk, wv, gain, grad_hidden)


def shards(
    sizes,
    inputs,
    prefix_keys,
    prefix_values,
    gain_attn,
    w_query,
    w_key,
    w_value,
    w_out,
    bias_table,
    gain_ffn,
    w_in,
    w_back,
    buckets,
    out_grad,
):
    nb, nc, nw = sizes
    b, c, w = lax.axis_index("batch"), lax.axis_index("ctx"), lax.axis_index("wt")
    x, g = inputs[0], out_grad[0]
    rows, width = x.shape
    all_heads = bias_table.shape[1]
    heads = all_heads // nc
    hsize = width // all_heads
    cols = heads * hsize
    mem = prefix_keys.shape[1]
    length = rows * nc
    part = width // nw
    ff_own = w_back.shape[0]
    ff_part = ff_own // nb
    nbuck = bias_table.shape[0] * nw
    index_c = jnp.reshape(c, (1,))

    xs = gather_flip(x, "ctx", nc)
    wq = gather_wt(w_query, nw).reshape(width, width)
    wk = gather_wt(w_key, nw).reshape(width, width)
    wv = gather_wt(w_value, nw).reshape(width, width)
    small = gather_wt(
        jnp.concatenate([gain_attn, gain_ffn, bias_table.reshape(-1)]).reshape(1, -1), nw
    ).reshape(nw, -1)
    gain_one = small[:, :part].reshape(1, width).astype(F32)
    gain_two = small[:, part : 2 * part].reshape(1, width).astype(F32)
    table = small[:, 2 * part :].reshape(nbuck, all_heads)
    wo = gather_wt(w_out, nw).reshape(width, width)
    in_cut = jnp.concatenate(
        [
            lax.dynamic_slice_in_dim(w_in, o * ff_own + b * ff_part, ff_part, 1)
            for o in range(nw)
        ],
        axis=1,
    )
    w_first = gather_wt(in_cut, nw).reshape(width, nw * ff_part)
    back_cut = lax.dynamic_slice_in_dim(w_back, b * ff_part, ff_part, 0)
    w_second = gather_wt(back_cut, nw).reshape(nw * ff_part, width)
    gs = gather_flip(g, "batch", nb)

    def head_cols(value):
        return lax.dynamic_slice_in_dim(value, c * cols, cols, 1)

    pk, pv = head_cols(prefix_keys[0]), head_cols(prefix_values[0])
    tab = jnp.pad(
        lax.dynamic_slice_in_dim(table, c * heads, heads, 1).T.astype(F32), ((0, 8 - heads), (0, 0))
    )
    bucket_row = jnp.pad(buckets[::-1].reshape(1, -1), ((0, 0), (1, 0)), constant_values=-1)

    (normed1, q, k, v, pt, pm, mix, *mixed) = attend(
        nc, heads, hsize, index_c, xs, head_cols(wq), head_cols(wk), head_cols(wv),
        gain_one, pk, pv, tab, bucket_row,
    )
    mixed = mixed[:1] + [flip(mixed[s], "ctx", nc, s) for s in range(1, nc)]
    hidden, normed2, attended = branch(nc, index_c, mixed, x, wo, gain_two)

    n2 = jnp.concatenate(gather_flip(normed2, "batch", nb), axis=0)
    g_all = jnp.concatenate(gs, axis=0)
    inner = nn(n2, w_first)
    act_value, act_pull = jax.vjp(functools.partial(jax.nn.gelu, approximate=True), inner)
    act = act_value.astype(BF)
    grad_act = nt(g_all, w_second)
    grad_inner = act_pull(grad_act)[0].astype(BF)
    part_norm = nt(grad_inner, w_first).astype(BF)
    part_out = nn(act, w_second).astype(BF)
    grad_second = tn(act, g_all).astype(BF)
    grad_first = tn(n2, grad_inner).astype(BF)

    def cut(value, s):
        return value[s * rows : (s + 1) * rows]

    norm_parts = [cut(part_norm, 0)] + [
        flip(cut(part_norm, s), "batch", nb, s) for s in range(1, nb)
    ]
    (grad_hidden, grad_low, *gms) = branch_back(
        nb, nc, index_c, norm_parts, hidden, gain_two, g, wo
    )
    gms = gms[:1] + [flip(gms[s], "ctx", nc, s) for s in range(1, nc)]
    (grad_heads, grad_table, *sends) = attend_back(
        nc, heads, hsize, index_c, gms, pt, pm, q, k, v, mix, pk, pv, bucket_row, nbuck
    )
    sends = sends[:1] + [flip(sends[s], "ctx", nc, s) for s in range(1, nc)]
    grad_x, grad_memk, grad_memv = input_back(
        nc, mem, index_c, sends, x, wq, wk, wv, gain_one, grad_hidden
    )

    result = hidden + cut(part_out, 0).astype(F32)
    for s in range(1, nb):
        result = result + flip(cut(part_out, s), "batch", nb, s).astype(F32)

    def ctx_total(value):
        own = sum_wt(value, nw)
        size = own.shape[0] // nc
        own = sum_flip(own.astype(BF).reshape(nc, size, own.shape[1]), c, "ctx", nc)
        whole = canonical(gather_flip(own.astype(BF), "ctx", nc), c)
        return whole.reshape(nc * size, -1)

    second = gather_flip(ctx_total(grad_second), "batch", nb)
    out_second = canonical([p.astype(F32) for p in second], b).reshape(ff_own, width)
    first = gather_flip(ctx_total(grad_first), "batch", nb)
    out_first = jnp.zeros((part, nw * ff_own), F32)
    for s, piece in enumerate(first):
        for o in range(nw):
            out_first = lax.dynamic_update_slice(
                out_first,
                piece[:, o * ff_part : (o + 1) * ff_part].astype(F32),
                (0, o * ff_own + (b ^ s) * ff_part),
            )

    grad_wo = jnp.einsum("cqd,qe->cde", attended, grad_low, preferred_element_type=F32)
    own_wo = sum_wt(grad_wo.astype(BF).reshape(width, width), nw).astype(BF)
    own_wo = sum_flip(own_wo.reshape(nc, part // nc, width), c, "ctx", nc).astype(BF)
    own_wo = sum_flip(own_wo.reshape(nb, part // nc // nb, width), b, "batch", nb).astype(BF)
    own_wo = canonical(gather_flip(own_wo, "batch", nb), b).reshape(part // nc, width)
    out_wo = canonical(gather_flip(own_wo, "ctx", nc), c).reshape(part, width).astype(F32)

    grad_qkv = sum_wt(tn(normed1, grad_heads).astype(BF), nw).astype(BF)
    line = jnp.pad(grad_table[:, :heads].reshape(1, -1), ((0, 15), (0, 3 * cols - heads * nbuck)))
    if nw == 2:
        line = line.astype(BF)
        line = line.astype(F32) + flip(line, "wt", 2, 1).astype(F32)
    else:
        line = lax.psum(line, "wt")
    size = part // nb
    blocks = jnp.concatenate(
        [
            grad_qkv.reshape(nb, size, 3 * cols),
            jnp.broadcast_to(line.astype(BF)[None], (nb, 16, 3 * cols)),
        ],
        axis=1,
    )
    block = sum_flip(blocks, b, "batch", nb).astype(BF)
    pieces = canonical(gather_flip(block, "ctx", nc), c)
    table_sum = pieces[:, size, : heads * nbuck].astype(F32).reshape(nc, nbuck, heads)
    table_sum = jnp.transpose(table_sum, (1, 0, 2)).reshape(nbuck, all_heads)
    own_buckets = nbuck // nw
    out_table = lax.dynamic_slice_in_dim(table_sum, w * own_buckets, own_buckets, 0)
    wide = canonical(gather_flip(pieces[:, :size], "batch", nb), b)
    wide = wide.reshape(nb, nc, size, 3, cols)
    wide = jnp.transpose(wide, (3, 0, 2, 1, 4)).reshape(3, part, width).astype(F32)
    out_q, out_k, out_v = wide[0], wide[1], wide[2]

    def gain_sum(pairs, gain):
        total = sum(jnp.sum(left * right.astype(F32), axis=1) for left, right in pairs)
        return total / gain.astype(F32)

    gain_two_grad = gain_sum([(out_first, w_in)], gain_ffn)
    gain_one_grad = gain_sum([(out_q, w_query), (out_k, w_key), (out_v, w_value)], gain_attn)
    return (
        result.astype(BF)[None],
        grad_x[None],
        grad_memk[None],
        grad_memv[None],
        gain_one_grad,
        gain_two_grad,
        out_table,
        out_q,
        out_k,
        out_v,
        out_wo,
        out_first,
        out_second,
    )


def solution(mesh):
    tokens = P(("batch", "wt"), "ctx", None)
    memory = P(("batch", "wt"), None, None)
    matrix = P("wt", None)
    vector = P("wt")
    sizes = (mesh.shape["batch"], mesh.shape["ctx"], mesh.shape["wt"])
    return jax.shard_map(
        functools.partial(shards, sizes),
        mesh=mesh,
        in_specs=(
            tokens, memory, memory, vector, matrix, matrix, matrix, matrix, matrix, vector,
            matrix, matrix, P(), tokens,
        ),
        out_specs=(
            tokens, tokens, memory, memory, vector, vector, matrix, matrix, matrix, matrix,
            matrix, matrix, matrix,
        ),
        check_vma=False,
    )
```

time: 1360 us -> 336 us (0.25)
  local copies, waits for them, and re-layouts: 816 us -> 52.8 us
  waiting for transfers between devices: 295 us -> 112 us
  blocking collectives: 109 us -> 0 us
  starting transfers between devices: 0.64 us -> 103 us
  matrix products: 87.6 us -> 8.53 us
  other arithmetic: 27.3 us -> 42.9 us
  between operations: 15.4 us -> 1.75 us
    gather x14 -> x0, local copies, waits for them, and re-layouts: 781 us -> none  [scores_at(): bucket_ids = buckets[where]]
    psum x1 -> x0, waiting for transfers between devices: 168 us -> none  [shards(): lax.psum(part_wq.astype(jnp.bfloat16), ('batch', 'ctx')).astype(jnp.float32)]
    ppermute x0 -> x75, waiting for transfers between devices: none -> 112 us  [flip(): return lax.ppermute(value, axis, [(i, i ^ step) for i in range(size)])]
    reduce_scatter x8 -> x0, waiting for transfers between devices: 110 us -> none  [the longest x1 22.8 us: shards(): lax.psum_scatter(grad_value_all.astype(jnp.bfloat16), 'ctx', scatter_dime...]
    ppermute x0 -> x75, starting transfers between devices: none -> 103 us  [flip(): return lax.ppermute(value, axis, [(i, i ^ step) for i in range(size)])]
    dot_general x46 -> x8, matrix products: 87.6 us -> 8.53 us  [the longest x3 3.83 us: tn(): lax.dot_general(left, right, (((0,), (0,)), ((), ())), preferred_element_...]
    psum x2 -> x0, blocking collectives: 62.8 us -> none  [the longest x1 42.3 us: shards(): lax.psum(part_table.astype(jnp.bfloat16), ('batch', 'ctx'))]
    all_gather x5 -> x0, blocking collectives: 43.7 us -> none  [the longest x1 19.8 us: shards(): lax.all_gather(keys, 'ctx', axis=0, tiled=True)]
  transfers between devices with their start and end apart: 16 -> 75, of which waited for: 10 -> 26; matrix products, arithmetic and copies ran while one was open for 45% -> 28% of each run, Pallas kernels for 0% -> 4%
where the time goes in v1:
time: 336 us; the launch traced here: 335 us
  waiting for transfers between devices  112 us (33%)
  starting transfers between devices  103 us (31%)
  local copies, waits for them, and re-layouts  52.8 us (16%)
  other arithmetic  42.9 us (13%)
  Pallas kernels  13.5 us (4%)
  matrix products  8.53 us (3%)
    ppermute x75, waiting for transfers between devices, flip(): return lax.ppermute(value, axis, [(i, i ^ step) for i in range(size)])  112 us
    ppermute x75, starting transfers between devices, flip(): return lax.ppermute(value, axis, [(i, i ^ step) for i in range(size)])  103 us
    dynamic_update_slice x8, other arithmetic, shards(): lax.dynamic_update_slice(out_first, piece[:, o * ff_part:(o + 1) * ff_par...  14.7 us
    unnamed x83, local copies, waits for them, and re-layouts  9.52 us
    dynamic_update_slice x7, other arithmetic, canonical(): whole = lax.dynamic_update_index_in_dim(whole, part, index ^ step, 0)  9.28 us
    squeeze x3, local copies, waits for them, and re-layouts, shards(): out_q, out_k, out_v = (wide[0], wide[1], wide[2])  8.12 us
    slice x4, local copies, waits for them, and re-layouts, shards(): out_q, out_k, out_v = (wide[0], wide[1], wide[2])  6.8 us
  transfers between devices with their start and end apart: 75, of which 26 were waited for; matrix products, arithmetic and copies ran while one was open for 28% of the time, Pallas kernels for 4%

profile of v1, /device:TPU:0, one launch (start us, length us, event | category | flops | bytes accessed | tf_op | source)
XLA Modules:
  0.0 335.0 jit_solution(3580874493882759557)
XLA Ops:
  22.0 3.4 %collective-permute-done.2.refs_3_ = bf16[128,768]{1,0:T(8,128)(2,1)S(1)} collective-permute-done((bf16[128,768]{1,0:T(8,128)(2,1)}, bf16[128,768]{1,0:T(8,128)(2,1)S(1)}, u32[]{:S(2)}, u32[]{:S(2)}) %collective-permute-start.2) | collective-permute-done | bytes 196640 | tf_op jit(solution)/shard_map/ppermute | solution.py:45
  27.0 4.4 %attend.1 = (bf16[512,768]{1,0:T(8,128)(2,1)S(1)}, bf16[512,192]{1,0:T(8,128)(2,1)S(1)}, bf16[512,192]{1,0:T(8,128)(2,1)S(1)}, bf16[512,192]{1,0:T(8,128)(2,1)S(...) custom-call(s32[1]{0:T(128)} %bitcast.idx, ...), custom_call_target="tpu_custom_call" | custom-call | tf_op jit(solution)/shard_map/attend/pallas_call | solution.py:158
  47.0 3.7 %collective-permute-done.11 = bf16[128,768]{1,0:T(8,128)(2,1)S(1)} collective-permute-done((bf16[128,768]{1,0:T(8,128)(2,1)S(1)}, bf16[128,768]{1,0:T(8,128)(2,1)S(1)}, u32[]{:S(2)}, u32[]{:S(2)}) %collective-permute-start.11) | collective-permute-done | bytes 196640 | tf_op jit(solution)/shard_map/ppermute | solution.py:45
  75.3 3.4 %collective-permute-done.23.refs_2_ = bf16[128,768]{1,0:T(8,128)(2,1)S(1)} collective-permute-done((bf16[128,768]{1,0:T(8,128)(2,1)S(1)}, bf16[128,768]{1,0:T(8,128)(2,1)S(1)}, u32[]{:S(2)}, u32[]{:S(2)}) %collective-permute-start.23) | collective-permute-done | bytes 196640 | tf_op jit(solution)/shard_map/ppermute | solution.py:45
  80.5 3.6 %collective-permute-start.25 = (bf16[128,192]{1,0:T(8,128)(2,1)S(1)}, bf16[128,192]{1,0:T(8,128)(2,1)S(1)}, u32[]{:S(2)}, u32[]{:S(2)}) collective-permute-start(bf16[128,192]{1,0:T(8,128)(2,1)S(1)} %get-tuple-element.49), channel_id=1, source_target_pairs={{0,2},{2,0},{4,6},{6,4},{1,3},{3,1},{5,7},{7,5},{8,10},{10,8},{12,... | collective-permute-start | bytes 147464 | tf_op jit(solution)/shard_map/ppermute | solution.py:45
  88.2 3.4 %collective-permute-done.26.refs_2_ = bf16[128,192]{1,0:T(8,128)(2,1)S(1)} collective-permute-done((bf16[128,192]{1,0:T(8,128)(2,1)S(1)}, bf16[128,192]{1,0:T(8,128)(2,1)S(1)}, u32[]{:S(2)}, u32[]{:S(2)}) %collective-permute-start.26) | collective-permute-done | bytes 49184 | tf_op jit(solution)/shard_map/ppermute | solution.py:45
  91.6 3.5 %attend_back.1 = (bf16[512,576]{1,0:T(8,128)(2,1)S(1)}, f32[32,8]{1,0:T(8,128)S(1)}, bf16[448,192]{1,0:T(8,128)(2,1)S(1)}, bf16[448,192]{1,0:T(8,128)(2,1)}, bf1...) custom-call(s32[1]{0:T(128)} %bitcast.idx, bf16[128,192]{1,0:T(8,128)(2,1)S(1)} %get-tuple-element.48.refs_0_, ...), custom_call_target="tpu_custom_call" | custom-call | tf_op jit(solution)/shard_map/attend_back/pallas_call | solution.py:309
  107.9 10.7 %collective-permute-done.29.refs_2_ = bf16[448,192]{1,0:T(8,128)(2,1)} collective-permute-done((bf16[448,192]{1,0:T(8,128)(2,1)}, bf16[448,192]{1,0:T(8,128)(2,1)}, u32[]{:S(2)}, u32[]{:S(2)}) %collective-permute-start.29) | collective-permute-done | bytes 172064 | tf_op jit(solution)/shard_map/ppermute | solution.py:45
  118.7 3.4 %input_back.1 = (bf16[128,768]{1,0:T(8,128)(2,1)}, f32[20,768]{1,0:T(8,128)S(1)}, f32[20,768]{1,0:T(8,128)S(1)}) custom-call(s32[1]{0:T(128)} %bitcast.idx, bf16[448,192]{1,0:T(8,128)(2,1)S(1)} %copy-done.3, bf16[448,192]{1,0:T(8,128)(2,1)} %collective-permute-done.28.refs_1_, bf16[448,192]{1,0:T(8,128)(2,1)} %collective-permute-done.29.refs_2_, ...), custom_call_target="tpu_custom_call" | custom-call | tf_op jit(solution)/shard_map/input_back/pallas_call | solution.py:355
  125.5 5.4 %collective-permute-start.44 = (bf16[96,768]{1,0:T(8,128)(2,1)}, bf16[96,768]{1,0:T(8,128)(2,1)S(1)}, u32[]{:S(2)}, u32[]{:S(2)}) collective-permute-start(bf16[96,768]{1,0:T(8,128)(2,1)} %get-tuple-element.161), channel_id=1, source_target_pairs={{0,4},{2,6},{4,0},{6,2},{1,5},{3,7},{5,1},{7,3},{8,12},{10,14},{12... | collective-permute-start | bytes 442376 | tf_op jit(solution)/shard_map/ppermute | solution.py:45
  134.2 6.9 %collective-permute-start.67 = (bf16[96,768]{1,0:T(8,128)(2,1)S(1)}, bf16[96,768]{1,0:T(8,128)(2,1)S(1)}, u32[]{:S(2)}, u32[]{:S(2)}) collective-permute-start(bf16[96,768]{1,0:T(8,128)(2,1)S(1)} %get-tuple-element.155), channel_id=1, source_target_pairs={{0,4},{2,6},{4,0},{6,2},{1,5},{3,7},{5,1},{7,3},{8,12},{10,14},{12... | collective-permute-start | bytes 442376 | tf_op jit(solution)/shard_map/ppermute | solution.py:45
  141.1 8.5 %collective-permute-done.44 = bf16[96,768]{1,0:T(8,128)(2,1)S(1)} collective-permute-done((bf16[96,768]{1,0:T(8,128)(2,1)}, bf16[96,768]{1,0:T(8,128)(2,1)S(1)}, u32[]{:S(2)}, u32[]{:S(2)}) %collective-permute-start.44) | collective-permute-done | bytes 147488 | tf_op jit(solution)/shard_map/ppermute | solution.py:45
  171.0 4.0 %collective-permute-done.47 = bf16[96,768]{1,0:T(8,128)(2,1)S(1)} collective-permute-done((bf16[96,768]{1,0:T(8,128)(2,1)S(1)}, bf16[96,768]{1,0:T(8,128)(2,1)S(1)}, u32[]{:S(2)}, u32[]{:S(2)}) %collective-permute-start.47) | collective-permute-done | bytes 147488 | tf_op jit(solution)/shard_map/ppermute | solution.py:45
  177.5 9.0 %collective-permute-start.54 = (bf16[96,768]{1,0:T(8,128)(2,1)S(1)}, bf16[96,768]{1,0:T(8,128)(2,1)S(1)}, u32[]{:S(2)}, u32[]{:S(2)}) collective-permute-start(bf16[96,768]{1,0:T(8,128)(2,1)S(1)} %get-tuple-element.158), channel_id=1, source_target_pairs={{0,4},{2,6},{4,0},{6,2},{1,5},{3,7},{5,1},{7,3},{8,12},{10,14},{12... | collective-permute-start | bytes 442376 | tf_op jit(solution)/shard_map/ppermute | solution.py:45
  214.0 6.3 %collective-permute-done.58 = bf16[24,768]{1,0:T(8,128)(2,1)S(1)} collective-permute-done((bf16[24,768]{1,0:T(8,128)(2,1)S(1)}, bf16[24,768]{1,0:T(8,128)(2,1)S(1)}, u32[]{:S(2)}, u32[]{:S(2)}) %collective-permute-start.58) | collective-permute-done | bytes 36896 | tf_op jit(solution)/shard_map/ppermute | solution.py:45
  222.2 6.2 %collective-permute-done.57 = bf16[24,768]{1,0:T(8,128)(2,1)S(1)} collective-permute-done((bf16[24,768]{1,0:T(8,128)(2,1)S(1)}, bf16[24,768]{1,0:T(8,128)(2,1)S(1)}, u32[]{:S(2)}, u32[]{:S(2)}) %collective-permute-start.57) | collective-permute-done | bytes 36896 | tf_op jit(solution)/shard_map/ppermute | solution.py:45
  231.9 6.6 %collective-permute-done.59 = bf16[24,768]{1,0:T(8,128)(2,1)S(1)} collective-permute-done((bf16[24,768]{1,0:T(8,128)(2,1)S(1)}, bf16[24,768]{1,0:T(8,128)(2,1)S(1)}, u32[]{:S(2)}, u32[]{:S(2)}) %collective-permute-start.59) | collective-permute-done | bytes 36896 | tf_op jit(solution)/shard_map/ppermute | solution.py:45
  239.1 3.5 %collective-permute-done.60 = bf16[24,768]{1,0:T(8,128)(2,1)S(1)} collective-permute-done((bf16[24,768]{1,0:T(8,128)(2,1)S(1)}, bf16[24,768]{1,0:T(8,128)(2,1)S(1)}, u32[]{:S(2)}, u32[]{:S(2)}) %collective-permute-start.60) | collective-permute-done | bytes 36896 | tf_op jit(solution)/shard_map/ppermute | solution.py:45
  244.0 3.4 %collective-permute-done.61 = bf16[24,768]{1,0:T(8,128)(2,1)S(1)} collective-permute-done((bf16[24,768]{1,0:T(8,128)(2,1)S(1)}, bf16[24,768]{1,0:T(8,128)(2,1)S(1)}, u32[]{:S(2)}, u32[]{:S(2)}) %collective-permute-start.61) | collective-permute-done | bytes 36896 | tf_op jit(solution)/shard_map/ppermute | solution.py:45
  248.3 4.3 %collective-permute-done.62 = bf16[96,768]{1,0:T(8,128)(2,1)S(1)} collective-permute-done((bf16[96,768]{1,0:T(8,128)(2,1)S(1)}, bf16[96,768]{1,0:T(8,128)(2,1)S(1)}, u32[]{:S(2)}, u32[]{:S(2)}) %collective-permute-start.62) | collective-permute-done | bytes 147488 | tf_op jit(solution)/shard_map/ppermute | solution.py:45
  253.2 6.4 %collective-permute-done.63 = bf16[96,768]{1,0:T(8,128)(2,1)S(1)} collective-permute-done((bf16[96,768]{1,0:T(8,128)(2,1)S(1)}, bf16[96,768]{1,0:T(8,128)(2,1)S(1)}, u32[]{:S(2)}, u32[]{:S(2)}) %collective-permute-start.63) | collective-permute-done | bytes 147488 | tf_op jit(solution)/shard_map/ppermute | solution.py:45
  261.7 4.8 %collective-permute-done.64 = bf16[96,768]{1,0:T(8,128)(2,1)S(1)} collective-permute-done((bf16[96,768]{1,0:T(8,128)(2,1)S(1)}, bf16[96,768]{1,0:T(8,128)(2,1)S(1)}, u32[]{:S(2)}, u32[]{:S(2)}) %collective-permute-start.64) | collective-permute-done | bytes 147488 | tf_op jit(solution)/shard_map/ppermute | solution.py:45
  271.8 8.7 %collective-permute-done.40 = bf16[4,96,576]{2,1,0:T(8,128)(2,1)S(1)} collective-permute-done((bf16[4,96,576]{2,1,0:T(8,128)(2,1)}, bf16[4,96,576]{2,1,0:T(8,128)(2,1)S(1)}, u32[]{:S(2)}, u32[]{:S(2)}) %collective-permute-start.40) | collective-permute-done | bytes 442400 | tf_op jit(solution)/shard_map/ppermute | solution.py:45
  284.6 6.8 %collective-permute-done.41 = bf16[4,96,576]{2,1,0:T(8,128)(2,1)} collective-permute-done((bf16[4,96,576]{2,1,0:T(8,128)(2,1)}, bf16[4,96,576]{2,1,0:T(8,128)(2,1)}, u32[]{:S(2)}, u32[]{:S(2)}) %collective-permute-start.41) | collective-permute-done | bytes 442400 | tf_op jit(solution)/shard_map/ppermute | solution.py:45
  (347 shorter events, 202.8 us)
Async XLA Ops:
  17.0 19.4 %collective-permute-start.14 = (bf16[384,768]{1,0:T(8,128)(2,1)}, bf16[384,768]{1,0:T(8,128)(2,1)S(1)}, u32[]{:S(2)}, u32[]{:S(2)}) collective-permute-start(bf16[384,768]{1,0:T(8,128)(2,1)} %pad_maximum_fusion.7), channel_id=1, source_target_pairs={{0,1},{1,0},{2,3},{3,2},{4,5},{5,4},{6,7},{7,6},{8,9},{9,8},{10,11... | collective-permute-start | bytes 1769480 | tf_op jit(solution)/shard_map/ppermute | solution.py:45
  19.4 39.7 %collective-permute-start.21 = (bf16[128,768]{1,0:T(8,128)(2,1)S(1)}, bf16[128,768]{1,0:T(8,128)(2,1)S(1)}, u32[]{:S(2)}, u32[]{:S(2)}) collective-permute-start(bf16[128,768]{1,0:T(8,128)(2,1)S(1)} %bitcast.210), channel_id=1, source_target_pairs={{0,24},{8,16},{16,8},{24,0},{1,25},{9,17},{17,9},{25,1},{2,26},{10... | collective-permute-start | bytes 589832 | tf_op jit(solution)/shard_map/ppermute | solution.py:45
  25.4 33.7 %collective-permute-start.20 = (bf16[128,768]{1,0:T(8,128)(2,1)S(1)}, bf16[128,768]{1,0:T(8,128)(2,1)S(1)}, u32[]{:S(2)}, u32[]{:S(2)}) collective-permute-start(bf16[128,768]{1,0:T(8,128)(2,1)S(1)} %bitcast.211), channel_id=1, source_target_pairs={{0,16},{8,24},{16,0},{24,8},{1,17},{9,25},{17,1},{25,9},{2,18},{10... | collective-permute-start | bytes 589832 | tf_op jit(solution)/shard_map/ppermute | solution.py:45
  39.5 19.7 %collective-permute-start.19 = (bf16[128,768]{1,0:T(8,128)(2,1)S(1)}, bf16[128,768]{1,0:T(8,128)(2,1)S(1)}, u32[]{:S(2)}, u32[]{:S(2)}) collective-permute-start(bf16[128,768]{1,0:T(8,128)(2,1)S(1)} %bitcast.212), channel_id=1, source_target_pairs={{0,8},{8,0},{16,24},{24,16},{1,9},{9,1},{17,25},{25,17},{2,10},{10... | collective-permute-start | bytes 589832 | tf_op jit(solution)/shard_map/ppermute | solution.py:45
  63.7 20.4 %collective-permute-start.17 = (bf16[128,768]{1,0:T(8,128)(2,1)S(1)}, bf16[128,768]{1,0:T(8,128)(2,1)S(1)}, u32[]{:S(2)}, u32[]{:S(2)}) collective-permute-start(bf16[128,768]{1,0:T(8,128)(2,1)S(1)} %get-tuple-element.152), channel_id=1, source_target_pairs={{0,16},{8,24},{16,0},{24,8},{1,17},{9,25},{17,1},{25,9},{2,18},{10... | collective-permute-start | bytes 589832 | tf_op jit(solution)/shard_map/ppermute | solution.py:45
  78.7 44.8 %collective-permute-start.42 = (bf16[384,768]{1,0:T(8,128)(2,1)}, bf16[384,768]{1,0:T(8,128)(2,1)}, u32[]{:S(2)}, u32[]{:S(2)}) collective-permute-start(bf16[384,768]{1,0:T(8,128)(2,1)} %constant_dynamic-slice_fusion.3), channel_id=1, source_target_pairs={{0,1},{1,0},{2,3},{3,2},{4,5},{5,4},{6,7},{7,6},{8,9},{9,8},{10,11... | collective-permute-start | bytes 1769480 | tf_op jit(solution)/shard_map/ppermute | solution.py:45
  78.7 52.2 %collective-permute-start.65 = (bf16[384,768]{1,0:T(8,128)(2,1)}, bf16[384,768]{1,0:T(8,128)(2,1)}, u32[]{:S(2)}, u32[]{:S(2)}) collective-permute-start(bf16[384,768]{1,0:T(8,128)(2,1)} %constant_dynamic-slice_fusion), channel_id=1, source_target_pairs={{0,1},{1,0},{2,3},{3,2},{4,5},{5,4},{6,7},{7,6},{8,9},{9,8},{10,11... | collective-permute-start | bytes 1769480 | tf_op jit(solution)/shard_map/ppermute | solution.py:45
  99.1 19.5 %collective-permute-start.29 = (bf16[448,192]{1,0:T(8,128)(2,1)}, bf16[448,192]{1,0:T(8,128)(2,1)}, u32[]{:S(2)}, u32[]{:S(2)}) collective-permute-start(bf16[448,192]{1,0:T(8,128)(2,1)} %get-tuple-element.60), channel_id=1, source_target_pairs={{0,4},{2,6},{4,0},{6,2},{1,5},{3,7},{5,1},{7,3},{8,12},{10,14},{12... | collective-permute-start | bytes 516104 | tf_op jit(solution)/shard_map/ppermute | solution.py:45
  107.9 51.9 %collective-permute-start.52 = (bf16[384,768]{1,0:T(8,128)(2,1)}, bf16[384,768]{1,0:T(8,128)(2,1)}, u32[]{:S(2)}, u32[]{:S(2)}) collective-permute-start(bf16[384,768]{1,0:T(8,128)(2,1)} %constant_dynamic-slice_fusion.1), channel_id=1, source_target_pairs={{0,1},{1,0},{2,3},{3,2},{4,5},{5,4},{6,7},{7,6},{8,9},{9,8},{10,11... | collective-permute-start | bytes 1769480 | tf_op jit(solution)/shard_map/ppermute | solution.py:45
  125.5 24.2 %collective-permute-start.44 = (bf16[96,768]{1,0:T(8,128)(2,1)}, bf16[96,768]{1,0:T(8,128)(2,1)S(1)}, u32[]{:S(2)}, u32[]{:S(2)}) collective-permute-start(bf16[96,768]{1,0:T(8,128)(2,1)} %get-tuple-element.161), channel_id=1, source_target_pairs={{0,4},{2,6},{4,0},{6,2},{1,5},{3,7},{5,1},{7,3},{8,12},{10,14},{12... | collective-permute-start | bytes 442376 | tf_op jit(solution)/shard_map/ppermute | solution.py:45
  132.2 20.5 %collective-permute-start.68 = (bf16[96,768]{1,0:T(8,128)(2,1)S(1)}, bf16[96,768]{1,0:T(8,128)(2,1)S(1)}, u32[]{:S(2)}, u32[]{:S(2)}) collective-permute-start(bf16[96,768]{1,0:T(8,128)(2,1)S(1)} %get-tuple-element.154), channel_id=1, source_target_pairs={{0,6},{2,4},{4,2},{6,0},{1,7},{3,5},{5,3},{7,1},{8,14},{10,12},{12... | collective-permute-start | bytes 442376 | tf_op jit(solution)/shard_map/ppermute | solution.py:45
  134.2 21.6 %collective-permute-start.67 = (bf16[96,768]{1,0:T(8,128)(2,1)S(1)}, bf16[96,768]{1,0:T(8,128)(2,1)S(1)}, u32[]{:S(2)}, u32[]{:S(2)}) collective-permute-start(bf16[96,768]{1,0:T(8,128)(2,1)S(1)} %get-tuple-element.155), channel_id=1, source_target_pairs={{0,4},{2,6},{4,0},{6,2},{1,5},{3,7},{5,1},{7,3},{8,12},{10,14},{12... | collective-permute-start | bytes 442376 | tf_op jit(solution)/shard_map/ppermute | solution.py:45
  165.5 26.2 %collective-permute-start.69 = (bf16[96,768]{1,0:T(8,128)(2,1)S(1)}, bf16[96,768]{1,0:T(8,128)(2,1)S(1)}, u32[]{:S(2)}, u32[]{:S(2)}) collective-permute-start(bf16[96,768]{1,0:T(8,128)(2,1)S(1)} %get-tuple-element.124), channel_id=1, source_target_pairs={{0,2},{2,0},{4,6},{6,4},{1,3},{3,1},{5,7},{7,5},{8,10},{10,8},{12,... | collective-permute-start | bytes 442376 | tf_op jit(solution)/shard_map/ppermute | solution.py:45
  165.5 27.0 %collective-permute-start.70 = (bf16[96,768]{1,0:T(8,128)(2,1)S(1)}, bf16[96,768]{1,0:T(8,128)(2,1)S(1)}, u32[]{:S(2)}, u32[]{:S(2)}) collective-permute-start(bf16[96,768]{1,0:T(8,128)(2,1)S(1)} %get-tuple-element.124), channel_id=1, source_target_pairs={{0,4},{2,6},{4,0},{6,2},{1,5},{3,7},{5,1},{7,3},{8,12},{10,14},{12... | collective-permute-start | bytes 442376 | tf_op jit(solution)/shard_map/ppermute | solution.py:45
  167.0 28.0 %collective-permute-start.71 = (bf16[96,768]{1,0:T(8,128)(2,1)S(1)}, bf16[96,768]{1,0:T(8,128)(2,1)S(1)}, u32[]{:S(2)}, u32[]{:S(2)}) collective-permute-start(bf16[96,768]{1,0:T(8,128)(2,1)S(1)} %get-tuple-element.124), channel_id=1, source_target_pairs={{0,6},{2,4},{4,2},{6,0},{1,7},{3,5},{5,3},{7,1},{8,14},{10,12},{12... | collective-permute-start | bytes 442376 | tf_op jit(solution)/shard_map/ppermute | solution.py:45
  175.0 28.5 %collective-permute-start.55 = (bf16[96,768]{1,0:T(8,128)(2,1)S(1)}, bf16[96,768]{1,0:T(8,128)(2,1)S(1)}, u32[]{:S(2)}, u32[]{:S(2)}) collective-permute-start(bf16[96,768]{1,0:T(8,128)(2,1)S(1)} %get-tuple-element.157), channel_id=1, source_target_pairs={{0,6},{2,4},{4,2},{6,0},{1,7},{3,5},{5,3},{7,1},{8,14},{10,12},{12... | collective-permute-start | bytes 442376 | tf_op jit(solution)/shard_map/ppermute | solution.py:45
  177.5 28.4 %collective-permute-start.54 = (bf16[96,768]{1,0:T(8,128)(2,1)S(1)}, bf16[96,768]{1,0:T(8,128)(2,1)S(1)}, u32[]{:S(2)}, u32[]{:S(2)}) collective-permute-start(bf16[96,768]{1,0:T(8,128)(2,1)S(1)} %get-tuple-element.158), channel_id=1, source_target_pairs={{0,4},{2,6},{4,0},{6,2},{1,5},{3,7},{5,1},{7,3},{8,12},{10,14},{12... | collective-permute-start | bytes 442376 | tf_op jit(solution)/shard_map/ppermute | solution.py:45
  205.9 107.7 %collective-permute-start.49 = (bf16[384,768]{1,0:T(8,128)(2,1)}, bf16[384,768]{1,0:T(8,128)(2,1)}, u32[]{:S(2)}, u32[]{:S(2)}) collective-permute-start(bf16[384,768]{1,0:T(8,128)(2,1)} %bitcast.57), channel_id=1, source_target_pairs={{0,8},{8,0},{16,24},{24,16},{1,9},{9,1},{17,25},{25,17},{2,10},{10... | collective-permute-start | bytes 1769480 | tf_op jit(solution)/shard_map/ppermute | solution.py:45
  206.7 111.9 %collective-permute-start.50 = (bf16[384,768]{1,0:T(8,128)(2,1)}, bf16[384,768]{1,0:T(8,128)(2,1)}, u32[]{:S(2)}, u32[]{:S(2)}) collective-permute-start(bf16[384,768]{1,0:T(8,128)(2,1)} %bitcast.57), channel_id=1, source_target_pairs={{0,16},{8,24},{16,0},{24,8},{1,17},{9,25},{17,1},{25,9},{2,18},{10... | collective-permute-start | bytes 1769480 | tf_op jit(solution)/shard_map/ppermute | solution.py:45
  220.4 102.1 %collective-permute-start.51 = (bf16[384,768]{1,0:T(8,128)(2,1)}, bf16[384,768]{1,0:T(8,128)(2,1)}, u32[]{:S(2)}, u32[]{:S(2)}) collective-permute-start(bf16[384,768]{1,0:T(8,128)(2,1)} %bitcast.57), channel_id=1, source_target_pairs={{0,24},{8,16},{16,8},{24,0},{1,25},{9,17},{17,9},{25,1},{2,26},{10... | collective-permute-start | bytes 1769480 | tf_op jit(solution)/shard_map/ppermute | solution.py:45
  230.5 37.7 %collective-permute-start.39 = (bf16[4,96,576]{2,1,0:T(8,128)(2,1)}, bf16[4,96,576]{2,1,0:T(8,128)(2,1)S(1)}, u32[]{:S(2)}, u32[]{:S(2)}) collective-permute-start(bf16[4,96,576]{2,1,0:T(8,128)(2,1)} %copy.62), channel_id=1, source_target_pairs={{0,8},{8,0},{16,24},{24,16},{1,9},{9,1},{17,25},{25,17},{2,10},{10... | collective-permute-start | bytes 1327112 | tf_op jit(solution)/shard_map/ppermute | solution.py:45
  269.0 60.6 %collective-permute-start.72 = (bf16[384,768]{1,0:T(8,128)(2,1)}, bf16[384,768]{1,0:T(8,128)(2,1)}, u32[]{:S(2)}, u32[]{:S(2)}) collective-permute-start(bf16[384,768]{1,0:T(8,128)(2,1)} %bitcast.91), channel_id=1, source_target_pairs={{0,8},{8,0},{16,24},{24,16},{1,9},{9,1},{17,25},{25,17},{2,10},{10... | collective-permute-start | bytes 1769480 | tf_op jit(solution)/shard_map/ppermute | solution.py:45
  291.4 40.4 %collective-permute-start.73 = (bf16[384,768]{1,0:T(8,128)(2,1)}, bf16[384,768]{1,0:T(8,128)(2,1)}, u32[]{:S(2)}, u32[]{:S(2)}) collective-permute-start(bf16[384,768]{1,0:T(8,128)(2,1)} %bitcast.91), channel_id=1, source_target_pairs={{0,16},{8,24},{16,0},{24,8},{1,17},{9,25},{17,1},{25,9},{2,18},{10... | collective-permute-start | bytes 1769480 | tf_op jit(solution)/shard_map/ppermute | solution.py:45
  313.6 20.4 %collective-permute-start.74 = (bf16[384,768]{1,0:T(8,128)(2,1)}, bf16[384,768]{1,0:T(8,128)(2,1)S(1)}, u32[]{:S(2)}, u32[]{:S(2)}) collective-permute-start(bf16[384,768]{1,0:T(8,128)(2,1)} %bitcast.91), channel_id=1, source_target_pairs={{0,24},{8,16},{16,8},{24,0},{1,25},{9,17},{17,9},{25,1},{2,26},{10... | collective-permute-start | bytes 1769480 | tf_op jit(solution)/shard_map/ppermute | solution.py:45
  (87 other events, 755.8 us)

commit v2 on v1

--- a/solution.py
+++ b/solution.py
@@ -80,6 +80,31 @@
         block = lax.dynamic_index_in_dim(blocks, index ^ step, 0, keepdims=False)
         total = total + flip(block, axis, size, step).astype(F32)
     return total
+
+
+def after(value, *earlier):
+    return lax.optimization_barrier((value, *earlier))[0]
+
+
+def pair(mine, theirs, bit, axis):
+    first = jnp.where(bit == 0, mine, theirs)
+    second = jnp.where(bit == 0, theirs, mine)
+    return jnp.stack([first, second], axis=axis)
+
+
+def halves(value, bit, axis=0):
+    mine = lax.dynamic_index_in_dim(value, bit, axis, keepdims=False)
+    theirs = lax.dynamic_index_in_dim(value, 1 - bit, axis, keepdims=False)
+    return mine, theirs
+
+
+def add(left, right):
+    return (left.astype(F32) + right.astype(F32)).astype(BF)
+
+
+def halve(value, bit, axis, name, step):
+    mine, theirs = halves(value, bit, axis)
+    return add(mine, flip(theirs, name, 4, step))
 
 
 def norm(values):
@@ -321,6 +346,48 @@
     )(index, *gms, pt, pm, q, k, v, mix, pk, pv, bucket_row)
 
 
+NEAR_LAST = (0, 2, 1, 3)
+
+
+def weight_back_kernel(pairs, extra, idx, *refs):
+    ins = refs[: 2 * pairs + extra]
+    outs = refs[2 * pairs + extra : -1]
+    scr = refs[-1]
+    wt, here = idx[0], idx[1]
+    for p in range(pairs):
+        left, right = ins[2 * p], ins[2 * p + 1]
+        total = left.shape[-1] if len(left.shape) == 2 else left.shape[0] * left.shape[2]
+        if len(left.shape) == 2:
+            scr[...] = tn(left[...], right[...]).astype(BF)
+        else:
+            size = left.shape[2]
+            for j in range(left.shape[0]):
+                scr[j * size : (j + 1) * size, :] = tn(left[j], right[...]).astype(BF)
+        rows = total // 8
+        for i, out in enumerate(outs):
+            for j, place in enumerate(NEAR_LAST):
+                at = pl.multiple_of(((wt ^ i) * 4 + (here ^ place)) * rows, rows)
+                out[p, j * rows : (j + 1) * rows, :] = scr[pl.ds(at, rows), :]
+            if extra:
+                out[p, 4 * rows :, :] = ins[2 * pairs][...]
+
+
+def weight_back(name, index, pairs, extra=()):
+    count, width = len(pairs), pairs[0][1].shape[1]
+    left = pairs[0][0]
+    rows = (left.shape[1] if left.ndim == 2 else left.shape[0] * left.shape[2]) // 2
+    more = sum(e.shape[0] for e in extra)
+    return pl.pallas_call(
+        functools.partial(weight_back_kernel, count, len(extra)),
+        out_shape=[shape((count, rows + more, width), BF)] * 2,
+        in_specs=[smem()] + vmem(2 * count + len(extra)),
+        out_specs=vmem(2),
+        scratch_shapes=[pltpu.VMEM((2 * rows, width), BF)],
+        compiler_params=params(48),
+        name=name,
+    )(index, *[side for pair in pairs for side in pair], *extra)
+
+
 def input_back_kernel(nc, mem, idx, *refs):
     parts = refs[:nc]
     x, wq, wk, wv, gain, grad_hidden = refs[nc : nc + 6]
@@ -361,6 +428,233 @@
         compiler_params=params(32),
         name="input_back",
     )(index, *parts, x, wq, wk, wv, gain, grad_hidden)
+
+
+def row_sums(values):
+    return lax.dot_general(
+        jnp.ones((8, values.shape[1]), F32),
+        values,
+        (((1,), (1,)), ((), ())),
+        precision=lax.Precision.HIGHEST,
+        preferred_element_type=F32,
+    )
+
+
+def batch_piece(refs, at):
+    own, one, two, own2, one2, two2 = refs
+    near = (own, one, two.at[0], two.at[1])[at]
+    far = (own2, two2.at[0], one2, two2.at[1])[at]
+    return ((0, near.at[0]), (2, near.at[1]), (1, far.at[0]), (3, far.at[1]))
+
+
+def fill_rows_kernel(idx, *refs):
+    out = refs[6]
+    step = pl.program_id(0)
+    for at in range(4):
+
+        @pl.when(step == at)
+        def _():
+            for place, piece in batch_piece(refs[:6], at):
+                size = piece.shape[0]
+                row = pl.multiple_of((idx[1] ^ place) * size, 8)
+                out[pl.ds(row, size), :] = piece[...].astype(F32)
+
+
+def fill_rows(index, pieces):
+    _, size, width = pieces[0].shape
+    specs = [
+        pl.BlockSpec(p.shape, functools.partial(lambda n, step, idx: (0,) * n, p.ndim))
+        for p in pieces
+    ]
+    return pl.pallas_call(
+        fill_rows_kernel,
+        out_shape=shape((16 * size, width), F32),
+        grid_spec=pltpu.PrefetchScalarGridSpec(
+            num_scalar_prefetch=1,
+            grid=(4,),
+            in_specs=specs,
+            out_specs=pl.BlockSpec((4 * size, width), lambda step, idx: (idx[0] ^ step, 0)),
+        ),
+        compiler_params=params(32),
+        name="fill_rows",
+    )(index, *pieces)
+
+
+def fill_cols_kernel(idx, *refs):
+    weight, gain, out, sums = refs[6:]
+    step = pl.program_id(0)
+
+    @pl.when(step == 0)
+    def _():
+        sums[...] = jnp.zeros_like(sums)
+
+    for at in range(4):
+
+        @pl.when(step // 2 == at)
+        def _():
+            for place, piece in batch_piece(refs[:6], at):
+                size = piece.shape[0]
+                row = pl.multiple_of((idx[1] ^ place) * size, 8)
+                out[pl.ds(row, size), :] = piece[...].astype(F32)
+
+    sums[...] += row_sums(out[...] * weight[...].astype(F32))
+
+    @pl.when(step == 7)
+    def _():
+        sums[...] = sums[...] / gain[...]
+
+
+def fill_cols(index, pieces, weight, gain):
+    _, size, width = pieces[0].shape
+    rows, block = 4 * size, width // 2
+
+    def source(n, step, idx):
+        return (0,) * (n - 1) + (step % 2,)
+
+    def place(step, idx):
+        return (0, (step % 2) * 4 + (idx[0] ^ (step // 2)))
+
+    specs = [
+        pl.BlockSpec(p.shape[:-1] + (block,), functools.partial(source, p.ndim)) for p in pieces
+    ]
+    return pl.pallas_call(
+        fill_cols_kernel,
+        out_shape=[shape((rows, 4 * width), F32), shape((8, rows), F32)],
+        grid_spec=pltpu.PrefetchScalarGridSpec(
+            num_scalar_prefetch=1,
+            grid=(8,),
+            in_specs=specs
+            + [
+                pl.BlockSpec((rows, block), place),
+                pl.BlockSpec((1, rows), lambda step, idx: (0, 0)),
+            ],
+            out_specs=[
+                pl.BlockSpec((rows, block), place),
+                pl.BlockSpec((8, rows), lambda step, idx: (0, 0)),
+            ],
+        ),
+        compiler_params=params(32),
+        name="fill_cols",
+    )(index, *pieces, weight, gain)
+
+
+def fill_heads_kernel(size, idx, *refs):
+    wq, wk, wv, gain = refs[6:10]
+    oq, ok, ov, oo, sums, scr = refs[10:]
+    cols = oq.shape[1] // 4
+    wide = 3 * cols
+    more = size // 4
+    third = more // 3
+    for at in range(4):
+        there = idx[0] ^ at
+        for place, piece in batch_piece(refs[:6], at):
+            scr[idx[1] ^ place] = piece[...]
+        at_row = pl.multiple_of(there * size, 8)
+        for c in range(4):
+            part = scr[c].astype(F32)
+            for o, out in enumerate((oq, ok, ov)):
+                out[pl.ds(at_row, size), c * cols : (c + 1) * cols] = part[
+                    :size, o * cols : (o + 1) * cols
+                ]
+            row = pl.multiple_of(c * size + there * more, 8)
+            oo[pl.ds(row, more), :wide] = part[size : size + more]
+            for o in range(3):
+                row = pl.multiple_of(c * size + there * more + o * third, 8)
+                oo[pl.ds(row, third), wide:] = part[size + more :, o * cols : (o + 1) * cols]
+    sums[...] = (
+        row_sums(oq[...] * wq[...].astype(F32))
+        + row_sums(ok[...] * wk[...].astype(F32))
+        + row_sums(ov[...] * wv[...].astype(F32))
+    ) / gain[...]
+
+
+def fill_heads(index, size, pieces, wq, wk, wv, gain):
+    out = [shape(wq.shape, F32)] * 4 + [shape((8, wq.shape[0]), F32)]
+    return pl.pallas_call(
+        functools.partial(fill_heads_kernel, size),
+        out_shape=out,
+        in_specs=[smem()] + vmem(10),
+        out_specs=vmem(5),
+        scratch_shapes=[pltpu.VMEM((4,) + pieces[0].shape[1:], BF)],
+        compiler_params=params(48),
+        name="fill_heads",
+    )(index, *pieces, wq, wk, wv, gain)
+
+
+def spread_grads(
+    sizes, grad_first, grad_second, attended, grad_low, normed1, grad_heads, grad_table,
+    weights, gains, nbuck, all_heads,
+):
+    nb, nc, nw = sizes
+    b, c, w = lax.axis_index("batch"), lax.axis_index("ctx"), lax.axis_index("wt")
+    w_query, w_key, w_value, w_in = weights
+    gain_attn, gain_ffn = gains
+    width = attended.shape[0] * attended.shape[2]
+    heads = all_heads // nc
+    cols = width // nc
+    part = width // nw
+    ff_part = grad_second.shape[0] // nw
+    ff_own = ff_part * nb
+
+    def ctx_total(value):
+        own = sum_wt(value, nw)
+        size = own.shape[0] // nc
+        own = sum_flip(own.astype(BF).reshape(nc, size, own.shape[1]), c, "ctx", nc)
+        whole = canonical(gather_flip(own.astype(BF), "ctx", nc), c)
+        return whole.reshape(nc * size, -1)
+
+    second = gather_flip(ctx_total(grad_second), "batch", nb)
+    out_second = canonical([p.astype(F32) for p in second], b).reshape(ff_own, width)
+    first = gather_flip(ctx_total(grad_first), "batch", nb)
+    out_first = jnp.zeros((part, nw * ff_own), F32)
+    for s, piece in enumerate(first):
+        for o in range(nw):
+            out_first = lax.dynamic_update_slice(
+                out_first,
+                piece[:, o * ff_part : (o + 1) * ff_part].astype(F32),
+                (0, o * ff_own + (b ^ s) * ff_part),
+            )
+
+    grad_wo = jnp.einsum("cqd,qe->cde", attended, grad_low, preferred_element_type=F32)
+    own_wo = sum_wt(grad_wo.astype(BF).reshape(width, width), nw).astype(BF)
+    own_wo = sum_flip(own_wo.reshape(nc, part // nc, width), c, "ctx", nc).astype(BF)
+    own_wo = sum_flip(own_wo.reshape(nb, part // nc // nb, width), b, "batch", nb).astype(BF)
+    own_wo = canonical(gather_flip(own_wo, "batch", nb), b).reshape(part // nc, width)
+    out_wo = canonical(gather_flip(own_wo, "ctx", nc), c).reshape(part, width).astype(F32)
+
+    grad_qkv = sum_wt(tn(normed1, grad_heads).astype(BF), nw).astype(BF)
+    line = jnp.pad(grad_table[:, :heads].reshape(1, -1), ((0, 15), (0, 3 * cols - heads * nbuck)))
+    if nw == 2:
+        line = line.astype(BF)
+        line = line.astype(F32) + flip(line, "wt", 2, 1).astype(F32)
+    else:
+        line = lax.psum(line, "wt")
+    size = part // nb
+    blocks = jnp.concatenate(
+        [
+            grad_qkv.reshape(nb, size, 3 * cols),
+            jnp.broadcast_to(line.astype(BF)[None], (nb, 16, 3 * cols)),
+        ],
+        axis=1,
+    )
+    block = sum_flip(blocks, b, "batch", nb).astype(BF)
+    pieces = canonical(gather_flip(block, "ctx", nc), c)
+    table_sum = pieces[:, size, : heads * nbuck].astype(F32).reshape(nc, nbuck, heads)
+    table_sum = jnp.transpose(table_sum, (1, 0, 2)).reshape(nbuck, all_heads)
+    own_buckets = nbuck // nw
+    out_table = lax.dynamic_slice_in_dim(table_sum, w * own_buckets, own_buckets, 0)
+    wide = canonical(gather_flip(pieces[:, :size], "batch", nb), b)
+    wide = wide.reshape(nb, nc, size, 3, cols)
+    wide = jnp.transpose(wide, (3, 0, 2, 1, 4)).reshape(3, part, width).astype(F32)
+    out_q, out_k, out_v = wide[0], wide[1], wide[2]
+
+    def gain_sum(pairs, gain):
+        total = sum(jnp.sum(left * right.astype(F32), axis=1) for left, right in pairs)
+        return total / gain.astype(F32)
+
+    gain_two_grad = gain_sum([(out_first, w_in)], gain_ffn)
+    gain_one_grad = gain_sum([(out_q, w_query), (out_k, w_key), (out_v, w_value)], gain_attn)
+    return gain_one_grad, gain_two_grad, out_table, out_q, out_k, out_v, out_wo, out_first, out_second
 
 
 def shards(
@@ -428,6 +722,7 @@
     )
     bucket_row = jnp.pad(buckets[::-1].reshape(1, -1), ((0, 0), (1, 0)), constant_values=-1)
 
+    paired = sizes == (4, 4, 2)
     (normed1, q, k, v, pt, pm, mix, *mixed) = attend(
         nc, heads, hsize, index_c, xs, head_cols(wq), head_cols(wk), head_cols(wv),
         gain_one, pk, pv, tab, bucket_row,
@@ -444,89 +739,123 @@
     grad_inner = act_pull(grad_act)[0].astype(BF)
     part_norm = nt(grad_inner, w_first).astype(BF)
     part_out = nn(act, w_second).astype(BF)
-    grad_second = tn(act, g_all).astype(BF)
-    grad_first = tn(n2, grad_inner).astype(BF)
-
     def cut(value, s):
         return value[s * rows : (s + 1) * rows]
 
     norm_parts = [cut(part_norm, 0)] + [
         flip(cut(part_norm, s), "batch", nb, s) for s in range(1, nb)
     ]
+    if paired:
+        index_bc = jnp.stack([b, c])
+        index_wb = jnp.stack([w, b])
+        index_wc = jnp.stack([w, c])
+        mine, theirs = weight_back("ffn_back", index_wc, [(n2, grad_inner), (act, g_all)])
+        ffn = add(mine, flip(theirs, "wt", 2, 1))
+        half = ffn.shape[1] // 2
+        ffn_keep, ffn_send = ffn[:, :half], ffn[:, half:]
+        norm_parts[0] = after(norm_parts[0], ffn_keep, ffn_send)
     (grad_hidden, grad_low, *gms) = branch_back(
         nb, nc, index_c, norm_parts, hidden, gain_two, g, wo
     )
     gms = gms[:1] + [flip(gms[s], "ctx", nc, s) for s in range(1, nc)]
+    if paired:
+        ffn = add(ffn_keep, flip(ffn_send, "ctx", nc, 1))
+        gms[0] = after(gms[0], ffn)
+        half = ffn.shape[1] // 2
+        ffn = add(ffn[:, :half], flip(ffn[:, half:], "ctx", nc, 2))
     (grad_heads, grad_table, *sends) = attend_back(
         nc, heads, hsize, index_c, gms, pt, pm, q, k, v, mix, pk, pv, bucket_row, nbuck
     )
+    outs = part_out.reshape(nb, rows, width)
+    if paired:
+        outs = add(outs[0::2], flip(outs[1::2], "batch", nb, 1))
+        result = hidden + outs[0].astype(F32) + flip(outs[1], "batch", nb, 2).astype(F32)
+    else:
+        result = hidden + outs[0].astype(F32)
+        for s in range(1, nb):
+            result = result + flip(outs[s], "batch", nb, s).astype(F32)
+
+    if paired:
+
+        def spread_ctx(value):
+            near = jnp.stack([value, flip(value, "ctx", nc, 2)])
+            return near, flip(near, "ctx", nc, 1)
+
+        def spread_batch(near, far):
+            one = flip(near, "batch", nb, 1)
+            one2 = flip(far, "batch", nb, 2)
+            two = flip(jnp.stack([near, one]), "batch", nb, 2)
+            two2 = flip(jnp.stack([far, one2]), "batch", nb, 1)
+            return near, one, two, far, one2, two2
+
+        wide = 3 * cols
+        quarter = part // 4
+        line = jnp.pad(
+            grad_table[:, :heads].reshape(1, -1), ((0, 15), (0, wide - heads * nbuck))
+        ).astype(BF)
+        mine, theirs = weight_back("qkv_back", index_wb, [(normed1, grad_heads)], (line,))
+        total = add(mine[0], flip(theirs[0], "wt", 2, 1))
+        total, line = total[:part], total[part:]
+        for step in (1, 2):
+            half = total.shape[0] // 2
+            send = jnp.concatenate([total[half:], line])
+            keep = jnp.concatenate([total[:half], line])
+            total = add(keep, flip(send, "batch", nb, step))
+            total, line = total[:half], total[half:]
+
+        mine, theirs = weight_back("wo_back", index_wc, [(attended, grad_low)])
+        wo_sum = add(mine[0], flip(theirs[0], "wt", 2, 1)).reshape(4, quarter, width)
+        small = quarter // 4
+        wo_sum = wo_sum.reshape(4, 4, small, width)
+        for name, step, bit in (("batch", 1, b & 1), ("batch", 2, b >> 1)):
+            pair_at = wo_sum.reshape(4, -1, 2, small, width) if step == 1 else wo_sum
+            axis = pair_at.ndim - 3
+            mine, theirs = halves(pair_at, bit, axis)
+            wo_sum = add(mine, flip(theirs, name, 4, step))
+        wo_sum = add(wo_sum[:2], flip(wo_sum[2:], "ctx", 4, 1))
+        wo_sum = add(wo_sum[0], flip(wo_sum[1], "ctx", 4, 2)).reshape(small, width)
+        third = small // 3
+        rest = [wo_sum[o * third : (o + 1) * third, wide:] for o in range(3)]
+        piece = jnp.concatenate([total, wo_sum[:, :wide], jnp.concatenate(rest, axis=1), line])
+        height = piece.shape[0] - 16
+        first_ctx, second_ctx = spread_ctx(ffn[0]), spread_ctx(ffn[1])
+        out_second = fill_rows(index_bc, spread_batch(*second_ctx))
+        out_first, sum_first = fill_cols(
+            index_bc, spread_batch(*first_ctx), w_in, gain_ffn.astype(F32).reshape(1, part)
+        )
+        near, far = spread_ctx(piece)
+        tables = pair(
+            pair(near[0, height], near[1, height], c >> 1, 0),
+            pair(far[0, height], far[1, height], c >> 1, 0),
+            c & 1,
+            1,
+        )
+        tables = tables[:, :, : heads * nbuck].astype(F32).reshape(nc, nbuck, heads)
+        tables = jnp.transpose(tables, (1, 0, 2)).reshape(nbuck, all_heads)
+        out_table = lax.dynamic_slice_in_dim(tables, w * (nbuck // nw), nbuck // nw, 0)
+        out_q, out_k, out_v, out_wo, sum_heads = fill_heads(
+            index_bc,
+            quarter,
+            spread_batch(near[:, :height], far[:, :height]),
+            w_query,
+            w_key,
+            w_value,
+            gain_attn.astype(F32).reshape(1, part),
+        )
+        gain_one_grad, gain_two_grad = sum_heads[0], sum_first[0]
+        sends[1:] = lax.optimization_barrier((*sends[1:], *first_ctx, *second_ctx))[: nc - 1]
+    else:
+        grad_second = tn(act, g_all).astype(BF)
+        grad_first = tn(n2, grad_inner).astype(BF)
+        (gain_one_grad, gain_two_grad, out_table, out_q, out_k, out_v, out_wo, out_first,
+         out_second) = spread_grads(
+            sizes, grad_first, grad_second, attended, grad_low, normed1, grad_heads, grad_table,
+            (w_query, w_key, w_value, w_in), (gain_attn, gain_ffn), nbuck, all_heads,
+        )
     sends = sends[:1] + [flip(sends[s], "ctx", nc, s) for s in range(1, nc)]
     grad_x, grad_memk, grad_memv = input_back(
         nc, mem, index_c, sends, x, wq, wk, wv, gain_one, grad_hidden
     )
-
-    result = hidden + cut(part_out, 0).astype(F32)
-    for s in range(1, nb):
-        result = result + flip(cut(part_out, s), "batch", nb, s).astype(F32)
-
-    def ctx_total(value):
-        own = sum_wt(value, nw)
-        size = own.shape[0] // nc
-        own = sum_flip(own.astype(BF).reshape(nc, size, own.shape[1]), c, "ctx", nc)
-        whole = canonical(gather_flip(own.astype(BF), "ctx", nc), c)
-        return whole.reshape(nc * size, -1)
-
-    second = gather_flip(ctx_total(grad_second), "batch", nb)
-    out_second = canonical([p.astype(F32) for p in second], b).reshape(ff_own, width)
-    first = gather_flip(ctx_total(grad_first), "batch", nb)
-    out_first = jnp.zeros((part, nw * ff_own), F32)
-    for s, piece in enumerate(first):
-        for o in range(nw):
-            out_first = lax.dynamic_update_slice(
-                out_first,
-                piece[:, o * ff_part : (o + 1) * ff_part].astype(F32),
-                (0, o * ff_own + (b ^ s) * ff_part),
-            )
-
-    grad_wo = jnp.einsum("cqd,qe->cde", attended, grad_low, preferred_element_type=F32)
-    own_wo = sum_wt(grad_wo.astype(BF).reshape(width, width), nw).astype(BF)
-    own_wo = sum_flip(own_wo.reshape(nc, part // nc, width), c, "ctx", nc).astype(BF)
-    own_wo = sum_flip(own_wo.reshape(nb, part // nc // nb, width), b, "batch", nb).astype(BF)
-    own_wo = canonical(gather_flip(own_wo, "batch", nb), b).reshape(part // nc, width)
-    out_wo = canonical(gather_flip(own_wo, "ctx", nc), c).reshape(part, width).astype(F32)
-
-    grad_qkv = sum_wt(tn(normed1, grad_heads).astype(BF), nw).astype(BF)
-    line = jnp.pad(grad_table[:, :heads].reshape(1, -1), ((0, 15), (0, 3 * cols - heads * nbuck)))
-    if nw == 2:
-        line = line.astype(BF)
-        line = line.astype(F32) + flip(line, "wt", 2, 1).astype(F32)
-    else:
-        line = lax.psum(line, "wt")
-    size = part // nb
-    blocks = jnp.concatenate(
-        [
-            grad_qkv.reshape(nb, size, 3 * cols),
-            jnp.broadcast_to(line.astype(BF)[None], (nb, 16, 3 * cols)),
-        ],
-        axis=1,
-    )
-    block = sum_flip(blocks, b, "batch", nb).astype(BF)
-    pieces = canonical(gather_flip(block, "ctx", nc), c)
-    table_sum = pieces[:, size, : heads * nbuck].astype(F32).reshape(nc, nbuck, heads)
-    table_sum = jnp.transpose(table_sum, (1, 0, 2)).reshape(nbuck, all_heads)
-    own_buckets = nbuck // nw
-    out_table = lax.dynamic_slice_in_dim(table_sum, w * own_buckets, own_buckets, 0)
-    wide = canonical(gather_flip(pieces[:, :size], "batch", nb), b)
-    wide = wide.reshape(nb, nc, size, 3, cols)
-    wide = jnp.transpose(wide, (3, 0, 2, 1, 4)).reshape(3, part, width).astype(F32)
-    out_q, out_k, out_v = wide[0], wide[1], wide[2]
-
-    def gain_sum(pairs, gain):
-        total = sum(jnp.sum(left * right.astype(F32), axis=1) for left, right in pairs)
-        return total / gain.astype(F32)
-
-    gain_two_grad = gain_sum([(out_first, w_in)], gain_ffn)
-    gain_one_grad = gain_sum([(out_q, w_query), (out_k, w_key), (out_v, w_value)], gain_attn)
     return (
         result.astype(BF)[None],
         grad_x[None],

time: 336 us -> 268 us (0.80)
  starting transfers between devices: 103 us -> 67.7 us
  Pallas kernels: 13.5 us -> 39.2 us
  other arithmetic: 42.9 us -> 21.6 us
  local copies, waits for them, and re-layouts: 52.8 us -> 34.3 us
  waiting for transfers between devices: 112 us -> 95.6 us
    ppermute x75 -> x59, starting transfers between devices: 103 us -> 67.7 us  [flip(): return lax.ppermute(value, axis, [(i, i ^ step) for i in range(size)])]
    pallas_call x0 -> x6, Pallas kernels: none -> 26.8 us  [the longest x1 9.62 us: fill_cols(): pl.pallas_call(fill_cols_kernel, out_shape=[shape((rows, 4 * width), F32)...]
    dynamic_update_slice x15 -> x0, other arithmetic: 23.9 us -> none  [the longest x8 14.7 us: shards(): lax.dynamic_update_slice(out_first, piece[:, o * ff_part:(o + 1) * ff_par...]
    ppermute x75 -> x59, waiting for transfers between devices: 112 us -> 95.6 us  [flip(): return lax.ppermute(value, axis, [(i, i ^ step) for i in range(size)])]
    squeeze x7 -> x3, local copies, waits for them, and re-layouts: 8.97 us -> 0.71 us  [the longest x1 0.69 us: shards(): outs[1]]
    another operation x0 -> x15, other arithmetic: none -> 7.88 us  [the longest x3 3.72 us: spread_batch(): two2 = flip(jnp.stack([far, one2]), 'batch', nb, 1)]
    broadcast_in_dim x10 -> x0, local copies, waits for them, and re-layouts: 6.48 us -> none  [the longest x4 3.13 us: canonical(): whole = jnp.zeros((len(parts),) + parts[0].shape, parts[0].dtype)]
    reduce_sum x4 -> x0, other arithmetic: 6.2 us -> none  [gain_sum(): jnp.sum(left * right.astype(F32), axis=1)]
  transfers between devices with their start and end apart: 75 -> 59, of which waited for: 26 -> 20; matrix products, arithmetic and copies ran while one was open for 28% -> 17% of each run, Pallas kernels for 4% -> 11%
where the time goes in v2:
time: 268 us; the launch traced here: 267 us
  waiting for transfers between devices  95.6 us (36%)
  starting transfers between devices  67.7 us (25%)
  Pallas kernels  39.2 us (15%)
  local copies, waits for them, and re-layouts  34.3 us (13%)
  other arithmetic  21.6 us (8%)
  matrix products  5.9 us (2%)
    ppermute x59, waiting for transfers between devices, flip(): return lax.ppermute(value, axis, [(i, i ^ step) for i in range(size)])  95.6 us
    ppermute x59, starting transfers between devices, flip(): return lax.ppermute(value, axis, [(i, i ^ step) for i in range(size)])  67.7 us
    unnamed x221, local copies, waits for them, and re-layouts  15.3 us
    pallas_call x1, Pallas kernels, fill_cols(): pl.pallas_call(fill_cols_kernel, out_shape=[shape((rows, 4 * width), F32)...  9.62 us
    pallas_call x3, Pallas kernels, weight_back(): pl.pallas_call(functools.partial(weight_back_kernel, count, len(extra)),...  6.47 us
    pallas_call x1, Pallas kernels, fill_heads(): pl.pallas_call(functools.partial(fill_heads_kernel, size), out_shape=out,...  6.34 us
  transfers between devices with their start and end apart: 59, of which 20 were waited for; matrix products, arithmetic and copies ran while one was open for 17% of the time, Pallas kernels for 11%

profile of v2, /device:TPU:0, one launch (start us, length us, event | category | flops | bytes accessed | tf_op | source)
XLA Modules:
  0.0 266.5 jit_solution(10696772183472019505)
XLA Ops:
  0.6 4.0 %collective-permute-start.20 = (bf16[128,768]{1,0:T(8,128)(2,1)}, bf16[128,768]{1,0:T(8,128)(2,1)S(1)}, u32[]{:S(2)}, u32[]{:S(2)}) collective-permute-start(bf16[128,768]{1,0:T(8,128)(2,1)} %bitcast.149), channel_id=1, source_target_pairs={{0,24},{8,16},{16,8},{24,0},{1,25},{9,17},{17,9},{25,1},{2,26},{10... | collective-permute-start | bytes 589832 | tf_op jit(solution)/shard_map/ppermute | solution.py:45
  27.1 7.8 %collective-permute-done.1.refs_2_ = bf16[128,768]{1,0:T(8,128)(2,1)S(1)} collective-permute-done((bf16[128,768]{1,0:T(8,128)(2,1)}, bf16[128,768]{1,0:T(8,128)(2,1)S(1)}, u32[]{:S(2)}, u32[]{:S(2)}) %collective-permute-start.1) | collective-permute-done | bytes 196640 | tf_op jit(solution)/shard_map/ppermute | solution.py:45
  34.9 4.3 %attend.1 = (bf16[512,768]{1,0:T(8,128)(2,1)S(1)}, bf16[512,192]{1,0:T(8,128)(2,1)S(1)}, bf16[512,192]{1,0:T(8,128)(2,1)S(1)}, bf16[512,192]{1,0:T(8,128)(2,1)S(...) custom-call(s32[1]{0:T(128)} %bitcast.idx, ...), custom_call_target="tpu_custom_call" | custom-call | tf_op jit(solution)/shard_map/attend/pallas_call | solution.py:183
  39.3 3.7 %collective-permute-start.7 = (bf16[128,192]{1,0:T(8,128)(2,1)S(1)}, bf16[128,192]{1,0:T(8,128)(2,1)S(1)}, u32[]{:S(2)}, u32[]{:S(2)}) collective-permute-start(bf16[128,192]{1,0:T(8,128)(2,1)S(1)} %get-tuple-element.61), channel_id=1, source_target_pairs={{0,2},{2,0},{4,6},{6,4},{1,3},{3,1},{5,7},{7,5},{8,10},{10,8},{12,... | collective-permute-start | bytes 147464 | tf_op jit(solution)/shard_map/ppermute | solution.py:45
  55.3 4.0 %collective-permute-done.11 = bf16[128,768]{1,0:T(8,128)(2,1)S(1)} collective-permute-done((bf16[128,768]{1,0:T(8,128)(2,1)S(1)}, bf16[128,768]{1,0:T(8,128)(2,1)S(1)}, u32[]{:S(2)}, u32[]{:S(2)}) %collective-permute-start.11) | collective-permute-done | bytes 196640 | tf_op jit(solution)/shard_map/ppermute | solution.py:45
  59.3 3.4 %collective-permute-done.12 = bf16[128,768]{1,0:T(8,128)(2,1)S(1)} collective-permute-done((bf16[128,768]{1,0:T(8,128)(2,1)S(1)}, bf16[128,768]{1,0:T(8,128)(2,1)S(1)}, u32[]{:S(2)}, u32[]{:S(2)}) %collective-permute-start.12) | collective-permute-done | bytes 196640 | tf_op jit(solution)/shard_map/ppermute | solution.py:45
  65.6 3.1 %ffn_back.1 = (bf16[2,384,768]{2,1,0:T(8,128)(2,1)S(1)}, bf16[2,384,768]{2,1,0:T(8,128)(2,1)}) custom-call(s32[2]{0:T(128)S(1)} %copy-done.73, bf16[512,768]{1,0:T(8,128)(2,1)S(1)} %constant_dynamic-update-slice_fusion.refs_0_, bf16[512,768]{1,0:T(8,128)(2,1)S(1)} %fusion.6.refs_1_, bf16[512,768]{1,0:T(8,128)(2,1)S(1)} %get-tuple-element.189.refs_2_, ...), custom_call_target="tpu_custom_call" | custom-call | tf_op jit(solution)/shard_map/ffn_back/pallas_call | solution.py:380
  83.6 8.0 %collective-permute-done.22.refs_1_ = bf16[128,768]{1,0:T(8,128)(2,1)S(1)} collective-permute-done((bf16[128,768]{1,0:T(8,128)(2,1)S(1)}, bf16[128,768]{1,0:T(8,128)(2,1)S(1)}, u32[]{:S(2)}, u32[]{:S(2)}) %collective-permute-start.22) | collective-permute-done | bytes 196640 | tf_op jit(solution)/shard_map/ppermute | solution.py:45
  91.6 4.4 %collective-permute-done.24.refs_3_ = bf16[128,768]{1,0:T(8,128)(2,1)S(1)} collective-permute-done((bf16[128,768]{1,0:T(8,128)(2,1)S(1)}, bf16[128,768]{1,0:T(8,128)(2,1)S(1)}, u32[]{:S(2)}, u32[]{:S(2)}) %collective-permute-start.24) | collective-permute-done | bytes 196640 | tf_op jit(solution)/shard_map/ppermute | solution.py:45
  109.2 8.2 %collective-permute-done.27.refs_2_ = bf16[128,192]{1,0:T(8,128)(2,1)S(1)} collective-permute-done((bf16[128,192]{1,0:T(8,128)(2,1)S(1)}, bf16[128,192]{1,0:T(8,128)(2,1)S(1)}, u32[]{:S(2)}, u32[]{:S(2)}) %collective-permute-start.27) | collective-permute-done | bytes 49184 | tf_op jit(solution)/shard_map/ppermute | solution.py:45
  117.5 2.8 %attend_back.1 = (bf16[512,576]{1,0:T(8,128)(2,1)S(1)}, f32[32,8]{1,0:T(8,128)S(1)}, bf16[448,192]{1,0:T(8,128)(2,1)S(1)}, bf16[448,192]{1,0:T(8,128)(2,1)S(1)},...) custom-call(s32[1]{0:T(128)} %bitcast.idx, bf16[128,192]{1,0:T(8,128)(2,1)S(1)} %get-tuple-element.70.refs_0_, ...), custom_call_target="tpu_custom_call" | custom-call | tf_op jit(solution)/shard_map/attend_back/pallas_call | solution.py:334
  128.6 3.4 %collective-permute-start.30 = (bf16[96,768]{1,0:T(8,128)(2,1)S(1)}, bf16[96,768]{1,0:T(8,128)(2,1)S(1)}, u32[]{:S(2)}, u32[]{:S(2)}) collective-permute-start(bf16[96,768]{1,0:T(8,128)(2,1)S(1)} %get-tuple-element.177), channel_id=1, source_target_pairs={{0,4},{2,6},{4,0},{6,2},{1,5},{3,7},{5,1},{7,3},{8,12},{10,14},{12... | collective-permute-start | bytes 442376 | tf_op jit(solution)/shard_map/ppermute | solution.py:45
  132.0 4.8 %collective-permute-done.41 = bf16[4,2,24,768]{3,2,0,1:T(8,128)(2,1)S(1)} collective-permute-done((bf16[4,2,24,768]{3,2,0,1:T(8,128)(2,1)S(1)}, bf16[4,2,24,768]{3,2,0,1:T(8,128)(2,1)S(1)}, u32[]{:S(2)}, u32[]{:S(2)}) %collective-permute-start.41) | collective-permute-done | bytes 294944 | tf_op jit(solution)/shard_map/ppermute | solution.py:45
  138.7 3.9 %collective-permute-start.32 = (bf16[96,768]{1,0:T(8,128)(2,1)S(1)}, bf16[96,768]{1,0:T(8,128)(2,1)S(1)}, u32[]{:S(2)}, u32[]{:S(2)}) collective-permute-start(bf16[96,768]{1,0:T(8,128)(2,1)S(1)} %get-tuple-element.178), channel_id=1, source_target_pairs={{0,4},{2,6},{4,0},{6,2},{1,5},{3,7},{5,1},{7,3},{8,12},{10,14},{12... | collective-permute-start | bytes 442376 | tf_op jit(solution)/shard_map/ppermute | solution.py:45
  147.2 7.1 %collective-permute-done.43 = bf16[2,24,768]{2,1,0:T(8,128)(2,1)S(1)} collective-permute-done((bf16[2,24,768]{2,1,0:T(8,128)(2,1)S(1)}, bf16[2,24,768]{2,1,0:T(8,128)(2,1)S(1)}, u32[]{:S(2)}, u32[]{:S(2)}) %collective-permute-start.43) | collective-permute-done | bytes 73760 | tf_op jit(solution)/shard_map/ppermute | solution.py:45
  174.5 12.1 %collective-permute-done.35.refs_2_ = bf16[448,192]{1,0:T(8,128)(2,1)S(1)} collective-permute-done((bf16[448,192]{1,0:T(8,128)(2,1)S(1)}, bf16[448,192]{1,0:T(8,128)(2,1)S(1)}, u32[]{:S(2)}, u32[]{:S(2)}) %collective-permute-start.35) | collective-permute-done | bytes 172064 | tf_op jit(solution)/shard_map/ppermute | solution.py:45
  188.6 3.1 %input_back.1 = (bf16[128,768]{1,0:T(8,128)(2,1)}, f32[20,768]{1,0:T(8,128)S(1)}, f32[20,768]{1,0:T(8,128)S(1)}) custom-call(s32[1]{0:T(128)} %bitcast.idx, bf16[448,192]{1,0:T(8,128)(2,1)S(1)} %get-tuple-element.80.refs_0_, bf16[448,192]{1,0:T(8,128)(2,1)S(1)} %collective-permute-done.34.refs_1_, bf16[448,192]{1,0:T(8,128)(2,1)S(1)} %collective-permute-done.35.refs_2_, ...), custom_call_target="tpu_custom_call" | custom-call | tf_op jit(solution)/shard_map/input_back/pallas_call | solution.py:422
  193.8 3.2 %collective-permute-start.48 = (bf16[2,144,576]{2,1,0:T(8,128)(2,1)S(1)}, bf16[2,144,576]{2,1,0:T(8,128)(2,1)S(1)}, u32[]{:S(2)}, u32[]{:S(2)}) collective-permute-start(bf16[2,144,576]{2,1,0:T(8,128)(2,1)S(1)} %pad_maximum_fusion.14), channel_id=1, source_target_pairs={{0,2},{2,0},{4,6},{6,4},{1,3},{3,1},{5,7},{7,5},{8,10},{10,8},{12,... | collective-permute-start | bytes 995336 | tf_op jit(solution)/shard_map/ppermute | solution.py:45
  197.1 5.6 %collective-permute-done.48 = bf16[2,144,576]{2,1,0:T(8,128)(2,1)S(1)} collective-permute-done((bf16[2,144,576]{2,1,0:T(8,128)(2,1)S(1)}, bf16[2,144,576]{2,1,0:T(8,128)(2,1)S(1)}, u32[]{:S(2)}, u32[]{:S(2)}) %collective-permute-start.48) | collective-permute-done | bytes 331808 | tf_op jit(solution)/shard_map/ppermute | solution.py:45
  206.6 3.5 %collective-permute-done.57.refs_4_ = bf16[2,96,768]{2,1,0:T(8,128)(2,1)S(1)} collective-permute-done((bf16[2,96,768]{2,1,0:T(8,128)(2,1)S(1)}, bf16[2,96,768]{2,1,0:T(8,128)(2,1)S(1)}, u32[]{:S(2)}, u32[]{:S(2)}) %collective-permute-start.57) | collective-permute-done | bytes 294944 | tf_op jit(solution)/shard_map/ppermute | solution.py:45
  224.3 14.9 %collective-permute-done.58.refs_5_ = bf16[2,2,96,768]{3,2,1,0:T(8,128)(2,1)S(1)} collective-permute-done((bf16[2,2,96,768]{3,2,1,0:T(8,128)(2,1)}, bf16[2,2,96,768]{3,2,1,0:T(8,128)(2,1)S(1)}, u32[]{:S(2)}, u32[]{:S(2)}) %collective-permute-start.58) | collective-permute-done | bytes 589856 | tf_op jit(solution)/shard_map/ppermute | solution.py:45
  239.2 4.4 %fill_rows.1 = f32[1536,768]{1,0:T(8,128)} custom-call(s32[2]{0:T(128)S(1)} %copy-done.72, bf16[2,96,768]{2,1,0:T(8,128)(2,1)S(1)} %copy-done.21, bf16[2,96,768]{2,1,0:T(8,128)(2,1)S(1)} %copy-done.25, bf16[2,2,96,768]{3,2,1,0:T(8,128)(2,1)} %collective-permute-done.56.refs_2_, bf16[2,96,768]{2,1,0:T(8,128)(2,1)S(1)} %copy-done.23, ...), custom_call_target="tpu_custom_call" | custom-call | tf_op jit(solution)/shard_map/fill_rows/pallas_call | solution.py:469
  243.7 9.6 %fill_cols.1 = (f32[384,3072]{1,0:T(8,128)}, f32[8,384]{1,0:T(8,128)S(1)}) custom-call(s32[2]{0:T(128)S(1)} %copy-done.72, bf16[2,96,768]{2,1,0:T(8,128)(2,1)S(1)} %copy-done.29, bf16[2,96,768]{2,1,0:T(8,128)(2,1)S(1)} %copy-done.35, bf16[2,2,96,768]{3,2,1,0:T(8,128)(2,1)} %collective-permute-done.52.refs_2_, bf16[2,96,768]{2,1,0:T(8,128)(2,1)S(1)} %copy-done.33, ...), custom_call_target="tpu_custom_call" | custom-call | tf_op jit(solution)/shard_map/fill_cols/pallas_call | solution.py:520
  259.6 6.3 %fill_heads.1 = (f32[384,768]{1,0:T(8,128)}, f32[384,768]{1,0:T(8,128)}, f32[384,768]{1,0:T(8,128)}, f32[384,768]{1,0:T(8,128)}, f32[8,384]{1,0:T(8,128)S(1)}) custom-call(s32[2]{0:T(128)S(1)} %copy-done.72, bf16[2,128,576]{2,1,0:T(8,128)(2,1)S(1)} %copy-done.17, bf16[2,128,576]{2,1,0:T(8,128)(2,1)S(1)} %collective-permute-done.46.refs_1_, ...), custom_call_target="tpu_custom_call" | custom-call | tf_op jit(solution)/shard_map/fill_heads/pallas_call | solution.py:573
  (430 shorter events, 128.8 us)
Async XLA Ops:
  17.6 17.3 %collective-permute-start.1 = (bf16[128,768]{1,0:T(8,128)(2,1)}, bf16[128,768]{1,0:T(8,128)(2,1)S(1)}, u32[]{:S(2)}, u32[]{:S(2)}) collective-permute-start(bf16[128,768]{1,0:T(8,128)(2,1)} %bitcast.1.refs_0_.refs_4_), channel_id=1, source_target_pairs={{0,4},{2,6},{4,0},{6,2},{1,5},{3,7},{5,1},{7,3},{8,12},{10,14},{12... | collective-permute-start | bytes 589832 | tf_op jit(solution)/shard_map/ppermute | solution.py:45
  23.8 20.3 %collective-permute-start.14 = (bf16[384,768]{1,0:T(8,128)(2,1)S(1)}, bf16[384,768]{1,0:T(8,128)(2,1)S(1)}, u32[]{:S(2)}, u32[]{:S(2)}) collective-permute-start(bf16[384,768]{1,0:T(8,128)(2,1)S(1)} %copy-done.96), channel_id=1, source_target_pairs={{0,1},{1,0},{2,3},{3,2},{4,5},{5,4},{6,7},{7,6},{8,9},{9,8},{10,11... | collective-permute-start | bytes 1769480 | tf_op jit(solution)/shard_map/ppermute | solution.py:45
  24.0 21.5 %collective-permute-start.10 = (bf16[384,768]{1,0:T(8,128)(2,1)S(1)}, bf16[384,768]{1,0:T(8,128)(2,1)S(1)}, u32[]{:S(2)}, u32[]{:S(2)}) collective-permute-start(bf16[384,768]{1,0:T(8,128)(2,1)S(1)} %copy-done.93), channel_id=1, source_target_pairs={{0,1},{1,0},{2,3},{3,2},{4,5},{5,4},{6,7},{7,6},{8,9},{9,8},{10,11... | collective-permute-start | bytes 1769480 | tf_op jit(solution)/shard_map/ppermute | solution.py:45
  26.8 19.3 %collective-permute-start.15 = (bf16[384,768]{1,0:T(8,128)(2,1)S(1)}, bf16[384,768]{1,0:T(8,128)(2,1)}, u32[]{:S(2)}, u32[]{:S(2)}) collective-permute-start(bf16[384,768]{1,0:T(8,128)(2,1)S(1)} %copy-done.95), channel_id=1, source_target_pairs={{0,1},{1,0},{2,3},{3,2},{4,5},{5,4},{6,7},{7,6},{8,9},{9,8},{10,11... | collective-permute-start | bytes 1769480 | tf_op jit(solution)/shard_map/ppermute | solution.py:45
  75.4 24.8 %collective-permute-start.16 = (bf16[2,128,768]{2,1,0:T(8,128)(2,1)S(1)}, bf16[2,128,768]{2,1,0:T(8,128)(2,1)S(1)}, u32[]{:S(2)}, u32[]{:S(2)}) collective-permute-start(bf16[2,128,768]{2,1,0:T(8,128)(2,1)S(1)} %slice.138), channel_id=1, source_target_pairs={{0,8},{8,0},{16,24},{24,16},{1,9},{9,1},{17,25},{25,17},{2,10},{10... | collective-permute-start | bytes 1179656 | tf_op jit(solution)/shard_map/ppermute | solution.py:45
  82.3 21.9 %collective-permute-start.25 = (bf16[2,192,768]{2,1,0:T(8,128)(2,1)S(1)}, bf16[2,192,768]{2,1,0:T(8,128)(2,1)S(1)}, u32[]{:S(2)}, u32[]{:S(2)}) collective-permute-start(bf16[2,192,768]{2,1,0:T(8,128)(2,1)S(1)} %slice.182), channel_id=1, source_target_pairs={{0,2},{2,0},{4,6},{6,4},{1,3},{3,1},{5,7},{7,5},{8,10},{10,8},{12,... | collective-permute-start | bytes 1769480 | tf_op jit(solution)/shard_map/ppermute | solution.py:45
  100.2 25.7 %collective-permute-start.40 = (bf16[384,768]{1,0:T(8,128)(2,1)}, bf16[384,768]{1,0:T(8,128)(2,1)}, u32[]{:S(2)}, u32[]{:S(2)}) collective-permute-start(bf16[384,768]{1,0:T(8,128)(2,1)} %bitcast.44), channel_id=1, source_target_pairs={{0,1},{1,0},{2,3},{3,2},{4,5},{5,4},{6,7},{7,6},{8,9},{9,8},{10,11... | collective-permute-start | bytes 1769480 | tf_op jit(solution)/shard_map/ppermute | solution.py:45
  101.1 35.9 %collective-permute-start.17 = (bf16[128,768]{1,0:T(8,128)(2,1)}, bf16[128,768]{1,0:T(8,128)(2,1)}, u32[]{:S(2)}, u32[]{:S(2)}) collective-permute-start(bf16[128,768]{1,0:T(8,128)(2,1)} %slice_bitcast_fusion), channel_id=1, source_target_pairs={{0,16},{8,24},{16,0},{24,8},{1,17},{9,25},{17,1},{25,9},{2,18},{10... | collective-permute-start | bytes 589832 | tf_op jit(solution)/shard_map/ppermute | solution.py:45
  107.4 20.0 %collective-permute-start.29 = (bf16[2,96,768]{2,1,0:T(8,128)(2,1)}, bf16[2,96,768]{2,1,0:T(8,128)(2,1)}, u32[]{:S(2)}, u32[]{:S(2)}) collective-permute-start(bf16[2,96,768]{2,1,0:T(8,128)(2,1)} %slice.187), channel_id=1, source_target_pairs={{0,4},{2,6},{4,0},{6,2},{1,5},{3,7},{5,1},{7,3},{8,12},{10,14},{12... | collective-permute-start | bytes 884744 | tf_op jit(solution)/shard_map/ppermute | solution.py:45
  125.9 19.6 %collective-permute-start.37 = (bf16[400,576]{1,0:T(8,128)(2,1)S(1)}, bf16[400,576]{1,0:T(8,128)(2,1)S(1)}, u32[]{:S(2)}, u32[]{:S(2)}) collective-permute-start(bf16[400,576]{1,0:T(8,128)(2,1)S(1)} %bitcast.161), channel_id=1, source_target_pairs={{0,1},{1,0},{2,3},{3,2},{4,5},{5,4},{6,7},{7,6},{8,9},{9,8},{10,11... | collective-permute-start | bytes 1382408 | tf_op jit(solution)/shard_map/ppermute | solution.py:45
  138.7 17.1 %collective-permute-start.32 = (bf16[96,768]{1,0:T(8,128)(2,1)S(1)}, bf16[96,768]{1,0:T(8,128)(2,1)S(1)}, u32[]{:S(2)}, u32[]{:S(2)}) collective-permute-start(bf16[96,768]{1,0:T(8,128)(2,1)S(1)} %get-tuple-element.178), channel_id=1, source_target_pairs={{0,4},{2,6},{4,0},{6,2},{1,5},{3,7},{5,1},{7,3},{8,12},{10,14},{12... | collective-permute-start | bytes 442376 | tf_op jit(solution)/shard_map/ppermute | solution.py:45
  142.7 18.5 %collective-permute-start.31 = (bf16[2,96,768]{2,1,0:T(8,128)(2,1)S(1)}, bf16[2,96,768]{2,1,0:T(8,128)(2,1)S(1)}, u32[]{:S(2)}, u32[]{:S(2)}) collective-permute-start(bf16[2,96,768]{2,1,0:T(8,128)(2,1)S(1)} %get-tuple-element.175.refs_0_), channel_id=1, source_target_pairs={{0,2},{2,0},{4,6},{6,4},{1,3},{3,1},{5,7},{7,5},{8,10},{10,8},{12,... | collective-permute-start | bytes 884744 | tf_op jit(solution)/shard_map/ppermute | solution.py:45
  142.8 23.8 %collective-permute-start.51 = (bf16[2,96,768]{2,1,0:T(8,128)(2,1)S(1)}, bf16[2,96,768]{2,1,0:T(8,128)(2,1)S(1)}, u32[]{:S(2)}, u32[]{:S(2)}) collective-permute-start(bf16[2,96,768]{2,1,0:T(8,128)(2,1)S(1)} %get-tuple-element.175.refs_0_), channel_id=1, source_target_pairs={{0,8},{8,0},{16,24},{24,16},{1,9},{9,1},{17,25},{25,17},{2,10},{10... | collective-permute-start | bytes 884744 | tf_op jit(solution)/shard_map/ppermute | solution.py:45
  164.8 21.8 %collective-permute-start.35 = (bf16[448,192]{1,0:T(8,128)(2,1)S(1)}, bf16[448,192]{1,0:T(8,128)(2,1)S(1)}, u32[]{:S(2)}, u32[]{:S(2)}) collective-permute-start(bf16[448,192]{1,0:T(8,128)(2,1)S(1)} %copy-done.79), channel_id=1, source_target_pairs={{0,4},{2,6},{4,0},{6,2},{1,5},{3,7},{5,1},{7,3},{8,12},{10,14},{12... | collective-permute-start | bytes 516104 | tf_op jit(solution)/shard_map/ppermute | solution.py:45
  166.6 20.4 %collective-permute-start.36 = (bf16[448,192]{1,0:T(8,128)(2,1)S(1)}, bf16[448,192]{1,0:T(8,128)(2,1)S(1)}, u32[]{:S(2)}, u32[]{:S(2)}) collective-permute-start(bf16[448,192]{1,0:T(8,128)(2,1)S(1)} %copy-done.77), channel_id=1, source_target_pairs={{0,6},{2,4},{4,2},{6,0},{1,7},{3,5},{5,3},{7,1},{8,14},{10,12},{12... | collective-permute-start | bytes 516104 | tf_op jit(solution)/shard_map/ppermute | solution.py:45
  168.9 74.7 %collective-permute-start.52 = (bf16[2,2,96,768]{3,2,1,0:T(8,128)(2,1)}, bf16[2,2,96,768]{3,2,1,0:T(8,128)(2,1)}, u32[]{:S(2)}, u32[]{:S(2)}) collective-permute-start(bf16[2,2,96,768]{3,2,1,0:T(8,128)(2,1)} %pad_maximum_fusion.10), channel_id=1, source_target_pairs={{0,16},{8,24},{16,0},{24,8},{1,17},{9,25},{17,1},{25,9},{2,18},{10... | collective-permute-start | bytes 1769480 | tf_op jit(solution)/shard_map/ppermute | solution.py:45
  170.1 23.6 %collective-permute-start.45 = (bf16[144,576]{1,0:T(8,128)(2,1)S(1)}, bf16[144,576]{1,0:T(8,128)(2,1)S(1)}, u32[]{:S(2)}, u32[]{:S(2)}) collective-permute-start(bf16[144,576]{1,0:T(8,128)(2,1)S(1)} %pad_maximum_fusion.17), channel_id=1, source_target_pairs={{0,4},{2,6},{4,0},{6,2},{1,5},{3,7},{5,1},{7,3},{8,12},{10,14},{12... | collective-permute-start | bytes 497672 | tf_op jit(solution)/shard_map/ppermute | solution.py:45
  172.9 48.1 %collective-permute-start.56 = (bf16[2,2,96,768]{3,2,1,0:T(8,128)(2,1)}, bf16[2,2,96,768]{3,2,1,0:T(8,128)(2,1)}, u32[]{:S(2)}, u32[]{:S(2)}) collective-permute-start(bf16[2,2,96,768]{3,2,1,0:T(8,128)(2,1)} %pad_maximum_fusion.12), channel_id=1, source_target_pairs={{0,16},{8,24},{16,0},{24,8},{1,17},{9,25},{17,1},{25,9},{2,18},{10... | collective-permute-start | bytes 1769480 | tf_op jit(solution)/shard_map/ppermute | solution.py:45
  186.6 18.0 %collective-permute-start.53 = (bf16[2,96,768]{2,1,0:T(8,128)(2,1)S(1)}, bf16[2,96,768]{2,1,0:T(8,128)(2,1)S(1)}, u32[]{:S(2)}, u32[]{:S(2)}) collective-permute-start(bf16[2,96,768]{2,1,0:T(8,128)(2,1)S(1)} %collective-permute-done.31.refs_3_), channel_id=1, source_target_pairs={{0,16},{8,24},{16,0},{24,8},{1,17},{9,25},{17,1},{25,9},{2,18},{10... | collective-permute-start | bytes 884744 | tf_op jit(solution)/shard_map/ppermute | solution.py:45
  187.0 23.0 %collective-permute-start.57 = (bf16[2,96,768]{2,1,0:T(8,128)(2,1)S(1)}, bf16[2,96,768]{2,1,0:T(8,128)(2,1)S(1)}, u32[]{:S(2)}, u32[]{:S(2)}) collective-permute-start(bf16[2,96,768]{2,1,0:T(8,128)(2,1)S(1)} %collective-permute-done.33.refs_3_), channel_id=1, source_target_pairs={{0,16},{8,24},{16,0},{24,8},{1,17},{9,25},{17,1},{25,9},{2,18},{10... | collective-permute-start | bytes 884744 | tf_op jit(solution)/shard_map/ppermute | solution.py:45
  210.1 33.5 %collective-permute-start.54 = (bf16[2,2,96,768]{3,2,1,0:T(8,128)(2,1)}, bf16[2,2,96,768]{3,2,1,0:T(8,128)(2,1)S(1)}, u32[]{:S(2)}, u32[]{:S(2)}) collective-permute-start(bf16[2,2,96,768]{3,2,1,0:T(8,128)(2,1)} %pad_maximum_fusion.11), channel_id=1, source_target_pairs={{0,8},{8,0},{16,24},{24,16},{1,9},{9,1},{17,25},{25,17},{2,10},{10... | collective-permute-start | bytes 1769480 | tf_op jit(solution)/shard_map/ppermute | solution.py:45
  213.4 25.8 %collective-permute-start.58 = (bf16[2,2,96,768]{3,2,1,0:T(8,128)(2,1)}, bf16[2,2,96,768]{3,2,1,0:T(8,128)(2,1)S(1)}, u32[]{:S(2)}, u32[]{:S(2)}) collective-permute-start(bf16[2,2,96,768]{3,2,1,0:T(8,128)(2,1)} %pad_maximum_fusion.13), channel_id=1, source_target_pairs={{0,8},{8,0},{16,24},{24,16},{1,9},{9,1},{17,25},{25,17},{2,10},{10... | collective-permute-start | bytes 1769480 | tf_op jit(solution)/shard_map/ppermute | solution.py:45
  215.8 38.1 %collective-permute-start.47 = (bf16[2,2,128,576]{2,3,1,0:T(8,128)(2,1)}, bf16[2,2,128,576]{2,3,1,0:T(8,128)(2,1)}, u32[]{:S(2)}, u32[]{:S(2)}) collective-permute-start(bf16[2,2,128,576]{2,3,1,0:T(8,128)(2,1)} %copy.40), channel_id=1, source_target_pairs={{0,16},{8,24},{16,0},{24,8},{1,17},{9,25},{17,1},{25,9},{2,18},{10... | collective-permute-start | bytes 1769480 | tf_op jit(solution)/shard_map/ppermute | solution.py:45
  221.0 34.2 %collective-permute-start.50 = (bf16[2,2,128,576]{2,3,1,0:T(8,128)(2,1)}, bf16[2,2,128,576]{2,3,1,0:T(8,128)(2,1)}, u32[]{:S(2)}, u32[]{:S(2)}) collective-permute-start(bf16[2,2,128,576]{2,3,1,0:T(8,128)(2,1)} %copy.41), channel_id=1, source_target_pairs={{0,8},{8,0},{16,24},{24,16},{1,9},{9,1},{17,25},{25,17},{2,10},{10... | collective-permute-start | bytes 1769480 | tf_op jit(solution)/shard_map/ppermute | solution.py:45
  (140 other events, 1422.0 us)

commit v3 on v1

--- a/solution.py
+++ b/solution.py
@@ -161,7 +161,7 @@
         in_specs=[smem()] + vmem(nc + 8),
         out_specs=vmem(len(out)),
         scratch_shapes=[pltpu.VMEM((length, cols), BF)],
-        compiler_params=params(48),
+        compiler_params=params(24),
         name="attend",
     )(index, *xs, wq, wk, wv, gain, pk, pv, tab, bucket_row)
 
@@ -316,7 +316,7 @@
             pltpu.VMEM((cols, length), F32),
             pltpu.VMEM((LANES, 2 * length), F32),
         ],
-        compiler_params=params(48),
+        compiler_params=params(24),
         name="attend_back",
     )(index, *gms, pt, pm, q, k, v, mix, pk, pv, bucket_row)
 
@@ -363,7 +363,7 @@
     )(index, *parts, x, wq, wk, wv, gain, grad_hidden)
 
 
-def shards(
+def general(
     sizes,
     inputs,
     prefix_keys,
@@ -544,14 +544,870 @@
     )
 
 
+NEAR_LAST = (0, 2, 1, 3)
+LINE = 8
+
+
+def call(kernel, name, index, args, out, scratch=(), mib=24, far=()):
+    stay = [pl.BlockSpec(memory_space=pltpu.HBM)] * len(far)
+    return pl.pallas_call(
+        kernel,
+        out_shape=out,
+        in_specs=[smem()] + stay + vmem(len(args)),
+        out_specs=vmem(len(out)),
+        scratch_shapes=list(scratch),
+        compiler_params=params(mib),
+        name=name,
+    )(index, *far, *args)
+
+
+def after(values, earlier):
+    return lax.optimization_barrier((tuple(values), tuple(earlier)))[0]
+
+
+def both_gains(wt, own, other, at, size):
+    mine, theirs = own[:, at : at + size].astype(F32), other[:, at : at + size].astype(F32)
+    first = jnp.where(wt == 0, mine, theirs)
+    second = jnp.where(wt == 0, theirs, mine)
+    return jnp.concatenate([first, second], axis=1)
+
+
+def fetch_rows(sems, wt, pairs):
+    copies = []
+    for i, (scr, own, other) in enumerate(pairs):
+        rows = own.shape[0]
+        for j, (source, place) in enumerate(((own, wt), (other, 1 - wt))):
+            to = scr.at[pl.ds(pl.multiple_of(place * rows, rows), rows), :]
+            copies.append(pltpu.make_async_copy(source, to, sems.at[2 * i + j]))
+            copies[-1].start()
+    return copies
+
+
+def heads_kernel(heads, hsize, idx, *refs):
+    wq, wk, wv, wq2, wk2, wv2 = refs[:6]
+    fars = refs[6:13]
+    xs = refs[13:17]
+    n1_ref, q_ref, k_ref, v_ref, pt_ref, pm_ref, mix_ref, wrow_ref, pk_ref, pv_ref = refs[17:27]
+    outs = refs[27:31]
+    att_scr, line_scr, sems, more_sems, *scrs = refs[31:]
+    w_scr, nears = scrs[:3], scrs[3:]
+    small, small2, tab, tab2, pk_all, pv_all, bucket_row = nears
+    more = [
+        pltpu.make_async_copy(source, to, more_sems.at[i])
+        for i, (source, to) in enumerate(zip(fars, nears))
+    ]
+    for copy in more:
+        copy.start()
+    batch, here, wt = idx[0], idx[1], idx[2]
+    rows, width = xs[0].shape
+    length = 4 * rows
+    half = wq.shape[0]
+    cols = heads * hsize
+    window = w_scr[0].shape[1]
+    shift = window - cols
+    odd = here % 2
+    lanes = pl.ds(pl.multiple_of((here * cols - odd * shift), LANES), window)
+    copies = fetch_rows(
+        sems,
+        wt,
+        [
+            (scr, own.at[:, lanes], other.at[:, lanes])
+            for scr, own, other in zip(w_scr, (wq, wk, wv), (wq2, wk2, wv2))
+        ],
+    )
+    for copy in more:
+        copy.wait()
+    for j in range(4):
+
+        @pl.when(here == j)
+        def _():
+            take = slice(j * cols, (j + 1) * cols)
+            pk_ref[...] = pk_all[:, take]
+            pv_ref[...] = pv_all[:, take]
+
+    def own_cols(value):
+        return jnp.where(odd == 0, value[:, :cols], value[:, shift:])
+
+    gain = both_gains(wt, small, small2, 0, half)
+    for step in range(4):
+        scaled, _ = norm(xs[step][...].astype(F32))
+        at = pl.multiple_of((here ^ step) * rows, rows)
+        n1_ref[pl.ds(at, rows), :] = (scaled * gain).astype(BF)
+    normed = n1_ref[...]
+    for copy in copies:
+        copy.wait()
+    quarter = half // 4
+    at = pl.multiple_of(wt * half + batch * quarter, quarter)
+    for p, (scr, out) in enumerate(zip(w_scr, (q_ref, k_ref, v_ref))):
+        out[...] = own_cols(nn(normed, scr[...])).astype(BF)
+        wrow_ref[:, p * cols : (p + 1) * cols] = own_cols(
+            scr[pl.ds(at, quarter), :].astype(F32)
+        ).astype(BF)
+    vals_t = v_ref[...].T
+    pv_t = pv_ref[...].astype(F32).T.astype(BF)
+    own_buckets = tab.shape[0]
+    ids = lax.broadcasted_iota(jnp.int32, (own_buckets, 2 * length), 0)
+    lines = tn(tab[...].astype(F32), (ids + wt * own_buckets == bucket_row[...]).astype(F32))
+    lines = lines + tn(
+        tab2[...].astype(F32), (ids + (1 - wt) * own_buckets == bucket_row[...]).astype(F32)
+    )
+    line_scr[: lines.shape[0], :] = lines
+    for h in range(heads):
+        part = slice(h * hsize, (h + 1) * hsize)
+        query = q_ref[:, part]
+        line = jnp.broadcast_to(line_scr[pl.ds(here * heads + h, 1), :], (LANES, 2 * length))
+        spread = pltpu.roll(line, 0, 1, stride=1, stride_axis=0)
+        bias = jnp.concatenate(
+            [spread[:, length - at : 2 * length - at] for at in range(0, length, LANES)], axis=0
+        )
+        score = nt(k_ref[:, part], query) + bias
+        front = nt(pk_ref[:, part], query)
+        top = jnp.maximum(
+            jnp.max(score, axis=0, keepdims=True), jnp.max(front, axis=0, keepdims=True)
+        )
+        score = jnp.exp(score - top)
+        front = jnp.exp(front - top)
+        total = jnp.sum(score, axis=0, keepdims=True) + jnp.sum(front, axis=0, keepdims=True)
+        scale = 1.0 / total
+        prob = (score * scale).astype(BF)
+        prob_mem = (front * scale).astype(BF)
+        pt_ref[h] = prob
+        pm_ref[h] = prob_mem
+        mix_ref[part, :] = nn(vals_t[part, :], prob) + nn(pv_t[part, :], prob_mem)
+    att_scr[...] = mix_ref[...].T.astype(BF)
+    for step in range(4):
+        at = pl.multiple_of((here ^ step) * rows, rows)
+        outs[step][...] = att_scr[pl.ds(at, rows), :]
+
+
+def hidden_kernel(idx, *refs):
+    wo, wo2 = refs[:2]
+    parts = refs[2:6]
+    x, small, small2 = refs[6:9]
+    hidden_ref, n2_ref, att_ref, wo_ref, sems = refs[9:]
+    here, wt = idx[1], idx[2]
+    cols = parts[0].shape[1]
+    half = wo.shape[0]
+    copies = fetch_rows(sems, wt, [(wo_ref, wo, wo2)])
+    for step in range(4):
+        att_ref[here ^ step] = parts[step][...]
+    for copy in copies:
+        copy.wait()
+    hidden = x[...].astype(F32)
+    for c in range(4):
+        hidden = hidden + nn(att_ref[c], wo_ref[c * cols : (c + 1) * cols, :])
+    hidden_ref[...] = hidden
+    scaled, _ = norm(hidden)
+    n2_ref[...] = (scaled * both_gains(wt, small, small2, half, half)).astype(BF)
+
+
+def gelu_parts(v):
+    scale = 0.7978845608028654
+    square = v * v
+    t = jnp.tanh(scale * v * (1.0 + 0.044715 * square))
+    grad = 0.5 * (1.0 + t) + 0.5 * v * (1.0 - t * t) * scale * (1.0 + 0.134145 * square)
+    return 0.5 * v * (1.0 + t), grad
+
+
+def ffn_kernel(idx, *refs):
+    w1, w1b, w2, w2b = refs[:4]
+    n2s, gs = refs[4:8], refs[8:12]
+    norms = refs[12:16]
+    act_ref, gi_ref, w2_ref, w1_scr, sems = refs[16:]
+    wt = idx[2]
+    copies = fetch_rows(sems, wt, [(w1_scr, w1, w1b), (w2_ref, w2, w2b)])
+    for copy in copies[:2]:
+        copy.wait()
+    rows = n2s[0].shape[0]
+    for s in range(4):
+        at = slice(s * rows, (s + 1) * rows)
+        act, slope = gelu_parts(nn(n2s[s][...], w1_scr[...]))
+        if s == 0:
+            for copy in copies[2:]:
+                copy.wait()
+        act_ref[at, :] = act.astype(BF)
+        grad = (nt(gs[s][...], w2_ref[...]).astype(BF).astype(F32) * slope).astype(BF)
+        gi_ref[at, :] = grad
+        norms[s][...] = nt(grad, w1_scr[...]).astype(BF)
+
+
+def ffn_back_kernel(idx, *refs):
+    n2s, gs = refs[:4], refs[4:8]
+    act, gi = refs[8:10]
+    mine, theirs, all_scr, scr = refs[10:]
+    here, wt = idx[1], idx[2]
+    rows = n2s[0].shape[0]
+    size = scr.shape[0] // 8
+
+    def spread(p):
+        for i, out in enumerate((mine, theirs)):
+            for j, place in enumerate(NEAR_LAST):
+                at = pl.multiple_of(((wt ^ i) * 4 + (here ^ place)) * size, size)
+                to = (2 * j + p) * size
+                out[to : to + size, :] = scr[pl.ds(at, size), :]
+
+    for s in range(4):
+        all_scr[s * rows : (s + 1) * rows, :] = n2s[s][...]
+    scr[...] = tn(all_scr[...], gi[...]).astype(BF)
+    spread(0)
+    for s in range(4):
+        all_scr[s * rows : (s + 1) * rows, :] = gs[s][...]
+    scr[...] = tn(act[...], all_scr[...]).astype(BF)
+    spread(1)
+
+
+def hidden_back_kernel(idx, *refs):
+    parts = refs[:4]
+    hidden_ref, small, small2, g, wo = refs[4:9]
+    grad_ref, low_ref = refs[9:11]
+    outs = refs[11:]
+    here, wt = idx[1], idx[2]
+    cols = outs[0].shape[1]
+    half = wo.shape[0] // 2
+    grad_norm = parts[0][...].astype(F32)
+    for part in parts[1:]:
+        grad_norm = grad_norm + part[...].astype(F32)
+    scaled, inverse = norm(hidden_ref[...])
+    e = grad_norm * both_gains(wt, small, small2, half, half)
+    grad = g[...].astype(F32) + inverse * (
+        e - scaled * jnp.mean(e * scaled, axis=-1, keepdims=True)
+    )
+    grad_ref[...] = grad
+    low = grad.astype(BF)
+    low_ref[...] = low
+    for step in range(4):
+        at = pl.multiple_of((here ^ step) * cols, cols)
+        outs[step][...] = nt(low, wo[pl.ds(at, cols), :]).astype(BF)
+
+
+def wo_back_kernel(idx, att, low, act, w2, mine, theirs, keep, send, scr):
+    batch, here, wt = idx[0], idx[1], idx[2]
+    rows = low.shape[0]
+    size = att.shape[2]
+    for c in range(4):
+        scr[c * size : (c + 1) * size, :] = tn(att[c], low[...])
+    size = scr.shape[0] // 32
+    for i, out in enumerate((mine, theirs)):
+        for q, far in enumerate(NEAR_LAST):
+            for p, place in enumerate(NEAR_LAST):
+                at = (((wt ^ i) * 4 + (here ^ place)) * 4 + (batch ^ far)) * size
+                to = (4 * q + p) * size
+                out[to : to + size, :] = scr[pl.ds(pl.multiple_of(at, 8), size), :].astype(BF)
+    for s, (out, to) in enumerate(((keep, 0), (keep, rows), (send, 0), (send, rows))):
+        out[to : to + rows, :] = nn(act[s * rows : (s + 1) * rows, :], w2[...]).astype(BF)
+
+
+def heads_back_kernel(heads, hsize, idx, *refs):
+    gms = refs[:4]
+    pt, pm, q, k, v, mix, pk, pv, bucket_row, n1 = refs[4:14]
+    mine, theirs = refs[14:16]
+    outs = refs[16:20]
+    gm_scr, gqt_scr, acc, grad_scr, w_scr = refs[20:]
+    batch, here, wt = idx[0], idx[1], idx[2]
+    rows, cols = gms[0].shape
+    length = 4 * rows
+    mem = pk.shape[0]
+    for step in range(4):
+        at = pl.multiple_of((here ^ step) * rows, rows)
+        gm_scr[pl.ds(at, rows), :] = gms[step][...]
+    gm_t = gm_scr[...].T
+    keys_t = k[...].T
+    pk_t = pk[...].astype(F32).T.astype(BF)
+    lines = []
+    for h in range(heads):
+        part = slice(h * hsize, (h + 1) * hsize)
+        gm = gm_scr[:, part]
+        query = q[:, part]
+        spread = jnp.sum(gm_t[part, :].astype(F32) * mix[part, :], axis=0, keepdims=True)
+        prob = pt[h]
+        prob_mem = pm[h]
+        score = prob.astype(F32) * (nt(v[:, part], gm) - spread)
+        front = (prob_mem.astype(F32) * (nt(pv[:, part], gm) - spread)).astype(BF)
+        low = score.astype(BF)
+        gqt_scr[part, :] = nn(keys_t[part, :], low) + nn(pk_t[part, :], front)
+        grad_scr[1, :, part] = nn(low, query).astype(BF)
+        grad_scr[2, :, part] = nn(prob, gm).astype(BF)
+        mem_k = nn(front, query).astype(BF)
+        mem_v = nn(prob_mem, gm).astype(BF)
+        for step in range(4):
+            outs[step][3 * rows + MEM_K : 3 * rows + MEM_K + mem, part] = mem_k
+            outs[step][3 * rows + MEM_V : 3 * rows + MEM_V + mem, part] = mem_v
+        acc[...] = jnp.zeros_like(acc)
+        for at in range(0, length, LANES):
+            acc[:, length - at : 2 * length - at] += score[at : at + LANES, :]
+        fold = acc[...]
+        size = LANES // 2
+        while size >= 8:
+            fold = fold[:size] + pltpu.roll(fold[size:], 2 * length - size, 1)
+            size //= 2
+        line = fold[0:1]
+        for i in range(1, 8):
+            line = line + pltpu.roll(fold[i : i + 1], 2 * length - i, 1)
+        lines.append(line)
+    grad_scr[0] = gqt_scr[...].T.astype(BF)
+    normed = n1[...]
+    for p in range(3):
+        w_scr[:, p * cols : (p + 1) * cols] = tn(normed, grad_scr[p]).astype(BF)
+    size = w_scr.shape[0] // 8
+    for i, out in enumerate((mine, theirs)):
+        for j, far in enumerate(NEAR_LAST):
+            at = pl.multiple_of(((wt ^ i) * 4 + (batch ^ far)) * size, size)
+            out[j * size : (j + 1) * size, :] = w_scr[pl.ds(at, size), :]
+    lines.append(jnp.zeros((LINE - heads, 2 * length), F32))
+    table = lax.dot_general(
+        jnp.concatenate(lines, axis=0),
+        one_hot_rows(bucket_row[...], LANES),
+        (((1,), (1,)), ((), ())),
+        precision=lax.Precision.HIGHEST,
+        preferred_element_type=F32,
+    )
+    wide = w_scr.shape[1]
+    table = jnp.concatenate([table, jnp.zeros((LINE, wide - LANES), F32)], axis=1)
+    for out in (mine, theirs):
+        out[4 * size :, :] = table.astype(BF)
+    for step in range(4):
+        at = pl.multiple_of((here ^ step) * rows, rows)
+        for p in range(3):
+            outs[step][p * rows : (p + 1) * rows, :] = grad_scr[p, pl.ds(at, rows), :]
+
+
+def halving_kernel(lines, *refs):
+    count = len(lines)
+    for i, line in enumerate(lines):
+        own, got = refs[2 * i], refs[2 * i + 1]
+        keep, send = refs[2 * count + 2 * i], refs[2 * count + 2 * i + 1]
+        total = (own[...].astype(F32) + got[...].astype(F32)).astype(BF)
+        half = (total.shape[0] - line) // 2
+        keep[:half, :] = total[:half]
+        send[:half, :] = total[half : 2 * half]
+        if line:
+            keep[half:, :] = total[2 * half :]
+            send[half:, :] = total[2 * half :]
+
+
+def halving(name, items):
+    args, out = [], []
+    for own, got, line in items:
+        args += [own, got]
+        out += [shape(((own.shape[0] - line) // 2 + line, own.shape[1]), BF)] * 2
+    return pl.pallas_call(
+        functools.partial(halving_kernel, [line for _, _, line in items]),
+        out_shape=out,
+        in_specs=vmem(len(args)),
+        out_specs=vmem(len(out)),
+        compiler_params=params(32),
+        name=name,
+    )(*args)
+
+
+def row_sums(values):
+    return lax.dot_general(
+        jnp.ones((8, values.shape[1]), F32),
+        values,
+        (((1,), (1,)), ((), ())),
+        precision=lax.Precision.HIGHEST,
+        preferred_element_type=F32,
+    )
+
+
+def ffn_piece_kernel(idx, ffn, ffn2, w_in, first_ref, second_ref, sum_ref):
+    here = idx[1]
+    quarter = first_ref.shape[0]
+    grad = ffn[...].astype(F32) + ffn2[...].astype(F32)
+    first_ref[...] = grad[:quarter].astype(BF)
+    second_ref[...] = grad[quarter:].astype(BF)
+    rows = w_in[pl.ds(pl.multiple_of(here * quarter, quarter), quarter), :].astype(F32)
+    sum_ref[...] = row_sums(grad[:quarter] * rows)
+
+
+def heads_piece_kernel(qkv, qkv2, wo, wo2, wrow, sum_in, piece_ref):
+    size, width = wo.shape
+    quarter = wrow.shape[0]
+    wide = wrow.shape[1]
+    heads = qkv[...].astype(F32) + qkv2[...].astype(F32)
+    piece_ref[:quarter, :] = heads[:quarter].astype(BF)
+    sum_heads = row_sums(heads[:quarter] * wrow[...].astype(F32))
+    out = wo[...].astype(F32) + wo2[...].astype(F32)
+    piece_ref[quarter : quarter + size, :] = out[:, :wide].astype(BF)
+    third = size // 3
+    cols = width - wide
+    for o in range(3):
+        piece_ref[quarter + size : quarter + size + third, o * cols : (o + 1) * cols] = out[
+            o * third : (o + 1) * third, wide:
+        ].astype(BF)
+    row = lax.broadcasted_iota(jnp.int32, (LINE, quarter), 0)
+    sums = jnp.where(row == LINE - 2, sum_heads, jnp.where(row == LINE - 1, sum_in[...], 0.0))
+    at = quarter + size + third
+    line = heads[quarter:]
+    pad = jnp.zeros((LINE, LANES), F32)
+    sums = jnp.concatenate([sums, jnp.zeros((LINE, LANES - quarter), F32)], axis=1)
+    line = line + jnp.concatenate([pad, sums, jnp.zeros((LINE, wide - 2 * LANES), F32)], axis=1)
+    piece_ref[at:, :] = line.astype(BF)
+
+
+def ctx_pieces(refs, at, order):
+    one, two, four, one2, two2, four2 = refs
+    rows = one.shape[0]
+    size = rows // 2
+    first = ((one, 0), (two, 0), (four, 0), (four, rows))
+    last = ((one2, 0), (four2, 0), (two2, 0), (four2, rows))
+    if order == 2:
+        first = ((one, 0), (four, 0), (two, 0), (four, rows))
+        last = ((one2, 0), (two2, 0), (four2, 0), (four2, rows))
+    near, far = first[at], last[at]
+    found = []
+    for (ref, start), places in ((near, (0, 2)), (far, (1, 3))):
+        for i, place in enumerate(places):
+            found.append((place, ref, start + i * size, size))
+    return found
+
+
+def rows_out_kernel(idx, *refs):
+    out = refs[6]
+    step = pl.program_id(0)
+    for at in range(4):
+
+        @pl.when(step == at)
+        def _():
+            for place, ref, start, size in ctx_pieces(refs[:6], at, 2):
+                row = pl.multiple_of((idx[1] ^ place) * size, 8)
+                out[pl.ds(row, size), :] = ref[start : start + size, :].astype(F32)
+
+
+def rows_out(index, pieces):
+    rows, width = pieces[0].shape
+    return pl.pallas_call(
+        rows_out_kernel,
+        out_shape=shape((8 * rows, width), F32),
+        grid_spec=pltpu.PrefetchScalarGridSpec(
+            num_scalar_prefetch=1,
+            grid=(4,),
+            in_specs=[pl.BlockSpec(p.shape, lambda step, idx: (0, 0)) for p in pieces],
+            out_specs=pl.BlockSpec((2 * rows, width), lambda step, idx: (idx[0] ^ step, 0)),
+        ),
+        compiler_params=params(32),
+        name="rows_out",
+    )(index, *pieces)
+
+
+def cols_out_kernel(idx, *refs):
+    out = refs[6]
+    step = pl.program_id(0)
+    for at in range(4):
+
+        @pl.when(step // 2 == at)
+        def _():
+            for place, ref, start, size in ctx_pieces(refs[:6], at, 1):
+                row = pl.multiple_of((idx[1] ^ place) * size, 8)
+                out[pl.ds(row, size), :] = ref[start : start + size, :].astype(F32)
+
+
+def cols_out(index, pieces):
+    rows, width = pieces[0].shape
+    block = width // 2
+
+    def place(step, idx):
+        return (0, (step % 2) * 4 + (idx[0] ^ (step // 2)))
+
+    return pl.pallas_call(
+        cols_out_kernel,
+        out_shape=shape((2 * rows, 4 * width), F32),
+        grid_spec=pltpu.PrefetchScalarGridSpec(
+            num_scalar_prefetch=1,
+            grid=(8,),
+            in_specs=[
+                pl.BlockSpec((p.shape[0], block), lambda step, idx: (0, step % 2)) for p in pieces
+            ],
+            out_specs=pl.BlockSpec((2 * rows, block), place),
+        ),
+        compiler_params=params(32),
+        name="cols_out",
+    )(index, *pieces)
+
+
+def heads_out_kernel(heads, buckets, idx, *refs):
+    small = refs[6]
+    oq, ok, ov, oo, gain_one, gain_two, table, scr, lines, tab_scr = refs[7:]
+    step = pl.program_id(0)
+    quarter, width = oq.shape
+    cols = width // 4
+    wide = 3 * cols
+    size = quarter // 4
+    third = size // 3
+    for at in range(4):
+
+        @pl.when(step == at)
+        def _():
+            for place, ref, start, height in ctx_pieces(refs[:6], at, 1):
+                scr[idx[1] ^ place] = ref[start : start + height, :]
+
+    for c in range(4):
+        part = scr[c].astype(F32)
+        for o, out in enumerate((oq, ok, ov)):
+            out[:, c * cols : (c + 1) * cols] = part[:quarter, o * cols : (o + 1) * cols]
+        oo[c, 0, :, :wide] = part[quarter : quarter + size]
+        for o in range(3):
+            oo[c, 0, o * third : (o + 1) * third, wide:] = part[
+                quarter + size : quarter + size + third, o * cols : (o + 1) * cols
+            ]
+        lines[idx[0] ^ step, c] = part[quarter + size + third :]
+
+    @pl.when(step == 3)
+    def _():
+        seen = [[lines[b, c] for c in range(4)] for b in range(4)]
+        take = slice(LANES, LANES + quarter)
+        for b in range(4):
+            total = sum(seen[b][c][LINE - 2 : LINE - 1, take] for c in range(4))
+            gain_one[:, b * quarter : (b + 1) * quarter] = total
+        for c in range(4):
+            total = sum(seen[b][c][LINE - 1 : LINE, take] for b in range(4))
+            gain_two[:, c * quarter : (c + 1) * quarter] = total
+        own = small[...].astype(F32)
+        rows = 4 * quarter
+        gain_one[...] = gain_one[...] / own[:, :rows]
+        gain_two[...] = gain_two[...] / own[:, rows : 2 * rows]
+        rest = [seen[0][c][:heads, :LANES] for c in range(4)]
+        rest.append(jnp.zeros((LANES - 4 * heads, LANES), F32))
+        tab_scr[...] = jnp.concatenate(rest, axis=0).T
+        own_buckets = buckets // 2
+        at = pl.multiple_of(idx[2] * own_buckets, 8)
+        table[...] = tab_scr[pl.ds(at, own_buckets), : 4 * heads]
+
+
+def heads_out(index, pieces, small, width, heads, buckets):
+    height, wide = pieces[0].shape[0] // 2, pieces[0].shape[1]
+    part = width // 2
+    quarter = part // 4
+    size = quarter // 4
+    block = pl.BlockSpec((quarter, width), lambda step, idx: (idx[0] ^ step, 0))
+    whole = [pl.BlockSpec(p.shape, lambda step, idx: (0, 0)) for p in (*pieces, small)]
+    return pl.pallas_call(
+        functools.partial(heads_out_kernel, heads, buckets),
+        out_shape=[shape((part, width), F32)] * 3
+        + [
+            shape((4, 4, size, width), F32),
+            shape((1, part), F32),
+            shape((1, part), F32),
+            shape((buckets // 2, 4 * heads), F32),
+        ],
+        grid_spec=pltpu.PrefetchScalarGridSpec(
+            num_scalar_prefetch=1,
+            grid=(4,),
+            in_specs=whole,
+            out_specs=[block] * 3
+            + [
+                pl.BlockSpec((4, 1, size, width), lambda step, idx: (0, idx[0] ^ step, 0, 0)),
+                pl.BlockSpec((1, part), lambda step, idx: (0, 0)),
+                pl.BlockSpec((1, part), lambda step, idx: (0, 0)),
+                pl.BlockSpec((buckets // 2, 4 * heads), lambda step, idx: (0, 0)),
+            ],
+            scratch_shapes=[
+                pltpu.VMEM((4, height, wide), BF),
+                pltpu.VMEM((4, 4, LINE, wide), F32),
+                pltpu.VMEM((LANES, LANES), F32),
+            ],
+        ),
+        compiler_params=params(32),
+        name="heads_out",
+    )(index, *pieces, small)
+
+
+def paired(
+    inputs,
+    prefix_keys,
+    prefix_values,
+    gain_attn,
+    w_query,
+    w_key,
+    w_value,
+    w_out,
+    bias_table,
+    gain_ffn,
+    w_in,
+    w_back,
+    buckets,
+    out_grad,
+):
+    b, c, w = lax.axis_index("batch"), lax.axis_index("ctx"), lax.axis_index("wt")
+    index = jnp.stack([b, c, w])
+    x, g = inputs[0], out_grad[0]
+    rows, width = x.shape
+    all_heads = bias_table.shape[1]
+    heads = all_heads // 4
+    hsize = width // all_heads
+    cols = heads * hsize
+    wide = 3 * cols
+    mem = prefix_keys.shape[1]
+    length = 4 * rows
+    part = width // 2
+    quarter = part // 4
+    ff_own = w_back.shape[0]
+    ff_part = ff_own // 4
+    nbuck = 2 * bias_table.shape[0]
+
+    def over_wt(value, name):
+        with jax.named_scope(name + "_w"):
+            return flip(value, "wt", 2, 1)
+
+    def over_ctx(value, step, name):
+        with jax.named_scope(name + "_z" + str(step)):
+            return flip(value, "ctx", 4, step)
+
+    def over_batch(value, step, name):
+        with jax.named_scope(name + "_b" + str(step)):
+            return flip(value, "batch", 4, step)
+
+    xs = [x] + [over_ctx(x, s, "x") for s in range(1, 4)]
+    bucket_row = jnp.pad(buckets[::-1].reshape(1, -1), ((0, 0), (1, 0)), constant_values=-1)
+    small = jnp.concatenate([gain_attn, gain_ffn]).reshape(1, -1)
+    w_query2, w_key2, w_value2, w_out2 = [
+        over_wt(v, "weight") for v in (w_query, w_key, w_value, w_out)
+    ]
+    table2 = over_wt(bias_table, "table")
+    small2 = over_wt(small, "gain")
+    gs = [g] + [over_batch(g, s, "g") for s in range(1, 4)]
+    w_in_cut, w_back_cut = after((w_in, w_back), (xs[1], bucket_row, small))
+    cut_in = jnp.concatenate(
+        [
+            lax.dynamic_slice_in_dim(w_in_cut, o * ff_own + b * ff_part, ff_part, 1)
+            for o in range(2)
+        ],
+        axis=1,
+    )
+    cut_back = lax.dynamic_slice_in_dim(w_back_cut, b * ff_part, ff_part, 0)
+    cut_in2, cut_back2 = over_wt(cut_in, "in"), over_wt(cut_back, "back")
+    xs = after(xs, (*gs, w_out2, cut_in2, cut_back2))
+
+    tokens = shape((length, cols), BF)
+    few = (small, small2, bias_table, table2, prefix_keys[0], prefix_values[0], bucket_row)
+    (n1, q, k, v, pt, pm, mix, wrow, pk, pv, *mixed) = call(
+        functools.partial(heads_kernel, heads, hsize),
+        "attend",
+        index,
+        [*xs],
+        [shape((length, width), BF)]
+        + [tokens] * 3
+        + [
+            shape((heads, length, length), BF),
+            shape((heads, mem, length), BF),
+            shape((cols, length), F32),
+            shape((quarter, wide), BF),
+            shape((mem, cols), BF),
+            shape((mem, cols), BF),
+        ]
+        + [shape((rows, cols), BF)] * 4,
+        [
+            pltpu.VMEM((length, cols), BF),
+            pltpu.VMEM((16, 2 * length), F32),
+            pltpu.SemaphoreType.DMA((6,)),
+            pltpu.SemaphoreType.DMA((len(few),)),
+        ]
+        + [pltpu.VMEM((width, -(-cols // LANES) * LANES), BF)] * 3
+        + [pltpu.VMEM(v.shape, v.dtype) for v in few],
+        far=(w_query, w_key, w_value, w_query2, w_key2, w_value2, *few),
+    )
+    mixed = mixed[:1] + [over_ctx(mixed[s], s, "mixed") for s in range(1, 4)]
+    square = shape((width, width), BF)
+    hidden, n2, attended, wo = call(
+        hidden_kernel,
+        "hidden",
+        index,
+        [*mixed, x, small, small2],
+        [shape((rows, width), F32), shape((rows, width), BF), shape((4, rows, cols), BF), square],
+        [pltpu.SemaphoreType.DMA((2,))],
+        far=(w_out, w_out2),
+    )
+
+    n2s = [n2] + [over_batch(n2, s, "n2") for s in range(1, 4)]
+    hid = shape((length, 2 * ff_part), BF)
+    *norms, act, gi, w_second = call(
+        ffn_kernel,
+        "ffn",
+        index,
+        [*n2s, *gs],
+        [shape((rows, width), BF)] * 4 + [hid, hid, shape((2 * ff_part, width), BF)],
+        [pltpu.VMEM((width, 2 * ff_part), BF), pltpu.SemaphoreType.DMA((4,))],
+        far=(cut_in, cut_in2, cut_back, cut_back2),
+    )
+    norms = norms[:1] + [over_batch(norms[s], s, "norm") for s in range(1, 4)]
+    ffn, ffn_sent = call(
+        ffn_back_kernel,
+        "ffn_back",
+        index,
+        [*n2s, *gs, act, gi],
+        [square, square],
+        [pltpu.VMEM((length, width), BF), pltpu.VMEM((width, width), BF)],
+    )
+    ffn, ffn_sent = halving("ffn_wt", [(ffn, over_wt(ffn_sent, "ffn"), 0)])
+    ffn_got = over_ctx(ffn_sent, 1, "ffn")
+    norms = after(norms, (ffn, ffn_got))
+    grad_hidden, low, *gms = call(
+        hidden_back_kernel,
+        "hidden_back",
+        index,
+        [*norms, hidden, small, small2, g, wo],
+        [shape((rows, width), F32), shape((rows, width), BF)] + [shape((rows, cols), BF)] * 4,
+    )
+    ffn, ffn_sent = halving("ffn_near", [(ffn, ffn_got, 0)])
+    ffn_got = over_ctx(ffn_sent, 2, "ffn")
+    gms = after(gms, (ffn, ffn_sent))
+    gms = list(gms[:1]) + [over_ctx(gms[s], s, "gm") for s in range(1, 4)]
+    wo_sum, wo_sent, outs, outs_sent = call(
+        wo_back_kernel,
+        "wo_back",
+        index,
+        [attended, low, act, w_second],
+        [shape((part, width), BF)] * 2 + [shape((2 * rows, width), BF)] * 2,
+        [pltpu.VMEM((width, width), F32)],
+    )
+    outs_got = over_batch(outs_sent, 2, "outs")
+    wo_sum, wo_sent = halving("wo_wt", [(wo_sum, over_wt(wo_sent, "wo"), 0)])
+    wo_got = over_batch(wo_sent, 1, "wo")
+    first, second, sum_in = call(
+        ffn_piece_kernel,
+        "ffn_piece",
+        index,
+        [ffn, ffn_got, cut_in],
+        [shape((quarter, width), BF)] * 2 + [shape((8, quarter), F32)],
+    )
+    gms = after(gms, (first, second, wo_got, outs_got))
+    (qkv, qkv_sent, *sends) = call(
+        functools.partial(heads_back_kernel, heads, hsize),
+        "attend_back",
+        index,
+        [*gms, pt, pm, q, k, v, mix, pk, pv, bucket_row, n1],
+        [shape((part + LINE, wide), BF)] * 2 + [shape((3 * rows + MEM_END, cols), BF)] * 4,
+        [
+            pltpu.VMEM((length, cols), BF),
+            pltpu.VMEM((cols, length), F32),
+            pltpu.VMEM((LANES, 2 * length), F32),
+            pltpu.VMEM((3, length, cols), BF),
+            pltpu.VMEM((width, wide), BF),
+        ],
+    )
+
+    qkv, qkv_sent, wo_sum, wo_sent, outs, outs_sent = halving(
+        "step_a",
+        [
+            (qkv, over_wt(qkv_sent, "qkv"), LINE),
+            (wo_sum, wo_got, 0),
+            (outs, outs_got, 0),
+        ],
+    )
+    outs_got = over_batch(outs_sent, 1, "outs")
+    qkv, qkv_sent, wo_sum, wo_sent = halving(
+        "step_b",
+        [(qkv, over_batch(qkv_sent, 1, "qkv"), LINE), (wo_sum, over_batch(wo_sent, 2, "wo"), 0)],
+    )
+    qkv_got = over_batch(qkv_sent, 2, "qkv")
+    result = (hidden + outs.astype(F32) + outs_got.astype(F32)).astype(BF)
+    wo_sum, wo_sent = halving("step_c", [(wo_sum, over_ctx(wo_sent, 1, "wo"), 0)])
+    wo_got = over_ctx(wo_sent, 2, "wo")
+    height = quarter + quarter // 4 + quarter // 12 + LINE
+    piece = pl.pallas_call(
+        heads_piece_kernel,
+        out_shape=shape((height, wide), BF),
+        in_specs=vmem(6),
+        out_specs=vmem(1)[0],
+        compiler_params=params(32),
+        name="heads_piece",
+    )(qkv, qkv_got, wo_sum, wo_got, wrow, sum_in)
+
+    def pile(one, two):
+        return jnp.concatenate([one, two])
+
+    in_far, out_far = over_ctx(first, 2, "in_back"), over_ctx(second, 2, "out_back")
+    (piece,) = after((piece,), (in_far, out_far, result))
+    heads_far = over_ctx(piece, 2, "heads_back")
+    a1, b1 = pile(first, in_far), pile(second, out_far)
+    a2, b2 = over_batch(a1, 1, "in_near"), over_batch(b1, 2, "out_near")
+    c1, d1 = over_ctx(a1, 1, "in_back"), over_ctx(b1, 1, "out_back")
+    pile_a, pile_b = pile(a1, a2), pile(b1, b2)
+    a3 = over_batch(pile_a, 2, "in_near2")
+    b3 = over_batch(pile_b, 1, "out_near2")
+    (heads_far,) = after((heads_far,), (c1, d1))
+    e1 = pile(piece, heads_far)
+    f1 = over_ctx(e1, 1, "heads_back")
+    (c1, d1) = after((c1, d1), (pile_a, pile_b))
+    c2, d2 = over_batch(c1, 2, "in_far"), over_batch(d1, 1, "out_far")
+    (e1, f1) = after((e1, f1), (a3, b3, c2, d2))
+    c3 = over_batch(pile(c1, c2), 1, "in_far2")
+    d3 = over_batch(pile(d1, d2), 2, "out_far2")
+    e2, f2 = over_batch(e1, 1, "heads_near"), over_batch(f1, 2, "heads_far")
+    sends[1:] = after(sends[1:], (f1,))
+    sends = sends[:1] + [over_ctx(sends[s], s, "sends") for s in range(1, 4)]
+    (e1, e2, f1, f2) = after((e1, e2, f1, f2), (c3, d3))
+    e3 = over_batch(pile(e1, e2), 2, "heads_near2")
+    f3 = over_batch(pile(f1, f2), 1, "heads_far2")
+    out_second = rows_out(index, (b1, b2, b3, d1, d2, d3))
+    out_first = cols_out(index, (a1, a2, a3, c1, c2, c3))
+    out_q, out_k, out_v, out_wo, gain_one, gain_two, out_table = heads_out(
+        index, (e1, e2, e3, f1, f2, f3), small, width, heads, nbuck
+    )
+    grad_x, grad_memk, grad_memv = call(
+        input_end_kernel,
+        "input_back",
+        index,
+        [*sends, x, small, small2, grad_hidden],
+        [shape((rows, width), BF), shape((mem, width), F32), shape((mem, width), F32)],
+        [pltpu.VMEM((4,) + sends[0].shape, BF), pltpu.SemaphoreType.DMA((6,))]
+        + [pltpu.VMEM((width, width), BF)] * 3,
+        far=(w_query, w_key, w_value, w_query2, w_key2, w_value2),
+    )
+    return (
+        result[None],
+        grad_x[None],
+        grad_memk[None],
+        grad_memv[None],
+        gain_one.reshape(part),
+        gain_two.reshape(part),
+        out_table,
+        out_q,
+        out_k,
+        out_v,
+        out_wo.reshape(part, width),
+        out_first,
+        out_second,
+    )
+
+
+def input_end_kernel(idx, *refs):
+    wq, wk, wv, wq2, wk2, wv2 = refs[:6]
+    parts = refs[6:10]
+    x, small, small2, grad_hidden = refs[10:14]
+    out_ref, memk_ref, memv_ref, scr, sems, *w_scr = refs[14:]
+    here, wt = idx[1], idx[2]
+    rows = x.shape[0]
+    mem = memk_ref.shape[0]
+    copies = fetch_rows(sems, wt, list(zip(w_scr, (wq, wk, wv), (wq2, wk2, wv2))))
+    for step in range(4):
+        scr[here ^ step] = parts[step][...]
+    for copy in copies:
+        copy.wait()
+
+    def wide(at, count):
+        return jnp.concatenate([scr[c, at : at + count, :] for c in range(4)], axis=1)
+
+    grad_norm = sum(nt(wide(p * rows, rows), whole[...]) for p, whole in enumerate(w_scr))
+    scaled, inverse = norm(x[...].astype(F32))
+    e = grad_norm * both_gains(wt, small, small2, 0, wq.shape[0])
+    grad = grad_hidden[...] + inverse * (
+        e - scaled * jnp.mean(e * scaled, axis=-1, keepdims=True)
+    )
+    out_ref[...] = grad.astype(BF)
+    memk_ref[...] = wide(3 * rows + MEM_K, mem).astype(F32)
+    memv_ref[...] = wide(3 * rows + MEM_V, mem).astype(F32)
+
+
 def solution(mesh):
     tokens = P(("batch", "wt"), "ctx", None)
     memory = P(("batch", "wt"), None, None)
     matrix = P("wt", None)
     vector = P("wt")
     sizes = (mesh.shape["batch"], mesh.shape["ctx"], mesh.shape["wt"])
+    body = paired if sizes == (4, 4, 2) else functools.partial(general, sizes)
     return jax.shard_map(
-        functools.partial(shards, sizes),
+        body,
         mesh=mesh,
         in_specs=(
             tokens, memory, memory, vector, matrix, matrix, matrix, matrix, matrix, vector,

time: 336 us -> 233 us (0.69)
  local copies, waits for them, and re-layouts: 52.8 us -> 10.8 us
  starting transfers between devices: 103 us -> 61.7 us
  other arithmetic: 42.9 us -> 2.98 us
  Pallas kernels: 13.5 us -> 42.4 us
  matrix products: 8.53 us -> 0 us
    ppermute x75 -> x60, starting transfers between devices: 103 us -> 61.7 us  [flip(): return lax.ppermute(value, axis, [(i, i ^ step) for i in range(size)])]
    pallas_call x5 -> x19, Pallas kernels: 13.5 us -> 42.4 us  [the longest x9 29.3 us: call(): pl.pallas_call(kernel, out_shape=out, in_specs=[smem()] + stay + vmem(len...]
    dynamic_update_slice x15 -> x0, other arithmetic: 23.9 us -> none  [the longest x8 14.7 us: shards(): lax.dynamic_update_slice(out_first, piece[:, o * ff_part:(o + 1) * ff_par...]
    squeeze x7 -> x0, local copies, waits for them, and re-layouts: 8.97 us -> none  [the longest x3 8.12 us: shards(): out_q, out_k, out_v = (wide[0], wide[1], wide[2])]
    dot_general x8 -> x0, matrix products: 8.53 us -> none  [the longest x3 3.83 us: tn(): lax.dot_general(left, right, (((0,), (0,)), ((), ())), preferred_element_...]
    slice x9 -> x0, local copies, waits for them, and re-layouts: 7.93 us -> none  [the longest x4 6.8 us: shards(): out_q, out_k, out_v = (wide[0], wide[1], wide[2])]
    dynamic_slice x12 -> x2, local copies, waits for them, and re-layouts: 7.98 us -> 1.15 us  [the longest x1 1.11 us: paired(): lax.dynamic_slice_in_dim(w_in_cut, o * ff_own + b * ff_part, ff_part, 1)]
    broadcast_in_dim x10 -> x0, local copies, waits for them, and re-layouts: 6.48 us -> none  [the longest x4 3.13 us: canonical(): whole = jnp.zeros((len(parts),) + parts[0].shape, parts[0].dtype)]
  transfers between devices with their start and end apart: 75 -> 60, of which waited for: 26 -> 27; matrix products, arithmetic and copies ran while one was open for 28% -> 2% of each run, Pallas kernels for 4% -> 8%
where the time goes in v3:
time: 233 us
  waiting for transfers between devices  114 us (49%)
  starting transfers between devices  61.7 us (26%)
  Pallas kernels  42.4 us (18%)
  local copies, waits for them, and re-layouts  10.8 us (5%)
  other arithmetic  2.98 us (1%)
    ppermute x60, waiting for transfers between devices, flip(): return lax.ppermute(value, axis, [(i, i ^ step) for i in range(size)])  114 us
    ppermute x60, starting transfers between devices, flip(): return lax.ppermute(value, axis, [(i, i ^ step) for i in range(size)])  61.7 us
    pallas_call x9, Pallas kernels, call(): pl.pallas_call(kernel, out_shape=out, in_specs=[smem()] + stay + vmem(len...  29.3 us
    unnamed x48, local copies, waits for them, and re-layouts  9.53 us
    pallas_call x1, Pallas kernels, cols_out(): pl.pallas_call(cols_out_kernel, out_shape=shape((2 * rows, 4 * width), F3...  5 us
  transfers between devices with their start and end apart: 60, of which 27 were waited for; matrix products, arithmetic and copies ran while one was open for 2% of the time, Pallas kernels for 8%

profile of v3, /device:TPU:0, one launch (start us, length us, event | category | flops | bytes accessed | tf_op | source)
XLA Modules:
  0.0 232.5 jit_solution(16530858902420703302)
XLA Ops:
  12.2 4.3 %collective-permute-done.8.refs_16_ = bf16[128,768]{1,0:T(8,128)(2,1)S(1)} collective-permute-done((bf16[128,768]{1,0:T(8,128)(2,1)}, bf16[128,768]{1,0:T(8,128)(2,1)S(1)}, u32[]{:S(2)}, u32[]{:S(2)}) %collective-permute-start.8) | collective-permute-done | bytes 196640 | tf_op jit(solution)/shard_map/x_z3/ppermute | solution.py:45
  18.7 5.2 %collective-permute-done.7.refs_15_ = bf16[128,768]{1,0:T(8,128)(2,1)} collective-permute-done((bf16[128,768]{1,0:T(8,128)(2,1)}, bf16[128,768]{1,0:T(8,128)(2,1)}, u32[]{:S(2)}, u32[]{:S(2)}) %collective-permute-start.7) | collective-permute-done | bytes 196640 | tf_op jit(solution)/shard_map/x_z2/ppermute | solution.py:45
  33.9 5.5 %attend.1 = (bf16[512,768]{1,0:T(8,128)(2,1)S(1)}, bf16[512,192]{1,0:T(8,128)(2,1)S(1)}, bf16[512,192]{1,0:T(8,128)(2,1)S(1)}, bf16[512,192]{1,0:T(8,128)(2,1)S(...) custom-call(s32[3]{0:T(128)S(1)} %pad_add_fusion.idx, ...), custom_call_target="tpu_custom_call" | custom-call | tf_op jit(solution)/shard_map/attend/pallas_call | solution.py:553
  44.3 5.3 %collective-permute-done.15.refs_4_ = bf16[128,192]{1,0:T(8,128)(2,1)S(1)} collective-permute-done((bf16[128,192]{1,0:T(8,128)(2,1)S(1)}, bf16[128,192]{1,0:T(8,128)(2,1)S(1)}, u32[]{:S(2)}, u32[]{:S(2)}) %collective-permute-start.15) | collective-permute-done | bytes 49184 | tf_op jit(solution)/shard_map/mixed_z2/ppermute | solution.py:45
  55.4 5.2 %collective-permute-done.19.refs_7_.refs_3_ = bf16[128,768]{1,0:T(8,128)(2,1)S(1)} collective-permute-done((bf16[128,768]{1,0:T(8,128)(2,1)S(1)}, bf16[128,768]{1,0:T(8,128)(2,1)S(1)}, u32[]{:S(2)}, u32[]{:S(2)}) %collective-permute-start.19) | collective-permute-done | bytes 196640 | tf_op jit(solution)/shard_map/n2_b3/ppermute | solution.py:45
  63.1 6.4 %ffn.1 = (bf16[128,768]{1,0:T(8,128)(2,1)S(1)}, bf16[128,768]{1,0:T(8,128)(2,1)S(1)}, bf16[128,768]{1,0:T(8,128)(2,1)S(1)}, bf16[128,768]{1,0:T(8,128)(2,1)S(1)}...) custom-call(s32[3]{0:T(128)S(1)} %pad_add_fusion.idx, ...), custom_call_target="tpu_custom_call" | custom-call | tf_op jit(solution)/shard_map/ffn/pallas_call | solution.py:553
  81.0 4.3 %collective-permute-done.20.refs_1_ = bf16[128,768]{1,0:T(8,128)(2,1)S(1)} collective-permute-done((bf16[128,768]{1,0:T(8,128)(2,1)S(1)}, bf16[128,768]{1,0:T(8,128)(2,1)S(1)}, u32[]{:S(2)}, u32[]{:S(2)}) %collective-permute-start.20) | collective-permute-done | bytes 196640 | tf_op jit(solution)/shard_map/norm_b1/ppermute | solution.py:45
  85.3 4.3 %collective-permute-done.21.refs_2_ = bf16[128,768]{1,0:T(8,128)(2,1)S(1)} collective-permute-done((bf16[128,768]{1,0:T(8,128)(2,1)S(1)}, bf16[128,768]{1,0:T(8,128)(2,1)S(1)}, u32[]{:S(2)}, u32[]{:S(2)}) %collective-permute-start.21) | collective-permute-done | bytes 196640 | tf_op jit(solution)/shard_map/norm_b2/ppermute | solution.py:45
  101.6 12.8 %collective-permute-done.28.ffn2 = bf16[192,768]{1,0:T(8,128)(2,1)S(1)} collective-permute-done((bf16[192,768]{1,0:T(8,128)(2,1)S(1)}, bf16[192,768]{1,0:T(8,128)(2,1)S(1)}, u32[]{:S(2)}, u32[]{:S(2)}) %collective-permute-start.28) | collective-permute-done | bytes 294944 | tf_op jit(solution)/shard_map/ffn_z2/ppermute | solution.py:45
  121.2 4.4 %attend_back.1 = (bf16[392,576]{1,0:T(8,128)(2,1)S(1)}, bf16[392,576]{1,0:T(8,128)(2,1)S(1)}, bf16[448,192]{1,0:T(8,128)(2,1)S(1)}, bf16[448,192]{1,0:T(8,128)(2...) custom-call(s32[3]{0:T(128)S(1)} %pad_add_fusion.idx, ...), custom_call_target="tpu_custom_call" | custom-call | tf_op jit(solution)/shard_map/attend_back/pallas_call | solution.py:553
  126.9 8.7 %collective-permute-done.40 = bf16[96,768]{1,0:T(8,128)(2,1)S(1)} collective-permute-done((bf16[96,768]{1,0:T(8,128)(2,1)S(1)}, bf16[96,768]{1,0:T(8,128)(2,1)S(1)}, u32[]{:S(2)}, u32[]{:S(2)}) %collective-permute-start.40) | collective-permute-done | bytes 147488 | tf_op jit(solution)/shard_map/out_back_z2/ppermute | solution.py:45
  140.9 6.9 %collective-permute-done.35.refs_3_ = bf16[96,768]{1,0:T(8,128)(2,1)S(1)} collective-permute-done((bf16[96,768]{1,0:T(8,128)(2,1)S(1)}, bf16[96,768]{1,0:T(8,128)(2,1)S(1)}, u32[]{:S(2)}, u32[]{:S(2)}) %collective-permute-start.35) | collective-permute-done | bytes 147488 | tf_op jit(solution)/shard_map/wo_b2/ppermute | solution.py:45
  148.9 5.2 %collective-permute-done.43.refs_3_ = bf16[192,768]{1,0:T(8,128)(2,1)S(1)} collective-permute-done((bf16[192,768]{1,0:T(8,128)(2,1)S(1)}, bf16[192,768]{1,0:T(8,128)(2,1)S(1)}, u32[]{:S(2)}, u32[]{:S(2)}) %collective-permute-start.43) | collective-permute-done | bytes 294944 | tf_op jit(solution)/shard_map/out_back_z1/ppermute | solution.py:45
  159.3 3.8 %collective-permute-done.38.wo2 = bf16[24,768]{1,0:T(8,128)(2,1)S(1)} collective-permute-done((bf16[24,768]{1,0:T(8,128)(2,1)S(1)}, bf16[24,768]{1,0:T(8,128)(2,1)S(1)}, u32[]{:S(2)}, u32[]{:S(2)}) %collective-permute-start.38) | collective-permute-done | bytes 36896 | tf_op jit(solution)/shard_map/wo_z2/ppermute | solution.py:45
  164.5 11.5 %collective-permute-done.36.qkv2 = bf16[104,576]{1,0:T(8,128)(2,1)S(1)} collective-permute-done((bf16[104,576]{1,0:T(8,128)(2,1)S(1)}, bf16[104,576]{1,0:T(8,128)(2,1)S(1)}, u32[]{:S(2)}, u32[]{:S(2)}) %collective-permute-start.36) | collective-permute-done | bytes 119840 | tf_op jit(solution)/shard_map/qkv_b2/ppermute | solution.py:45
  178.5 6.2 %collective-permute-done.41 = bf16[136,576]{1,0:T(8,128)(2,1)S(1)} collective-permute-done((bf16[136,576]{1,0:T(8,128)(2,1)S(1)}, bf16[136,576]{1,0:T(8,128)(2,1)S(1)}, u32[]{:S(2)}, u32[]{:S(2)}) %collective-permute-start.41) | collective-permute-done | bytes 156704 | tf_op jit(solution)/shard_map/heads_back_z2/ppermute | solution.py:45
  186.3 5.8 %collective-permute-done.44.refs_3_ = bf16[272,576]{1,0:T(8,128)(2,1)S(1)} collective-permute-done((bf16[272,576]{1,0:T(8,128)(2,1)S(1)}, bf16[272,576]{1,0:T(8,128)(2,1)S(1)}, u32[]{:S(2)}, u32[]{:S(2)}) %collective-permute-start.44) | collective-permute-done | bytes 313376 | tf_op jit(solution)/shard_map/heads_back_z1/ppermute | solution.py:45
  193.9 5.2 %collective-permute-done.57.refs_5_ = bf16[384,768]{1,0:T(8,128)(2,1)S(1)} collective-permute-done((bf16[384,768]{1,0:T(8,128)(2,1)S(1)}, bf16[384,768]{1,0:T(8,128)(2,1)S(1)}, u32[]{:S(2)}, u32[]{:S(2)}) %collective-permute-start.57) | collective-permute-done | bytes 589856 | tf_op jit(solution)/shard_map/out_far2_b2/ppermute | solution.py:45
  199.4 3.6 %collective-permute-done.55.refs_4_ = bf16[272,576]{1,0:T(8,128)(2,1)S(1)} collective-permute-done((bf16[272,576]{1,0:T(8,128)(2,1)S(1)}, bf16[272,576]{1,0:T(8,128)(2,1)S(1)}, u32[]{:S(2)}, u32[]{:S(2)}) %collective-permute-start.55) | collective-permute-done | bytes 313376 | tf_op jit(solution)/shard_map/heads_far_b2/ppermute | solution.py:45
  205.1 3.5 %collective-permute-start.51 = (bf16[448,192]{1,0:T(8,128)(2,1)S(1)}, bf16[448,192]{1,0:T(8,128)(2,1)S(1)}, u32[]{:S(2)}, u32[]{:S(2)}) collective-permute-start(bf16[448,192]{1,0:T(8,128)(2,1)S(1)} %get-tuple-element.204), channel_id=1, source_target_pairs={{0,2},{2,0},{4,6},{6,4},{1,3},{3,1},{5,7},{7,5},{8,10},{10,8},{12,... | collective-permute-start | bytes 516104 | tf_op jit(solution)/shard_map/sends_z1/ppermute | solution.py:45
  211.0 3.2 %rows_out.1 = f32[1536,768]{1,0:T(8,128)} custom-call(s32[3]{0:T(128)S(1)} %pad_add_fusion.idx, bf16[192,768]{1,0:T(8,128)(2,1)S(1)} %get-tuple-element.239.refs_0_, bf16[192,768]{1,0:T(8,128)(2,1)S(1)} %collective-permute-done.47.refs_1_, bf16[384,768]{1,0:T(8,128)(2,1)S(1)} %collective-permute-done.48.refs_2_, ...), custom_call_target="tpu_custom_call" | custom-call | tf_op jit(solution)/shard_map/rows_out/pallas_call | solution.py:979
  214.1 5.0 %cols_out.1 = f32[384,3072]{1,0:T(8,128)} custom-call(s32[3]{0:T(128)S(1)} %pad_add_fusion.idx, bf16[192,768]{1,0:T(8,128)(2,1)S(1)} %get-tuple-element.243.refs_0_, bf16[192,768]{1,0:T(8,128)(2,1)S(1)} %collective-permute-done.45.refs_1_, bf16[384,768]{1,0:T(8,128)(2,1)S(1)} %collective-permute-done.46.refs_2_, ...), custom_call_target="tpu_custom_call" | custom-call | tf_op jit(solution)/shard_map/cols_out/pallas_call | solution.py:1012
  222.1 4.2 %input_back.1 = (bf16[128,768]{1,0:T(8,128)(2,1)}, f32[20,768]{1,0:T(8,128)S(1)}, f32[20,768]{1,0:T(8,128)S(1)}) custom-call(s32[3]{0:T(128)S(1)} %pad_add_fusion.idx, bf16[384,768]{1,0:T(8,128)(2,1)} %refs_0_.5, bf16[384,768]{1,0:T(8,128)(2,1)} %refs_1_.3, bf16[384,768]{1,0:T(8,128)(2,1)} %refs_2_.3, bf16[384,768]{1,0:T(8,128)(2,1)S(1)} %collective-permute-done.1.refs_3_, ...), custom_call_target="tpu_custom_call" | custom-call | tf_op jit(solution)/shard_map/input_back/pallas_call | solution.py:553
  227.7 3.6 %heads_out.1 = (f32[384,768]{1,0:T(8,128)}, f32[384,768]{1,0:T(8,128)}, f32[384,768]{1,0:T(8,128)}, f32[4,4,24,768]{3,2,1,0:T(8,128)}, f32[1,384]{1,0:T(1,128)S(...) custom-call(s32[3]{0:T(128)S(1)} %pad_add_fusion.idx, bf16[272,576]{1,0:T(8,128)(2,1)S(1)} %constant_dynamic-update-slice_fusion.4.refs_0_, ...), custom_call_target="tpu_custom_call" | custom-call | tf_op jit(solution)/shard_map/heads_out/pallas_call | solution.py:1084
  (180 shorter events, 97.4 us)
Async XLA Ops:
  6.2 17.7 %collective-permute-start.7 = (bf16[128,768]{1,0:T(8,128)(2,1)}, bf16[128,768]{1,0:T(8,128)(2,1)}, u32[]{:S(2)}, u32[]{:S(2)}) collective-permute-start(bf16[128,768]{1,0:T(8,128)(2,1)} %bitcast.16), channel_id=1, source_target_pairs={{0,4},{2,6},{4,0},{6,2},{1,5},{3,7},{5,1},{7,3},{8,12},{10,14},{12... | collective-permute-start | bytes 589832 | tf_op jit(solution)/shard_map/x_z2/ppermute | solution.py:45
  6.3 17.6 %collective-permute-start.11 = (bf16[128,768]{1,0:T(8,128)(2,1)}, bf16[128,768]{1,0:T(8,128)(2,1)}, u32[]{:S(2)}, u32[]{:S(2)}) collective-permute-start(bf16[128,768]{1,0:T(8,128)(2,1)} %bitcast.20), channel_id=1, source_target_pairs={{0,24},{8,16},{16,8},{24,0},{1,25},{9,17},{17,9},{25,1},{2,26},{10... | collective-permute-start | bytes 589832 | tf_op jit(solution)/shard_map/g_b3/ppermute | solution.py:45
  8.8 17.5 %collective-permute-start = (bf16[384,768]{1,0:T(8,128)(2,1)}, bf16[384,768]{1,0:T(8,128)(2,1)}, u32[]{:S(2)}, u32[]{:S(2)}) collective-permute-start(bf16[384,768]{1,0:T(8,128)(2,1)} %refs_0_.4), channel_id=1, source_target_pairs={{0,1},{1,0},{2,3},{3,2},{4,5},{5,4},{6,7},{7,6},{8,9},{9,8},{10,11... | collective-permute-start | bytes 1769480 | tf_op jit(solution)/shard_map/weight_w/ppermute | solution.py:45
  10.4 14.0 %collective-permute-start.10 = (bf16[128,768]{1,0:T(8,128)(2,1)}, bf16[128,768]{1,0:T(8,128)(2,1)S(1)}, u32[]{:S(2)}, u32[]{:S(2)}) collective-permute-start(bf16[128,768]{1,0:T(8,128)(2,1)} %bitcast.21), channel_id=1, source_target_pairs={{0,16},{8,24},{16,0},{24,8},{1,17},{9,25},{17,1},{25,9},{2,18},{10... | collective-permute-start | bytes 589832 | tf_op jit(solution)/shard_map/g_b2/ppermute | solution.py:45
  75.3 15.9 %collective-permute-start.24 = (bf16[384,768]{1,0:T(8,128)(2,1)S(1)}, bf16[384,768]{1,0:T(8,128)(2,1)S(1)}, u32[]{:S(2)}, u32[]{:S(2)}) collective-permute-start(bf16[384,768]{1,0:T(8,128)(2,1)S(1)} %get-tuple-element.139), channel_id=1, source_target_pairs={{0,2},{2,0},{4,6},{6,4},{1,3},{3,1},{5,7},{7,5},{8,10},{10,8},{12,... | collective-permute-start | bytes 1769480 | tf_op jit(solution)/shard_map/ffn_z1/ppermute | solution.py:45
  94.2 27.0 %collective-permute-start.31 = (bf16[256,768]{1,0:T(8,128)(2,1)S(1)}, bf16[256,768]{1,0:T(8,128)(2,1)S(1)}, u32[]{:S(2)}, u32[]{:S(2)}) collective-permute-start(bf16[256,768]{1,0:T(8,128)(2,1)S(1)} %get-tuple-element.163), channel_id=1, source_target_pairs={{0,16},{8,24},{16,0},{24,8},{1,17},{9,25},{17,1},{25,9},{2,18},{10... | collective-permute-start | bytes 1179656 | tf_op jit(solution)/shard_map/outs_b2/ppermute | solution.py:45
  95.9 18.5 %collective-permute-start.28 = (bf16[192,768]{1,0:T(8,128)(2,1)S(1)}, bf16[192,768]{1,0:T(8,128)(2,1)S(1)}, u32[]{:S(2)}, u32[]{:S(2)}) collective-permute-start(bf16[192,768]{1,0:T(8,128)(2,1)S(1)} %get-tuple-element.150), channel_id=1, source_target_pairs={{0,4},{2,6},{4,0},{6,2},{1,5},{3,7},{5,1},{7,3},{8,12},{10,14},{12... | collective-permute-start | bytes 884744 | tf_op jit(solution)/shard_map/ffn_z2/ppermute | solution.py:45
  99.0 22.2 %collective-permute-start.30 = (bf16[192,768]{1,0:T(8,128)(2,1)S(1)}, bf16[192,768]{1,0:T(8,128)(2,1)S(1)}, u32[]{:S(2)}, u32[]{:S(2)}) collective-permute-start(bf16[192,768]{1,0:T(8,128)(2,1)S(1)} %get-tuple-element.162), channel_id=1, source_target_pairs={{0,8},{8,0},{16,24},{24,16},{1,9},{9,1},{17,25},{25,17},{2,10},{10... | collective-permute-start | bytes 884744 | tf_op jit(solution)/shard_map/wo_b1/ppermute | solution.py:45
  99.9 18.1 %collective-permute-start.25 = (bf16[128,192]{1,0:T(8,128)(2,1)S(1)}, bf16[128,192]{1,0:T(8,128)(2,1)S(1)}, u32[]{:S(2)}, u32[]{:S(2)}) collective-permute-start(bf16[128,192]{1,0:T(8,128)(2,1)S(1)} %get-tuple-element.152), channel_id=1, source_target_pairs={{0,2},{2,0},{4,6},{6,4},{1,3},{3,1},{5,7},{7,5},{8,10},{10,8},{12,... | collective-permute-start | bytes 147464 | tf_op jit(solution)/shard_map/gm_z1/ppermute | solution.py:45
  100.2 17.9 %collective-permute-start.26 = (bf16[128,192]{1,0:T(8,128)(2,1)S(1)}, bf16[128,192]{1,0:T(8,128)(2,1)S(1)}, u32[]{:S(2)}, u32[]{:S(2)}) collective-permute-start(bf16[128,192]{1,0:T(8,128)(2,1)S(1)} %get-tuple-element.153), channel_id=1, source_target_pairs={{0,4},{2,6},{4,0},{6,2},{1,5},{3,7},{5,1},{7,3},{8,12},{10,14},{12... | collective-permute-start | bytes 147464 | tf_op jit(solution)/shard_map/gm_z2/ppermute | solution.py:45
  135.6 13.2 %collective-permute-start.47 = (bf16[192,768]{1,0:T(8,128)(2,1)S(1)}, bf16[192,768]{1,0:T(8,128)(2,1)S(1)}, u32[]{:S(2)}, u32[]{:S(2)}) collective-permute-start(bf16[192,768]{1,0:T(8,128)(2,1)S(1)} %get-tuple-element.239.refs_0_), channel_id=1, source_target_pairs={{0,16},{8,24},{16,0},{24,8},{1,17},{9,25},{17,1},{25,9},{2,18},{10... | collective-permute-start | bytes 884744 | tf_op jit(solution)/shard_map/out_near_b2/ppermute | solution.py:45
  138.9 15.2 %collective-permute-start.43 = (bf16[192,768]{1,0:T(8,128)(2,1)S(1)}, bf16[192,768]{1,0:T(8,128)(2,1)S(1)}, u32[]{:S(2)}, u32[]{:S(2)}) collective-permute-start(bf16[192,768]{1,0:T(8,128)(2,1)S(1)} %get-tuple-element.239.refs_0_), channel_id=1, source_target_pairs={{0,2},{2,0},{4,6},{6,4},{1,3},{3,1},{5,7},{7,5},{8,10},{10,8},{12,... | collective-permute-start | bytes 884744 | tf_op jit(solution)/shard_map/out_back_z1/ppermute | solution.py:45
  154.1 23.1 %collective-permute-start.49 = (bf16[192,768]{1,0:T(8,128)(2,1)S(1)}, bf16[192,768]{1,0:T(8,128)(2,1)S(1)}, u32[]{:S(2)}, u32[]{:S(2)}) collective-permute-start(bf16[192,768]{1,0:T(8,128)(2,1)S(1)} %collective-permute-done.42.refs_3_), channel_id=1, source_target_pairs={{0,16},{8,24},{16,0},{24,8},{1,17},{9,25},{17,1},{25,9},{2,18},{10... | collective-permute-start | bytes 884744 | tf_op jit(solution)/shard_map/in_far_b2/ppermute | solution.py:45
  155.4 30.8 %collective-permute-start.46 = (bf16[384,768]{1,0:T(8,128)(2,1)S(1)}, bf16[384,768]{1,0:T(8,128)(2,1)S(1)}, u32[]{:S(2)}, u32[]{:S(2)}) collective-permute-start(bf16[384,768]{1,0:T(8,128)(2,1)S(1)} %constant_dynamic-update-slice_fusion.6), channel_id=1, source_target_pairs={{0,16},{8,24},{16,0},{24,8},{1,17},{9,25},{17,1},{25,9},{2,18},{10... | collective-permute-start | bytes 1769480 | tf_op jit(solution)/shard_map/in_near2_b2/ppermute | solution.py:45
  156.1 30.1 %collective-permute-start.48 = (bf16[384,768]{1,0:T(8,128)(2,1)S(1)}, bf16[384,768]{1,0:T(8,128)(2,1)S(1)}, u32[]{:S(2)}, u32[]{:S(2)}) collective-permute-start(bf16[384,768]{1,0:T(8,128)(2,1)S(1)} %constant_dynamic-update-slice_fusion.9), channel_id=1, source_target_pairs={{0,8},{8,0},{16,24},{24,16},{1,9},{9,1},{17,25},{25,17},{2,10},{10... | collective-permute-start | bytes 1769480 | tf_op jit(solution)/shard_map/out_near2_b1/ppermute | solution.py:45
  157.4 18.7 %collective-permute-start.36 = (bf16[104,576]{1,0:T(8,128)(2,1)S(1)}, bf16[104,576]{1,0:T(8,128)(2,1)S(1)}, u32[]{:S(2)}, u32[]{:S(2)}) collective-permute-start(bf16[104,576]{1,0:T(8,128)(2,1)S(1)} %get-tuple-element.192), channel_id=1, source_target_pairs={{0,16},{8,24},{16,0},{24,8},{1,17},{9,25},{17,1},{25,9},{2,18},{10... | collective-permute-start | bytes 359432 | tf_op jit(solution)/shard_map/qkv_b2/ppermute | solution.py:45
  163.0 21.8 %collective-permute-start.50 = (bf16[192,768]{1,0:T(8,128)(2,1)S(1)}, bf16[192,768]{1,0:T(8,128)(2,1)S(1)}, u32[]{:S(2)}, u32[]{:S(2)}) collective-permute-start(bf16[192,768]{1,0:T(8,128)(2,1)S(1)} %collective-permute-done.43.refs_3_), channel_id=1, source_target_pairs={{0,8},{8,0},{16,24},{24,16},{1,9},{9,1},{17,25},{25,17},{2,10},{10... | collective-permute-start | bytes 884744 | tf_op jit(solution)/shard_map/out_far_b1/ppermute | solution.py:45
  177.2 16.7 %collective-permute-start.56 = (bf16[384,768]{1,0:T(8,128)(2,1)S(1)}, bf16[384,768]{1,0:T(8,128)(2,1)S(1)}, u32[]{:S(2)}, u32[]{:S(2)}) collective-permute-start(bf16[384,768]{1,0:T(8,128)(2,1)S(1)} %pad_maximum_fusion.3), channel_id=1, source_target_pairs={{0,8},{8,0},{16,24},{24,16},{1,9},{9,1},{17,25},{25,17},{2,10},{10... | collective-permute-start | bytes 1769480 | tf_op jit(solution)/shard_map/in_far2_b1/ppermute | solution.py:45
  184.9 14.2 %collective-permute-start.57 = (bf16[384,768]{1,0:T(8,128)(2,1)S(1)}, bf16[384,768]{1,0:T(8,128)(2,1)S(1)}, u32[]{:S(2)}, u32[]{:S(2)}) collective-permute-start(bf16[384,768]{1,0:T(8,128)(2,1)S(1)} %pad_maximum_fusion.4), channel_id=1, source_target_pairs={{0,16},{8,24},{16,0},{24,8},{1,17},{9,25},{17,1},{25,9},{2,18},{10... | collective-permute-start | bytes 1769480 | tf_op jit(solution)/shard_map/out_far2_b2/ppermute | solution.py:45
  203.1 24.7 %collective-permute-start.59 = (bf16[544,576]{1,0:T(8,128)(2,1)S(1)}, bf16[544,576]{1,0:T(8,128)(2,1)S(1)}, u32[]{:S(2)}, u32[]{:S(2)}) collective-permute-start(bf16[544,576]{1,0:T(8,128)(2,1)S(1)} %pad_maximum_fusion.1), channel_id=1, source_target_pairs={{0,8},{8,0},{16,24},{24,16},{1,9},{9,1},{17,25},{25,17},{2,10},{10... | collective-permute-start | bytes 1880072 | tf_op jit(solution)/shard_map/heads_far2_b1/ppermute | solution.py:45
  204.4 23.3 %collective-permute-start.58 = (bf16[544,576]{1,0:T(8,128)(2,1)S(1)}, bf16[544,576]{1,0:T(8,128)(2,1)S(1)}, u32[]{:S(2)}, u32[]{:S(2)}) collective-permute-start(bf16[544,576]{1,0:T(8,128)(2,1)S(1)} %pad_maximum_fusion), channel_id=1, source_target_pairs={{0,16},{8,24},{16,0},{24,8},{1,17},{9,25},{17,1},{25,9},{2,18},{10... | collective-permute-start | bytes 1880072 | tf_op jit(solution)/shard_map/heads_near2_b2/ppermute | solution.py:45
  205.1 14.1 %collective-permute-start.51 = (bf16[448,192]{1,0:T(8,128)(2,1)S(1)}, bf16[448,192]{1,0:T(8,128)(2,1)S(1)}, u32[]{:S(2)}, u32[]{:S(2)}) collective-permute-start(bf16[448,192]{1,0:T(8,128)(2,1)S(1)} %get-tuple-element.204), channel_id=1, source_target_pairs={{0,2},{2,0},{4,6},{6,4},{1,3},{3,1},{5,7},{7,5},{8,10},{10,8},{12,... | collective-permute-start | bytes 516104 | tf_op jit(solution)/shard_map/sends_z1/ppermute | solution.py:45
  208.5 13.6 %collective-permute-start.52 = (bf16[448,192]{1,0:T(8,128)(2,1)S(1)}, bf16[448,192]{1,0:T(8,128)(2,1)S(1)}, u32[]{:S(2)}, u32[]{:S(2)}) collective-permute-start(bf16[448,192]{1,0:T(8,128)(2,1)S(1)} %get-tuple-element.205), channel_id=1, source_target_pairs={{0,4},{2,6},{4,0},{6,2},{1,5},{3,7},{5,1},{7,3},{8,12},{10,14},{12... | collective-permute-start | bytes 516104 | tf_op jit(solution)/shard_map/sends_z2/ppermute | solution.py:45
  208.8 13.3 %collective-permute-start.53 = (bf16[448,192]{1,0:T(8,128)(2,1)S(1)}, bf16[448,192]{1,0:T(8,128)(2,1)S(1)}, u32[]{:S(2)}, u32[]{:S(2)}) collective-permute-start(bf16[448,192]{1,0:T(8,128)(2,1)S(1)} %get-tuple-element.206), channel_id=1, source_target_pairs={{0,6},{2,4},{4,2},{6,0},{1,7},{3,5},{5,3},{7,1},{8,14},{10,12},{12... | collective-permute-start | bytes 516104 | tf_op jit(solution)/shard_map/sends_z3/ppermute | solution.py:45
  (56 other events, 450.1 us)

commit v4 on v3

--- a/solution.py
+++ b/solution.py
@@ -565,8 +565,8 @@
     return lax.optimization_barrier((tuple(values), tuple(earlier)))[0]
 
 
-def both_gains(wt, own, other, at, size):
-    mine, theirs = own[:, at : at + size].astype(F32), other[:, at : at + size].astype(F32)
+def both_gains(wt, own, other, row):
+    mine, theirs = own[row : row + 1, :].astype(F32), other[row : row + 1, :].astype(F32)
     first = jnp.where(wt == 0, mine, theirs)
     second = jnp.where(wt == 0, theirs, mine)
     return jnp.concatenate([first, second], axis=1)
@@ -583,15 +583,18 @@
     return copies
 
 
-def heads_kernel(heads, hsize, idx, *refs):
+TABLE_ROW = 8
+
+
+def heads_kernel(heads, hsize, own_buckets, idx, *refs):
     wq, wk, wv, wq2, wk2, wv2 = refs[:6]
-    fars = refs[6:13]
-    xs = refs[13:17]
-    n1_ref, q_ref, k_ref, v_ref, pt_ref, pm_ref, mix_ref, wrow_ref, pk_ref, pv_ref = refs[17:27]
-    outs = refs[27:31]
-    att_scr, line_scr, sems, more_sems, *scrs = refs[31:]
+    fars = refs[6:11]
+    x = refs[11]
+    n1_ref, q_ref, k_ref, v_ref, pt_ref, pm_ref, mix_ref, wrow_ref, pk_ref, pv_ref = refs[12:22]
+    outs = refs[22:26]
+    att_scr, line_scr, sems, more_sems, *scrs = refs[26:]
     w_scr, nears = scrs[:3], scrs[3:]
-    small, small2, tab, tab2, pk_all, pv_all, bucket_row = nears
+    small, small2, pk_all, pv_all, bucket_row = nears
     more = [
         pltpu.make_async_copy(source, to, more_sems.at[i])
         for i, (source, to) in enumerate(zip(fars, nears))
@@ -599,8 +602,8 @@
     for copy in more:
         copy.start()
     batch, here, wt = idx[0], idx[1], idx[2]
-    rows, width = xs[0].shape
-    length = 4 * rows
+    length, width = x.shape
+    rows = length // 4
     half = wq.shape[0]
     cols = heads * hsize
     window = w_scr[0].shape[1]
@@ -628,11 +631,9 @@
     def own_cols(value):
         return jnp.where(odd == 0, value[:, :cols], value[:, shift:])
 
-    gain = both_gains(wt, small, small2, 0, half)
-    for step in range(4):
-        scaled, _ = norm(xs[step][...].astype(F32))
-        at = pl.multiple_of((here ^ step) * rows, rows)
-        n1_ref[pl.ds(at, rows), :] = (scaled * gain).astype(BF)
+    gain = both_gains(wt, small, small2, 0)
+    scaled, _ = norm(x[...].astype(F32))
+    n1_ref[...] = (scaled * gain).astype(BF)
     normed = n1_ref[...]
     for copy in copies:
         copy.wait()
@@ -645,13 +646,15 @@
         ).astype(BF)
     vals_t = v_ref[...].T
     pv_t = pv_ref[...].astype(F32).T.astype(BF)
-    own_buckets = tab.shape[0]
+    tab, tab2 = (
+        ref[TABLE_ROW : TABLE_ROW + own_buckets, :LANES].astype(F32) for ref in (small, small2)
+    )
     ids = lax.broadcasted_iota(jnp.int32, (own_buckets, 2 * length), 0)
-    lines = tn(tab[...].astype(F32), (ids + wt * own_buckets == bucket_row[...]).astype(F32))
+    lines = tn(tab, (ids + wt * own_buckets == bucket_row[...]).astype(F32))
     lines = lines + tn(
-        tab2[...].astype(F32), (ids + (1 - wt) * own_buckets == bucket_row[...]).astype(F32)
-    )
-    line_scr[: lines.shape[0], :] = lines
+        tab2, (ids + (1 - wt) * own_buckets == bucket_row[...]).astype(F32)
+    )
+    line_scr[...] = lines[: line_scr.shape[0]]
     for h in range(heads):
         part = slice(h * hsize, (h + 1) * hsize)
         query = q_ref[:, part]
@@ -698,7 +701,7 @@
         hidden = hidden + nn(att_ref[c], wo_ref[c * cols : (c + 1) * cols, :])
     hidden_ref[...] = hidden
     scaled, _ = norm(hidden)
-    n2_ref[...] = (scaled * both_gains(wt, small, small2, half, half)).astype(BF)
+    n2_ref[...] = (scaled * both_gains(wt, small, small2, 1)).astype(BF)
 
 
 def gelu_parts(v):
@@ -709,21 +712,44 @@
     return 0.5 * v * (1.0 + t), grad
 
 
+def own_columns(batch, ff_own, block):
+    return [pl.ds(pl.multiple_of(o * ff_own + batch * block, block), block) for o in range(2)]
+
+
 def ffn_kernel(idx, *refs):
     w1, w1b, w2, w2b = refs[:4]
     n2s, gs = refs[4:8], refs[8:12]
     norms = refs[12:16]
     act_ref, gi_ref, w2_ref, w1_scr, sems = refs[16:]
-    wt = idx[2]
-    copies = fetch_rows(sems, wt, [(w1_scr, w1, w1b), (w2_ref, w2, w2b)])
-    for copy in copies[:2]:
+    batch, wt = idx[0], idx[2]
+    half = w1.shape[0]
+    block = w1_scr.shape[1] // 2
+    ff_own = w2.shape[0]
+    copies = []
+    for j, (source, place) in enumerate(((w1, wt), (w1b, 1 - wt))):
+        to = pl.ds(pl.multiple_of(place * half, half), half)
+        for o, cut in enumerate(own_columns(batch, ff_own, block)):
+            copies.append(
+                pltpu.make_async_copy(
+                    source.at[:, cut],
+                    w1_scr.at[to, o * block : (o + 1) * block],
+                    sems.at[2 * j + o],
+                )
+            )
+    cut = pl.ds(pl.multiple_of(batch * block, block), block)
+    for j, (source, place) in enumerate(((w2, wt), (w2b, 1 - wt))):
+        to = pl.ds(pl.multiple_of(place * block, block), block)
+        copies.append(pltpu.make_async_copy(source.at[cut, :], w2_ref.at[to, :], sems.at[4 + j]))
+    for copy in copies:
+        copy.start()
+    for copy in copies[:4]:
         copy.wait()
     rows = n2s[0].shape[0]
     for s in range(4):
         at = slice(s * rows, (s + 1) * rows)
         act, slope = gelu_parts(nn(n2s[s][...], w1_scr[...]))
         if s == 0:
-            for copy in copies[2:]:
+            for copy in copies[4:]:
                 copy.wait()
         act_ref[at, :] = act.astype(BF)
         grad = (nt(gs[s][...], w2_ref[...]).astype(BF).astype(F32) * slope).astype(BF)
@@ -733,8 +759,8 @@
 
 def ffn_back_kernel(idx, *refs):
     n2s, gs = refs[:4], refs[4:8]
-    act, gi = refs[8:10]
-    mine, theirs, all_scr, scr = refs[10:]
+    act, gi, w2 = refs[8:11]
+    mine, theirs, keep, send, all_scr, scr = refs[11:]
     here, wt = idx[1], idx[2]
     rows = n2s[0].shape[0]
     size = scr.shape[0] // 8
@@ -754,6 +780,8 @@
         all_scr[s * rows : (s + 1) * rows, :] = gs[s][...]
     scr[...] = tn(act[...], all_scr[...]).astype(BF)
     spread(1)
+    for s, (out, to) in enumerate(((keep, 0), (keep, rows), (send, 0), (send, rows))):
+        out[to : to + rows, :] = nn(act[s * rows : (s + 1) * rows, :], w2[...]).astype(BF)
 
 
 def hidden_back_kernel(idx, *refs):
@@ -768,7 +796,7 @@
     for part in parts[1:]:
         grad_norm = grad_norm + part[...].astype(F32)
     scaled, inverse = norm(hidden_ref[...])
-    e = grad_norm * both_gains(wt, small, small2, half, half)
+    e = grad_norm * both_gains(wt, small, small2, 1)
     grad = g[...].astype(F32) + inverse * (
         e - scaled * jnp.mean(e * scaled, axis=-1, keepdims=True)
     )
@@ -780,9 +808,8 @@
         outs[step][...] = nt(low, wo[pl.ds(at, cols), :]).astype(BF)
 
 
-def wo_back_kernel(idx, att, low, act, w2, mine, theirs, keep, send, scr):
+def wo_back_kernel(idx, att, low, mine, theirs, scr):
     batch, here, wt = idx[0], idx[1], idx[2]
-    rows = low.shape[0]
     size = att.shape[2]
     for c in range(4):
         scr[c * size : (c + 1) * size, :] = tn(att[c], low[...])
@@ -793,20 +820,20 @@
                 at = (((wt ^ i) * 4 + (here ^ place)) * 4 + (batch ^ far)) * size
                 to = (4 * q + p) * size
                 out[to : to + size, :] = scr[pl.ds(pl.multiple_of(at, 8), size), :].astype(BF)
-    for s, (out, to) in enumerate(((keep, 0), (keep, rows), (send, 0), (send, rows))):
-        out[to : to + rows, :] = nn(act[s * rows : (s + 1) * rows, :], w2[...]).astype(BF)
 
 
 def heads_back_kernel(heads, hsize, idx, *refs):
     gms = refs[:4]
     pt, pm, q, k, v, mix, pk, pv, bucket_row, n1 = refs[4:14]
     mine, theirs = refs[14:16]
-    outs = refs[16:20]
-    gm_scr, gqt_scr, acc, grad_scr, w_scr = refs[20:]
+    own_out, near_out, far_out = refs[16:19]
+    gm_scr, gqt_scr, acc, grad_scr, w_scr = refs[19:]
     batch, here, wt = idx[0], idx[1], idx[2]
     rows, cols = gms[0].shape
     length = 4 * rows
     mem = pk.shape[0]
+    high = own_out.shape[0]
+    outs = (own_out, far_out, near_out.at[:high], near_out.at[high:])
     for step in range(4):
         at = pl.multiple_of((here ^ step) * rows, rows)
         gm_scr[pl.ds(at, rows), :] = gms[step][...]
@@ -910,14 +937,24 @@
     )
 
 
-def ffn_piece_kernel(idx, ffn, ffn2, w_in, first_ref, second_ref, sum_ref):
-    here = idx[1]
-    quarter = first_ref.shape[0]
+def ffn_piece_kernel(idx, w_in, ffn, ffn2, piece_ref, sum_ref, w_scr, sems):
+    batch, here = idx[0], idx[1]
+    quarter, width = w_scr.shape
+    block = width // 2
+    rows = pl.ds(pl.multiple_of(here * quarter, quarter), quarter)
+    copies = [
+        pltpu.make_async_copy(
+            w_in.at[rows, cut], w_scr.at[:, o * block : (o + 1) * block], sems.at[o]
+        )
+        for o, cut in enumerate(own_columns(batch, w_in.shape[1] // 2, block))
+    ]
+    for copy in copies:
+        copy.start()
     grad = ffn[...].astype(F32) + ffn2[...].astype(F32)
-    first_ref[...] = grad[:quarter].astype(BF)
-    second_ref[...] = grad[quarter:].astype(BF)
-    rows = w_in[pl.ds(pl.multiple_of(here * quarter, quarter), quarter), :].astype(F32)
-    sum_ref[...] = row_sums(grad[:quarter] * rows)
+    piece_ref[...] = grad.astype(BF)
+    for copy in copies:
+        copy.wait()
+    sum_ref[...] = row_sums(grad[:quarter] * w_scr[...].astype(F32))
 
 
 def heads_piece_kernel(qkv, qkv2, wo, wo2, wrow, sum_in, piece_ref):
@@ -963,65 +1000,59 @@
 
 
 def rows_out_kernel(idx, *refs):
-    out = refs[6]
-    step = pl.program_id(0)
+    out, scr, sems = refs[6:]
+    copies = []
     for at in range(4):
-
-        @pl.when(step == at)
-        def _():
-            for place, ref, start, size in ctx_pieces(refs[:6], at, 2):
-                row = pl.multiple_of((idx[1] ^ place) * size, 8)
-                out[pl.ds(row, size), :] = ref[start : start + size, :].astype(F32)
-
-
-def rows_out(index, pieces):
+        for place, ref, start, size in ctx_pieces(refs[:6], at, 2):
+            row = len(copies) * size
+            scr[row : row + size, :] = ref[start : start + size, :].astype(F32)
+            to = pl.multiple_of(((idx[0] ^ at) * 4 + (idx[1] ^ place)) * size, size)
+            copies.append(
+                pltpu.make_async_copy(
+                    scr.at[row : row + size, :], out.at[pl.ds(to, size), :], sems.at[len(copies)]
+                )
+            )
+            copies[-1].start()
+    for copy in copies:
+        copy.wait()
+
+
+def cols_out_kernel(idx, *refs):
+    out, scr, sems = refs[6:]
+    copies = []
+    block = scr.shape[1] // 2
+    for at in range(4):
+        for place, ref, start, size in ctx_pieces(refs[:6], at, 1):
+            row = (len(copies) // 2) * size
+            scr[row : row + size, :] = ref[start : start + size, :].astype(F32)
+            to = pl.multiple_of((idx[1] ^ place) * size, size)
+            for o in range(2):
+                col = pl.multiple_of((4 * o + (idx[0] ^ at)) * block, block)
+                copies.append(
+                    pltpu.make_async_copy(
+                        scr.at[row : row + size, o * block : (o + 1) * block],
+                        out.at[pl.ds(to, size), pl.ds(col, block)],
+                        sems.at[len(copies)],
+                    )
+                )
+                copies[-1].start()
+    for copy in copies:
+        copy.wait()
+
+
+def pieces_out(kernel, name, index, pieces, dims, copies):
     rows, width = pieces[0].shape
     return pl.pallas_call(
-        rows_out_kernel,
-        out_shape=shape((8 * rows, width), F32),
-        grid_spec=pltpu.PrefetchScalarGridSpec(
-            num_scalar_prefetch=1,
-            grid=(4,),
-            in_specs=[pl.BlockSpec(p.shape, lambda step, idx: (0, 0)) for p in pieces],
-            out_specs=pl.BlockSpec((2 * rows, width), lambda step, idx: (idx[0] ^ step, 0)),
-        ),
-        compiler_params=params(32),
-        name="rows_out",
-    )(index, *pieces)
-
-
-def cols_out_kernel(idx, *refs):
-    out = refs[6]
-    step = pl.program_id(0)
-    for at in range(4):
-
-        @pl.when(step // 2 == at)
-        def _():
-            for place, ref, start, size in ctx_pieces(refs[:6], at, 1):
-                row = pl.multiple_of((idx[1] ^ place) * size, 8)
-                out[pl.ds(row, size), :] = ref[start : start + size, :].astype(F32)
-
-
-def cols_out(index, pieces):
-    rows, width = pieces[0].shape
-    block = width // 2
-
-    def place(step, idx):
-        return (0, (step % 2) * 4 + (idx[0] ^ (step // 2)))
-
-    return pl.pallas_call(
-        cols_out_kernel,
-        out_shape=shape((2 * rows, 4 * width), F32),
-        grid_spec=pltpu.PrefetchScalarGridSpec(
-            num_scalar_prefetch=1,
-            grid=(8,),
-            in_specs=[
-                pl.BlockSpec((p.shape[0], block), lambda step, idx: (0, step % 2)) for p in pieces
-            ],
-            out_specs=pl.BlockSpec((2 * rows, block), place),
-        ),
-        compiler_params=params(32),
-        name="cols_out",
+        kernel,
+        out_shape=shape(dims, F32),
+        in_specs=[smem()] + vmem(6),
+        out_specs=pl.BlockSpec(memory_space=pltpu.HBM),
+        scratch_shapes=[
+            pltpu.VMEM((8 * rows, width), F32),
+            pltpu.SemaphoreType.DMA((copies,)),
+        ],
+        compiler_params=params(16),
+        name=name,
     )(index, *pieces)
 
 
@@ -1056,16 +1087,14 @@
     def _():
         seen = [[lines[b, c] for c in range(4)] for b in range(4)]
         take = slice(LANES, LANES + quarter)
-        for b in range(4):
-            total = sum(seen[b][c][LINE - 2 : LINE - 1, take] for c in range(4))
-            gain_one[:, b * quarter : (b + 1) * quarter] = total
-        for c in range(4):
-            total = sum(seen[b][c][LINE - 1 : LINE, take] for b in range(4))
-            gain_two[:, c * quarter : (c + 1) * quarter] = total
-        own = small[...].astype(F32)
-        rows = 4 * quarter
-        gain_one[...] = gain_one[...] / own[:, :rows]
-        gain_two[...] = gain_two[...] / own[:, rows : 2 * rows]
+        one = jnp.concatenate(
+            [sum(seen[b][c][LINE - 2 : LINE - 1, take] for c in range(4)) for b in range(4)], axis=1
+        )
+        two = jnp.concatenate(
+            [sum(seen[b][c][LINE - 1 : LINE, take] for b in range(4)) for c in range(4)], axis=1
+        )
+        gain_one[...] = (one / small[0:1, :].astype(F32))[0]
+        gain_two[...] = (two / small[1:2, :].astype(F32))[0]
         rest = [seen[0][c][:heads, :LANES] for c in range(4)]
         rest.append(jnp.zeros((LANES - 4 * heads, LANES), F32))
         tab_scr[...] = jnp.concatenate(rest, axis=0).T
@@ -1086,8 +1115,8 @@
         out_shape=[shape((part, width), F32)] * 3
         + [
             shape((4, 4, size, width), F32),
-            shape((1, part), F32),
-            shape((1, part), F32),
+            shape((part,), F32),
+            shape((part,), F32),
             shape((buckets // 2, 4 * heads), F32),
         ],
         grid_spec=pltpu.PrefetchScalarGridSpec(
@@ -1097,8 +1126,8 @@
             out_specs=[block] * 3
             + [
                 pl.BlockSpec((4, 1, size, width), lambda step, idx: (0, idx[0] ^ step, 0, 0)),
-                pl.BlockSpec((1, part), lambda step, idx: (0, 0)),
-                pl.BlockSpec((1, part), lambda step, idx: (0, 0)),
+                pl.BlockSpec((part,), lambda step, idx: (0,)),
+                pl.BlockSpec((part,), lambda step, idx: (0,)),
                 pl.BlockSpec((buckets // 2, 4 * heads), lambda step, idx: (0, 0)),
             ],
             scratch_shapes=[
@@ -1157,34 +1186,26 @@
         with jax.named_scope(name + "_b" + str(step)):
             return flip(value, "batch", 4, step)
 
-    xs = [x] + [over_ctx(x, s, "x") for s in range(1, 4)]
+    own_buckets = nbuck // 2
+    small = jnp.concatenate(
+        [
+            jnp.pad(jnp.stack([gain_attn, gain_ffn]), ((0, TABLE_ROW - 2), (0, 0))),
+            jnp.pad(bias_table, ((0, 0), (0, part - all_heads))),
+        ]
+    )
+    w_query2, w_key2, w_value2 = [over_wt(v, "weight") for v in (w_query, w_key, w_value)]
+    small2 = over_wt(small, "small")
+    g_near = over_batch(g, 1, "g")
+    x_all = lax.all_gather(x, "ctx", axis=0, tiled=True)
     bucket_row = jnp.pad(buckets[::-1].reshape(1, -1), ((0, 0), (1, 0)), constant_values=-1)
-    small = jnp.concatenate([gain_attn, gain_ffn]).reshape(1, -1)
-    w_query2, w_key2, w_value2, w_out2 = [
-        over_wt(v, "weight") for v in (w_query, w_key, w_value, w_out)
-    ]
-    table2 = over_wt(bias_table, "table")
-    small2 = over_wt(small, "gain")
-    gs = [g] + [over_batch(g, s, "g") for s in range(1, 4)]
-    w_in_cut, w_back_cut = after((w_in, w_back), (xs[1], bucket_row, small))
-    cut_in = jnp.concatenate(
-        [
-            lax.dynamic_slice_in_dim(w_in_cut, o * ff_own + b * ff_part, ff_part, 1)
-            for o in range(2)
-        ],
-        axis=1,
-    )
-    cut_back = lax.dynamic_slice_in_dim(w_back_cut, b * ff_part, ff_part, 0)
-    cut_in2, cut_back2 = over_wt(cut_in, "in"), over_wt(cut_back, "back")
-    xs = after(xs, (*gs, w_out2, cut_in2, cut_back2))
 
     tokens = shape((length, cols), BF)
-    few = (small, small2, bias_table, table2, prefix_keys[0], prefix_values[0], bucket_row)
+    few = (small, small2, prefix_keys[0], prefix_values[0], bucket_row)
     (n1, q, k, v, pt, pm, mix, wrow, pk, pv, *mixed) = call(
-        functools.partial(heads_kernel, heads, hsize),
+        functools.partial(heads_kernel, heads, hsize, own_buckets),
         "attend",
         index,
-        [*xs],
+        [x_all],
         [shape((length, width), BF)]
         + [tokens] * 3
         + [
@@ -1206,7 +1227,11 @@
         + [pltpu.VMEM(v.shape, v.dtype) for v in few],
         far=(w_query, w_key, w_value, w_query2, w_key2, w_value2, *few),
     )
+    (g_pair, w_out_sent) = after((jnp.concatenate([g, g_near]), w_out), mixed[:1])
+    w_out2 = over_wt(w_out_sent, "weight")
+    g_far = over_batch(g_pair, 2, "g")
     mixed = mixed[:1] + [over_ctx(mixed[s], s, "mixed") for s in range(1, 4)]
+    (*mixed, w_out2, g_far) = after((*mixed, w_out2, g_far), ())
     square = shape((width, width), BF)
     hidden, n2, attended, wo = call(
         hidden_kernel,
@@ -1219,6 +1244,9 @@
     )
 
     n2s = [n2] + [over_batch(n2, s, "n2") for s in range(1, 4)]
+    (w_in_sent, w_back_sent) = after((w_in, w_back), (n2,))
+    w_in2, w_back2 = over_wt(w_in_sent, "in"), over_wt(w_back_sent, "back")
+    gs = (g, g_near, g_far[:rows], g_far[rows:])
     hid = shape((length, 2 * ff_part), BF)
     *norms, act, gi, w_second = call(
         ffn_kernel,
@@ -1226,16 +1254,16 @@
         index,
         [*n2s, *gs],
         [shape((rows, width), BF)] * 4 + [hid, hid, shape((2 * ff_part, width), BF)],
-        [pltpu.VMEM((width, 2 * ff_part), BF), pltpu.SemaphoreType.DMA((4,))],
-        far=(cut_in, cut_in2, cut_back, cut_back2),
+        [pltpu.VMEM((width, 2 * ff_part), BF), pltpu.SemaphoreType.DMA((6,))],
+        far=(w_in, w_in2, w_back, w_back2),
     )
     norms = norms[:1] + [over_batch(norms[s], s, "norm") for s in range(1, 4)]
-    ffn, ffn_sent = call(
+    ffn, ffn_sent, outs, outs_sent = call(
         ffn_back_kernel,
         "ffn_back",
         index,
-        [*n2s, *gs, act, gi],
-        [square, square],
+        [*n2s, *gs, act, gi, w_second],
+        [square, square] + [shape((2 * rows, width), BF)] * 2,
         [pltpu.VMEM((length, width), BF), pltpu.VMEM((width, width), BF)],
     )
     ffn, ffn_sent = halving("ffn_wt", [(ffn, over_wt(ffn_sent, "ffn"), 0)])
@@ -1249,34 +1277,44 @@
         [shape((rows, width), F32), shape((rows, width), BF)] + [shape((rows, cols), BF)] * 4,
     )
     ffn, ffn_sent = halving("ffn_near", [(ffn, ffn_got, 0)])
-    ffn_got = over_ctx(ffn_sent, 2, "ffn")
-    gms = after(gms, (ffn, ffn_sent))
-    gms = list(gms[:1]) + [over_ctx(gms[s], s, "gm") for s in range(1, 4)]
-    wo_sum, wo_sent, outs, outs_sent = call(
+    outs_got = over_batch(outs_sent, 2, "outs")
+    wo_sum, wo_sent = call(
         wo_back_kernel,
         "wo_back",
         index,
-        [attended, low, act, w_second],
-        [shape((part, width), BF)] * 2 + [shape((2 * rows, width), BF)] * 2,
+        [attended, low],
+        [shape((part, width), BF)] * 2,
         [pltpu.VMEM((width, width), F32)],
     )
-    outs_got = over_batch(outs_sent, 2, "outs")
+    gms = after(gms, (ffn, ffn_sent, outs_got))
+    ffn_got = over_ctx(ffn_sent, 2, "ffn")
     wo_sum, wo_sent = halving("wo_wt", [(wo_sum, over_wt(wo_sent, "wo"), 0)])
-    wo_got = over_batch(wo_sent, 1, "wo")
-    first, second, sum_in = call(
+    wo_sum, wo_sent = halving("wo_near", [(wo_sum, over_batch(wo_sent, 1, "wo"), 0)])
+    wo_got = over_batch(wo_sent, 2, "wo")
+    gms = list(gms[:1]) + [over_ctx(gms[s], s, "gm") for s in range(1, 4)]
+    (ffn_got, wo_got, *gms) = after((ffn_got, wo_got, *gms), ())
+    ffn, sum_in = call(
         ffn_piece_kernel,
         "ffn_piece",
         index,
-        [ffn, ffn_got, cut_in],
-        [shape((quarter, width), BF)] * 2 + [shape((8, quarter), F32)],
-    )
-    gms = after(gms, (first, second, wo_got, outs_got))
-    (qkv, qkv_sent, *sends) = call(
+        [ffn, ffn_got],
+        [shape((2 * quarter, width), BF), shape((8, quarter), F32)],
+        [pltpu.VMEM((quarter, width), BF), pltpu.SemaphoreType.DMA((2,))],
+        far=(w_in,),
+    )
+    wo_sum, wo_sent = halving("wo_far", [(wo_sum, wo_got, 0)])
+    gms = after(gms, (ffn, wo_sum, wo_sent))
+    outs, outs_sent = halving("outs_far", [(outs, outs_got, 0)])
+    (outs_sent,) = after((outs_sent,), (ffn, wo_sum))
+    ffn_far = over_ctx(ffn, 2, "ffn_back")
+    high = 3 * rows + MEM_END
+    (qkv, qkv_sent, own_block, near_blocks, far_block) = call(
         functools.partial(heads_back_kernel, heads, hsize),
         "attend_back",
         index,
         [*gms, pt, pm, q, k, v, mix, pk, pv, bucket_row, n1],
-        [shape((part + LINE, wide), BF)] * 2 + [shape((3 * rows + MEM_END, cols), BF)] * 4,
+        [shape((part + LINE, wide), BF)] * 2
+        + [shape((n * high, cols), BF) for n in (1, 2, 1)],
         [
             pltpu.VMEM((length, cols), BF),
             pltpu.VMEM((cols, length), F32),
@@ -1285,24 +1323,28 @@
             pltpu.VMEM((width, wide), BF),
         ],
     )
-
-    qkv, qkv_sent, wo_sum, wo_sent, outs, outs_sent = halving(
-        "step_a",
-        [
-            (qkv, over_wt(qkv_sent, "qkv"), LINE),
-            (wo_sum, wo_got, 0),
-            (outs, outs_got, 0),
-        ],
-    )
+    wo_sum, wo_sent = halving("wo_last", [(wo_sum, over_ctx(wo_sent, 1, "wo"), 0)])
+    wo_got = over_ctx(wo_sent, 2, "wo")
     outs_got = over_batch(outs_sent, 1, "outs")
-    qkv, qkv_sent, wo_sum, wo_sent = halving(
-        "step_b",
-        [(qkv, over_batch(qkv_sent, 1, "qkv"), LINE), (wo_sum, over_batch(wo_sent, 2, "wo"), 0)],
-    )
+    qkv, qkv_sent = halving("qkv_wt", [(qkv, over_wt(qkv_sent, "qkv"), LINE)])
+    qkv_got = over_batch(qkv_sent, 1, "qkv")
+    (qkv_got,) = after((qkv_got,), (ffn_far, outs_got))
+    qkv, qkv_sent = halving("qkv_near", [(qkv, qkv_got, LINE)])
     qkv_got = over_batch(qkv_sent, 2, "qkv")
+    (ffn_far, wo_got) = after((ffn_far, wo_got), (qkv_sent,))
+
+    def pile(one, two):
+        return jnp.concatenate([one, two])
+
     result = (hidden + outs.astype(F32) + outs_got.astype(F32)).astype(BF)
-    wo_sum, wo_sent = halving("step_c", [(wo_sum, over_ctx(wo_sent, 1, "wo"), 0)])
-    wo_got = over_ctx(wo_sent, 2, "wo")
+    a1 = pile(ffn[:quarter], ffn_far[:quarter])
+    b1 = pile(ffn[quarter:], ffn_far[quarter:])
+    a2, b2 = over_batch(a1, 1, "in_near"), over_batch(b1, 2, "out_near")
+    c1, d1 = over_ctx(a1, 1, "in_back"), over_ctx(b1, 1, "out_back")
+    pile_a, pile_b = pile(a1, a2), pile(b1, b2)
+    a3, b3 = over_batch(pile_a, 2, "in_near2"), over_batch(pile_b, 1, "out_near2")
+    (c1, d1) = after((c1, d1), (pile_a, pile_b))
+    c2, d2 = over_batch(c1, 2, "in_far"), over_batch(d1, 1, "out_far")
     height = quarter + quarter // 4 + quarter // 12 + LINE
     piece = pl.pallas_call(
         heads_piece_kernel,
@@ -1313,34 +1355,28 @@
         name="heads_piece",
     )(qkv, qkv_got, wo_sum, wo_got, wrow, sum_in)
 
-    def pile(one, two):
-        return jnp.concatenate([one, two])
-
-    in_far, out_far = over_ctx(first, 2, "in_back"), over_ctx(second, 2, "out_back")
-    (piece,) = after((piece,), (in_far, out_far, result))
+    (piece,) = after((piece,), (c1, d1))
     heads_far = over_ctx(piece, 2, "heads_back")
-    a1, b1 = pile(first, in_far), pile(second, out_far)
-    a2, b2 = over_batch(a1, 1, "in_near"), over_batch(b1, 2, "out_near")
-    c1, d1 = over_ctx(a1, 1, "in_back"), over_ctx(b1, 1, "out_back")
-    pile_a, pile_b = pile(a1, a2), pile(b1, b2)
-    a3 = over_batch(pile_a, 2, "in_near2")
-    b3 = over_batch(pile_b, 1, "out_near2")
-    (heads_far,) = after((heads_far,), (c1, d1))
+    pile_c, pile_d = pile(c1, c2), pile(d1, d2)
+    c3, d3 = over_batch(pile_c, 1, "in_far2"), over_batch(pile_d, 2, "out_far2")
+    (heads_far,) = after((heads_far,), (a3, b3))
+    (near_blocks,) = after((near_blocks,), (heads_far,))
+    near_got = over_ctx(near_blocks, 2, "sends")
+    far_pile = pile(far_block, near_got[high:])
+    far_got = over_ctx(far_pile, 1, "sends")
     e1 = pile(piece, heads_far)
     f1 = over_ctx(e1, 1, "heads_back")
-    (c1, d1) = after((c1, d1), (pile_a, pile_b))
-    c2, d2 = over_batch(c1, 2, "in_far"), over_batch(d1, 1, "out_far")
-    (e1, f1) = after((e1, f1), (a3, b3, c2, d2))
-    c3 = over_batch(pile(c1, c2), 1, "in_far2")
-    d3 = over_batch(pile(d1, d2), 2, "out_far2")
+    (e1, f1) = after((e1, f1), (pile_c, pile_d))
     e2, f2 = over_batch(e1, 1, "heads_near"), over_batch(f1, 2, "heads_far")
-    sends[1:] = after(sends[1:], (f1,))
-    sends = sends[:1] + [over_ctx(sends[s], s, "sends") for s in range(1, 4)]
-    (e1, e2, f1, f2) = after((e1, e2, f1, f2), (c3, d3))
+    (e1, e2, f1, f2) = after((e1, e2, f1, f2), (c3, d3, far_pile))
     e3 = over_batch(pile(e1, e2), 2, "heads_near2")
     f3 = over_batch(pile(f1, f2), 1, "heads_far2")
-    out_second = rows_out(index, (b1, b2, b3, d1, d2, d3))
-    out_first = cols_out(index, (a1, a2, a3, c1, c2, c3))
+    out_second = pieces_out(
+        rows_out_kernel, "rows_out", index, (b1, b2, b3, d1, d2, d3), (ff_own, width), 16
+    )
+    out_first = pieces_out(
+        cols_out_kernel, "cols_out", index, (a1, a2, a3, c1, c2, c3), (part, 2 * ff_own), 32
+    )
     out_q, out_k, out_v, out_wo, gain_one, gain_two, out_table = heads_out(
         index, (e1, e2, e3, f1, f2, f3), small, width, heads, nbuck
     )
@@ -1348,9 +1384,9 @@
         input_end_kernel,
         "input_back",
         index,
-        [*sends, x, small, small2, grad_hidden],
+        [own_block, near_got, far_got, x, small, small2, grad_hidden],
         [shape((rows, width), BF), shape((mem, width), F32), shape((mem, width), F32)],
-        [pltpu.VMEM((4,) + sends[0].shape, BF), pltpu.SemaphoreType.DMA((6,))]
+        [pltpu.VMEM((4,) + own_block.shape, BF), pltpu.SemaphoreType.DMA((6,))]
         + [pltpu.VMEM((width, width), BF)] * 3,
         far=(w_query, w_key, w_value, w_query2, w_key2, w_value2),
     )
@@ -1359,8 +1395,8 @@
         grad_x[None],
         grad_memk[None],
         grad_memv[None],
-        gain_one.reshape(part),
-        gain_two.reshape(part),
+        gain_one,
+        gain_two,
         out_table,
         out_q,
         out_k,
@@ -1373,9 +1409,10 @@
 
 def input_end_kernel(idx, *refs):
     wq, wk, wv, wq2, wk2, wv2 = refs[:6]
-    parts = refs[6:10]
-    x, small, small2, grad_hidden = refs[10:14]
-    out_ref, memk_ref, memv_ref, scr, sems, *w_scr = refs[14:]
+    own, near, far, x, small, small2, grad_hidden = refs[6:13]
+    out_ref, memk_ref, memv_ref, scr, sems, *w_scr = refs[13:]
+    high = own.shape[0]
+    parts = (own, far.at[:high], near.at[:high], far.at[high:])
     here, wt = idx[1], idx[2]
     rows = x.shape[0]
     mem = memk_ref.shape[0]
@@ -1390,7 +1427,7 @@
 
     grad_norm = sum(nt(wide(p * rows, rows), whole[...]) for p, whole in enumerate(w_scr))
     scaled, inverse = norm(x[...].astype(F32))
-    e = grad_norm * both_gains(wt, small, small2, 0, wq.shape[0])
+    e = grad_norm * both_gains(wt, small, small2, 0)
     grad = grad_hidden[...] + inverse * (
         e - scaled * jnp.mean(e * scaled, axis=-1, keepdims=True)
     )

time: 233 us -> 215 us (0.923)
  waiting for transfers between devices: 114 us -> 91.6 us
  blocking collectives: 0 us -> 20.1 us
  starting transfers between devices: 61.7 us -> 52.2 us
  local copies, waits for them, and re-layouts: 10.8 us -> 7.54 us
  Pallas kernels: 42.4 us -> 39.5 us
    ppermute x60 -> x53, waiting for transfers between devices: 114 us -> 91.6 us  [flip(): return lax.ppermute(value, axis, [(i, i ^ step) for i in range(size)])]
    all_gather x0 -> x1, blocking collectives: none -> 20.1 us  [paired(): x_all = lax.all_gather(x, 'ctx', axis=0, tiled=True)]
    ppermute x60 -> x53, starting transfers between devices: 61.7 us -> 52.2 us  [flip(): return lax.ppermute(value, axis, [(i, i ^ step) for i in range(size)])]
    unnamed x48 -> x29, local copies, waits for them, and re-layouts: 9.53 us -> 5.96 us
  transfers between devices with their start and end apart: 60 -> 53, of which waited for: 27 -> 27; matrix products, arithmetic and copies ran while one was open for 2% -> 3% of each run, Pallas kernels for 8% -> 5%
where the time goes in v4:
time: 215 us
  waiting for transfers between devices  91.6 us (43%)
  starting transfers between devices  52.2 us (24%)
  Pallas kernels  39.5 us (18%)
  blocking collectives  20.1 us (9%)
  local copies, waits for them, and re-layouts  7.54 us (4%)
  other arithmetic  2.48 us (1%)
    ppermute x53, waiting for transfers between devices, flip(): return lax.ppermute(value, axis, [(i, i ^ step) for i in range(size)])  91.6 us
    ppermute x53, starting transfers between devices, flip(): return lax.ppermute(value, axis, [(i, i ^ step) for i in range(size)])  52.2 us
    pallas_call x9, Pallas kernels, call(): pl.pallas_call(kernel, out_shape=out, in_specs=[smem()] + stay + vmem(len...  28 us
    all_gather x1, blocking collectives, paired(): x_all = lax.all_gather(x, 'ctx', axis=0, tiled=True)  20.1 us
    unnamed x29, local copies, waits for them, and re-layouts  5.96 us
    pallas_call x2, Pallas kernels, pieces_out(): pl.pallas_call(kernel, out_shape=shape(dims, F32), in_specs=[smem()] + vm...  5.87 us
  transfers between devices with their start and end apart: 53, of which 27 were waited for; matrix products, arithmetic and copies ran while one was open for 3% of the time, Pallas kernels for 5%

profile of v4, /device:TPU:0, one launch (start us, length us, event | category | flops | bytes accessed | tf_op | source)
XLA Modules:
  0.0 214.7 jit_solution(4314508163423262087)
XLA Ops:
  4.5 2.9 %collective-permute-start.7 = (bf16[128,768]{1,0:T(8,128)(2,1)}, bf16[128,768]{1,0:T(8,128)(2,1)S(1)}, u32[]{:S(2)}, u32[]{:S(2)}) collective-permute-start(bf16[128,768]{1,0:T(8,128)(2,1)} %bitcast.16), channel_id=1, source_target_pairs={{0,8},{8,0},{16,24},{24,16},{1,9},{9,1},{17,25},{25,17},{2,10},{10... | collective-permute-start | bytes 589832 | tf_op jit(solution)/shard_map/g_b1/ppermute | solution.py:45
  7.4 20.1 %all-gather = bf16[1,512,768]{2,1,0:T(8,128)(2,1)S(1)} all-gather(bf16[1,128,768]{2,1,0:T(8,128)(2,1)} %param.14), channel_id=2, replica_groups=mesh['batch'=4,'ctx'=4,'wt'=2] {'ctx'}, dimensions={1}, use_global_device_ids=true | all-gather | bytes 983040 | tf_op jit(solution)/shard_map/all_gather | solution.py:1199
  31.1 5.4 %attend.1 = (bf16[512,768]{1,0:T(8,128)(2,1)S(1)}, bf16[512,192]{1,0:T(8,128)(2,1)S(1)}, bf16[512,192]{1,0:T(8,128)(2,1)S(1)}, bf16[512,192]{1,0:T(8,128)(2,1)S(...) custom-call(s32[3]{0:T(128)S(1)} %pad_add_fusion.idx, ...), custom_call_target="tpu_custom_call" | custom-call | tf_op jit(solution)/shard_map/attend/pallas_call | solution.py:553
  43.4 3.4 %collective-permute-done.5.refs_4_ = bf16[128,192]{1,0:T(8,128)(2,1)S(1)} collective-permute-done((bf16[128,192]{1,0:T(8,128)(2,1)S(1)}, bf16[128,192]{1,0:T(8,128)(2,1)S(1)}, u32[]{:S(2)}, u32[]{:S(2)}) %collective-permute-start.5) | collective-permute-done | bytes 49184 | tf_op jit(solution)/shard_map/mixed_z2/ppermute | solution.py:45
  55.0 5.2 %collective-permute-done.12.refs_7_.refs_3_ = bf16[128,768]{1,0:T(8,128)(2,1)S(1)} collective-permute-done((bf16[128,768]{1,0:T(8,128)(2,1)S(1)}, bf16[128,768]{1,0:T(8,128)(2,1)S(1)}, u32[]{:S(2)}, u32[]{:S(2)}) %collective-permute-start.12) | collective-permute-done | bytes 196640 | tf_op jit(solution)/shard_map/n2_b3/ppermute | solution.py:45
  60.2 3.3 %collective-permute-done.11.refs_6_.refs_2_ = bf16[128,768]{1,0:T(8,128)(2,1)S(1)} collective-permute-done((bf16[128,768]{1,0:T(8,128)(2,1)S(1)}, bf16[128,768]{1,0:T(8,128)(2,1)S(1)}, u32[]{:S(2)}, u32[]{:S(2)}) %collective-permute-start.11) | collective-permute-done | bytes 196640 | tf_op jit(solution)/shard_map/n2_b2/ppermute | solution.py:45
  63.6 5.2 %ffn.1 = (bf16[128,768]{1,0:T(8,128)(2,1)S(1)}, bf16[128,768]{1,0:T(8,128)(2,1)S(1)}, bf16[128,768]{1,0:T(8,128)(2,1)S(1)}, bf16[128,768]{1,0:T(8,128)(2,1)S(1)}...) custom-call(s32[3]{0:T(128)S(1)} %pad_add_fusion.idx, ...), custom_call_target="tpu_custom_call" | custom-call | tf_op jit(solution)/shard_map/ffn/pallas_call | solution.py:553
  71.7 2.8 %collective-permute-done.16.refs_1_ = bf16[768,768]{1,0:T(8,128)(2,1)S(1)} collective-permute-done((bf16[768,768]{1,0:T(8,128)(2,1)S(1)}, bf16[768,768]{1,0:T(8,128)(2,1)S(1)}, u32[]{:S(2)}, u32[]{:S(2)}) %collective-permute-start.16) | collective-permute-done | bytes 1179680 | tf_op jit(solution)/shard_map/ffn_w/ppermute | solution.py:45
  78.5 4.3 %collective-permute-done.19.refs_1_ = bf16[128,768]{1,0:T(8,128)(2,1)S(1)} collective-permute-done((bf16[128,768]{1,0:T(8,128)(2,1)S(1)}, bf16[128,768]{1,0:T(8,128)(2,1)S(1)}, u32[]{:S(2)}, u32[]{:S(2)}) %collective-permute-start.19) | collective-permute-done | bytes 196640 | tf_op jit(solution)/shard_map/norm_b1/ppermute | solution.py:45
  83.0 3.4 %collective-permute-done.21.refs_3_ = bf16[128,768]{1,0:T(8,128)(2,1)S(1)} collective-permute-done((bf16[128,768]{1,0:T(8,128)(2,1)S(1)}, bf16[128,768]{1,0:T(8,128)(2,1)S(1)}, u32[]{:S(2)}, u32[]{:S(2)}) %collective-permute-start.21) | collective-permute-done | bytes 196640 | tf_op jit(solution)/shard_map/norm_b3/ppermute | solution.py:45
  86.4 3.9 %collective-permute-done.17.refs_1_ = bf16[384,768]{1,0:T(8,128)(2,1)S(1)} collective-permute-done((bf16[384,768]{1,0:T(8,128)(2,1)S(1)}, bf16[384,768]{1,0:T(8,128)(2,1)S(1)}, u32[]{:S(2)}, u32[]{:S(2)}) %collective-permute-start.17) | collective-permute-done | bytes 589856 | tf_op jit(solution)/shard_map/ffn_z1/ppermute | solution.py:45
  96.8 7.5 %collective-permute-done.23.refs_1_ = bf16[192,768]{1,0:T(8,128)(2,1)S(1)} collective-permute-done((bf16[192,768]{1,0:T(8,128)(2,1)S(1)}, bf16[192,768]{1,0:T(8,128)(2,1)S(1)}, u32[]{:S(2)}, u32[]{:S(2)}) %collective-permute-start.23) | collective-permute-done | bytes 294944 | tf_op jit(solution)/shard_map/wo_b1/ppermute | solution.py:45
  111.8 4.2 %collective-permute-done.26.refs_2_ = bf16[128,192]{1,0:T(8,128)(2,1)S(1)} collective-permute-done((bf16[128,192]{1,0:T(8,128)(2,1)S(1)}, bf16[128,192]{1,0:T(8,128)(2,1)S(1)}, u32[]{:S(2)}, u32[]{:S(2)}) %collective-permute-start.26) | collective-permute-done | bytes 49184 | tf_op jit(solution)/shard_map/gm_z2/ppermute | solution.py:45
  117.3 4.4 %attend_back.1 = (bf16[392,576]{1,0:T(8,128)(2,1)S(1)}, bf16[392,576]{1,0:T(8,128)(2,1)S(1)}, bf16[448,192]{1,0:T(8,128)(2,1)S(1)}, bf16[896,192]{1,0:T(8,128)(2,1)S(1)}, bf16[448,192]{1,0:T(8,128)(2,1)S(1)}) custom-call(s32[3]{0:T(128)S(1)} %pad_add_fusion.idx, bf16[128,192]{1,0:T(8,128)(2,1)S(1)} %get-tuple-element.192.refs_0_, ...), custom_call_target="tpu_custom_call" | custom-call | tf_op jit(solution)/shard_map/attend_back/pallas_call | solution.py:553
  131.6 9.6 %collective-permute-done.31 = bf16[192,768]{1,0:T(8,128)(2,1)S(1)} collective-permute-done((bf16[192,768]{1,0:T(8,128)(2,1)S(1)}, bf16[192,768]{1,0:T(8,128)(2,1)S(1)}, u32[]{:S(2)}, u32[]{:S(2)}) %collective-permute-start.31) | collective-permute-done | bytes 294944 | tf_op jit(solution)/shard_map/ffn_back_z2/ppermute | solution.py:45
  147.3 4.2 %collective-permute-done.38.refs_1_ = bf16[192,768]{1,0:T(8,128)(2,1)S(1)} collective-permute-done((bf16[192,768]{1,0:T(8,128)(2,1)S(1)}, bf16[192,768]{1,0:T(8,128)(2,1)S(1)}, u32[]{:S(2)}, u32[]{:S(2)}) %collective-permute-start.38) | collective-permute-done | bytes 294944 | tf_op jit(solution)/shard_map/out_near_b2/ppermute | solution.py:45
  155.3 3.9 %collective-permute-done.36.refs_3_ = bf16[192,768]{1,0:T(8,128)(2,1)S(1)} collective-permute-done((bf16[192,768]{1,0:T(8,128)(2,1)S(1)}, bf16[192,768]{1,0:T(8,128)(2,1)S(1)}, u32[]{:S(2)}, u32[]{:S(2)}) %collective-permute-start.36) | collective-permute-done | bytes 294944 | tf_op jit(solution)/shard_map/out_back_z1/ppermute | solution.py:45
  162.2 8.1 %collective-permute-done.46.refs_4_ = bf16[192,768]{1,0:T(8,128)(2,1)S(1)} collective-permute-done((bf16[192,768]{1,0:T(8,128)(2,1)S(1)}, bf16[192,768]{1,0:T(8,128)(2,1)S(1)}, u32[]{:S(2)}, u32[]{:S(2)}) %collective-permute-start.46) | collective-permute-done | bytes 294944 | tf_op jit(solution)/shard_map/out_far_b1/ppermute | solution.py:45
  176.1 6.4 %collective-permute-done.44.refs_3_ = bf16[272,576]{1,0:T(8,128)(2,1)S(1)} collective-permute-done((bf16[272,576]{1,0:T(8,128)(2,1)S(1)}, bf16[272,576]{1,0:T(8,128)(2,1)S(1)}, u32[]{:S(2)}, u32[]{:S(2)}) %collective-permute-start.44) | collective-permute-done | bytes 313376 | tf_op jit(solution)/shard_map/heads_back_z1/ppermute | solution.py:45
  184.9 8.7 %collective-permute-done.42.refs_7_ = bf16[896,192]{1,0:T(8,128)(2,1)S(1)} collective-permute-done((bf16[896,192]{1,0:T(8,128)(2,1)S(1)}, bf16[896,192]{1,0:T(8,128)(2,1)S(1)}, u32[]{:S(2)}, u32[]{:S(2)}) %collective-permute-start.42) | collective-permute-done | bytes 344096 | tf_op jit(solution)/shard_map/sends_z2/ppermute | solution.py:45
  196.5 2.9 %rows_out.1 = f32[1536,768]{1,0:T(8,128)} custom-call(s32[3]{0:T(128)S(1)} %pad_add_fusion.idx, bf16[192,768]{1,0:T(8,128)(2,1)S(1)} %pad_maximum_fusion.7.refs_0_, bf16[192,768]{1,0:T(8,128)(2,1)S(1)} %collective-permute-done.38.refs_1_, bf16[384,768]{1,0:T(8,128)(2,1)S(1)} %collective-permute-done.41.refs_2_, ...), custom_call_target="tpu_custom_call" | custom-call | tf_op jit(solution)/shard_map/rows_out/pallas_call | solution.py:1045
  199.4 3.0 %cols_out.1 = f32[384,3072]{1,0:T(8,128)} custom-call(s32[3]{0:T(128)S(1)} %pad_add_fusion.idx, bf16[192,768]{1,0:T(8,128)(2,1)S(1)} %pad_maximum_fusion.6.refs_0_, bf16[192,768]{1,0:T(8,128)(2,1)S(1)} %collective-permute-done.37.refs_1_, bf16[384,768]{1,0:T(8,128)(2,1)S(1)} %collective-permute-done.40.refs_2_, ...), custom_call_target="tpu_custom_call" | custom-call | tf_op jit(solution)/shard_map/cols_out/pallas_call | solution.py:1045
  204.2 4.7 %input_back.1 = (bf16[128,768]{1,0:T(8,128)(2,1)}, f32[20,768]{1,0:T(8,128)S(1)}, f32[20,768]{1,0:T(8,128)S(1)}) custom-call(s32[3]{0:T(128)S(1)} %pad_add_fusion.idx, bf16[384,768]{1,0:T(8,128)(2,1)S(1)} %copy-done.2, bf16[384,768]{1,0:T(8,128)(2,1)S(1)} %copy-done.3, bf16[384,768]{1,0:T(8,128)(2,1)S(1)} %copy-done.5, ...), custom_call_target="tpu_custom_call" | custom-call | tf_op jit(solution)/shard_map/input_back/pallas_call | solution.py:553
  210.3 4.3 %heads_out.1 = (f32[384,768]{1,0:T(8,128)}, f32[384,768]{1,0:T(8,128)}, f32[384,768]{1,0:T(8,128)}, f32[4,4,24,768]{3,2,1,0:T(8,128)}, f32[384]{0:T(512)}, /*index=5*/f32[384]{0:T(512)}, f32[16,12]{1,0:T(8,128)}) custom-call(s32[3]{0:T(128)S(1)} %pad_add_fusion.idx, bf16[272,576]{1,0:T(8,128)(2,1)S(1)} %constant_dynamic-update-slice_fusion.refs_0_, ...), custom_call_target="tpu_custom_call" | custom-call | tf_op jit(solution)/shard_map/heads_out/pallas_call | solution.py:1113
  (156 shorter events, 81.6 us)
Async XLA Ops:
  0.7 27.8 %collective-permute-start = (bf16[384,768]{1,0:T(8,128)(2,1)}, bf16[384,768]{1,0:T(8,128)(2,1)S(1)}, u32[]{:S(2)}, u32[]{:S(2)}) collective-permute-start(bf16[384,768]{1,0:T(8,128)(2,1)} %refs_0_.7), channel_id=1, source_target_pairs={{0,1},{1,0},{2,3},{3,2},{4,5},{5,4},{6,7},{7,6},{8,9},{9,8},{10,11... | collective-permute-start | bytes 1769480 | tf_op jit(solution)/shard_map/weight_w/ppermute | solution.py:45
  1.2 27.3 %collective-permute-start.1 = (bf16[384,768]{1,0:T(8,128)(2,1)}, bf16[384,768]{1,0:T(8,128)(2,1)S(1)}, u32[]{:S(2)}, u32[]{:S(2)}) collective-permute-start(bf16[384,768]{1,0:T(8,128)(2,1)} %refs_1_.3), channel_id=1, source_target_pairs={{0,1},{1,0},{2,3},{3,2},{4,5},{5,4},{6,7},{7,6},{8,9},{9,8},{10,11... | collective-permute-start | bytes 1769480 | tf_op jit(solution)/shard_map/weight_w/ppermute | solution.py:45
  1.3 27.2 %collective-permute-start.2 = (bf16[384,768]{1,0:T(8,128)(2,1)}, bf16[384,768]{1,0:T(8,128)(2,1)}, u32[]{:S(2)}, u32[]{:S(2)}) collective-permute-start(bf16[384,768]{1,0:T(8,128)(2,1)} %refs_2_.5), channel_id=1, source_target_pairs={{0,1},{1,0},{2,3},{3,2},{4,5},{5,4},{6,7},{7,6},{8,9},{9,8},{10,11... | collective-permute-start | bytes 1769480 | tf_op jit(solution)/shard_map/weight_w/ppermute | solution.py:45
  4.4 24.1 %collective-permute-start.3 = (bf16[24,384]{1,0:T(8,128)(2,1)}, bf16[24,384]{1,0:T(8,128)(2,1)}, u32[]{:S(2)}, u32[]{:S(2)}) collective-permute-start(bf16[24,384]{1,0:T(8,128)(2,1)} %fusion.2.refs_6_.refs_7_.refs_5_.refs_10_), channel_id=1, source_target_pairs={{0,1},{1,0},{2,3},{3,2},{4,5},{5,4},{6,7},{7,6},{8,9},{9,8},{10,11... | collective-permute-start | bytes 55304 | tf_op jit(solution)/shard_map/small_w/ppermute | solution.py:45
  4.5 24.0 %collective-permute-start.7 = (bf16[128,768]{1,0:T(8,128)(2,1)}, bf16[128,768]{1,0:T(8,128)(2,1)S(1)}, u32[]{:S(2)}, u32[]{:S(2)}) collective-permute-start(bf16[128,768]{1,0:T(8,128)(2,1)} %bitcast.16), channel_id=1, source_target_pairs={{0,8},{8,0},{16,24},{24,16},{1,9},{9,1},{17,25},{25,17},{2,10},{10... | collective-permute-start | bytes 589832 | tf_op jit(solution)/shard_map/g_b1/ppermute | solution.py:45
  36.5 11.6 %collective-permute-start.8 = (bf16[384,768]{1,0:T(8,128)(2,1)}, bf16[384,768]{1,0:T(8,128)(2,1)S(1)}, u32[]{:S(2)}, u32[]{:S(2)}) collective-permute-start(bf16[384,768]{1,0:T(8,128)(2,1)} %refs_0_.5), channel_id=1, source_target_pairs={{0,1},{1,0},{2,3},{3,2},{4,5},{5,4},{6,7},{7,6},{8,9},{9,8},{10,11... | collective-permute-start | bytes 1769480 | tf_op jit(solution)/shard_map/weight_w/ppermute | solution.py:45
  50.9 12.7 %collective-permute-start.13 = (bf16[384,3072]{1,0:T(8,128)(2,1)S(1)}, bf16[384,3072]{1,0:T(8,128)(2,1)S(1)}, u32[]{:S(2)}, u32[]{:S(2)}) collective-permute-start(bf16[384,3072]{1,0:T(8,128)(2,1)S(1)} %copy-done), channel_id=1, source_target_pairs={{0,1},{1,0},{2,3},{3,2},{4,5},{5,4},{6,7},{7,6},{8,9},{9,8},{10,11... | collective-permute-start | bytes 7077896 | tf_op jit(solution)/shard_map/in_w/ppermute | solution.py:45
  51.0 12.6 %collective-permute-start.14 = (bf16[1536,768]{1,0:T(8,128)(2,1)S(1)}, bf16[1536,768]{1,0:T(8,128)(2,1)S(1)}, u32[]{:S(2)}, u32[]{:S(2)}) collective-permute-start(bf16[1536,768]{1,0:T(8,128)(2,1)S(1)} %copy-done.6), channel_id=1, source_target_pairs={{0,1},{1,0},{2,3},{3,2},{4,5},{5,4},{6,7},{7,6},{8,9},{9,8},{10,11... | collective-permute-start | bytes 7077896 | tf_op jit(solution)/shard_map/back_w/ppermute | solution.py:45
  74.8 15.4 %collective-permute-start.17 = (bf16[384,768]{1,0:T(8,128)(2,1)S(1)}, bf16[384,768]{1,0:T(8,128)(2,1)S(1)}, u32[]{:S(2)}, u32[]{:S(2)}) collective-permute-start(bf16[384,768]{1,0:T(8,128)(2,1)S(1)} %get-tuple-element.154), channel_id=1, source_target_pairs={{0,2},{2,0},{4,6},{6,4},{1,3},{3,1},{5,7},{7,5},{8,10},{10,8},{12,... | collective-permute-start | bytes 1769480 | tf_op jit(solution)/shard_map/ffn_z1/ppermute | solution.py:45
  93.0 12.1 %collective-permute-start.15 = (bf16[256,768]{1,0:T(8,128)(2,1)S(1)}, bf16[256,768]{1,0:T(8,128)(2,1)S(1)}, u32[]{:S(2)}, u32[]{:S(2)}) collective-permute-start(bf16[256,768]{1,0:T(8,128)(2,1)S(1)} %get-tuple-element.148), channel_id=1, source_target_pairs={{0,16},{8,24},{16,0},{24,8},{1,17},{9,25},{17,1},{25,9},{2,18},{10... | collective-permute-start | bytes 1179656 | tf_op jit(solution)/shard_map/outs_b2/ppermute | solution.py:45
  95.9 20.1 %collective-permute-start.18 = (bf16[192,768]{1,0:T(8,128)(2,1)S(1)}, bf16[192,768]{1,0:T(8,128)(2,1)S(1)}, u32[]{:S(2)}, u32[]{:S(2)}) collective-permute-start(bf16[192,768]{1,0:T(8,128)(2,1)S(1)} %get-tuple-element.156), channel_id=1, source_target_pairs={{0,4},{2,6},{4,0},{6,2},{1,5},{3,7},{5,1},{7,3},{8,12},{10,14},{12... | collective-permute-start | bytes 884744 | tf_op jit(solution)/shard_map/ffn_z2/ppermute | solution.py:45
  104.3 11.7 %collective-permute-start.24 = (bf16[96,768]{1,0:T(8,128)(2,1)S(1)}, bf16[96,768]{1,0:T(8,128)(2,1)S(1)}, u32[]{:S(2)}, u32[]{:S(2)}) collective-permute-start(bf16[96,768]{1,0:T(8,128)(2,1)S(1)} %get-tuple-element.172), channel_id=1, source_target_pairs={{0,16},{8,24},{16,0},{24,8},{1,17},{9,25},{17,1},{25,9},{2,18},{10... | collective-permute-start | bytes 442376 | tf_op jit(solution)/shard_map/wo_b2/ppermute | solution.py:45
  123.7 17.5 %collective-permute-start.31 = (bf16[192,768]{1,0:T(8,128)(2,1)S(1)}, bf16[192,768]{1,0:T(8,128)(2,1)S(1)}, u32[]{:S(2)}, u32[]{:S(2)}) collective-permute-start(bf16[192,768]{1,0:T(8,128)(2,1)S(1)} %get-tuple-element.182), channel_id=1, source_target_pairs={{0,4},{2,6},{4,0},{6,2},{1,5},{3,7},{5,1},{7,3},{8,12},{10,14},{12... | collective-permute-start | bytes 884744 | tf_op jit(solution)/shard_map/ffn_back_z2/ppermute | solution.py:45
  126.6 15.0 %collective-permute-start.34 = (bf16[24,768]{1,0:T(8,128)(2,1)S(1)}, bf16[24,768]{1,0:T(8,128)(2,1)S(1)}, u32[]{:S(2)}, u32[]{:S(2)}) collective-permute-start(bf16[24,768]{1,0:T(8,128)(2,1)S(1)} %get-tuple-element.215), channel_id=1, source_target_pairs={{0,4},{2,6},{4,0},{6,2},{1,5},{3,7},{5,1},{7,3},{8,12},{10,14},{12... | collective-permute-start | bytes 110600 | tf_op jit(solution)/shard_map/wo_z2/ppermute | solution.py:45
  129.6 11.7 %collective-permute-start.30 = (bf16[200,576]{1,0:T(8,128)(2,1)S(1)}, bf16[200,576]{1,0:T(8,128)(2,1)S(1)}, u32[]{:S(2)}, u32[]{:S(2)}) collective-permute-start(bf16[200,576]{1,0:T(8,128)(2,1)S(1)} %get-tuple-element.210), channel_id=1, source_target_pairs={{0,8},{8,0},{16,24},{24,16},{1,9},{9,1},{17,25},{25,17},{2,10},{10... | collective-permute-start | bytes 691208 | tf_op jit(solution)/shard_map/qkv_b1/ppermute | solution.py:45
  145.3 13.9 %collective-permute-start.36 = (bf16[192,768]{1,0:T(8,128)(2,1)S(1)}, bf16[192,768]{1,0:T(8,128)(2,1)S(1)}, u32[]{:S(2)}, u32[]{:S(2)}) collective-permute-start(bf16[192,768]{1,0:T(8,128)(2,1)S(1)} %pad_maximum_fusion.7.refs_0_), channel_id=1, source_target_pairs={{0,2},{2,0},{4,6},{6,4},{1,3},{3,1},{5,7},{7,5},{8,10},{10,8},{12,... | collective-permute-start | bytes 884744 | tf_op jit(solution)/shard_map/out_back_z1/ppermute | solution.py:45
  151.6 20.3 %collective-permute-start.41 = (bf16[384,768]{1,0:T(8,128)(2,1)S(1)}, bf16[384,768]{1,0:T(8,128)(2,1)S(1)}, u32[]{:S(2)}, u32[]{:S(2)}) collective-permute-start(bf16[384,768]{1,0:T(8,128)(2,1)S(1)} %pad_maximum_fusion.3), channel_id=1, source_target_pairs={{0,8},{8,0},{16,24},{24,16},{1,9},{9,1},{17,25},{25,17},{2,10},{10... | collective-permute-start | bytes 1769480 | tf_op jit(solution)/shard_map/out_near2_b1/ppermute | solution.py:45
  153.2 18.7 %collective-permute-start.40 = (bf16[384,768]{1,0:T(8,128)(2,1)S(1)}, bf16[384,768]{1,0:T(8,128)(2,1)S(1)}, u32[]{:S(2)}, u32[]{:S(2)}) collective-permute-start(bf16[384,768]{1,0:T(8,128)(2,1)S(1)} %pad_maximum_fusion.2), channel_id=1, source_target_pairs={{0,16},{8,24},{16,0},{24,8},{1,17},{9,25},{17,1},{25,9},{2,18},{10... | collective-permute-start | bytes 1769480 | tf_op jit(solution)/shard_map/in_near2_b2/ppermute | solution.py:45
  159.2 15.3 %collective-permute-start.45 = (bf16[192,768]{1,0:T(8,128)(2,1)S(1)}, bf16[192,768]{1,0:T(8,128)(2,1)S(1)}, u32[]{:S(2)}, u32[]{:S(2)}) collective-permute-start(bf16[192,768]{1,0:T(8,128)(2,1)S(1)} %collective-permute-done.35.refs_3_), channel_id=1, source_target_pairs={{0,16},{8,24},{16,0},{24,8},{1,17},{9,25},{17,1},{25,9},{2,18},{10... | collective-permute-start | bytes 884744 | tf_op jit(solution)/shard_map/in_far_b2/ppermute | solution.py:45
  170.4 23.2 %collective-permute-start.50 = (bf16[384,768]{1,0:T(8,128)(2,1)S(1)}, bf16[384,768]{1,0:T(8,128)(2,1)S(1)}, u32[]{:S(2)}, u32[]{:S(2)}) collective-permute-start(bf16[384,768]{1,0:T(8,128)(2,1)S(1)} %constant_dynamic-update-slice_fusion.4), channel_id=1, source_target_pairs={{0,16},{8,24},{16,0},{24,8},{1,17},{9,25},{17,1},{25,9},{2,18},{10... | collective-permute-start | bytes 1769480 | tf_op jit(solution)/shard_map/out_far2_b2/ppermute | solution.py:45
  174.6 19.1 %collective-permute-start.49 = (bf16[384,768]{1,0:T(8,128)(2,1)S(1)}, bf16[384,768]{1,0:T(8,128)(2,1)S(1)}, u32[]{:S(2)}, u32[]{:S(2)}) collective-permute-start(bf16[384,768]{1,0:T(8,128)(2,1)S(1)} %constant_dynamic-update-slice_fusion.2), channel_id=1, source_target_pairs={{0,8},{8,0},{16,24},{24,16},{1,9},{9,1},{17,25},{25,17},{2,10},{10... | collective-permute-start | bytes 1769480 | tf_op jit(solution)/shard_map/in_far2_b1/ppermute | solution.py:45
  176.1 17.4 %collective-permute-start.42 = (bf16[896,192]{1,0:T(8,128)(2,1)S(1)}, bf16[896,192]{1,0:T(8,128)(2,1)S(1)}, u32[]{:S(2)}, u32[]{:S(2)}) collective-permute-start(bf16[896,192]{1,0:T(8,128)(2,1)S(1)} %get-tuple-element.224), channel_id=1, source_target_pairs={{0,4},{2,6},{4,0},{6,2},{1,5},{3,7},{5,1},{7,3},{8,12},{10,14},{12... | collective-permute-start | bytes 1032200 | tf_op jit(solution)/shard_map/sends_z2/ppermute | solution.py:45
  193.8 16.5 %collective-permute-start.52 = (bf16[544,576]{1,0:T(8,128)(2,1)S(1)}, bf16[544,576]{1,0:T(8,128)(2,1)S(1)}, u32[]{:S(2)}, u32[]{:S(2)}) collective-permute-start(bf16[544,576]{1,0:T(8,128)(2,1)S(1)} %pad_maximum_fusion.1), channel_id=1, source_target_pairs={{0,8},{8,0},{16,24},{24,16},{1,9},{9,1},{17,25},{25,17},{2,10},{10... | collective-permute-start | bytes 1880072 | tf_op jit(solution)/shard_map/heads_far2_b1/ppermute | solution.py:45
  194.3 16.0 %collective-permute-start.51 = (bf16[544,576]{1,0:T(8,128)(2,1)S(1)}, bf16[544,576]{1,0:T(8,128)(2,1)S(1)}, u32[]{:S(2)}, u32[]{:S(2)}) collective-permute-start(bf16[544,576]{1,0:T(8,128)(2,1)S(1)} %pad_maximum_fusion), channel_id=1, source_target_pairs={{0,16},{8,24},{16,0},{24,8},{1,17},{9,25},{17,1},{25,9},{2,18},{10... | collective-permute-start | bytes 1880072 | tf_op jit(solution)/shard_map/heads_near2_b2/ppermute | solution.py:45
  (40 other events, 397.7 us)

commit v5 on v4

--- a/solution.py
+++ b/solution.py
@@ -759,8 +759,8 @@
 
 def ffn_back_kernel(idx, *refs):
     n2s, gs = refs[:4], refs[4:8]
-    act, gi, w2 = refs[8:11]
-    mine, theirs, keep, send, all_scr, scr = refs[11:]
+    act, gi = refs[8:10]
+    mine, theirs, all_scr, scr = refs[10:]
     here, wt = idx[1], idx[2]
     rows = n2s[0].shape[0]
     size = scr.shape[0] // 8
@@ -769,7 +769,7 @@
         for i, out in enumerate((mine, theirs)):
             for j, place in enumerate(NEAR_LAST):
                 at = pl.multiple_of(((wt ^ i) * 4 + (here ^ place)) * size, size)
-                to = (2 * j + p) * size
+                to = (4 * (j // 2) + 2 * p + j % 2) * size
                 out[to : to + size, :] = scr[pl.ds(at, size), :]
 
     for s in range(4):
@@ -780,8 +780,6 @@
         all_scr[s * rows : (s + 1) * rows, :] = gs[s][...]
     scr[...] = tn(act[...], all_scr[...]).astype(BF)
     spread(1)
-    for s, (out, to) in enumerate(((keep, 0), (keep, rows), (send, 0), (send, rows))):
-        out[to : to + rows, :] = nn(act[s * rows : (s + 1) * rows, :], w2[...]).astype(BF)
 
 
 def hidden_back_kernel(idx, *refs):
@@ -808,7 +806,8 @@
         outs[step][...] = nt(low, wo[pl.ds(at, cols), :]).astype(BF)
 
 
-def wo_back_kernel(idx, att, low, mine, theirs, scr):
+def wo_back_kernel(idx, att, low, act, w2, mine, theirs, keep, send, scr):
+    rows = low.shape[0]
     batch, here, wt = idx[0], idx[1], idx[2]
     size = att.shape[2]
     for c in range(4):
@@ -820,6 +819,8 @@
                 at = (((wt ^ i) * 4 + (here ^ place)) * 4 + (batch ^ far)) * size
                 to = (4 * q + p) * size
                 out[to : to + size, :] = scr[pl.ds(pl.multiple_of(at, 8), size), :].astype(BF)
+    for s, (out, to) in enumerate(((keep, 0), (keep, rows), (send, 0), (send, rows))):
+        out[to : to + rows, :] = nn(act[s * rows : (s + 1) * rows, :], w2[...]).astype(BF)
 
 
 def heads_back_kernel(heads, hsize, idx, *refs):
@@ -927,6 +928,10 @@
     )(*args)
 
 
+def add_kernel(left, right, out):
+    out[...] = (left[...].astype(F32) + right[...].astype(F32)).astype(BF)
+
+
 def row_sums(values):
     return lax.dot_general(
         jnp.ones((8, values.shape[1]), F32),
@@ -937,7 +942,14 @@
     )
 
 
-def ffn_piece_kernel(idx, w_in, ffn, ffn2, piece_ref, sum_ref, w_scr, sems):
+def add_swapped(out, own, got, half):
+    for i in range(2):
+        left = own[i * half : (i + 1) * half, :].astype(F32)
+        right = got[(1 - i) * half : (2 - i) * half, :].astype(F32)
+        out[i * half : (i + 1) * half, :] = (left + right).astype(BF)
+
+
+def ffn_piece_kernel(idx, w_in, own, got, a_ref, b_ref, sum_ref, w_scr, sems):
     batch, here = idx[0], idx[1]
     quarter, width = w_scr.shape
     block = width // 2
@@ -950,11 +962,21 @@
     ]
     for copy in copies:
         copy.start()
-    grad = ffn[...].astype(F32) + ffn2[...].astype(F32)
-    piece_ref[...] = grad.astype(BF)
+    add_swapped(a_ref, own.at[: 2 * quarter], got.at[: 2 * quarter], quarter)
+    add_swapped(b_ref, own.at[2 * quarter :], got.at[2 * quarter :], quarter)
     for copy in copies:
         copy.wait()
-    sum_ref[...] = row_sums(grad[:quarter] * w_scr[...].astype(F32))
+    sum_ref[...] = row_sums(a_ref[:quarter, :].astype(F32) * w_scr[...].astype(F32))
+
+
+def heads_pair_kernel(size, height, own, got, out):
+    rest = own.shape[0] - height
+    out[:height, :] = own[:height, :]
+    out[height:, :] = got[:height, :]
+    for at, left, right in ((size, size, height), (height + size, height, size)):
+        out[at : at + rest, :] = (
+            own[left : left + rest, :].astype(F32) + got[right : right + rest, :].astype(F32)
+        ).astype(BF)
 
 
 def heads_piece_kernel(qkv, qkv2, wo, wo2, wrow, sum_in, piece_ref):
@@ -964,14 +986,14 @@
     heads = qkv[...].astype(F32) + qkv2[...].astype(F32)
     piece_ref[:quarter, :] = heads[:quarter].astype(BF)
     sum_heads = row_sums(heads[:quarter] * wrow[...].astype(F32))
-    out = wo[...].astype(F32) + wo2[...].astype(F32)
-    piece_ref[quarter : quarter + size, :] = out[:, :wide].astype(BF)
     third = size // 3
     cols = width - wide
-    for o in range(3):
-        piece_ref[quarter + size : quarter + size + third, o * cols : (o + 1) * cols] = out[
-            o * third : (o + 1) * third, wide:
-        ].astype(BF)
+    for part, at in ((wo, quarter), (wo2, quarter + size + third + LINE)):
+        piece_ref[at : at + size, :] = part[:, :wide]
+        for o in range(3):
+            piece_ref[at + size : at + size + third, o * cols : (o + 1) * cols] = part[
+                o * third : (o + 1) * third, wide:
+            ]
     row = lax.broadcasted_iota(jnp.int32, (LINE, quarter), 0)
     sums = jnp.where(row == LINE - 2, sum_heads, jnp.where(row == LINE - 1, sum_in[...], 0.0))
     at = quarter + size + third
@@ -979,7 +1001,7 @@
     pad = jnp.zeros((LINE, LANES), F32)
     sums = jnp.concatenate([sums, jnp.zeros((LINE, LANES - quarter), F32)], axis=1)
     line = line + jnp.concatenate([pad, sums, jnp.zeros((LINE, wide - 2 * LANES), F32)], axis=1)
-    piece_ref[at:, :] = line.astype(BF)
+    piece_ref[at : at + LINE, :] = line.astype(BF)
 
 
 def ctx_pieces(refs, at, order):
@@ -1258,17 +1280,17 @@
         far=(w_in, w_in2, w_back, w_back2),
     )
     norms = norms[:1] + [over_batch(norms[s], s, "norm") for s in range(1, 4)]
-    ffn, ffn_sent, outs, outs_sent = call(
+    ffn, ffn_sent = call(
         ffn_back_kernel,
         "ffn_back",
         index,
-        [*n2s, *gs, act, gi, w_second],
-        [square, square] + [shape((2 * rows, width), BF)] * 2,
+        [*n2s, *gs, act, gi],
+        [square, square],
         [pltpu.VMEM((length, width), BF), pltpu.VMEM((width, width), BF)],
     )
     ffn, ffn_sent = halving("ffn_wt", [(ffn, over_wt(ffn_sent, "ffn"), 0)])
     ffn_got = over_ctx(ffn_sent, 1, "ffn")
-    norms = after(norms, (ffn, ffn_got))
+    norms = after(norms, (ffn, ffn_sent))
     grad_hidden, low, *gms = call(
         hidden_back_kernel,
         "hidden_back",
@@ -1276,37 +1298,29 @@
         [*norms, hidden, small, small2, g, wo],
         [shape((rows, width), F32), shape((rows, width), BF)] + [shape((rows, cols), BF)] * 4,
     )
-    ffn, ffn_sent = halving("ffn_near", [(ffn, ffn_got, 0)])
-    outs_got = over_batch(outs_sent, 2, "outs")
-    wo_sum, wo_sent = call(
+    ffn = pl.pallas_call(
+        add_kernel,
+        out_shape=shape((part, width), BF),
+        in_specs=vmem(2),
+        out_specs=vmem(1)[0],
+        compiler_params=params(16),
+        name="ffn_near",
+    )(ffn, ffn_got)
+    gms = list(gms[:1]) + [over_ctx(gms[s], s, "gm") for s in range(1, 4)]
+    (ffn_sent, low) = after((ffn, low), gms[1:])
+    ffn_got = over_ctx(ffn_sent, 2, "ffn")
+    wo_sum, wo_sent, outs, outs_sent = call(
         wo_back_kernel,
         "wo_back",
         index,
-        [attended, low],
-        [shape((part, width), BF)] * 2,
+        [attended, low, act, w_second],
+        [shape((part, width), BF)] * 2 + [shape((2 * rows, width), BF)] * 2,
         [pltpu.VMEM((width, width), F32)],
     )
-    gms = after(gms, (ffn, ffn_sent, outs_got))
-    ffn_got = over_ctx(ffn_sent, 2, "ffn")
+    outs_got = over_batch(outs_sent, 2, "outs")
     wo_sum, wo_sent = halving("wo_wt", [(wo_sum, over_wt(wo_sent, "wo"), 0)])
     wo_sum, wo_sent = halving("wo_near", [(wo_sum, over_batch(wo_sent, 1, "wo"), 0)])
-    wo_got = over_batch(wo_sent, 2, "wo")
-    gms = list(gms[:1]) + [over_ctx(gms[s], s, "gm") for s in range(1, 4)]
-    (ffn_got, wo_got, *gms) = after((ffn_got, wo_got, *gms), ())
-    ffn, sum_in = call(
-        ffn_piece_kernel,
-        "ffn_piece",
-        index,
-        [ffn, ffn_got],
-        [shape((2 * quarter, width), BF), shape((8, quarter), F32)],
-        [pltpu.VMEM((quarter, width), BF), pltpu.SemaphoreType.DMA((2,))],
-        far=(w_in,),
-    )
-    wo_sum, wo_sent = halving("wo_far", [(wo_sum, wo_got, 0)])
-    gms = after(gms, (ffn, wo_sum, wo_sent))
-    outs, outs_sent = halving("outs_far", [(outs, outs_got, 0)])
-    (outs_sent,) = after((outs_sent,), (ffn, wo_sum))
-    ffn_far = over_ctx(ffn, 2, "ffn_back")
+
     high = 3 * rows + MEM_END
     (qkv, qkv_sent, own_block, near_blocks, far_block) = call(
         functools.partial(heads_back_kernel, heads, hsize),
@@ -1323,22 +1337,29 @@
             pltpu.VMEM((width, wide), BF),
         ],
     )
+    outs, outs_sent = halving("outs_far", [(outs, outs_got, 0)])
+    (outs_sent, wo_sent) = after((outs_sent, wo_sent), (outs, wo_sum))
+    wo_sum, wo_sent = halving("wo_far", [(wo_sum, over_batch(wo_sent, 2, "wo"), 0)])
     wo_sum, wo_sent = halving("wo_last", [(wo_sum, over_ctx(wo_sent, 1, "wo"), 0)])
-    wo_got = over_ctx(wo_sent, 2, "wo")
     outs_got = over_batch(outs_sent, 1, "outs")
     qkv, qkv_sent = halving("qkv_wt", [(qkv, over_wt(qkv_sent, "qkv"), LINE)])
-    qkv_got = over_batch(qkv_sent, 1, "qkv")
-    (qkv_got,) = after((qkv_got,), (ffn_far, outs_got))
-    qkv, qkv_sent = halving("qkv_near", [(qkv, qkv_got, LINE)])
+    qkv, qkv_sent = halving("qkv_near", [(qkv, over_batch(qkv_sent, 1, "qkv"), LINE)])
     qkv_got = over_batch(qkv_sent, 2, "qkv")
-    (ffn_far, wo_got) = after((ffn_far, wo_got), (qkv_sent,))
+    (ffn_got,) = after((ffn_got,), (qkv_got, outs_got, wo_sum, wo_sent))
+    a1, b1, sum_in = call(
+        ffn_piece_kernel,
+        "ffn_piece",
+        index,
+        [ffn, ffn_got],
+        [shape((2 * quarter, width), BF)] * 2 + [shape((8, quarter), F32)],
+        [pltpu.VMEM((quarter, width), BF), pltpu.SemaphoreType.DMA((2,))],
+        far=(w_in,),
+    )
 
     def pile(one, two):
         return jnp.concatenate([one, two])
 
     result = (hidden + outs.astype(F32) + outs_got.astype(F32)).astype(BF)
-    a1 = pile(ffn[:quarter], ffn_far[:quarter])
-    b1 = pile(ffn[quarter:], ffn_far[quarter:])
     a2, b2 = over_batch(a1, 1, "in_near"), over_batch(b1, 2, "out_near")
     c1, d1 = over_ctx(a1, 1, "in_back"), over_ctx(b1, 1, "out_back")
     pile_a, pile_b = pile(a1, a2), pile(b1, b2)
@@ -1348,12 +1369,12 @@
     height = quarter + quarter // 4 + quarter // 12 + LINE
     piece = pl.pallas_call(
         heads_piece_kernel,
-        out_shape=shape((height, wide), BF),
+        out_shape=shape((2 * height - quarter - LINE, wide), BF),
         in_specs=vmem(6),
         out_specs=vmem(1)[0],
         compiler_params=params(32),
         name="heads_piece",
-    )(qkv, qkv_got, wo_sum, wo_got, wrow, sum_in)
+    )(qkv, qkv_got, wo_sum, wo_sent, wrow, sum_in)
 
     (piece,) = after((piece,), (c1, d1))
     heads_far = over_ctx(piece, 2, "heads_back")
@@ -1364,7 +1385,14 @@
     near_got = over_ctx(near_blocks, 2, "sends")
     far_pile = pile(far_block, near_got[high:])
     far_got = over_ctx(far_pile, 1, "sends")
-    e1 = pile(piece, heads_far)
+    e1 = pl.pallas_call(
+        functools.partial(heads_pair_kernel, quarter, height),
+        out_shape=shape((2 * height, wide), BF),
+        in_specs=vmem(2),
+        out_specs=vmem(1)[0],
+        compiler_params=params(16),
+        name="heads_pair",
+    )(piece, heads_far)
     f1 = over_ctx(e1, 1, "heads_back")
     (e1, f1) = after((e1, f1), (pile_c, pile_d))
     e2, f2 = over_batch(e1, 1, "heads_near"), over_batch(f1, 2, "heads_far")

time: 215 us -> 209 us (0.972)
  local copies, waits for them, and re-layouts: 7.54 us -> 3.9 us
  starting transfers between devices: 52.2 us -> 50 us
    unnamed x29 -> x28, local copies, waits for them, and re-layouts: 5.96 us -> 2.34 us
    ppermute x53 -> x51, starting transfers between devices: 52.2 us -> 50 us  [flip(): return lax.ppermute(value, axis, [(i, i ^ step) for i in range(size)])]
    ppermute x53 -> x51, waiting for transfers between devices: 91.6 us -> 92.2 us  [flip(): return lax.ppermute(value, axis, [(i, i ^ step) for i in range(size)])]
  transfers between devices with their start and end apart: 53 -> 51, of which waited for: 27 -> 24; matrix products, arithmetic and copies ran while one was open for 3% -> 3% of each run, Pallas kernels for 5% -> 8%
where the time goes in v5:
time: 209 us; the launch traced here: 208 us
  waiting for transfers between devices  92.2 us (44%)
  starting transfers between devices  50 us (24%)
  Pallas kernels  38.2 us (18%)
  blocking collectives  20.1 us (10%)
  local copies, waits for them, and re-layouts  3.9 us (2%)
  other arithmetic  2.76 us (1%)
    ppermute x51, waiting for transfers between devices, flip(): return lax.ppermute(value, axis, [(i, i ^ step) for i in range(size)])  92.2 us
    ppermute x51, starting transfers between devices, flip(): return lax.ppermute(value, axis, [(i, i ^ step) for i in range(size)])  50 us
    pallas_call x9, Pallas kernels, call(): pl.pallas_call(kernel, out_shape=out, in_specs=[smem()] + stay + vmem(len...  27.3 us
    all_gather x1, blocking collectives, paired(): x_all = lax.all_gather(x, 'ctx', axis=0, tiled=True)  20.1 us
    pallas_call x2, Pallas kernels, pieces_out(): pl.pallas_call(kernel, out_shape=shape(dims, F32), in_specs=[smem()] + vm...  5.87 us
  transfers between devices with their start and end apart: 51, of which 24 were waited for; matrix products, arithmetic and copies ran while one was open for 3% of the time, Pallas kernels for 8%

profile of v5, /device:TPU:0, one launch (start us, length us, event | category | flops | bytes accessed | tf_op | source)
XLA Modules:
  0.0 208.3 jit_solution(7092683392023003085)
XLA Ops:
  3.9 2.9 %collective-permute-start.7 = (bf16[128,768]{1,0:T(8,128)(2,1)}, bf16[128,768]{1,0:T(8,128)(2,1)S(1)}, u32[]{:S(2)}, u32[]{:S(2)}) collective-permute-start(bf16[128,768]{1,0:T(8,128)(2,1)} %bitcast.17), channel_id=1, source_target_pairs={{0,8},{8,0},{16,24},{24,16},{1,9},{9,1},{17,25},{25,17},{2,10},{10... | collective-permute-start | bytes 589832 | tf_op jit(solution)/shard_map/g_b1/ppermute | solution.py:45
  6.8 20.1 %all-gather = bf16[1,512,768]{2,1,0:T(8,128)(2,1)S(1)} all-gather(bf16[1,128,768]{2,1,0:T(8,128)(2,1)} %param.14), channel_id=2, replica_groups=mesh['batch'=4,'ctx'=4,'wt'=2] {'ctx'}, dimensions={1}, use_global_device_ids=true | all-gather | bytes 983040 | tf_op jit(solution)/shard_map/all_gather | solution.py:1221
  29.0 5.4 %attend.1 = (bf16[512,768]{1,0:T(8,128)(2,1)S(1)}, bf16[512,192]{1,0:T(8,128)(2,1)S(1)}, bf16[512,192]{1,0:T(8,128)(2,1)S(1)}, bf16[512,192]{1,0:T(8,128)(2,1)S(...) custom-call(s32[3]{0:T(128)S(1)} %pad_add_fusion.idx, ...), custom_call_target="tpu_custom_call" | custom-call | tf_op jit(solution)/shard_map/attend/pallas_call | solution.py:553
  41.3 3.4 %collective-permute-done.5.refs_4_ = bf16[128,192]{1,0:T(8,128)(2,1)S(1)} collective-permute-done((bf16[128,192]{1,0:T(8,128)(2,1)S(1)}, bf16[128,192]{1,0:T(8,128)(2,1)S(1)}, u32[]{:S(2)}, u32[]{:S(2)}) %collective-permute-start.5) | collective-permute-done | bytes 49184 | tf_op jit(solution)/shard_map/mixed_z2/ppermute | solution.py:45
  51.5 5.2 %collective-permute-done.12.refs_7_.refs_3_ = bf16[128,768]{1,0:T(8,128)(2,1)S(1)} collective-permute-done((bf16[128,768]{1,0:T(8,128)(2,1)S(1)}, bf16[128,768]{1,0:T(8,128)(2,1)S(1)}, u32[]{:S(2)}, u32[]{:S(2)}) %collective-permute-start.12) | collective-permute-done | bytes 196640 | tf_op jit(solution)/shard_map/n2_b3/ppermute | solution.py:45
  56.6 3.3 %collective-permute-done.11.refs_6_.refs_2_ = bf16[128,768]{1,0:T(8,128)(2,1)S(1)} collective-permute-done((bf16[128,768]{1,0:T(8,128)(2,1)S(1)}, bf16[128,768]{1,0:T(8,128)(2,1)S(1)}, u32[]{:S(2)}, u32[]{:S(2)}) %collective-permute-start.11) | collective-permute-done | bytes 196640 | tf_op jit(solution)/shard_map/n2_b2/ppermute | solution.py:45
  60.1 5.4 %ffn.1 = (bf16[128,768]{1,0:T(8,128)(2,1)S(1)}, bf16[128,768]{1,0:T(8,128)(2,1)S(1)}, bf16[128,768]{1,0:T(8,128)(2,1)S(1)}, bf16[128,768]{1,0:T(8,128)(2,1)S(1)}...) custom-call(s32[3]{0:T(128)S(1)} %pad_add_fusion.idx, ...), custom_call_target="tpu_custom_call" | custom-call | tf_op jit(solution)/shard_map/ffn/pallas_call | solution.py:553
  74.4 4.3 %collective-permute-done.17.refs_1_ = bf16[128,768]{1,0:T(8,128)(2,1)S(1)} collective-permute-done((bf16[128,768]{1,0:T(8,128)(2,1)S(1)}, bf16[128,768]{1,0:T(8,128)(2,1)S(1)}, u32[]{:S(2)}, u32[]{:S(2)}) %collective-permute-start.17) | collective-permute-done | bytes 196640 | tf_op jit(solution)/shard_map/norm_b1/ppermute | solution.py:45
  78.9 3.4 %collective-permute-done.19.refs_3_ = bf16[128,768]{1,0:T(8,128)(2,1)S(1)} collective-permute-done((bf16[128,768]{1,0:T(8,128)(2,1)S(1)}, bf16[128,768]{1,0:T(8,128)(2,1)S(1)}, u32[]{:S(2)}, u32[]{:S(2)}) %collective-permute-start.19) | collective-permute-done | bytes 196640 | tf_op jit(solution)/shard_map/norm_b3/ppermute | solution.py:45
  88.2 4.2 %collective-permute-done.21.refs_2_ = bf16[128,192]{1,0:T(8,128)(2,1)S(1)} collective-permute-done((bf16[128,192]{1,0:T(8,128)(2,1)S(1)}, bf16[128,192]{1,0:T(8,128)(2,1)S(1)}, u32[]{:S(2)}, u32[]{:S(2)}) %collective-permute-start.21) | collective-permute-done | bytes 49184 | tf_op jit(solution)/shard_map/gm_z2/ppermute | solution.py:45
  94.3 4.4 %attend_back.1 = (bf16[392,576]{1,0:T(8,128)(2,1)S(1)}, bf16[392,576]{1,0:T(8,128)(2,1)S(1)}, bf16[448,192]{1,0:T(8,128)(2,1)S(1)}, bf16[896,192]{1,0:T(8,128)(2,1)S(1)}, bf16[448,192]{1,0:T(8,128)(2,1)S(1)}) custom-call(s32[3]{0:T(128)S(1)} %pad_add_fusion.idx, bf16[128,192]{1,0:T(8,128)(2,1)S(1)} %get-tuple-element.163.refs_0_, ...), custom_call_target="tpu_custom_call" | custom-call | tf_op jit(solution)/shard_map/attend_back/pallas_call | solution.py:553
  104.6 5.7 %collective-permute-done.23.refs_1_ = bf16[256,768]{1,0:T(8,128)(2,1)S(1)} collective-permute-done((bf16[256,768]{1,0:T(8,128)(2,1)S(1)}, bf16[256,768]{1,0:T(8,128)(2,1)S(1)}, u32[]{:S(2)}, u32[]{:S(2)}) %collective-permute-start.23) | collective-permute-done | bytes 393248 | tf_op jit(solution)/shard_map/outs_b2/ppermute | solution.py:45
  114.5 3.3 %collective-permute-done.28.refs_1_ = bf16[200,576]{1,0:T(8,128)(2,1)S(1)} collective-permute-done((bf16[200,576]{1,0:T(8,128)(2,1)S(1)}, bf16[200,576]{1,0:T(8,128)(2,1)S(1)}, u32[]{:S(2)}, u32[]{:S(2)}) %collective-permute-start.28) | collective-permute-done | bytes 230432 | tf_op jit(solution)/shard_map/qkv_b1/ppermute | solution.py:45
  119.5 11.2 %collective-permute-done.31.refs_1_ = bf16[48,768]{1,0:T(8,128)(2,1)S(1)} collective-permute-done((bf16[48,768]{1,0:T(8,128)(2,1)S(1)}, bf16[48,768]{1,0:T(8,128)(2,1)S(1)}, u32[]{:S(2)}, u32[]{:S(2)}) %collective-permute-start.31) | collective-permute-done | bytes 73760 | tf_op jit(solution)/shard_map/wo_z1/ppermute | solution.py:45
  136.4 4.8 %collective-permute-done.36.refs_1_ = bf16[192,768]{1,0:T(8,128)(2,1)S(1)} collective-permute-done((bf16[192,768]{1,0:T(8,128)(2,1)S(1)}, bf16[192,768]{1,0:T(8,128)(2,1)S(1)}, u32[]{:S(2)}, u32[]{:S(2)}) %collective-permute-start.36) | collective-permute-done | bytes 294944 | tf_op jit(solution)/shard_map/out_near_b2/ppermute | solution.py:45
  144.2 4.7 %collective-permute-done.34.refs_3_ = bf16[192,768]{1,0:T(8,128)(2,1)S(1)} collective-permute-done((bf16[192,768]{1,0:T(8,128)(2,1)S(1)}, bf16[192,768]{1,0:T(8,128)(2,1)S(1)}, u32[]{:S(2)}, u32[]{:S(2)}) %collective-permute-start.34) | collective-permute-done | bytes 294944 | tf_op jit(solution)/shard_map/out_back_z1/ppermute | solution.py:45
  152.1 9.8 %collective-permute-done.44.refs_4_ = bf16[192,768]{1,0:T(8,128)(2,1)S(1)} collective-permute-done((bf16[192,768]{1,0:T(8,128)(2,1)S(1)}, bf16[192,768]{1,0:T(8,128)(2,1)S(1)}, u32[]{:S(2)}, u32[]{:S(2)}) %collective-permute-start.44) | collective-permute-done | bytes 294944 | tf_op jit(solution)/shard_map/out_far_b1/ppermute | solution.py:45
  166.8 11.3 %collective-permute-done.42.refs_3_ = bf16[272,576]{1,0:T(8,128)(2,1)S(1)} collective-permute-done((bf16[272,576]{1,0:T(8,128)(2,1)S(1)}, bf16[272,576]{1,0:T(8,128)(2,1)S(1)}, u32[]{:S(2)}, u32[]{:S(2)}) %collective-permute-start.42) | collective-permute-done | bytes 313376 | tf_op jit(solution)/shard_map/heads_back_z1/ppermute | solution.py:45
  180.3 5.4 %collective-permute-done.40.refs_7_ = bf16[896,192]{1,0:T(8,128)(2,1)S(1)} collective-permute-done((bf16[896,192]{1,0:T(8,128)(2,1)S(1)}, bf16[896,192]{1,0:T(8,128)(2,1)S(1)}, u32[]{:S(2)}, u32[]{:S(2)}) %collective-permute-start.40) | collective-permute-done | bytes 344096 | tf_op jit(solution)/shard_map/sends_z2/ppermute | solution.py:45
  190.0 2.9 %rows_out.1 = f32[1536,768]{1,0:T(8,128)} custom-call(s32[3]{0:T(128)S(1)} %pad_add_fusion.idx, bf16[192,768]{1,0:T(8,128)(2,1)S(1)} %get-tuple-element.191.refs_0_, bf16[192,768]{1,0:T(8,128)(2,1)S(1)} %collective-permute-done.36.refs_1_, bf16[384,768]{1,0:T(8,128)(2,1)S(1)} %collective-permute-done.39.refs_2_, ...), custom_call_target="tpu_custom_call" | custom-call | tf_op jit(solution)/shard_map/rows_out/pallas_call | solution.py:1067
  192.9 3.0 %cols_out.1 = f32[384,3072]{1,0:T(8,128)} custom-call(s32[3]{0:T(128)S(1)} %pad_add_fusion.idx, bf16[192,768]{1,0:T(8,128)(2,1)S(1)} %get-tuple-element.190.refs_0_, bf16[192,768]{1,0:T(8,128)(2,1)S(1)} %collective-permute-done.35.refs_1_, bf16[384,768]{1,0:T(8,128)(2,1)S(1)} %collective-permute-done.38.refs_2_, ...), custom_call_target="tpu_custom_call" | custom-call | tf_op jit(solution)/shard_map/cols_out/pallas_call | solution.py:1067
  195.9 2.9 %collective-permute-done.41.refs_8_ = bf16[896,192]{1,0:T(8,128)(2,1)S(1)} collective-permute-done((bf16[896,192]{1,0:T(8,128)(2,1)S(1)}, bf16[896,192]{1,0:T(8,128)(2,1)S(1)}, u32[]{:S(2)}, u32[]{:S(2)}) %collective-permute-start.41) | collective-permute-done | bytes 344096 | tf_op jit(solution)/shard_map/sends_z1/ppermute | solution.py:45
  198.8 4.4 %input_back.1 = (bf16[128,768]{1,0:T(8,128)(2,1)}, f32[20,768]{1,0:T(8,128)S(1)}, f32[20,768]{1,0:T(8,128)S(1)}) custom-call(s32[3]{0:T(128)S(1)} %pad_add_fusion.idx, bf16[384,768]{1,0:T(8,128)(2,1)S(1)} %copy-done.2, bf16[384,768]{1,0:T(8,128)(2,1)S(1)} %copy-done.3, bf16[384,768]{1,0:T(8,128)(2,1)S(1)} %copy-done.4, ...), custom_call_target="tpu_custom_call" | custom-call | tf_op jit(solution)/shard_map/input_back/pallas_call | solution.py:553
  204.6 3.6 %heads_out.1 = (f32[384,768]{1,0:T(8,128)}, f32[384,768]{1,0:T(8,128)}, f32[384,768]{1,0:T(8,128)}, f32[4,4,24,768]{3,2,1,0:T(8,128)}, f32[384]{0:T(512)}, /*index=5*/f32[384]{0:T(512)}, f32[16,12]{1,0:T(8,128)}) custom-call(s32[3]{0:T(128)S(1)} %pad_add_fusion.idx, bf16[272,576]{1,0:T(8,128)(2,1)S(1)} %heads_pair.1.refs_0_, ...), custom_call_target="tpu_custom_call" | custom-call | tf_op jit(solution)/shard_map/heads_out/pallas_call | solution.py:1135
  (147 shorter events, 72.1 us)
Async XLA Ops:
  0.7 28.2 %collective-permute-start = (bf16[384,768]{1,0:T(8,128)(2,1)}, bf16[384,768]{1,0:T(8,128)(2,1)S(1)}, u32[]{:S(2)}, u32[]{:S(2)}) collective-permute-start(bf16[384,768]{1,0:T(8,128)(2,1)} %refs_0_.7), channel_id=1, source_target_pairs={{0,1},{1,0},{2,3},{3,2},{4,5},{5,4},{6,7},{7,6},{8,9},{9,8},{10,11... | collective-permute-start | bytes 1769480 | tf_op jit(solution)/shard_map/weight_w/ppermute | solution.py:45
  1.2 27.7 %collective-permute-start.1 = (bf16[384,768]{1,0:T(8,128)(2,1)}, bf16[384,768]{1,0:T(8,128)(2,1)}, u32[]{:S(2)}, u32[]{:S(2)}) collective-permute-start(bf16[384,768]{1,0:T(8,128)(2,1)} %refs_1_.3), channel_id=1, source_target_pairs={{0,1},{1,0},{2,3},{3,2},{4,5},{5,4},{6,7},{7,6},{8,9},{9,8},{10,11... | collective-permute-start | bytes 1769480 | tf_op jit(solution)/shard_map/weight_w/ppermute | solution.py:45
  1.3 27.6 %collective-permute-start.2 = (bf16[384,768]{1,0:T(8,128)(2,1)}, bf16[384,768]{1,0:T(8,128)(2,1)}, u32[]{:S(2)}, u32[]{:S(2)}) collective-permute-start(bf16[384,768]{1,0:T(8,128)(2,1)} %refs_2_.5), channel_id=1, source_target_pairs={{0,1},{1,0},{2,3},{3,2},{4,5},{5,4},{6,7},{7,6},{8,9},{9,8},{10,11... | collective-permute-start | bytes 1769480 | tf_op jit(solution)/shard_map/weight_w/ppermute | solution.py:45
  3.8 25.1 %collective-permute-start.3 = (bf16[24,384]{1,0:T(8,128)(2,1)S(1)}, bf16[24,384]{1,0:T(8,128)(2,1)S(1)}, u32[]{:S(2)}, u32[]{:S(2)}) collective-permute-start(bf16[24,384]{1,0:T(8,128)(2,1)S(1)} %fusion.2.refs_6_.refs_7_.refs_5_.refs_10_), channel_id=1, source_target_pairs={{0,1},{1,0},{2,3},{3,2},{4,5},{5,4},{6,7},{7,6},{8,9},{9,8},{10,11... | collective-permute-start | bytes 55304 | tf_op jit(solution)/shard_map/small_w/ppermute | solution.py:45
  3.9 24.0 %collective-permute-start.7 = (bf16[128,768]{1,0:T(8,128)(2,1)}, bf16[128,768]{1,0:T(8,128)(2,1)S(1)}, u32[]{:S(2)}, u32[]{:S(2)}) collective-permute-start(bf16[128,768]{1,0:T(8,128)(2,1)} %bitcast.17), channel_id=1, source_target_pairs={{0,8},{8,0},{16,24},{24,16},{1,9},{9,1},{17,25},{25,17},{2,10},{10... | collective-permute-start | bytes 589832 | tf_op jit(solution)/shard_map/g_b1/ppermute | solution.py:45
  47.4 12.7 %collective-permute-start.13 = (bf16[384,3072]{1,0:T(8,128)(2,1)S(1)}, bf16[384,3072]{1,0:T(8,128)(2,1)S(1)}, u32[]{:S(2)}, u32[]{:S(2)}) collective-permute-start(bf16[384,3072]{1,0:T(8,128)(2,1)S(1)} %copy-done), channel_id=1, source_target_pairs={{0,1},{1,0},{2,3},{3,2},{4,5},{5,4},{6,7},{7,6},{8,9},{9,8},{10,11... | collective-permute-start | bytes 7077896 | tf_op jit(solution)/shard_map/in_w/ppermute | solution.py:45
  47.5 12.6 %collective-permute-start.14 = (bf16[1536,768]{1,0:T(8,128)(2,1)S(1)}, bf16[1536,768]{1,0:T(8,128)(2,1)S(1)}, u32[]{:S(2)}, u32[]{:S(2)}) collective-permute-start(bf16[1536,768]{1,0:T(8,128)(2,1)S(1)} %copy-done.5), channel_id=1, source_target_pairs={{0,1},{1,0},{2,3},{3,2},{4,5},{5,4},{6,7},{7,6},{8,9},{9,8},{10,11... | collective-permute-start | bytes 7077896 | tf_op jit(solution)/shard_map/back_w/ppermute | solution.py:45
  70.8 17.3 %collective-permute-start.16 = (bf16[384,768]{1,0:T(8,128)(2,1)S(1)}, bf16[384,768]{1,0:T(8,128)(2,1)S(1)}, u32[]{:S(2)}, u32[]{:S(2)}) collective-permute-start(bf16[384,768]{1,0:T(8,128)(2,1)S(1)} %get-tuple-element.136), channel_id=1, source_target_pairs={{0,2},{2,0},{4,6},{6,4},{1,3},{3,1},{5,7},{7,5},{8,10},{10,8},{12,... | collective-permute-start | bytes 1769480 | tf_op jit(solution)/shard_map/ffn_z1/ppermute | solution.py:45
  100.6 30.2 %collective-permute-start.32 = (bf16[384,768]{1,0:T(8,128)(2,1)S(1)}, bf16[384,768]{1,0:T(8,128)(2,1)S(1)}, u32[]{:S(2)}, u32[]{:S(2)}) collective-permute-start(bf16[384,768]{1,0:T(8,128)(2,1)S(1)} %ffn_near.1.own), channel_id=1, source_target_pairs={{0,4},{2,6},{4,0},{6,2},{1,5},{3,7},{5,1},{7,3},{8,12},{10,14},{12... | collective-permute-start | bytes 1769480 | tf_op jit(solution)/shard_map/ffn_z2/ppermute | solution.py:45
  103.2 14.6 %collective-permute-start.28 = (bf16[200,576]{1,0:T(8,128)(2,1)S(1)}, bf16[200,576]{1,0:T(8,128)(2,1)S(1)}, u32[]{:S(2)}, u32[]{:S(2)}) collective-permute-start(bf16[200,576]{1,0:T(8,128)(2,1)S(1)} %get-tuple-element.178), channel_id=1, source_target_pairs={{0,8},{8,0},{16,24},{24,16},{1,9},{9,1},{17,25},{25,17},{2,10},{10... | collective-permute-start | bytes 691208 | tf_op jit(solution)/shard_map/qkv_b1/ppermute | solution.py:45
  113.1 17.7 %collective-permute-start.26 = (bf16[128,768]{1,0:T(8,128)(2,1)S(1)}, bf16[128,768]{1,0:T(8,128)(2,1)S(1)}, u32[]{:S(2)}, u32[]{:S(2)}) collective-permute-start(bf16[128,768]{1,0:T(8,128)(2,1)S(1)} %get-tuple-element.162), channel_id=1, source_target_pairs={{0,8},{8,0},{16,24},{24,16},{1,9},{9,1},{17,25},{25,17},{2,10},{10... | collective-permute-start | bytes 589832 | tf_op jit(solution)/shard_map/outs_b1/ppermute | solution.py:45
  117.9 12.9 %collective-permute-start.29 = (bf16[104,576]{1,0:T(8,128)(2,1)S(1)}, bf16[104,576]{1,0:T(8,128)(2,1)S(1)}, u32[]{:S(2)}, u32[]{:S(2)}) collective-permute-start(bf16[104,576]{1,0:T(8,128)(2,1)S(1)} %get-tuple-element.180), channel_id=1, source_target_pairs={{0,16},{8,24},{16,0},{24,8},{1,17},{9,25},{17,1},{25,9},{2,18},{10... | collective-permute-start | bytes 359432 | tf_op jit(solution)/shard_map/qkv_b2/ppermute | solution.py:45
  118.6 12.1 %collective-permute-start.31 = (bf16[48,768]{1,0:T(8,128)(2,1)S(1)}, bf16[48,768]{1,0:T(8,128)(2,1)S(1)}, u32[]{:S(2)}, u32[]{:S(2)}) collective-permute-start(bf16[48,768]{1,0:T(8,128)(2,1)S(1)} %get-tuple-element.183), channel_id=1, source_target_pairs={{0,2},{2,0},{4,6},{6,4},{1,3},{3,1},{5,7},{7,5},{8,10},{10,8},{12,... | collective-permute-start | bytes 221192 | tf_op jit(solution)/shard_map/wo_z1/ppermute | solution.py:45
  134.3 14.7 %collective-permute-start.34 = (bf16[192,768]{1,0:T(8,128)(2,1)S(1)}, bf16[192,768]{1,0:T(8,128)(2,1)S(1)}, u32[]{:S(2)}, u32[]{:S(2)}) collective-permute-start(bf16[192,768]{1,0:T(8,128)(2,1)S(1)} %get-tuple-element.191.refs_0_), channel_id=1, source_target_pairs={{0,2},{2,0},{4,6},{6,4},{1,3},{3,1},{5,7},{7,5},{8,10},{10,8},{12,... | collective-permute-start | bytes 884744 | tf_op jit(solution)/shard_map/out_back_z1/ppermute | solution.py:45
  141.1 21.5 %collective-permute-start.39 = (bf16[384,768]{1,0:T(8,128)(2,1)S(1)}, bf16[384,768]{1,0:T(8,128)(2,1)S(1)}, u32[]{:S(2)}, u32[]{:S(2)}) collective-permute-start(bf16[384,768]{1,0:T(8,128)(2,1)S(1)} %constant_dynamic-update-slice_fusion.2), channel_id=1, source_target_pairs={{0,8},{8,0},{16,24},{24,16},{1,9},{9,1},{17,25},{25,17},{2,10},{10... | collective-permute-start | bytes 1769480 | tf_op jit(solution)/shard_map/out_near2_b1/ppermute | solution.py:45
  142.0 20.7 %collective-permute-start.38 = (bf16[384,768]{1,0:T(8,128)(2,1)S(1)}, bf16[384,768]{1,0:T(8,128)(2,1)S(1)}, u32[]{:S(2)}, u32[]{:S(2)}) collective-permute-start(bf16[384,768]{1,0:T(8,128)(2,1)S(1)} %constant_dynamic-update-slice_fusion), channel_id=1, source_target_pairs={{0,16},{8,24},{16,0},{24,8},{1,17},{9,25},{17,1},{25,9},{2,18},{10... | collective-permute-start | bytes 1769480 | tf_op jit(solution)/shard_map/in_near2_b2/ppermute | solution.py:45
  149.0 13.0 %collective-permute-start.44 = (bf16[192,768]{1,0:T(8,128)(2,1)S(1)}, bf16[192,768]{1,0:T(8,128)(2,1)S(1)}, u32[]{:S(2)}, u32[]{:S(2)}) collective-permute-start(bf16[192,768]{1,0:T(8,128)(2,1)S(1)} %collective-permute-done.34.refs_3_), channel_id=1, source_target_pairs={{0,8},{8,0},{16,24},{24,16},{1,9},{9,1},{17,25},{25,17},{2,10},{10... | collective-permute-start | bytes 884744 | tf_op jit(solution)/shard_map/out_far_b1/ppermute | solution.py:45
  149.9 12.9 %collective-permute-start.43 = (bf16[192,768]{1,0:T(8,128)(2,1)S(1)}, bf16[192,768]{1,0:T(8,128)(2,1)S(1)}, u32[]{:S(2)}, u32[]{:S(2)}) collective-permute-start(bf16[192,768]{1,0:T(8,128)(2,1)S(1)} %collective-permute-done.33.refs_3_), channel_id=1, source_target_pairs={{0,16},{8,24},{16,0},{24,8},{1,17},{9,25},{17,1},{25,9},{2,18},{10... | collective-permute-start | bytes 884744 | tf_op jit(solution)/shard_map/in_far_b2/ppermute | solution.py:45
  162.0 23.8 %collective-permute-start.48 = (bf16[384,768]{1,0:T(8,128)(2,1)S(1)}, bf16[384,768]{1,0:T(8,128)(2,1)S(1)}, u32[]{:S(2)}, u32[]{:S(2)}) collective-permute-start(bf16[384,768]{1,0:T(8,128)(2,1)S(1)} %constant_dynamic-update-slice_fusion.6), channel_id=1, source_target_pairs={{0,16},{8,24},{16,0},{24,8},{1,17},{9,25},{17,1},{25,9},{2,18},{10... | collective-permute-start | bytes 1769480 | tf_op jit(solution)/shard_map/out_far2_b2/ppermute | solution.py:45
  162.7 15.3 %collective-permute-start.42 = (bf16[272,576]{1,0:T(8,128)(2,1)S(1)}, bf16[272,576]{1,0:T(8,128)(2,1)S(1)}, u32[]{:S(2)}, u32[]{:S(2)}) collective-permute-start(bf16[272,576]{1,0:T(8,128)(2,1)S(1)} %heads_pair.1.refs_0_), channel_id=1, source_target_pairs={{0,2},{2,0},{4,6},{6,4},{1,3},{3,1},{5,7},{7,5},{8,10},{10,8},{12,... | collective-permute-start | bytes 940040 | tf_op jit(solution)/shard_map/heads_back_z1/ppermute | solution.py:45
  162.9 22.9 %collective-permute-start.47 = (bf16[384,768]{1,0:T(8,128)(2,1)S(1)}, bf16[384,768]{1,0:T(8,128)(2,1)S(1)}, u32[]{:S(2)}, u32[]{:S(2)}) collective-permute-start(bf16[384,768]{1,0:T(8,128)(2,1)S(1)} %constant_dynamic-update-slice_fusion.4), channel_id=1, source_target_pairs={{0,8},{8,0},{16,24},{24,16},{1,9},{9,1},{17,25},{25,17},{2,10},{10... | collective-permute-start | bytes 1769480 | tf_op jit(solution)/shard_map/in_far2_b1/ppermute | solution.py:45
  164.4 21.3 %collective-permute-start.40 = (bf16[896,192]{1,0:T(8,128)(2,1)S(1)}, bf16[896,192]{1,0:T(8,128)(2,1)S(1)}, u32[]{:S(2)}, u32[]{:S(2)}) collective-permute-start(bf16[896,192]{1,0:T(8,128)(2,1)S(1)} %get-tuple-element.196), channel_id=1, source_target_pairs={{0,4},{2,6},{4,0},{6,2},{1,5},{3,7},{5,1},{7,3},{8,12},{10,14},{12... | collective-permute-start | bytes 1032200 | tf_op jit(solution)/shard_map/sends_z2/ppermute | solution.py:45
  187.0 17.6 %collective-permute-start.50 = (bf16[544,576]{1,0:T(8,128)(2,1)S(1)}, bf16[544,576]{1,0:T(8,128)(2,1)S(1)}, u32[]{:S(2)}, u32[]{:S(2)}) collective-permute-start(bf16[544,576]{1,0:T(8,128)(2,1)S(1)} %pad_maximum_fusion.1), channel_id=1, source_target_pairs={{0,8},{8,0},{16,24},{24,16},{1,9},{9,1},{17,25},{25,17},{2,10},{10... | collective-permute-start | bytes 1880072 | tf_op jit(solution)/shard_map/heads_far2_b1/ppermute | solution.py:45
  188.5 16.1 %collective-permute-start.49 = (bf16[544,576]{1,0:T(8,128)(2,1)S(1)}, bf16[544,576]{1,0:T(8,128)(2,1)S(1)}, u32[]{:S(2)}, u32[]{:S(2)}) collective-permute-start(bf16[544,576]{1,0:T(8,128)(2,1)S(1)} %pad_maximum_fusion), channel_id=1, source_target_pairs={{0,16},{8,24},{16,0},{24,8},{1,17},{9,25},{17,1},{25,9},{2,18},{10... | collective-permute-start | bytes 1880072 | tf_op jit(solution)/shard_map/heads_near2_b2/ppermute | solution.py:45
  (37 other events, 452.6 us)

commit v6 on v5

--- a/solution.py
+++ b/solution.py
@@ -1307,20 +1307,8 @@
         name="ffn_near",
     )(ffn, ffn_got)
     gms = list(gms[:1]) + [over_ctx(gms[s], s, "gm") for s in range(1, 4)]
-    (ffn_sent, low) = after((ffn, low), gms[1:])
+    (ffn_sent,) = after((ffn,), gms[1:])
     ffn_got = over_ctx(ffn_sent, 2, "ffn")
-    wo_sum, wo_sent, outs, outs_sent = call(
-        wo_back_kernel,
-        "wo_back",
-        index,
-        [attended, low, act, w_second],
-        [shape((part, width), BF)] * 2 + [shape((2 * rows, width), BF)] * 2,
-        [pltpu.VMEM((width, width), F32)],
-    )
-    outs_got = over_batch(outs_sent, 2, "outs")
-    wo_sum, wo_sent = halving("wo_wt", [(wo_sum, over_wt(wo_sent, "wo"), 0)])
-    wo_sum, wo_sent = halving("wo_near", [(wo_sum, over_batch(wo_sent, 1, "wo"), 0)])
-
     high = 3 * rows + MEM_END
     (qkv, qkv_sent, own_block, near_blocks, far_block) = call(
         functools.partial(heads_back_kernel, heads, hsize),
@@ -1337,6 +1325,19 @@
             pltpu.VMEM((width, wide), BF),
         ],
     )
+    (low,) = after((low,), (qkv,))
+    wo_sum, wo_sent, outs, outs_sent = call(
+        wo_back_kernel,
+        "wo_back",
+        index,
+        [attended, low, act, w_second],
+        [shape((part, width), BF)] * 2 + [shape((2 * rows, width), BF)] * 2,
+        [pltpu.VMEM((width, width), F32)],
+    )
+    outs_got = over_batch(outs_sent, 2, "outs")
+    wo_sum, wo_sent = halving("wo_wt", [(wo_sum, over_wt(wo_sent, "wo"), 0)])
+    wo_sum, wo_sent = halving("wo_near", [(wo_sum, over_batch(wo_sent, 1, "wo"), 0)])
+
     outs, outs_sent = halving("outs_far", [(outs, outs_got, 0)])
     (outs_sent, wo_sent) = after((outs_sent, wo_sent), (outs, wo_sum))
     wo_sum, wo_sent = halving("wo_far", [(wo_sum, over_batch(wo_sent, 2, "wo"), 0)])

time: 209 us -> 207 us (level)
  transfers between devices with their start and end apart: 51 -> 51, of which waited for: 24 -> 24; matrix products, arithmetic and copies ran while one was open for 3% -> 3% of each run, Pallas kernels for 8% -> 9%
where the time goes in v6:
time: 207 us; the launch traced here: 206 us
  waiting for transfers between devices  90.8 us (44%)
  starting transfers between devices  49.5 us (24%)
  Pallas kernels  38.1 us (18%)
  blocking collectives  20.1 us (10%)
  local copies, waits for them, and re-layouts  3.9 us (2%)
  other arithmetic  2.76 us (1%)
    ppermute x51, waiting for transfers between devices, flip(): return lax.ppermute(value, axis, [(i, i ^ step) for i in range(size)])  90.8 us
    ppermute x51, starting transfers between devices, flip(): return lax.ppermute(value, axis, [(i, i ^ step) for i in range(size)])  49.5 us
    pallas_call x9, Pallas kernels, call(): pl.pallas_call(kernel, out_shape=out, in_specs=[smem()] + stay + vmem(len...  27.3 us
    all_gather x1, blocking collectives, paired(): x_all = lax.all_gather(x, 'ctx', axis=0, tiled=True)  20.1 us
    pallas_call x2, Pallas kernels, pieces_out(): pl.pallas_call(kernel, out_shape=shape(dims, F32), in_specs=[smem()] + vm...  5.87 us
  transfers between devices with their start and end apart: 51, of which 24 were waited for; matrix products, arithmetic and copies ran while one was open for 3% of the time, Pallas kernels for 9%

profile of v6, /device:TPU:0, one launch (start us, length us, event | category | flops | bytes accessed | tf_op | source)
XLA Modules:
  0.0 206.5 jit_solution(8687463779872278294)
XLA Ops:
  3.9 2.9 %collective-permute-start.7 = (bf16[128,768]{1,0:T(8,128)(2,1)}, bf16[128,768]{1,0:T(8,128)(2,1)S(1)}, u32[]{:S(2)}, u32[]{:S(2)}) collective-permute-start(bf16[128,768]{1,0:T(8,128)(2,1)} %bitcast.17), channel_id=1, source_target_pairs={{0,8},{8,0},{16,24},{24,16},{1,9},{9,1},{17,25},{25,17},{2,10},{10... | collective-permute-start | bytes 589832 | tf_op jit(solution)/shard_map/g_b1/ppermute | solution.py:45
  6.8 20.1 %all-gather = bf16[1,512,768]{2,1,0:T(8,128)(2,1)S(1)} all-gather(bf16[1,128,768]{2,1,0:T(8,128)(2,1)} %param.14), channel_id=2, replica_groups=mesh['batch'=4,'ctx'=4,'wt'=2] {'ctx'}, dimensions={1}, use_global_device_ids=true | all-gather | bytes 983040 | tf_op jit(solution)/shard_map/all_gather | solution.py:1221
  29.0 5.4 %attend.1 = (bf16[512,768]{1,0:T(8,128)(2,1)S(1)}, bf16[512,192]{1,0:T(8,128)(2,1)S(1)}, bf16[512,192]{1,0:T(8,128)(2,1)S(1)}, bf16[512,192]{1,0:T(8,128)(2,1)S(...) custom-call(s32[3]{0:T(128)S(1)} %pad_add_fusion.idx, ...), custom_call_target="tpu_custom_call" | custom-call | tf_op jit(solution)/shard_map/attend/pallas_call | solution.py:553
  41.3 3.4 %collective-permute-done.5.refs_4_ = bf16[128,192]{1,0:T(8,128)(2,1)S(1)} collective-permute-done((bf16[128,192]{1,0:T(8,128)(2,1)S(1)}, bf16[128,192]{1,0:T(8,128)(2,1)S(1)}, u32[]{:S(2)}, u32[]{:S(2)}) %collective-permute-start.5) | collective-permute-done | bytes 49184 | tf_op jit(solution)/shard_map/mixed_z2/ppermute | solution.py:45
  51.5 5.2 %collective-permute-done.14.refs_7_.refs_3_ = bf16[128,768]{1,0:T(8,128)(2,1)S(1)} collective-permute-done((bf16[128,768]{1,0:T(8,128)(2,1)S(1)}, bf16[128,768]{1,0:T(8,128)(2,1)S(1)}, u32[]{:S(2)}, u32[]{:S(2)}) %collective-permute-start.14) | collective-permute-done | bytes 196640 | tf_op jit(solution)/shard_map/n2_b3/ppermute | solution.py:45
  56.6 3.3 %collective-permute-done.13.refs_6_.refs_2_ = bf16[128,768]{1,0:T(8,128)(2,1)S(1)} collective-permute-done((bf16[128,768]{1,0:T(8,128)(2,1)S(1)}, bf16[128,768]{1,0:T(8,128)(2,1)S(1)}, u32[]{:S(2)}, u32[]{:S(2)}) %collective-permute-start.13) | collective-permute-done | bytes 196640 | tf_op jit(solution)/shard_map/n2_b2/ppermute | solution.py:45
  60.1 5.4 %ffn.1 = (bf16[128,768]{1,0:T(8,128)(2,1)S(1)}, bf16[128,768]{1,0:T(8,128)(2,1)S(1)}, bf16[128,768]{1,0:T(8,128)(2,1)S(1)}, bf16[128,768]{1,0:T(8,128)(2,1)S(1)}...) custom-call(s32[3]{0:T(128)S(1)} %pad_add_fusion.idx, ...), custom_call_target="tpu_custom_call" | custom-call | tf_op jit(solution)/shard_map/ffn/pallas_call | solution.py:553
  71.6 3.9 %collective-permute-done.15.refs_1_ = bf16[128,768]{1,0:T(8,128)(2,1)S(1)} collective-permute-done((bf16[128,768]{1,0:T(8,128)(2,1)S(1)}, bf16[128,768]{1,0:T(8,128)(2,1)S(1)}, u32[]{:S(2)}, u32[]{:S(2)}) %collective-permute-start.15) | collective-permute-done | bytes 196640 | tf_op jit(solution)/shard_map/norm_b1/ppermute | solution.py:45
  75.7 3.8 %collective-permute-done.17.refs_3_ = bf16[128,768]{1,0:T(8,128)(2,1)S(1)} collective-permute-done((bf16[128,768]{1,0:T(8,128)(2,1)S(1)}, bf16[128,768]{1,0:T(8,128)(2,1)S(1)}, u32[]{:S(2)}, u32[]{:S(2)}) %collective-permute-start.17) | collective-permute-done | bytes 196640 | tf_op jit(solution)/shard_map/norm_b3/ppermute | solution.py:45
  85.2 4.8 %collective-permute-done.19.refs_1_ = bf16[128,192]{1,0:T(8,128)(2,1)S(1)} collective-permute-done((bf16[128,192]{1,0:T(8,128)(2,1)S(1)}, bf16[128,192]{1,0:T(8,128)(2,1)S(1)}, u32[]{:S(2)}, u32[]{:S(2)}) %collective-permute-start.19) | collective-permute-done | bytes 49184 | tf_op jit(solution)/shard_map/gm_z1/ppermute | solution.py:45
  90.9 4.4 %attend_back.1 = (bf16[392,576]{1,0:T(8,128)(2,1)S(1)}, bf16[392,576]{1,0:T(8,128)(2,1)S(1)}, bf16[448,192]{1,0:T(8,128)(2,1)S(1)}, bf16[896,192]{1,0:T(8,128)(2,1)S(1)}, bf16[448,192]{1,0:T(8,128)(2,1)S(1)}) custom-call(s32[3]{0:T(128)S(1)} %pad_add_fusion.idx, bf16[128,192]{1,0:T(8,128)(2,1)S(1)} %get-tuple-element.147.refs_0_, ...), custom_call_target="tpu_custom_call" | custom-call | tf_op jit(solution)/shard_map/attend_back/pallas_call | solution.py:553
  101.6 7.2 %collective-permute-done.22.refs_1_ = bf16[256,768]{1,0:T(8,128)(2,1)S(1)} collective-permute-done((bf16[256,768]{1,0:T(8,128)(2,1)S(1)}, bf16[256,768]{1,0:T(8,128)(2,1)S(1)}, u32[]{:S(2)}, u32[]{:S(2)}) %collective-permute-start.22) | collective-permute-done | bytes 393248 | tf_op jit(solution)/shard_map/outs_b2/ppermute | solution.py:45
  111.3 3.4 %collective-permute-done.27.refs_1_ = bf16[200,576]{1,0:T(8,128)(2,1)S(1)} collective-permute-done((bf16[200,576]{1,0:T(8,128)(2,1)S(1)}, bf16[200,576]{1,0:T(8,128)(2,1)S(1)}, u32[]{:S(2)}, u32[]{:S(2)}) %collective-permute-start.27) | collective-permute-done | bytes 230432 | tf_op jit(solution)/shard_map/qkv_b1/ppermute | solution.py:45
  118.2 9.9 %collective-permute-done.30.refs_1_ = bf16[48,768]{1,0:T(8,128)(2,1)S(1)} collective-permute-done((bf16[48,768]{1,0:T(8,128)(2,1)S(1)}, bf16[48,768]{1,0:T(8,128)(2,1)S(1)}, u32[]{:S(2)}, u32[]{:S(2)}) %collective-permute-start.30) | collective-permute-done | bytes 73760 | tf_op jit(solution)/shard_map/wo_z1/ppermute | solution.py:45
  133.4 5.0 %collective-permute-done.36.refs_1_ = bf16[192,768]{1,0:T(8,128)(2,1)S(1)} collective-permute-done((bf16[192,768]{1,0:T(8,128)(2,1)S(1)}, bf16[192,768]{1,0:T(8,128)(2,1)S(1)}, u32[]{:S(2)}, u32[]{:S(2)}) %collective-permute-start.36) | collective-permute-done | bytes 294944 | tf_op jit(solution)/shard_map/out_near_b2/ppermute | solution.py:45
  141.3 4.7 %collective-permute-done.34.refs_3_ = bf16[192,768]{1,0:T(8,128)(2,1)S(1)} collective-permute-done((bf16[192,768]{1,0:T(8,128)(2,1)S(1)}, bf16[192,768]{1,0:T(8,128)(2,1)S(1)}, u32[]{:S(2)}, u32[]{:S(2)}) %collective-permute-start.34) | collective-permute-done | bytes 294944 | tf_op jit(solution)/shard_map/out_back_z1/ppermute | solution.py:45
  149.4 9.8 %collective-permute-done.44.refs_4_ = bf16[192,768]{1,0:T(8,128)(2,1)S(1)} collective-permute-done((bf16[192,768]{1,0:T(8,128)(2,1)S(1)}, bf16[192,768]{1,0:T(8,128)(2,1)S(1)}, u32[]{:S(2)}, u32[]{:S(2)}) %collective-permute-start.44) | collective-permute-done | bytes 294944 | tf_op jit(solution)/shard_map/out_far_b1/ppermute | solution.py:45
  163.8 11.1 %collective-permute-done.42.refs_3_ = bf16[272,576]{1,0:T(8,128)(2,1)S(1)} collective-permute-done((bf16[272,576]{1,0:T(8,128)(2,1)S(1)}, bf16[272,576]{1,0:T(8,128)(2,1)S(1)}, u32[]{:S(2)}, u32[]{:S(2)}) %collective-permute-start.42) | collective-permute-done | bytes 313376 | tf_op jit(solution)/shard_map/heads_back_z1/ppermute | solution.py:45
  176.9 6.5 %collective-permute-done.40.refs_7_ = bf16[896,192]{1,0:T(8,128)(2,1)S(1)} collective-permute-done((bf16[896,192]{1,0:T(8,128)(2,1)S(1)}, bf16[896,192]{1,0:T(8,128)(2,1)S(1)}, u32[]{:S(2)}, u32[]{:S(2)}) %collective-permute-start.40) | collective-permute-done | bytes 344096 | tf_op jit(solution)/shard_map/sends_z2/ppermute | solution.py:45
  188.4 2.9 %rows_out.1 = f32[1536,768]{1,0:T(8,128)} custom-call(s32[3]{0:T(128)S(1)} %pad_add_fusion.idx, bf16[192,768]{1,0:T(8,128)(2,1)S(1)} %get-tuple-element.191.refs_0_, bf16[192,768]{1,0:T(8,128)(2,1)S(1)} %collective-permute-done.36.refs_1_, bf16[384,768]{1,0:T(8,128)(2,1)S(1)} %collective-permute-done.39.refs_2_, ...), custom_call_target="tpu_custom_call" | custom-call | tf_op jit(solution)/shard_map/rows_out/pallas_call | solution.py:1067
  191.3 3.0 %cols_out.1 = f32[384,3072]{1,0:T(8,128)} custom-call(s32[3]{0:T(128)S(1)} %pad_add_fusion.idx, bf16[192,768]{1,0:T(8,128)(2,1)S(1)} %get-tuple-element.190.refs_0_, bf16[192,768]{1,0:T(8,128)(2,1)S(1)} %collective-permute-done.35.refs_1_, bf16[384,768]{1,0:T(8,128)(2,1)S(1)} %collective-permute-done.38.refs_2_, ...), custom_call_target="tpu_custom_call" | custom-call | tf_op jit(solution)/shard_map/cols_out/pallas_call | solution.py:1067
  194.3 2.7 %collective-permute-done.41.refs_8_ = bf16[896,192]{1,0:T(8,128)(2,1)S(1)} collective-permute-done((bf16[896,192]{1,0:T(8,128)(2,1)S(1)}, bf16[896,192]{1,0:T(8,128)(2,1)S(1)}, u32[]{:S(2)}, u32[]{:S(2)}) %collective-permute-start.41) | collective-permute-done | bytes 344096 | tf_op jit(solution)/shard_map/sends_z1/ppermute | solution.py:45
  197.0 4.4 %input_back.1 = (bf16[128,768]{1,0:T(8,128)(2,1)}, f32[20,768]{1,0:T(8,128)S(1)}, f32[20,768]{1,0:T(8,128)S(1)}) custom-call(s32[3]{0:T(128)S(1)} %pad_add_fusion.idx, bf16[384,768]{1,0:T(8,128)(2,1)S(1)} %copy-done.2, bf16[384,768]{1,0:T(8,128)(2,1)S(1)} %copy-done.3, bf16[384,768]{1,0:T(8,128)(2,1)S(1)} %copy-done.4, ...), custom_call_target="tpu_custom_call" | custom-call | tf_op jit(solution)/shard_map/input_back/pallas_call | solution.py:553
  202.7 3.6 %heads_out.1 = (f32[384,768]{1,0:T(8,128)}, f32[384,768]{1,0:T(8,128)}, f32[384,768]{1,0:T(8,128)}, f32[4,4,24,768]{3,2,1,0:T(8,128)}, f32[384]{0:T(512)}, /*index=5*/f32[384]{0:T(512)}, f32[16,12]{1,0:T(8,128)}) custom-call(s32[3]{0:T(128)S(1)} %pad_add_fusion.idx, bf16[272,576]{1,0:T(8,128)(2,1)S(1)} %heads_pair.1.refs_0_, ...), custom_call_target="tpu_custom_call" | custom-call | tf_op jit(solution)/shard_map/heads_out/pallas_call | solution.py:1135
  (147 shorter events, 68.5 us)
Async XLA Ops:
  0.7 28.2 %collective-permute-start = (bf16[384,768]{1,0:T(8,128)(2,1)}, bf16[384,768]{1,0:T(8,128)(2,1)S(1)}, u32[]{:S(2)}, u32[]{:S(2)}) collective-permute-start(bf16[384,768]{1,0:T(8,128)(2,1)} %refs_0_.7), channel_id=1, source_target_pairs={{0,1},{1,0},{2,3},{3,2},{4,5},{5,4},{6,7},{7,6},{8,9},{9,8},{10,11... | collective-permute-start | bytes 1769480 | tf_op jit(solution)/shard_map/weight_w/ppermute | solution.py:45
  1.2 27.7 %collective-permute-start.1 = (bf16[384,768]{1,0:T(8,128)(2,1)}, bf16[384,768]{1,0:T(8,128)(2,1)}, u32[]{:S(2)}, u32[]{:S(2)}) collective-permute-start(bf16[384,768]{1,0:T(8,128)(2,1)} %refs_1_.3), channel_id=1, source_target_pairs={{0,1},{1,0},{2,3},{3,2},{4,5},{5,4},{6,7},{7,6},{8,9},{9,8},{10,11... | collective-permute-start | bytes 1769480 | tf_op jit(solution)/shard_map/weight_w/ppermute | solution.py:45
  1.3 27.6 %collective-permute-start.2 = (bf16[384,768]{1,0:T(8,128)(2,1)}, bf16[384,768]{1,0:T(8,128)(2,1)}, u32[]{:S(2)}, u32[]{:S(2)}) collective-permute-start(bf16[384,768]{1,0:T(8,128)(2,1)} %refs_2_.5), channel_id=1, source_target_pairs={{0,1},{1,0},{2,3},{3,2},{4,5},{5,4},{6,7},{7,6},{8,9},{9,8},{10,11... | collective-permute-start | bytes 1769480 | tf_op jit(solution)/shard_map/weight_w/ppermute | solution.py:45
  3.8 25.1 %collective-permute-start.3 = (bf16[24,384]{1,0:T(8,128)(2,1)S(1)}, bf16[24,384]{1,0:T(8,128)(2,1)S(1)}, u32[]{:S(2)}, u32[]{:S(2)}) collective-permute-start(bf16[24,384]{1,0:T(8,128)(2,1)S(1)} %fusion.2.refs_6_.refs_7_.refs_5_.refs_10_), channel_id=1, source_target_pairs={{0,1},{1,0},{2,3},{3,2},{4,5},{5,4},{6,7},{7,6},{8,9},{9,8},{10,11... | collective-permute-start | bytes 55304 | tf_op jit(solution)/shard_map/small_w/ppermute | solution.py:45
  3.9 24.0 %collective-permute-start.7 = (bf16[128,768]{1,0:T(8,128)(2,1)}, bf16[128,768]{1,0:T(8,128)(2,1)S(1)}, u32[]{:S(2)}, u32[]{:S(2)}) collective-permute-start(bf16[128,768]{1,0:T(8,128)(2,1)} %bitcast.17), channel_id=1, source_target_pairs={{0,8},{8,0},{16,24},{24,16},{1,9},{9,1},{17,25},{25,17},{2,10},{10... | collective-permute-start | bytes 589832 | tf_op jit(solution)/shard_map/g_b1/ppermute | solution.py:45
  47.4 12.7 %collective-permute-start.10 = (bf16[384,3072]{1,0:T(8,128)(2,1)S(1)}, bf16[384,3072]{1,0:T(8,128)(2,1)S(1)}, u32[]{:S(2)}, u32[]{:S(2)}) collective-permute-start(bf16[384,3072]{1,0:T(8,128)(2,1)S(1)} %copy-done), channel_id=1, source_target_pairs={{0,1},{1,0},{2,3},{3,2},{4,5},{5,4},{6,7},{7,6},{8,9},{9,8},{10,11... | collective-permute-start | bytes 7077896 | tf_op jit(solution)/shard_map/in_w/ppermute | solution.py:45
  47.5 12.6 %collective-permute-start.11 = (bf16[1536,768]{1,0:T(8,128)(2,1)S(1)}, bf16[1536,768]{1,0:T(8,128)(2,1)S(1)}, u32[]{:S(2)}, u32[]{:S(2)}) collective-permute-start(bf16[1536,768]{1,0:T(8,128)(2,1)S(1)} %copy-done.5), channel_id=1, source_target_pairs={{0,1},{1,0},{2,3},{3,2},{4,5},{5,4},{6,7},{7,6},{8,9},{9,8},{10,11... | collective-permute-start | bytes 7077896 | tf_op jit(solution)/shard_map/back_w/ppermute | solution.py:45
  71.5 26.9 %collective-permute-start.31 = (bf16[384,768]{1,0:T(8,128)(2,1)S(1)}, bf16[384,768]{1,0:T(8,128)(2,1)S(1)}, u32[]{:S(2)}, u32[]{:S(2)}) collective-permute-start(bf16[384,768]{1,0:T(8,128)(2,1)S(1)} %get-tuple-element.140), channel_id=1, source_target_pairs={{0,2},{2,0},{4,6},{6,4},{1,3},{3,1},{5,7},{7,5},{8,10},{10,8},{12,... | collective-permute-start | bytes 1769480 | tf_op jit(solution)/shard_map/ffn_z1/ppermute | solution.py:45
  98.5 29.6 %collective-permute-start.32 = (bf16[384,768]{1,0:T(8,128)(2,1)S(1)}, bf16[384,768]{1,0:T(8,128)(2,1)S(1)}, u32[]{:S(2)}, u32[]{:S(2)}) collective-permute-start(bf16[384,768]{1,0:T(8,128)(2,1)S(1)} %ffn_near.1.own), channel_id=1, source_target_pairs={{0,4},{2,6},{4,0},{6,2},{1,5},{3,7},{5,1},{7,3},{8,12},{10,14},{12... | collective-permute-start | bytes 1769480 | tf_op jit(solution)/shard_map/ffn_z2/ppermute | solution.py:45
  100.4 14.3 %collective-permute-start.27 = (bf16[200,576]{1,0:T(8,128)(2,1)S(1)}, bf16[200,576]{1,0:T(8,128)(2,1)S(1)}, u32[]{:S(2)}, u32[]{:S(2)}) collective-permute-start(bf16[200,576]{1,0:T(8,128)(2,1)S(1)} %get-tuple-element.178), channel_id=1, source_target_pairs={{0,8},{8,0},{16,24},{24,16},{1,9},{9,1},{17,25},{25,17},{2,10},{10... | collective-permute-start | bytes 691208 | tf_op jit(solution)/shard_map/qkv_b1/ppermute | solution.py:45
  110.3 17.7 %collective-permute-start.25 = (bf16[128,768]{1,0:T(8,128)(2,1)S(1)}, bf16[128,768]{1,0:T(8,128)(2,1)S(1)}, u32[]{:S(2)}, u32[]{:S(2)}) collective-permute-start(bf16[128,768]{1,0:T(8,128)(2,1)S(1)} %get-tuple-element.173), channel_id=1, source_target_pairs={{0,8},{8,0},{16,24},{24,16},{1,9},{9,1},{17,25},{25,17},{2,10},{10... | collective-permute-start | bytes 589832 | tf_op jit(solution)/shard_map/outs_b1/ppermute | solution.py:45
  114.7 13.3 %collective-permute-start.28 = (bf16[104,576]{1,0:T(8,128)(2,1)S(1)}, bf16[104,576]{1,0:T(8,128)(2,1)S(1)}, u32[]{:S(2)}, u32[]{:S(2)}) collective-permute-start(bf16[104,576]{1,0:T(8,128)(2,1)S(1)} %get-tuple-element.180), channel_id=1, source_target_pairs={{0,16},{8,24},{16,0},{24,8},{1,17},{9,25},{17,1},{25,9},{2,18},{10... | collective-permute-start | bytes 359432 | tf_op jit(solution)/shard_map/qkv_b2/ppermute | solution.py:45
  115.9 12.2 %collective-permute-start.30 = (bf16[48,768]{1,0:T(8,128)(2,1)S(1)}, bf16[48,768]{1,0:T(8,128)(2,1)S(1)}, u32[]{:S(2)}, u32[]{:S(2)}) collective-permute-start(bf16[48,768]{1,0:T(8,128)(2,1)S(1)} %get-tuple-element.183), channel_id=1, source_target_pairs={{0,2},{2,0},{4,6},{6,4},{1,3},{3,1},{5,7},{7,5},{8,10},{10,8},{12,... | collective-permute-start | bytes 221192 | tf_op jit(solution)/shard_map/wo_z1/ppermute | solution.py:45
  131.3 14.7 %collective-permute-start.34 = (bf16[192,768]{1,0:T(8,128)(2,1)S(1)}, bf16[192,768]{1,0:T(8,128)(2,1)S(1)}, u32[]{:S(2)}, u32[]{:S(2)}) collective-permute-start(bf16[192,768]{1,0:T(8,128)(2,1)S(1)} %get-tuple-element.191.refs_0_), channel_id=1, source_target_pairs={{0,2},{2,0},{4,6},{6,4},{1,3},{3,1},{5,7},{7,5},{8,10},{10,8},{12,... | collective-permute-start | bytes 884744 | tf_op jit(solution)/shard_map/out_back_z1/ppermute | solution.py:45
  138.4 22.2 %collective-permute-start.39 = (bf16[384,768]{1,0:T(8,128)(2,1)S(1)}, bf16[384,768]{1,0:T(8,128)(2,1)S(1)}, u32[]{:S(2)}, u32[]{:S(2)}) collective-permute-start(bf16[384,768]{1,0:T(8,128)(2,1)S(1)} %constant_dynamic-update-slice_fusion.2), channel_id=1, source_target_pairs={{0,8},{8,0},{16,24},{24,16},{1,9},{9,1},{17,25},{25,17},{2,10},{10... | collective-permute-start | bytes 1769480 | tf_op jit(solution)/shard_map/out_near2_b1/ppermute | solution.py:45
  139.8 20.9 %collective-permute-start.38 = (bf16[384,768]{1,0:T(8,128)(2,1)S(1)}, bf16[384,768]{1,0:T(8,128)(2,1)S(1)}, u32[]{:S(2)}, u32[]{:S(2)}) collective-permute-start(bf16[384,768]{1,0:T(8,128)(2,1)S(1)} %constant_dynamic-update-slice_fusion), channel_id=1, source_target_pairs={{0,16},{8,24},{16,0},{24,8},{1,17},{9,25},{17,1},{25,9},{2,18},{10... | collective-permute-start | bytes 1769480 | tf_op jit(solution)/shard_map/in_near2_b2/ppermute | solution.py:45
  146.0 13.2 %collective-permute-start.44 = (bf16[192,768]{1,0:T(8,128)(2,1)S(1)}, bf16[192,768]{1,0:T(8,128)(2,1)S(1)}, u32[]{:S(2)}, u32[]{:S(2)}) collective-permute-start(bf16[192,768]{1,0:T(8,128)(2,1)S(1)} %collective-permute-done.34.refs_3_), channel_id=1, source_target_pairs={{0,8},{8,0},{16,24},{24,16},{1,9},{9,1},{17,25},{25,17},{2,10},{10... | collective-permute-start | bytes 884744 | tf_op jit(solution)/shard_map/out_far_b1/ppermute | solution.py:45
  147.9 12.9 %collective-permute-start.43 = (bf16[192,768]{1,0:T(8,128)(2,1)S(1)}, bf16[192,768]{1,0:T(8,128)(2,1)S(1)}, u32[]{:S(2)}, u32[]{:S(2)}) collective-permute-start(bf16[192,768]{1,0:T(8,128)(2,1)S(1)} %collective-permute-done.33.refs_3_), channel_id=1, source_target_pairs={{0,16},{8,24},{16,0},{24,8},{1,17},{9,25},{17,1},{25,9},{2,18},{10... | collective-permute-start | bytes 884744 | tf_op jit(solution)/shard_map/in_far_b2/ppermute | solution.py:45
  159.2 24.3 %collective-permute-start.48 = (bf16[384,768]{1,0:T(8,128)(2,1)S(1)}, bf16[384,768]{1,0:T(8,128)(2,1)S(1)}, u32[]{:S(2)}, u32[]{:S(2)}) collective-permute-start(bf16[384,768]{1,0:T(8,128)(2,1)S(1)} %constant_dynamic-update-slice_fusion.6), channel_id=1, source_target_pairs={{0,16},{8,24},{16,0},{24,8},{1,17},{9,25},{17,1},{25,9},{2,18},{10... | collective-permute-start | bytes 1769480 | tf_op jit(solution)/shard_map/out_far2_b2/ppermute | solution.py:45
  160.7 14.2 %collective-permute-start.42 = (bf16[272,576]{1,0:T(8,128)(2,1)S(1)}, bf16[272,576]{1,0:T(8,128)(2,1)S(1)}, u32[]{:S(2)}, u32[]{:S(2)}) collective-permute-start(bf16[272,576]{1,0:T(8,128)(2,1)S(1)} %heads_pair.1.refs_0_), channel_id=1, source_target_pairs={{0,2},{2,0},{4,6},{6,4},{1,3},{3,1},{5,7},{7,5},{8,10},{10,8},{12,... | collective-permute-start | bytes 940040 | tf_op jit(solution)/shard_map/heads_back_z1/ppermute | solution.py:45
  160.8 22.7 %collective-permute-start.47 = (bf16[384,768]{1,0:T(8,128)(2,1)S(1)}, bf16[384,768]{1,0:T(8,128)(2,1)S(1)}, u32[]{:S(2)}, u32[]{:S(2)}) collective-permute-start(bf16[384,768]{1,0:T(8,128)(2,1)S(1)} %constant_dynamic-update-slice_fusion.4), channel_id=1, source_target_pairs={{0,8},{8,0},{16,24},{24,16},{1,9},{9,1},{17,25},{25,17},{2,10},{10... | collective-permute-start | bytes 1769480 | tf_op jit(solution)/shard_map/in_far2_b1/ppermute | solution.py:45
  161.4 22.0 %collective-permute-start.40 = (bf16[896,192]{1,0:T(8,128)(2,1)S(1)}, bf16[896,192]{1,0:T(8,128)(2,1)S(1)}, u32[]{:S(2)}, u32[]{:S(2)}) collective-permute-start(bf16[896,192]{1,0:T(8,128)(2,1)S(1)} %get-tuple-element.196), channel_id=1, source_target_pairs={{0,4},{2,6},{4,0},{6,2},{1,5},{3,7},{5,1},{7,3},{8,12},{10,14},{12... | collective-permute-start | bytes 1032200 | tf_op jit(solution)/shard_map/sends_z2/ppermute | solution.py:45
  184.8 17.9 %collective-permute-start.50 = (bf16[544,576]{1,0:T(8,128)(2,1)S(1)}, bf16[544,576]{1,0:T(8,128)(2,1)S(1)}, u32[]{:S(2)}, u32[]{:S(2)}) collective-permute-start(bf16[544,576]{1,0:T(8,128)(2,1)S(1)} %pad_maximum_fusion.1), channel_id=1, source_target_pairs={{0,8},{8,0},{16,24},{24,16},{1,9},{9,1},{17,25},{25,17},{2,10},{10... | collective-permute-start | bytes 1880072 | tf_op jit(solution)/shard_map/heads_far2_b1/ppermute | solution.py:45
  185.8 16.9 %collective-permute-start.49 = (bf16[544,576]{1,0:T(8,128)(2,1)S(1)}, bf16[544,576]{1,0:T(8,128)(2,1)S(1)}, u32[]{:S(2)}, u32[]{:S(2)}) collective-permute-start(bf16[544,576]{1,0:T(8,128)(2,1)S(1)} %pad_maximum_fusion), channel_id=1, source_target_pairs={{0,16},{8,24},{16,0},{24,8},{1,17},{9,25},{17,1},{25,9},{2,18},{10... | collective-permute-start | bytes 1880072 | tf_op jit(solution)/shard_map/heads_near2_b2/ppermute | solution.py:45
  (37 other events, 454.8 us)

commit v7 on v6

--- a/solution.py
+++ b/solution.py
@@ -1341,7 +1341,6 @@
     outs, outs_sent = halving("outs_far", [(outs, outs_got, 0)])
     (outs_sent, wo_sent) = after((outs_sent, wo_sent), (outs, wo_sum))
     wo_sum, wo_sent = halving("wo_far", [(wo_sum, over_batch(wo_sent, 2, "wo"), 0)])
-    wo_sum, wo_sent = halving("wo_last", [(wo_sum, over_ctx(wo_sent, 1, "wo"), 0)])
     outs_got = over_batch(outs_sent, 1, "outs")
     qkv, qkv_sent = halving("qkv_wt", [(qkv, over_wt(qkv_sent, "qkv"), LINE)])
     qkv, qkv_sent = halving("qkv_near", [(qkv, over_batch(qkv_sent, 1, "qkv"), LINE)])
@@ -1357,6 +1356,8 @@
         far=(w_in,),
     )
 
+    (wo_sent,) = after((wo_sent,), (a1,))
+    wo_sum, wo_sent = halving("wo_last", [(wo_sum, over_ctx(wo_sent, 1, "wo"), 0)])
     def pile(one, two):
         return jnp.concatenate([one, two])
 

time: 207 us -> 206 us (level)
  starting transfers between devices: 49.5 us -> 46.8 us
  waiting for transfers between devices: 90.8 us -> 93.2 us
    ppermute x51, starting transfers between devices: 49.5 us -> 46.8 us  [flip(): return lax.ppermute(value, axis, [(i, i ^ step) for i in range(size)])]
    ppermute x51, waiting for transfers between devices: 90.8 us -> 93.2 us  [flip(): return lax.ppermute(value, axis, [(i, i ^ step) for i in range(size)])]
  transfers between devices with their start and end apart: 51 -> 51, of which waited for: 24 -> 26; matrix products, arithmetic and copies ran while one was open for 3% -> 3% of each run, Pallas kernels for 9% -> 9%
where the time goes in v7:
time: 206 us
  waiting for transfers between devices  93.2 us (45%)
  starting transfers between devices  46.8 us (23%)
  Pallas kernels  38.1 us (18%)
  blocking collectives  20.1 us (10%)
  local copies, waits for them, and re-layouts  3.9 us (2%)
  other arithmetic  2.76 us (1%)
    ppermute x51, waiting for transfers between devices, flip(): return lax.ppermute(value, axis, [(i, i ^ step) for i in range(size)])  93.2 us
    ppermute x51, starting transfers between devices, flip(): return lax.ppermute(value, axis, [(i, i ^ step) for i in range(size)])  46.8 us
    pallas_call x9, Pallas kernels, call(): pl.pallas_call(kernel, out_shape=out, in_specs=[smem()] + stay + vmem(len...  27.3 us
    all_gather x1, blocking collectives, paired(): x_all = lax.all_gather(x, 'ctx', axis=0, tiled=True)  20.1 us
    pallas_call x2, Pallas kernels, pieces_out(): pl.pallas_call(kernel, out_shape=shape(dims, F32), in_specs=[smem()] + vm...  5.87 us
  transfers between devices with their start and end apart: 51, of which 26 were waited for; matrix products, arithmetic and copies ran while one was open for 3% of the time, Pallas kernels for 9%

profile of v7, /device:TPU:0, one launch (start us, length us, event | category | flops | bytes accessed | tf_op | source)
XLA Modules:
  0.0 206.2 jit_solution(15165656096495231787)
XLA Ops:
  3.9 2.9 %collective-permute-start.7 = (bf16[128,768]{1,0:T(8,128)(2,1)}, bf16[128,768]{1,0:T(8,128)(2,1)S(1)}, u32[]{:S(2)}, u32[]{:S(2)}) collective-permute-start(bf16[128,768]{1,0:T(8,128)(2,1)} %bitcast.17), channel_id=1, source_target_pairs={{0,8},{8,0},{16,24},{24,16},{1,9},{9,1},{17,25},{25,17},{2,10},{10... | collective-permute-start | bytes 589832 | tf_op jit(solution)/shard_map/g_b1/ppermute | solution.py:45
  6.8 20.1 %all-gather = bf16[1,512,768]{2,1,0:T(8,128)(2,1)S(1)} all-gather(bf16[1,128,768]{2,1,0:T(8,128)(2,1)} %param.14), channel_id=2, replica_groups=mesh['batch'=4,'ctx'=4,'wt'=2] {'ctx'}, dimensions={1}, use_global_device_ids=true | all-gather | bytes 983040 | tf_op jit(solution)/shard_map/all_gather | solution.py:1221
  29.0 5.4 %attend.1 = (bf16[512,768]{1,0:T(8,128)(2,1)S(1)}, bf16[512,192]{1,0:T(8,128)(2,1)S(1)}, bf16[512,192]{1,0:T(8,128)(2,1)S(1)}, bf16[512,192]{1,0:T(8,128)(2,1)S(...) custom-call(s32[3]{0:T(128)S(1)} %pad_add_fusion.idx, ...), custom_call_target="tpu_custom_call" | custom-call | tf_op jit(solution)/shard_map/attend/pallas_call | solution.py:553
  41.3 3.4 %collective-permute-done.5.refs_4_ = bf16[128,192]{1,0:T(8,128)(2,1)S(1)} collective-permute-done((bf16[128,192]{1,0:T(8,128)(2,1)S(1)}, bf16[128,192]{1,0:T(8,128)(2,1)S(1)}, u32[]{:S(2)}, u32[]{:S(2)}) %collective-permute-start.5) | collective-permute-done | bytes 49184 | tf_op jit(solution)/shard_map/mixed_z2/ppermute | solution.py:45
  51.5 5.2 %collective-permute-done.14.refs_7_.refs_3_ = bf16[128,768]{1,0:T(8,128)(2,1)S(1)} collective-permute-done((bf16[128,768]{1,0:T(8,128)(2,1)S(1)}, bf16[128,768]{1,0:T(8,128)(2,1)S(1)}, u32[]{:S(2)}, u32[]{:S(2)}) %collective-permute-start.14) | collective-permute-done | bytes 196640 | tf_op jit(solution)/shard_map/n2_b3/ppermute | solution.py:45
  56.6 3.3 %collective-permute-done.13.refs_6_.refs_2_ = bf16[128,768]{1,0:T(8,128)(2,1)S(1)} collective-permute-done((bf16[128,768]{1,0:T(8,128)(2,1)S(1)}, bf16[128,768]{1,0:T(8,128)(2,1)S(1)}, u32[]{:S(2)}, u32[]{:S(2)}) %collective-permute-start.13) | collective-permute-done | bytes 196640 | tf_op jit(solution)/shard_map/n2_b2/ppermute | solution.py:45
  60.1 5.4 %ffn.1 = (bf16[128,768]{1,0:T(8,128)(2,1)S(1)}, bf16[128,768]{1,0:T(8,128)(2,1)S(1)}, bf16[128,768]{1,0:T(8,128)(2,1)S(1)}, bf16[128,768]{1,0:T(8,128)(2,1)S(1)}...) custom-call(s32[3]{0:T(128)S(1)} %pad_add_fusion.idx, ...), custom_call_target="tpu_custom_call" | custom-call | tf_op jit(solution)/shard_map/ffn/pallas_call | solution.py:553
  71.6 3.9 %collective-permute-done.15.refs_1_ = bf16[128,768]{1,0:T(8,128)(2,1)S(1)} collective-permute-done((bf16[128,768]{1,0:T(8,128)(2,1)S(1)}, bf16[128,768]{1,0:T(8,128)(2,1)S(1)}, u32[]{:S(2)}, u32[]{:S(2)}) %collective-permute-start.15) | collective-permute-done | bytes 196640 | tf_op jit(solution)/shard_map/norm_b1/ppermute | solution.py:45
  75.7 3.8 %collective-permute-done.17.refs_3_ = bf16[128,768]{1,0:T(8,128)(2,1)S(1)} collective-permute-done((bf16[128,768]{1,0:T(8,128)(2,1)S(1)}, bf16[128,768]{1,0:T(8,128)(2,1)S(1)}, u32[]{:S(2)}, u32[]{:S(2)}) %collective-permute-start.17) | collective-permute-done | bytes 196640 | tf_op jit(solution)/shard_map/norm_b3/ppermute | solution.py:45
  85.2 4.8 %collective-permute-done.19.refs_1_ = bf16[128,192]{1,0:T(8,128)(2,1)S(1)} collective-permute-done((bf16[128,192]{1,0:T(8,128)(2,1)S(1)}, bf16[128,192]{1,0:T(8,128)(2,1)S(1)}, u32[]{:S(2)}, u32[]{:S(2)}) %collective-permute-start.19) | collective-permute-done | bytes 49184 | tf_op jit(solution)/shard_map/gm_z1/ppermute | solution.py:45
  90.9 4.4 %attend_back.1 = (bf16[392,576]{1,0:T(8,128)(2,1)S(1)}, bf16[392,576]{1,0:T(8,128)(2,1)S(1)}, bf16[448,192]{1,0:T(8,128)(2,1)S(1)}, bf16[896,192]{1,0:T(8,128)(2,1)S(1)}, bf16[448,192]{1,0:T(8,128)(2,1)S(1)}) custom-call(s32[3]{0:T(128)S(1)} %pad_add_fusion.idx, bf16[128,192]{1,0:T(8,128)(2,1)S(1)} %get-tuple-element.148.refs_0_, ...), custom_call_target="tpu_custom_call" | custom-call | tf_op jit(solution)/shard_map/attend_back/pallas_call | solution.py:553
  101.6 7.2 %collective-permute-done.22.refs_1_ = bf16[256,768]{1,0:T(8,128)(2,1)S(1)} collective-permute-done((bf16[256,768]{1,0:T(8,128)(2,1)S(1)}, bf16[256,768]{1,0:T(8,128)(2,1)S(1)}, u32[]{:S(2)}, u32[]{:S(2)}) %collective-permute-start.22) | collective-permute-done | bytes 393248 | tf_op jit(solution)/shard_map/outs_b2/ppermute | solution.py:45
  111.3 3.4 %collective-permute-done.27.refs_1_ = bf16[200,576]{1,0:T(8,128)(2,1)S(1)} collective-permute-done((bf16[200,576]{1,0:T(8,128)(2,1)S(1)}, bf16[200,576]{1,0:T(8,128)(2,1)S(1)}, u32[]{:S(2)}, u32[]{:S(2)}) %collective-permute-start.27) | collective-permute-done | bytes 230432 | tf_op jit(solution)/shard_map/qkv_b1/ppermute | solution.py:45
  115.9 3.9 %collective-permute-done.28.qkv2 = bf16[104,576]{1,0:T(8,128)(2,1)S(1)} collective-permute-done((bf16[104,576]{1,0:T(8,128)(2,1)S(1)}, bf16[104,576]{1,0:T(8,128)(2,1)S(1)}, u32[]{:S(2)}, u32[]{:S(2)}) %collective-permute-start.28) | collective-permute-done | bytes 119840 | tf_op jit(solution)/shard_map/qkv_b2/ppermute | solution.py:45
  119.8 6.7 %collective-permute-done.31.got = bf16[384,768]{1,0:T(8,128)(2,1)S(1)} collective-permute-done((bf16[384,768]{1,0:T(8,128)(2,1)S(1)}, bf16[384,768]{1,0:T(8,128)(2,1)S(1)}, u32[]{:S(2)}, u32[]{:S(2)}) %collective-permute-start.31) | collective-permute-done | bytes 589856 | tf_op jit(solution)/shard_map/ffn_z2/ppermute | solution.py:45
  131.7 5.0 %collective-permute-done.35.refs_1_ = bf16[192,768]{1,0:T(8,128)(2,1)S(1)} collective-permute-done((bf16[192,768]{1,0:T(8,128)(2,1)S(1)}, bf16[192,768]{1,0:T(8,128)(2,1)S(1)}, u32[]{:S(2)}, u32[]{:S(2)}) %collective-permute-start.35) | collective-permute-done | bytes 294944 | tf_op jit(solution)/shard_map/in_near_b1/ppermute | solution.py:45
  139.6 5.5 %collective-permute-done.33.refs_3_ = bf16[192,768]{1,0:T(8,128)(2,1)S(1)} collective-permute-done((bf16[192,768]{1,0:T(8,128)(2,1)S(1)}, bf16[192,768]{1,0:T(8,128)(2,1)S(1)}, u32[]{:S(2)}, u32[]{:S(2)}) %collective-permute-start.33) | collective-permute-done | bytes 294944 | tf_op jit(solution)/shard_map/in_back_z1/ppermute | solution.py:45
  148.6 10.1 %collective-permute-done.44.refs_4_ = bf16[192,768]{1,0:T(8,128)(2,1)S(1)} collective-permute-done((bf16[192,768]{1,0:T(8,128)(2,1)S(1)}, bf16[192,768]{1,0:T(8,128)(2,1)S(1)}, u32[]{:S(2)}, u32[]{:S(2)}) %collective-permute-start.44) | collective-permute-done | bytes 294944 | tf_op jit(solution)/shard_map/out_far_b1/ppermute | solution.py:45
  163.4 12.1 %collective-permute-done.42.refs_3_ = bf16[272,576]{1,0:T(8,128)(2,1)S(1)} collective-permute-done((bf16[272,576]{1,0:T(8,128)(2,1)S(1)}, bf16[272,576]{1,0:T(8,128)(2,1)S(1)}, u32[]{:S(2)}, u32[]{:S(2)}) %collective-permute-start.42) | collective-permute-done | bytes 313376 | tf_op jit(solution)/shard_map/heads_back_z1/ppermute | solution.py:45
  177.6 4.7 %collective-permute-done.40.refs_7_ = bf16[896,192]{1,0:T(8,128)(2,1)S(1)} collective-permute-done((bf16[896,192]{1,0:T(8,128)(2,1)S(1)}, bf16[896,192]{1,0:T(8,128)(2,1)S(1)}, u32[]{:S(2)}, u32[]{:S(2)}) %collective-permute-start.40) | collective-permute-done | bytes 344096 | tf_op jit(solution)/shard_map/sends_z2/ppermute | solution.py:45
  190.5 3.0 %cols_out.1 = f32[384,3072]{1,0:T(8,128)} custom-call(s32[3]{0:T(128)S(1)} %pad_add_fusion.idx, bf16[192,768]{1,0:T(8,128)(2,1)S(1)} %get-tuple-element.187.refs_0_, bf16[192,768]{1,0:T(8,128)(2,1)S(1)} %collective-permute-done.35.refs_1_, bf16[384,768]{1,0:T(8,128)(2,1)S(1)} %collective-permute-done.38.refs_2_, ...), custom_call_target="tpu_custom_call" | custom-call | tf_op jit(solution)/shard_map/cols_out/pallas_call | solution.py:1067
  193.5 3.2 %collective-permute-done.41.refs_8_ = bf16[896,192]{1,0:T(8,128)(2,1)S(1)} collective-permute-done((bf16[896,192]{1,0:T(8,128)(2,1)S(1)}, bf16[896,192]{1,0:T(8,128)(2,1)S(1)}, u32[]{:S(2)}, u32[]{:S(2)}) %collective-permute-start.41) | collective-permute-done | bytes 344096 | tf_op jit(solution)/shard_map/sends_z1/ppermute | solution.py:45
  196.6 4.4 %input_back.1 = (bf16[128,768]{1,0:T(8,128)(2,1)}, f32[20,768]{1,0:T(8,128)S(1)}, f32[20,768]{1,0:T(8,128)S(1)}) custom-call(s32[3]{0:T(128)S(1)} %pad_add_fusion.idx, bf16[384,768]{1,0:T(8,128)(2,1)S(1)} %copy-done.2, bf16[384,768]{1,0:T(8,128)(2,1)S(1)} %copy-done.3, bf16[384,768]{1,0:T(8,128)(2,1)S(1)} %copy-done.4, ...), custom_call_target="tpu_custom_call" | custom-call | tf_op jit(solution)/shard_map/input_back/pallas_call | solution.py:553
  202.4 3.6 %heads_out.1 = (f32[384,768]{1,0:T(8,128)}, f32[384,768]{1,0:T(8,128)}, f32[384,768]{1,0:T(8,128)}, f32[4,4,24,768]{3,2,1,0:T(8,128)}, f32[384]{0:T(512)}, /*index=5*/f32[384]{0:T(512)}, f32[16,12]{1,0:T(8,128)}) custom-call(s32[3]{0:T(128)S(1)} %pad_add_fusion.idx, bf16[272,576]{1,0:T(8,128)(2,1)S(1)} %heads_pair.1.refs_0_, ...), custom_call_target="tpu_custom_call" | custom-call | tf_op jit(solution)/shard_map/heads_out/pallas_call | solution.py:1135
  (147 shorter events, 69.6 us)
Async XLA Ops:
  0.7 28.2 %collective-permute-start = (bf16[384,768]{1,0:T(8,128)(2,1)}, bf16[384,768]{1,0:T(8,128)(2,1)S(1)}, u32[]{:S(2)}, u32[]{:S(2)}) collective-permute-start(bf16[384,768]{1,0:T(8,128)(2,1)} %refs_0_.7), channel_id=1, source_target_pairs={{0,1},{1,0},{2,3},{3,2},{4,5},{5,4},{6,7},{7,6},{8,9},{9,8},{10,11... | collective-permute-start | bytes 1769480 | tf_op jit(solution)/shard_map/weight_w/ppermute | solution.py:45
  1.2 27.7 %collective-permute-start.1 = (bf16[384,768]{1,0:T(8,128)(2,1)}, bf16[384,768]{1,0:T(8,128)(2,1)}, u32[]{:S(2)}, u32[]{:S(2)}) collective-permute-start(bf16[384,768]{1,0:T(8,128)(2,1)} %refs_1_.3), channel_id=1, source_target_pairs={{0,1},{1,0},{2,3},{3,2},{4,5},{5,4},{6,7},{7,6},{8,9},{9,8},{10,11... | collective-permute-start | bytes 1769480 | tf_op jit(solution)/shard_map/weight_w/ppermute | solution.py:45
  1.3 27.6 %collective-permute-start.2 = (bf16[384,768]{1,0:T(8,128)(2,1)}, bf16[384,768]{1,0:T(8,128)(2,1)}, u32[]{:S(2)}, u32[]{:S(2)}) collective-permute-start(bf16[384,768]{1,0:T(8,128)(2,1)} %refs_2_.5), channel_id=1, source_target_pairs={{0,1},{1,0},{2,3},{3,2},{4,5},{5,4},{6,7},{7,6},{8,9},{9,8},{10,11... | collective-permute-start | bytes 1769480 | tf_op jit(solution)/shard_map/weight_w/ppermute | solution.py:45
  3.8 25.1 %collective-permute-start.3 = (bf16[24,384]{1,0:T(8,128)(2,1)S(1)}, bf16[24,384]{1,0:T(8,128)(2,1)S(1)}, u32[]{:S(2)}, u32[]{:S(2)}) collective-permute-start(bf16[24,384]{1,0:T(8,128)(2,1)S(1)} %fusion.2.refs_6_.refs_7_.refs_5_.refs_10_), channel_id=1, source_target_pairs={{0,1},{1,0},{2,3},{3,2},{4,5},{5,4},{6,7},{7,6},{8,9},{9,8},{10,11... | collective-permute-start | bytes 55304 | tf_op jit(solution)/shard_map/small_w/ppermute | solution.py:45
  3.9 24.0 %collective-permute-start.7 = (bf16[128,768]{1,0:T(8,128)(2,1)}, bf16[128,768]{1,0:T(8,128)(2,1)S(1)}, u32[]{:S(2)}, u32[]{:S(2)}) collective-permute-start(bf16[128,768]{1,0:T(8,128)(2,1)} %bitcast.17), channel_id=1, source_target_pairs={{0,8},{8,0},{16,24},{24,16},{1,9},{9,1},{17,25},{25,17},{2,10},{10... | collective-permute-start | bytes 589832 | tf_op jit(solution)/shard_map/g_b1/ppermute | solution.py:45
  34.4 11.6 %collective-permute-start.8 = (bf16[384,768]{1,0:T(8,128)(2,1)S(1)}, bf16[384,768]{1,0:T(8,128)(2,1)S(1)}, u32[]{:S(2)}, u32[]{:S(2)}) collective-permute-start(bf16[384,768]{1,0:T(8,128)(2,1)S(1)} %copy-done.7), channel_id=1, source_target_pairs={{0,1},{1,0},{2,3},{3,2},{4,5},{5,4},{6,7},{7,6},{8,9},{9,8},{10,11... | collective-permute-start | bytes 1769480 | tf_op jit(solution)/shard_map/weight_w/ppermute | solution.py:45
  34.5 11.5 %collective-permute-start.9 = (bf16[256,768]{1,0:T(8,128)(2,1)S(1)}, bf16[256,768]{1,0:T(8,128)(2,1)S(1)}, u32[]{:S(2)}, u32[]{:S(2)}) collective-permute-start(bf16[256,768]{1,0:T(8,128)(2,1)S(1)} %pad_maximum_fusion.3), channel_id=1, source_target_pairs={{0,16},{8,24},{16,0},{24,8},{1,17},{9,25},{17,1},{25,9},{2,18},{10... | collective-permute-start | bytes 1179656 | tf_op jit(solution)/shard_map/g_b2/ppermute | solution.py:45
  47.4 12.7 %collective-permute-start.10 = (bf16[384,3072]{1,0:T(8,128)(2,1)S(1)}, bf16[384,3072]{1,0:T(8,128)(2,1)S(1)}, u32[]{:S(2)}, u32[]{:S(2)}) collective-permute-start(bf16[384,3072]{1,0:T(8,128)(2,1)S(1)} %copy-done), channel_id=1, source_target_pairs={{0,1},{1,0},{2,3},{3,2},{4,5},{5,4},{6,7},{7,6},{8,9},{9,8},{10,11... | collective-permute-start | bytes 7077896 | tf_op jit(solution)/shard_map/in_w/ppermute | solution.py:45
  47.5 12.6 %collective-permute-start.11 = (bf16[1536,768]{1,0:T(8,128)(2,1)S(1)}, bf16[1536,768]{1,0:T(8,128)(2,1)S(1)}, u32[]{:S(2)}, u32[]{:S(2)}) collective-permute-start(bf16[1536,768]{1,0:T(8,128)(2,1)S(1)} %copy-done.5), channel_id=1, source_target_pairs={{0,1},{1,0},{2,3},{3,2},{4,5},{5,4},{6,7},{7,6},{8,9},{9,8},{10,11... | collective-permute-start | bytes 7077896 | tf_op jit(solution)/shard_map/back_w/ppermute | solution.py:45
  71.5 26.9 %collective-permute-start.30 = (bf16[384,768]{1,0:T(8,128)(2,1)S(1)}, bf16[384,768]{1,0:T(8,128)(2,1)S(1)}, u32[]{:S(2)}, u32[]{:S(2)}) collective-permute-start(bf16[384,768]{1,0:T(8,128)(2,1)S(1)} %get-tuple-element.141), channel_id=1, source_target_pairs={{0,2},{2,0},{4,6},{6,4},{1,3},{3,1},{5,7},{7,5},{8,10},{10,8},{12,... | collective-permute-start | bytes 1769480 | tf_op jit(solution)/shard_map/ffn_z1/ppermute | solution.py:45
  98.5 28.0 %collective-permute-start.31 = (bf16[384,768]{1,0:T(8,128)(2,1)S(1)}, bf16[384,768]{1,0:T(8,128)(2,1)S(1)}, u32[]{:S(2)}, u32[]{:S(2)}) collective-permute-start(bf16[384,768]{1,0:T(8,128)(2,1)S(1)} %ffn_near.1.own), channel_id=1, source_target_pairs={{0,4},{2,6},{4,0},{6,2},{1,5},{3,7},{5,1},{7,3},{8,12},{10,14},{12... | collective-permute-start | bytes 1769480 | tf_op jit(solution)/shard_map/ffn_z2/ppermute | solution.py:45
  100.4 14.3 %collective-permute-start.27 = (bf16[200,576]{1,0:T(8,128)(2,1)S(1)}, bf16[200,576]{1,0:T(8,128)(2,1)S(1)}, u32[]{:S(2)}, u32[]{:S(2)}) collective-permute-start(bf16[200,576]{1,0:T(8,128)(2,1)S(1)} %get-tuple-element.179), channel_id=1, source_target_pairs={{0,8},{8,0},{16,24},{24,16},{1,9},{9,1},{17,25},{25,17},{2,10},{10... | collective-permute-start | bytes 691208 | tf_op jit(solution)/shard_map/qkv_b1/ppermute | solution.py:45
  129.7 15.5 %collective-permute-start.33 = (bf16[192,768]{1,0:T(8,128)(2,1)S(1)}, bf16[192,768]{1,0:T(8,128)(2,1)S(1)}, u32[]{:S(2)}, u32[]{:S(2)}) collective-permute-start(bf16[192,768]{1,0:T(8,128)(2,1)S(1)} %get-tuple-element.187.refs_0_), channel_id=1, source_target_pairs={{0,2},{2,0},{4,6},{6,4},{1,3},{3,1},{5,7},{7,5},{8,10},{10,8},{12,... | collective-permute-start | bytes 884744 | tf_op jit(solution)/shard_map/in_back_z1/ppermute | solution.py:45
  136.8 22.7 %collective-permute-start.38 = (bf16[384,768]{1,0:T(8,128)(2,1)S(1)}, bf16[384,768]{1,0:T(8,128)(2,1)S(1)}, u32[]{:S(2)}, u32[]{:S(2)}) collective-permute-start(bf16[384,768]{1,0:T(8,128)(2,1)S(1)} %constant_dynamic-update-slice_fusion), channel_id=1, source_target_pairs={{0,16},{8,24},{16,0},{24,8},{1,17},{9,25},{17,1},{25,9},{2,18},{10... | collective-permute-start | bytes 1769480 | tf_op jit(solution)/shard_map/in_near2_b2/ppermute | solution.py:45
  138.2 21.3 %collective-permute-start.39 = (bf16[384,768]{1,0:T(8,128)(2,1)S(1)}, bf16[384,768]{1,0:T(8,128)(2,1)S(1)}, u32[]{:S(2)}, u32[]{:S(2)}) collective-permute-start(bf16[384,768]{1,0:T(8,128)(2,1)S(1)} %constant_dynamic-update-slice_fusion.2), channel_id=1, source_target_pairs={{0,8},{8,0},{16,24},{24,16},{1,9},{9,1},{17,25},{25,17},{2,10},{10... | collective-permute-start | bytes 1769480 | tf_op jit(solution)/shard_map/out_near2_b1/ppermute | solution.py:45
  145.2 13.5 %collective-permute-start.44 = (bf16[192,768]{1,0:T(8,128)(2,1)S(1)}, bf16[192,768]{1,0:T(8,128)(2,1)S(1)}, u32[]{:S(2)}, u32[]{:S(2)}) collective-permute-start(bf16[192,768]{1,0:T(8,128)(2,1)S(1)} %collective-permute-done.34.refs_3_), channel_id=1, source_target_pairs={{0,8},{8,0},{16,24},{24,16},{1,9},{9,1},{17,25},{25,17},{2,10},{10... | collective-permute-start | bytes 884744 | tf_op jit(solution)/shard_map/out_far_b1/ppermute | solution.py:45
  147.1 12.6 %collective-permute-start.43 = (bf16[192,768]{1,0:T(8,128)(2,1)S(1)}, bf16[192,768]{1,0:T(8,128)(2,1)S(1)}, u32[]{:S(2)}, u32[]{:S(2)}) collective-permute-start(bf16[192,768]{1,0:T(8,128)(2,1)S(1)} %collective-permute-done.33.refs_3_), channel_id=1, source_target_pairs={{0,16},{8,24},{16,0},{24,8},{1,17},{9,25},{17,1},{25,9},{2,18},{10... | collective-permute-start | bytes 884744 | tf_op jit(solution)/shard_map/in_far_b2/ppermute | solution.py:45
  147.8 11.7 %collective-permute-start.37 = (bf16[168,576]{1,0:T(8,128)(2,1)S(1)}, bf16[168,576]{1,0:T(8,128)(2,1)S(1)}, u32[]{:S(2)}, u32[]{:S(2)}) collective-permute-start(bf16[168,576]{1,0:T(8,128)(2,1)S(1)} %heads_piece.1.own), channel_id=1, source_target_pairs={{0,4},{2,6},{4,0},{6,2},{1,5},{3,7},{5,1},{7,3},{8,12},{10,14},{12... | collective-permute-start | bytes 580616 | tf_op jit(solution)/shard_map/heads_back_z2/ppermute | solution.py:45
  158.7 23.7 %collective-permute-start.48 = (bf16[384,768]{1,0:T(8,128)(2,1)S(1)}, bf16[384,768]{1,0:T(8,128)(2,1)S(1)}, u32[]{:S(2)}, u32[]{:S(2)}) collective-permute-start(bf16[384,768]{1,0:T(8,128)(2,1)S(1)} %constant_dynamic-update-slice_fusion.6), channel_id=1, source_target_pairs={{0,16},{8,24},{16,0},{24,8},{1,17},{9,25},{17,1},{25,9},{2,18},{10... | collective-permute-start | bytes 1769480 | tf_op jit(solution)/shard_map/out_far2_b2/ppermute | solution.py:45
  159.6 16.0 %collective-permute-start.42 = (bf16[272,576]{1,0:T(8,128)(2,1)S(1)}, bf16[272,576]{1,0:T(8,128)(2,1)S(1)}, u32[]{:S(2)}, u32[]{:S(2)}) collective-permute-start(bf16[272,576]{1,0:T(8,128)(2,1)S(1)} %heads_pair.1.refs_0_), channel_id=1, source_target_pairs={{0,2},{2,0},{4,6},{6,4},{1,3},{3,1},{5,7},{7,5},{8,10},{10,8},{12,... | collective-permute-start | bytes 940040 | tf_op jit(solution)/shard_map/heads_back_z1/ppermute | solution.py:45
  159.7 22.7 %collective-permute-start.47 = (bf16[384,768]{1,0:T(8,128)(2,1)S(1)}, bf16[384,768]{1,0:T(8,128)(2,1)S(1)}, u32[]{:S(2)}, u32[]{:S(2)}) collective-permute-start(bf16[384,768]{1,0:T(8,128)(2,1)S(1)} %constant_dynamic-update-slice_fusion.4), channel_id=1, source_target_pairs={{0,8},{8,0},{16,24},{24,16},{1,9},{9,1},{17,25},{25,17},{2,10},{10... | collective-permute-start | bytes 1769480 | tf_op jit(solution)/shard_map/in_far2_b1/ppermute | solution.py:45
  161.0 21.3 %collective-permute-start.40 = (bf16[896,192]{1,0:T(8,128)(2,1)S(1)}, bf16[896,192]{1,0:T(8,128)(2,1)S(1)}, u32[]{:S(2)}, u32[]{:S(2)}) collective-permute-start(bf16[896,192]{1,0:T(8,128)(2,1)S(1)} %get-tuple-element.198), channel_id=1, source_target_pairs={{0,4},{2,6},{4,0},{6,2},{1,5},{3,7},{5,1},{7,3},{8,12},{10,14},{12... | collective-permute-start | bytes 1032200 | tf_op jit(solution)/shard_map/sends_z2/ppermute | solution.py:45
  184.6 17.8 %collective-permute-start.50 = (bf16[544,576]{1,0:T(8,128)(2,1)S(1)}, bf16[544,576]{1,0:T(8,128)(2,1)S(1)}, u32[]{:S(2)}, u32[]{:S(2)}) collective-permute-start(bf16[544,576]{1,0:T(8,128)(2,1)S(1)} %pad_maximum_fusion.1), channel_id=1, source_target_pairs={{0,8},{8,0},{16,24},{24,16},{1,9},{9,1},{17,25},{25,17},{2,10},{10... | collective-permute-start | bytes 1880072 | tf_op jit(solution)/shard_map/heads_far2_b1/ppermute | solution.py:45
  186.4 16.0 %collective-permute-start.49 = (bf16[544,576]{1,0:T(8,128)(2,1)S(1)}, bf16[544,576]{1,0:T(8,128)(2,1)S(1)}, u32[]{:S(2)}, u32[]{:S(2)}) collective-permute-start(bf16[544,576]{1,0:T(8,128)(2,1)S(1)} %pad_maximum_fusion), channel_id=1, source_target_pairs={{0,16},{8,24},{16,0},{24,8},{1,17},{9,25},{17,1},{25,9},{2,18},{10... | collective-permute-start | bytes 1880072 | tf_op jit(solution)/shard_map/heads_near2_b2/ppermute | solution.py:45
  (37 other events, 443.8 us)

commit v8 on v7

--- a/solution.py
+++ b/solution.py
@@ -1398,7 +1398,7 @@
     f1 = over_ctx(e1, 1, "heads_back")
     (e1, f1) = after((e1, f1), (pile_c, pile_d))
     e2, f2 = over_batch(e1, 1, "heads_near"), over_batch(f1, 2, "heads_far")
-    (e1, e2, f1, f2) = after((e1, e2, f1, f2), (c3, d3, far_pile))
+    (e1, e2, f1, f2) = after((e1, e2, f1, f2), (c3, d3, far_pile, result))
     e3 = over_batch(pile(e1, e2), 2, "heads_near2")
     f3 = over_batch(pile(f1, f2), 1, "heads_far2")
     out_second = pieces_out(

time: 206 us -> 206 us (level)
  no operation moved by 1% of the time
where the time goes in v8:
time: 206 us
  waiting for transfers between devices  93.2 us (45%)
  starting transfers between devices  46.8 us (23%)
  Pallas kernels  38.1 us (18%)
  blocking collectives  20.1 us (10%)
  local copies, waits for them, and re-layouts  3.9 us (2%)
  other arithmetic  2.76 us (1%)
    ppermute x51, waiting for transfers between devices, flip(): return lax.ppermute(value, axis, [(i, i ^ step) for i in range(size)])  93.2 us
    ppermute x51, starting transfers between devices, flip(): return lax.ppermute(value, axis, [(i, i ^ step) for i in range(size)])  46.8 us
    pallas_call x9, Pallas kernels, call(): pl.pallas_call(kernel, out_shape=out, in_specs=[smem()] + stay + vmem(len...  27.3 us
    all_gather x1, blocking collectives, paired(): x_all = lax.all_gather(x, 'ctx', axis=0, tiled=True)  20.1 us
    pallas_call x2, Pallas kernels, pieces_out(): pl.pallas_call(kernel, out_shape=shape(dims, F32), in_specs=[smem()] + vm...  5.87 us
  transfers between devices with their start and end apart: 51, of which 26 were waited for; matrix products, arithmetic and copies ran while one was open for 3% of the time, Pallas kernels for 9%

profile of v8, /device:TPU:0, one launch (start us, length us, event | category | flops | bytes accessed | tf_op | source)
XLA Modules:
  0.0 206.2 jit_solution(1451167913345560818)
XLA Ops:
  3.9 2.9 %collective-permute-start.7 = (bf16[128,768]{1,0:T(8,128)(2,1)}, bf16[128,768]{1,0:T(8,128)(2,1)S(1)}, u32[]{:S(2)}, u32[]{:S(2)}) collective-permute-start(bf16[128,768]{1,0:T(8,128)(2,1)} %bitcast.16), channel_id=1, source_target_pairs={{0,8},{8,0},{16,24},{24,16},{1,9},{9,1},{17,25},{25,17},{2,10},{10... | collective-permute-start | bytes 589832 | tf_op jit(solution)/shard_map/g_b1/ppermute | solution.py:45
  6.8 20.1 %all-gather = bf16[1,512,768]{2,1,0:T(8,128)(2,1)S(1)} all-gather(bf16[1,128,768]{2,1,0:T(8,128)(2,1)} %param.14), channel_id=2, replica_groups=mesh['batch'=4,'ctx'=4,'wt'=2] {'ctx'}, dimensions={1}, use_global_device_ids=true | all-gather | bytes 983040 | tf_op jit(solution)/shard_map/all_gather | solution.py:1221
  29.0 5.4 %attend.1 = (bf16[512,768]{1,0:T(8,128)(2,1)S(1)}, bf16[512,192]{1,0:T(8,128)(2,1)S(1)}, bf16[512,192]{1,0:T(8,128)(2,1)S(1)}, bf16[512,192]{1,0:T(8,128)(2,1)S(...) custom-call(s32[3]{0:T(128)S(1)} %pad_add_fusion.idx, ...), custom_call_target="tpu_custom_call" | custom-call | tf_op jit(solution)/shard_map/attend/pallas_call | solution.py:553
  41.3 3.4 %collective-permute-done.5.refs_4_ = bf16[128,192]{1,0:T(8,128)(2,1)S(1)} collective-permute-done((bf16[128,192]{1,0:T(8,128)(2,1)S(1)}, bf16[128,192]{1,0:T(8,128)(2,1)S(1)}, u32[]{:S(2)}, u32[]{:S(2)}) %collective-permute-start.5) | collective-permute-done | bytes 49184 | tf_op jit(solution)/shard_map/mixed_z2/ppermute | solution.py:45
  51.5 5.2 %collective-permute-done.14.refs_7_.refs_3_ = bf16[128,768]{1,0:T(8,128)(2,1)S(1)} collective-permute-done((bf16[128,768]{1,0:T(8,128)(2,1)S(1)}, bf16[128,768]{1,0:T(8,128)(2,1)S(1)}, u32[]{:S(2)}, u32[]{:S(2)}) %collective-permute-start.14) | collective-permute-done | bytes 196640 | tf_op jit(solution)/shard_map/n2_b3/ppermute | solution.py:45
  56.6 3.3 %collective-permute-done.13.refs_6_.refs_2_ = bf16[128,768]{1,0:T(8,128)(2,1)S(1)} collective-permute-done((bf16[128,768]{1,0:T(8,128)(2,1)S(1)}, bf16[128,768]{1,0:T(8,128)(2,1)S(1)}, u32[]{:S(2)}, u32[]{:S(2)}) %collective-permute-start.13) | collective-permute-done | bytes 196640 | tf_op jit(solution)/shard_map/n2_b2/ppermute | solution.py:45
  60.1 5.4 %ffn.1 = (bf16[128,768]{1,0:T(8,128)(2,1)S(1)}, bf16[128,768]{1,0:T(8,128)(2,1)S(1)}, bf16[128,768]{1,0:T(8,128)(2,1)S(1)}, bf16[128,768]{1,0:T(8,128)(2,1)S(1)}...) custom-call(s32[3]{0:T(128)S(1)} %pad_add_fusion.idx, ...), custom_call_target="tpu_custom_call" | custom-call | tf_op jit(solution)/shard_map/ffn/pallas_call | solution.py:553
  71.6 3.9 %collective-permute-done.15.refs_1_ = bf16[128,768]{1,0:T(8,128)(2,1)S(1)} collective-permute-done((bf16[128,768]{1,0:T(8,128)(2,1)S(1)}, bf16[128,768]{1,0:T(8,128)(2,1)S(1)}, u32[]{:S(2)}, u32[]{:S(2)}) %collective-permute-start.15) | collective-permute-done | bytes 196640 | tf_op jit(solution)/shard_map/norm_b1/ppermute | solution.py:45
  75.7 3.8 %collective-permute-done.17.refs_3_ = bf16[128,768]{1,0:T(8,128)(2,1)S(1)} collective-permute-done((bf16[128,768]{1,0:T(8,128)(2,1)S(1)}, bf16[128,768]{1,0:T(8,128)(2,1)S(1)}, u32[]{:S(2)}, u32[]{:S(2)}) %collective-permute-start.17) | collective-permute-done | bytes 196640 | tf_op jit(solution)/shard_map/norm_b3/ppermute | solution.py:45
  85.2 4.8 %collective-permute-done.19.refs_1_ = bf16[128,192]{1,0:T(8,128)(2,1)S(1)} collective-permute-done((bf16[128,192]{1,0:T(8,128)(2,1)S(1)}, bf16[128,192]{1,0:T(8,128)(2,1)S(1)}, u32[]{:S(2)}, u32[]{:S(2)}) %collective-permute-start.19) | collective-permute-done | bytes 49184 | tf_op jit(solution)/shard_map/gm_z1/ppermute | solution.py:45
  90.9 4.4 %attend_back.1 = (bf16[392,576]{1,0:T(8,128)(2,1)S(1)}, bf16[392,576]{1,0:T(8,128)(2,1)S(1)}, bf16[448,192]{1,0:T(8,128)(2,1)S(1)}, bf16[896,192]{1,0:T(8,128)(2,1)S(1)}, bf16[448,192]{1,0:T(8,128)(2,1)S(1)}) custom-call(s32[3]{0:T(128)S(1)} %pad_add_fusion.idx, bf16[128,192]{1,0:T(8,128)(2,1)S(1)} %get-tuple-element.148.refs_0_, ...), custom_call_target="tpu_custom_call" | custom-call | tf_op jit(solution)/shard_map/attend_back/pallas_call | solution.py:553
  101.6 7.2 %collective-permute-done.22.refs_1_ = bf16[256,768]{1,0:T(8,128)(2,1)S(1)} collective-permute-done((bf16[256,768]{1,0:T(8,128)(2,1)S(1)}, bf16[256,768]{1,0:T(8,128)(2,1)S(1)}, u32[]{:S(2)}, u32[]{:S(2)}) %collective-permute-start.22) | collective-permute-done | bytes 393248 | tf_op jit(solution)/shard_map/outs_b2/ppermute | solution.py:45
  111.3 3.4 %collective-permute-done.27.refs_1_ = bf16[200,576]{1,0:T(8,128)(2,1)S(1)} collective-permute-done((bf16[200,576]{1,0:T(8,128)(2,1)S(1)}, bf16[200,576]{1,0:T(8,128)(2,1)S(1)}, u32[]{:S(2)}, u32[]{:S(2)}) %collective-permute-start.27) | collective-permute-done | bytes 230432 | tf_op jit(solution)/shard_map/qkv_b1/ppermute | solution.py:45
  115.9 3.9 %collective-permute-done.28.qkv2 = bf16[104,576]{1,0:T(8,128)(2,1)S(1)} collective-permute-done((bf16[104,576]{1,0:T(8,128)(2,1)S(1)}, bf16[104,576]{1,0:T(8,128)(2,1)S(1)}, u32[]{:S(2)}, u32[]{:S(2)}) %collective-permute-start.28) | collective-permute-done | bytes 119840 | tf_op jit(solution)/shard_map/qkv_b2/ppermute | solution.py:45
  119.8 6.7 %collective-permute-done.31.got = bf16[384,768]{1,0:T(8,128)(2,1)S(1)} collective-permute-done((bf16[384,768]{1,0:T(8,128)(2,1)S(1)}, bf16[384,768]{1,0:T(8,128)(2,1)S(1)}, u32[]{:S(2)}, u32[]{:S(2)}) %collective-permute-start.31) | collective-permute-done | bytes 589856 | tf_op jit(solution)/shard_map/ffn_z2/ppermute | solution.py:45
  131.7 5.0 %collective-permute-done.35.refs_1_ = bf16[192,768]{1,0:T(8,128)(2,1)S(1)} collective-permute-done((bf16[192,768]{1,0:T(8,128)(2,1)S(1)}, bf16[192,768]{1,0:T(8,128)(2,1)S(1)}, u32[]{:S(2)}, u32[]{:S(2)}) %collective-permute-start.35) | collective-permute-done | bytes 294944 | tf_op jit(solution)/shard_map/in_near_b1/ppermute | solution.py:45
  139.6 5.5 %collective-permute-done.33.refs_3_ = bf16[192,768]{1,0:T(8,128)(2,1)S(1)} collective-permute-done((bf16[192,768]{1,0:T(8,128)(2,1)S(1)}, bf16[192,768]{1,0:T(8,128)(2,1)S(1)}, u32[]{:S(2)}, u32[]{:S(2)}) %collective-permute-start.33) | collective-permute-done | bytes 294944 | tf_op jit(solution)/shard_map/in_back_z1/ppermute | solution.py:45
  148.6 10.1 %collective-permute-done.44.refs_4_ = bf16[192,768]{1,0:T(8,128)(2,1)S(1)} collective-permute-done((bf16[192,768]{1,0:T(8,128)(2,1)S(1)}, bf16[192,768]{1,0:T(8,128)(2,1)S(1)}, u32[]{:S(2)}, u32[]{:S(2)}) %collective-permute-start.44) | collective-permute-done | bytes 294944 | tf_op jit(solution)/shard_map/out_far_b1/ppermute | solution.py:45
  163.4 12.1 %collective-permute-done.42.refs_3_ = bf16[272,576]{1,0:T(8,128)(2,1)S(1)} collective-permute-done((bf16[272,576]{1,0:T(8,128)(2,1)S(1)}, bf16[272,576]{1,0:T(8,128)(2,1)S(1)}, u32[]{:S(2)}, u32[]{:S(2)}) %collective-permute-start.42) | collective-permute-done | bytes 313376 | tf_op jit(solution)/shard_map/heads_back_z1/ppermute | solution.py:45
  178.4 3.9 %collective-permute-done.40.refs_7_ = bf16[896,192]{1,0:T(8,128)(2,1)S(1)} collective-permute-done((bf16[896,192]{1,0:T(8,128)(2,1)S(1)}, bf16[896,192]{1,0:T(8,128)(2,1)S(1)}, u32[]{:S(2)}, u32[]{:S(2)}) %collective-permute-start.40) | collective-permute-done | bytes 344096 | tf_op jit(solution)/shard_map/sends_z2/ppermute | solution.py:45
  189.7 3.0 %cols_out.1 = f32[384,3072]{1,0:T(8,128)} custom-call(s32[3]{0:T(128)S(1)} %pad_add_fusion.idx, bf16[192,768]{1,0:T(8,128)(2,1)S(1)} %get-tuple-element.187.refs_0_, bf16[192,768]{1,0:T(8,128)(2,1)S(1)} %collective-permute-done.35.refs_1_, bf16[384,768]{1,0:T(8,128)(2,1)S(1)} %collective-permute-done.38.refs_2_, ...), custom_call_target="tpu_custom_call" | custom-call | tf_op jit(solution)/shard_map/cols_out/pallas_call | solution.py:1067
  192.7 3.9 %collective-permute-done.41.refs_8_ = bf16[896,192]{1,0:T(8,128)(2,1)S(1)} collective-permute-done((bf16[896,192]{1,0:T(8,128)(2,1)S(1)}, bf16[896,192]{1,0:T(8,128)(2,1)S(1)}, u32[]{:S(2)}, u32[]{:S(2)}) %collective-permute-start.41) | collective-permute-done | bytes 344096 | tf_op jit(solution)/shard_map/sends_z1/ppermute | solution.py:45
  196.6 4.4 %input_back.1 = (bf16[128,768]{1,0:T(8,128)(2,1)}, f32[20,768]{1,0:T(8,128)S(1)}, f32[20,768]{1,0:T(8,128)S(1)}) custom-call(s32[3]{0:T(128)S(1)} %pad_add_fusion.idx, bf16[384,768]{1,0:T(8,128)(2,1)S(1)} %copy-done.2, bf16[384,768]{1,0:T(8,128)(2,1)S(1)} %copy-done.3, bf16[384,768]{1,0:T(8,128)(2,1)S(1)} %copy-done.4, ...), custom_call_target="tpu_custom_call" | custom-call | tf_op jit(solution)/shard_map/input_back/pallas_call | solution.py:553
  202.4 3.6 %heads_out.1 = (f32[384,768]{1,0:T(8,128)}, f32[384,768]{1,0:T(8,128)}, f32[384,768]{1,0:T(8,128)}, f32[4,4,24,768]{3,2,1,0:T(8,128)}, f32[384]{0:T(512)}, /*index=5*/f32[384]{0:T(512)}, f32[16,12]{1,0:T(8,128)}) custom-call(s32[3]{0:T(128)S(1)} %pad_add_fusion.idx, bf16[272,576]{1,0:T(8,128)(2,1)S(1)} %heads_pair.1.refs_0_, ...), custom_call_target="tpu_custom_call" | custom-call | tf_op jit(solution)/shard_map/heads_out/pallas_call | solution.py:1135
  (147 shorter events, 69.6 us)
Async XLA Ops:
  0.7 28.2 %collective-permute-start = (bf16[384,768]{1,0:T(8,128)(2,1)}, bf16[384,768]{1,0:T(8,128)(2,1)S(1)}, u32[]{:S(2)}, u32[]{:S(2)}) collective-permute-start(bf16[384,768]{1,0:T(8,128)(2,1)} %refs_0_.7), channel_id=1, source_target_pairs={{0,1},{1,0},{2,3},{3,2},{4,5},{5,4},{6,7},{7,6},{8,9},{9,8},{10,11... | collective-permute-start | bytes 1769480 | tf_op jit(solution)/shard_map/weight_w/ppermute | solution.py:45
  1.2 27.7 %collective-permute-start.1 = (bf16[384,768]{1,0:T(8,128)(2,1)}, bf16[384,768]{1,0:T(8,128)(2,1)}, u32[]{:S(2)}, u32[]{:S(2)}) collective-permute-start(bf16[384,768]{1,0:T(8,128)(2,1)} %refs_1_.3), channel_id=1, source_target_pairs={{0,1},{1,0},{2,3},{3,2},{4,5},{5,4},{6,7},{7,6},{8,9},{9,8},{10,11... | collective-permute-start | bytes 1769480 | tf_op jit(solution)/shard_map/weight_w/ppermute | solution.py:45
  1.3 27.6 %collective-permute-start.2 = (bf16[384,768]{1,0:T(8,128)(2,1)}, bf16[384,768]{1,0:T(8,128)(2,1)}, u32[]{:S(2)}, u32[]{:S(2)}) collective-permute-start(bf16[384,768]{1,0:T(8,128)(2,1)} %refs_2_.5), channel_id=1, source_target_pairs={{0,1},{1,0},{2,3},{3,2},{4,5},{5,4},{6,7},{7,6},{8,9},{9,8},{10,11... | collective-permute-start | bytes 1769480 | tf_op jit(solution)/shard_map/weight_w/ppermute | solution.py:45
  3.8 25.1 %collective-permute-start.3 = (bf16[24,384]{1,0:T(8,128)(2,1)S(1)}, bf16[24,384]{1,0:T(8,128)(2,1)S(1)}, u32[]{:S(2)}, u32[]{:S(2)}) collective-permute-start(bf16[24,384]{1,0:T(8,128)(2,1)S(1)} %fusion.1.refs_6_.refs_7_.refs_5_.refs_10_), channel_id=1, source_target_pairs={{0,1},{1,0},{2,3},{3,2},{4,5},{5,4},{6,7},{7,6},{8,9},{9,8},{10,11... | collective-permute-start | bytes 55304 | tf_op jit(solution)/shard_map/small_w/ppermute | solution.py:45
  3.9 24.0 %collective-permute-start.7 = (bf16[128,768]{1,0:T(8,128)(2,1)}, bf16[128,768]{1,0:T(8,128)(2,1)S(1)}, u32[]{:S(2)}, u32[]{:S(2)}) collective-permute-start(bf16[128,768]{1,0:T(8,128)(2,1)} %bitcast.16), channel_id=1, source_target_pairs={{0,8},{8,0},{16,24},{24,16},{1,9},{9,1},{17,25},{25,17},{2,10},{10... | collective-permute-start | bytes 589832 | tf_op jit(solution)/shard_map/g_b1/ppermute | solution.py:45
  34.4 11.6 %collective-permute-start.8 = (bf16[384,768]{1,0:T(8,128)(2,1)S(1)}, bf16[384,768]{1,0:T(8,128)(2,1)S(1)}, u32[]{:S(2)}, u32[]{:S(2)}) collective-permute-start(bf16[384,768]{1,0:T(8,128)(2,1)S(1)} %copy-done.7), channel_id=1, source_target_pairs={{0,1},{1,0},{2,3},{3,2},{4,5},{5,4},{6,7},{7,6},{8,9},{9,8},{10,11... | collective-permute-start | bytes 1769480 | tf_op jit(solution)/shard_map/weight_w/ppermute | solution.py:45
  34.5 11.5 %collective-permute-start.9 = (bf16[256,768]{1,0:T(8,128)(2,1)S(1)}, bf16[256,768]{1,0:T(8,128)(2,1)S(1)}, u32[]{:S(2)}, u32[]{:S(2)}) collective-permute-start(bf16[256,768]{1,0:T(8,128)(2,1)S(1)} %pad_maximum_fusion.3), channel_id=1, source_target_pairs={{0,16},{8,24},{16,0},{24,8},{1,17},{9,25},{17,1},{25,9},{2,18},{10... | collective-permute-start | bytes 1179656 | tf_op jit(solution)/shard_map/g_b2/ppermute | solution.py:45
  47.4 12.7 %collective-permute-start.10 = (bf16[384,3072]{1,0:T(8,128)(2,1)S(1)}, bf16[384,3072]{1,0:T(8,128)(2,1)S(1)}, u32[]{:S(2)}, u32[]{:S(2)}) collective-permute-start(bf16[384,3072]{1,0:T(8,128)(2,1)S(1)} %copy-done), channel_id=1, source_target_pairs={{0,1},{1,0},{2,3},{3,2},{4,5},{5,4},{6,7},{7,6},{8,9},{9,8},{10,11... | collective-permute-start | bytes 7077896 | tf_op jit(solution)/shard_map/in_w/ppermute | solution.py:45
  47.5 12.6 %collective-permute-start.11 = (bf16[1536,768]{1,0:T(8,128)(2,1)S(1)}, bf16[1536,768]{1,0:T(8,128)(2,1)S(1)}, u32[]{:S(2)}, u32[]{:S(2)}) collective-permute-start(bf16[1536,768]{1,0:T(8,128)(2,1)S(1)} %copy-done.5), channel_id=1, source_target_pairs={{0,1},{1,0},{2,3},{3,2},{4,5},{5,4},{6,7},{7,6},{8,9},{9,8},{10,11... | collective-permute-start | bytes 7077896 | tf_op jit(solution)/shard_map/back_w/ppermute | solution.py:45
  71.5 26.9 %collective-permute-start.30 = (bf16[384,768]{1,0:T(8,128)(2,1)S(1)}, bf16[384,768]{1,0:T(8,128)(2,1)S(1)}, u32[]{:S(2)}, u32[]{:S(2)}) collective-permute-start(bf16[384,768]{1,0:T(8,128)(2,1)S(1)} %get-tuple-element.141), channel_id=1, source_target_pairs={{0,2},{2,0},{4,6},{6,4},{1,3},{3,1},{5,7},{7,5},{8,10},{10,8},{12,... | collective-permute-start | bytes 1769480 | tf_op jit(solution)/shard_map/ffn_z1/ppermute | solution.py:45
  98.5 28.0 %collective-permute-start.31 = (bf16[384,768]{1,0:T(8,128)(2,1)S(1)}, bf16[384,768]{1,0:T(8,128)(2,1)S(1)}, u32[]{:S(2)}, u32[]{:S(2)}) collective-permute-start(bf16[384,768]{1,0:T(8,128)(2,1)S(1)} %ffn_near.1.own), channel_id=1, source_target_pairs={{0,4},{2,6},{4,0},{6,2},{1,5},{3,7},{5,1},{7,3},{8,12},{10,14},{12... | collective-permute-start | bytes 1769480 | tf_op jit(solution)/shard_map/ffn_z2/ppermute | solution.py:45
  100.4 14.3 %collective-permute-start.27 = (bf16[200,576]{1,0:T(8,128)(2,1)S(1)}, bf16[200,576]{1,0:T(8,128)(2,1)S(1)}, u32[]{:S(2)}, u32[]{:S(2)}) collective-permute-start(bf16[200,576]{1,0:T(8,128)(2,1)S(1)} %get-tuple-element.179), channel_id=1, source_target_pairs={{0,8},{8,0},{16,24},{24,16},{1,9},{9,1},{17,25},{25,17},{2,10},{10... | collective-permute-start | bytes 691208 | tf_op jit(solution)/shard_map/qkv_b1/ppermute | solution.py:45
  129.7 15.5 %collective-permute-start.33 = (bf16[192,768]{1,0:T(8,128)(2,1)S(1)}, bf16[192,768]{1,0:T(8,128)(2,1)S(1)}, u32[]{:S(2)}, u32[]{:S(2)}) collective-permute-start(bf16[192,768]{1,0:T(8,128)(2,1)S(1)} %get-tuple-element.187.refs_0_), channel_id=1, source_target_pairs={{0,2},{2,0},{4,6},{6,4},{1,3},{3,1},{5,7},{7,5},{8,10},{10,8},{12,... | collective-permute-start | bytes 884744 | tf_op jit(solution)/shard_map/in_back_z1/ppermute | solution.py:45
  136.8 22.7 %collective-permute-start.38 = (bf16[384,768]{1,0:T(8,128)(2,1)S(1)}, bf16[384,768]{1,0:T(8,128)(2,1)S(1)}, u32[]{:S(2)}, u32[]{:S(2)}) collective-permute-start(bf16[384,768]{1,0:T(8,128)(2,1)S(1)} %constant_dynamic-update-slice_fusion), channel_id=1, source_target_pairs={{0,16},{8,24},{16,0},{24,8},{1,17},{9,25},{17,1},{25,9},{2,18},{10... | collective-permute-start | bytes 1769480 | tf_op jit(solution)/shard_map/in_near2_b2/ppermute | solution.py:45
  138.2 21.3 %collective-permute-start.39 = (bf16[384,768]{1,0:T(8,128)(2,1)S(1)}, bf16[384,768]{1,0:T(8,128)(2,1)S(1)}, u32[]{:S(2)}, u32[]{:S(2)}) collective-permute-start(bf16[384,768]{1,0:T(8,128)(2,1)S(1)} %constant_dynamic-update-slice_fusion.2), channel_id=1, source_target_pairs={{0,8},{8,0},{16,24},{24,16},{1,9},{9,1},{17,25},{25,17},{2,10},{10... | collective-permute-start | bytes 1769480 | tf_op jit(solution)/shard_map/out_near2_b1/ppermute | solution.py:45
  145.2 13.5 %collective-permute-start.44 = (bf16[192,768]{1,0:T(8,128)(2,1)S(1)}, bf16[192,768]{1,0:T(8,128)(2,1)S(1)}, u32[]{:S(2)}, u32[]{:S(2)}) collective-permute-start(bf16[192,768]{1,0:T(8,128)(2,1)S(1)} %collective-permute-done.34.refs_3_), channel_id=1, source_target_pairs={{0,8},{8,0},{16,24},{24,16},{1,9},{9,1},{17,25},{25,17},{2,10},{10... | collective-permute-start | bytes 884744 | tf_op jit(solution)/shard_map/out_far_b1/ppermute | solution.py:45
  147.1 12.6 %collective-permute-start.43 = (bf16[192,768]{1,0:T(8,128)(2,1)S(1)}, bf16[192,768]{1,0:T(8,128)(2,1)S(1)}, u32[]{:S(2)}, u32[]{:S(2)}) collective-permute-start(bf16[192,768]{1,0:T(8,128)(2,1)S(1)} %collective-permute-done.33.refs_3_), channel_id=1, source_target_pairs={{0,16},{8,24},{16,0},{24,8},{1,17},{9,25},{17,1},{25,9},{2,18},{10... | collective-permute-start | bytes 884744 | tf_op jit(solution)/shard_map/in_far_b2/ppermute | solution.py:45
  147.8 11.7 %collective-permute-start.37 = (bf16[168,576]{1,0:T(8,128)(2,1)S(1)}, bf16[168,576]{1,0:T(8,128)(2,1)S(1)}, u32[]{:S(2)}, u32[]{:S(2)}) collective-permute-start(bf16[168,576]{1,0:T(8,128)(2,1)S(1)} %heads_piece.1.own), channel_id=1, source_target_pairs={{0,4},{2,6},{4,0},{6,2},{1,5},{3,7},{5,1},{7,3},{8,12},{10,14},{12... | collective-permute-start | bytes 580616 | tf_op jit(solution)/shard_map/heads_back_z2/ppermute | solution.py:45
  158.7 23.7 %collective-permute-start.48 = (bf16[384,768]{1,0:T(8,128)(2,1)S(1)}, bf16[384,768]{1,0:T(8,128)(2,1)S(1)}, u32[]{:S(2)}, u32[]{:S(2)}) collective-permute-start(bf16[384,768]{1,0:T(8,128)(2,1)S(1)} %constant_dynamic-update-slice_fusion.6), channel_id=1, source_target_pairs={{0,16},{8,24},{16,0},{24,8},{1,17},{9,25},{17,1},{25,9},{2,18},{10... | collective-permute-start | bytes 1769480 | tf_op jit(solution)/shard_map/out_far2_b2/ppermute | solution.py:45
  159.6 16.0 %collective-permute-start.42 = (bf16[272,576]{1,0:T(8,128)(2,1)S(1)}, bf16[272,576]{1,0:T(8,128)(2,1)S(1)}, u32[]{:S(2)}, u32[]{:S(2)}) collective-permute-start(bf16[272,576]{1,0:T(8,128)(2,1)S(1)} %heads_pair.1.refs_0_), channel_id=1, source_target_pairs={{0,2},{2,0},{4,6},{6,4},{1,3},{3,1},{5,7},{7,5},{8,10},{10,8},{12,... | collective-permute-start | bytes 940040 | tf_op jit(solution)/shard_map/heads_back_z1/ppermute | solution.py:45
  159.7 22.7 %collective-permute-start.47 = (bf16[384,768]{1,0:T(8,128)(2,1)S(1)}, bf16[384,768]{1,0:T(8,128)(2,1)S(1)}, u32[]{:S(2)}, u32[]{:S(2)}) collective-permute-start(bf16[384,768]{1,0:T(8,128)(2,1)S(1)} %constant_dynamic-update-slice_fusion.4), channel_id=1, source_target_pairs={{0,8},{8,0},{16,24},{24,16},{1,9},{9,1},{17,25},{25,17},{2,10},{10... | collective-permute-start | bytes 1769480 | tf_op jit(solution)/shard_map/in_far2_b1/ppermute | solution.py:45
  161.0 21.3 %collective-permute-start.40 = (bf16[896,192]{1,0:T(8,128)(2,1)S(1)}, bf16[896,192]{1,0:T(8,128)(2,1)S(1)}, u32[]{:S(2)}, u32[]{:S(2)}) collective-permute-start(bf16[896,192]{1,0:T(8,128)(2,1)S(1)} %get-tuple-element.198), channel_id=1, source_target_pairs={{0,4},{2,6},{4,0},{6,2},{1,5},{3,7},{5,1},{7,3},{8,12},{10,14},{12... | collective-permute-start | bytes 1032200 | tf_op jit(solution)/shard_map/sends_z2/ppermute | solution.py:45
  184.6 17.8 %collective-permute-start.50 = (bf16[544,576]{1,0:T(8,128)(2,1)S(1)}, bf16[544,576]{1,0:T(8,128)(2,1)S(1)}, u32[]{:S(2)}, u32[]{:S(2)}) collective-permute-start(bf16[544,576]{1,0:T(8,128)(2,1)S(1)} %pad_maximum_fusion.1), channel_id=1, source_target_pairs={{0,8},{8,0},{16,24},{24,16},{1,9},{9,1},{17,25},{25,17},{2,10},{10... | collective-permute-start | bytes 1880072 | tf_op jit(solution)/shard_map/heads_far2_b1/ppermute | solution.py:45
  186.4 16.0 %collective-permute-start.49 = (bf16[544,576]{1,0:T(8,128)(2,1)S(1)}, bf16[544,576]{1,0:T(8,128)(2,1)S(1)}, u32[]{:S(2)}, u32[]{:S(2)}) collective-permute-start(bf16[544,576]{1,0:T(8,128)(2,1)S(1)} %pad_maximum_fusion), channel_id=1, source_target_pairs={{0,16},{8,24},{16,0},{24,8},{1,17},{9,25},{17,1},{25,9},{2,18},{10... | collective-permute-start | bytes 1880072 | tf_op jit(solution)/shard_map/heads_near2_b2/ppermute | solution.py:45
  (37 other events, 443.8 us)
